TPU v7x, 256 devices: a whole 4x4x8 slice. The times are simulated.
256 devices in a mesh: group: 32 (over x, y, core), mp: 8 (over z).
Axes of the slice: x: 4, y: 4, z: 8, core: 2. Of those that a mesh axis runs over, the one named last changes fastest.
Arguments:
- hidden: bfloat16 [16384, 1792], P('group')
- norm_gain: float32 [1792], replicated, may hold values from 0.1 to 1.9
- qkv_weight: bfloat16 [1792, 2304], P(None, 'mp'), may hold values from -0.125 to 0.125
- out_weight: bfloat16 [1792, 1792], P('mp'), may hold values from -0.125 to 0.125
- adapter_down: bfloat16 [1792, 1024], P(None, 'mp'), may hold values from -0.125 to 0.125
- adapter_up: bfloat16 [1024, 1792], P('mp'), may hold values from -1.5 to 1.5
- vocab_rows: bfloat16 [4096, 1792], P(('group', 'mp')), may hold values from -0.125 to 0.125
- segments: int32 [16384], P('group'), may hold values from 0 to 127, never falling along the last dimension, each value on 1 to 512 neighbouring positions
- request_adapter: int32 [128], replicated, may hold values from 0 to 63
- adapter_slot: int32 [64], replicated, may hold values from 0 to 63, each once
- page_table: int32 [2048], replicated, may hold values from 0 to 2047, as said below
Outputs:
- layer_update: bfloat16 [16384, 1792], P('group', 'mp')
- state_norms: float32 [16, 16384], P('mp', 'group')
- max_logits: float32 [16384], P(('group', 'mp'))
Inputs may be any that keep to these rules, and one draw needn't show every extreme that they name: A permutation of all pages. Logical page k of group g (entry g * 64 + k) lies in group page_table[g * 64 + k] // 64, and every group holds exactly two of the logical pages of every group. `segments`: every request's tokens stand together and in order; no request has more than 512 tokens. `adapter_slot`: A permutation.
All inputs are finite; a program needn't handle non-finite values.
Results may differ from a plain program's by a relative error of at most 0.013.
Values may be sent and summed in bfloat16 or wider, within the bound.
A program may use at most 64 MiB of HBM per device.

v0:
```python
import jax
import jax.numpy as jnp
from jax import lax
from jax.sharding import PartitionSpec as P

FEAT = 16
HD = 112
RANK = 16


EPSILON = 1e-05
PRECISE = lax.Precision.HIGHEST


def from_behind(value, axis, by):
    size = lax.axis_size(axis)
    pairs = [(i, i + by) for i in range(size) if 0 <= i + by < size]
    return lax.ppermute(value, axis, pairs)


def rms_normed(values, norm_gain):
    wide = values.astype(jnp.float32)
    meansq = jnp.mean(wide * wide, axis=-1, keepdims=True)
    return (wide * lax.rsqrt(meansq + EPSILON) * norm_gain).astype(jnp.bfloat16)


def features(vectors, feat_width):
    linear_part = vectors / feat_width**0.25
    outer_part = (vectors[..., :, None] * vectors[..., None, :]).reshape(
        vectors.shape[:-1] + (feat_width * feat_width,)
    )
    outer_part = outer_part / (2.0 * feat_width) ** 0.5
    ones_part = jnp.ones(vectors.shape[:-1] + (1,), jnp.float32)
    return jnp.concatenate([ones_part, linear_part, outer_part], axis=-1)


def block_step(state_carry, block_inputs, feat_width):
    states, totals, owner_seg = state_carry
    phi_query, phi_key, query_rows, key_rows, value_rows, seg_ids = block_inputs
    scaling = feat_width ** (-0.5)
    block_len = seg_ids.shape[0]
    position = jnp.arange(block_len, dtype=jnp.int32)
    allowed = (
        (position[:, None] >= position[None, :]) & (seg_ids[:, None] == seg_ids[None, :])
    ).astype(jnp.float32)
    carried = (seg_ids == owner_seg).astype(jnp.float32)[None, :]
    scores = jnp.einsum("hcf,hdf->hcd", query_rows, key_rows, precision=PRECISE) * scaling
    weights = (1.0 + scores + 0.5 * scores * scores) * allowed[None]
    numerator = jnp.einsum("hcd,hde->hce", weights, value_rows, precision=PRECISE)
    numerator = numerator + carried[..., None] * jnp.einsum(
        "hcp,hpe->hce", phi_query, states, precision=PRECISE
    )
    denominator = jnp.sum(weights, axis=-1) + carried * jnp.einsum(
        "hcp,hp->hc", phi_query, totals, precision=PRECISE
    )
    mixed_out = numerator / denominator[..., None]
    key_scores = jnp.einsum("hcf,hdf->hcd", key_rows, key_rows, precision=PRECISE) * scaling
    value_gram = jnp.einsum("hce,hde->hcd", value_rows, value_rows, precision=PRECISE)
    key_gram = (1.0 + key_scores + 0.5 * key_scores * key_scores) * value_gram
    masked_gram = jnp.einsum("cd,hde->hce", allowed, key_gram, precision=PRECISE)
    local_squares = jnp.sum(masked_gram * allowed[None], axis=-1)
    along = jnp.sum(
        jnp.einsum("hcp,hpe->hce", phi_key, states, precision=PRECISE) * value_rows, axis=-1
    )
    cross_squares = jnp.einsum("cd,hd->hc", allowed, along, precision=PRECISE)
    state_squares = jnp.sum(states * states, axis=(1, 2))
    squares = carried * (state_squares[:, None] + 2.0 * cross_squares) + local_squares
    counted = carried * totals[:, :1] + jnp.sum(allowed, axis=-1)[None, :]
    state_norm = jnp.sqrt(squares / (counted * (feat_width * value_rows.shape[-1])))
    last_seg = seg_ids[-1]
    member = (seg_ids == last_seg).astype(jnp.float32)
    continues = (owner_seg == last_seg).astype(jnp.float32)
    new_states = continues * states + jnp.einsum(
        "hcp,hce->hpe", phi_key * member[None, :, None], value_rows, precision=PRECISE
    )
    new_totals = continues * totals + jnp.einsum("hcp,c->hp", phi_key, member, precision=PRECISE)
    return ((new_states, new_totals, last_seg), (mixed_out, state_norm))


def best_of(candidates, piece):
    logits = jnp.einsum("rd,vd->rv", candidates, piece, preferred_element_type=jnp.float32)
    return jnp.max(logits, axis=1)


def on_device(
    hidden,
    norm_gain,
    qkv_weight,
    out_weight,
    adapter_down,
    adapter_up,
    vocab_rows,
    segments,
    request_adapter,
    adapter_slot,
    page_table,
):
    groups = lax.axis_size("group")
    own_group = lax.axis_index("group")
    shards = lax.axis_size("mp")
    own_shard = lax.axis_index("mp")
    rows_here = segments.shape[0]
    model_width = hidden.shape[1]
    slice_width = model_width // shards
    table = page_table.reshape(groups, -1)
    per_group = table.shape[1]
    per_peer = per_group // groups
    page_len = rows_here // per_group
    holders = table // per_group
    position = jnp.arange(per_group, dtype=jnp.int32)
    sort_keys = jnp.where(holders == own_group, position[None, :], per_group + position[None, :])
    ranked = jnp.argsort(sort_keys, axis=1)[:, :per_peer]
    picked = jnp.take_along_axis(table, ranked, axis=1) - own_group * per_group
    outgoing = hidden.reshape(per_group, page_len, model_width)[picked]
    normed_pages = rms_normed(outgoing, norm_gain)
    projected_pages = jnp.einsum(
        "abrd,dc->abrc", normed_pages, qkv_weight, preferred_element_type=jnp.float32
    ).astype(jnp.bfloat16)
    lowered_pages = jnp.einsum(
        "abrd,dc->abrc", normed_pages, adapter_down, preferred_element_type=jnp.float32
    ).astype(jnp.bfloat16)
    kept_pages = lax.dynamic_slice_in_dim(outgoing, own_shard * slice_width, slice_width, 3)
    arrived = (
        lax.all_to_all(kept_pages, "group", split_axis=0, concat_axis=0, tiled=True),
        lax.all_to_all(projected_pages, "group", split_axis=0, concat_axis=0, tiled=True),
        lax.all_to_all(lowered_pages, "group", split_axis=0, concat_axis=0, tiled=True),
    )
    own_holders = lax.dynamic_index_in_dim(holders, own_group, 0, keepdims=False)
    onehot = (own_holders[:, None] == jnp.arange(groups, dtype=jnp.int32)[None, :]).astype(
        jnp.int32
    )
    earlier = jnp.sum((jnp.cumsum(onehot, axis=0) - onehot) * onehot, axis=1)
    source_rows = own_holders * per_peer + earlier

    def placed(received):
        gathered_rows = received.reshape((groups * per_peer,) + received.shape[2:])[source_rows]
        return gathered_rows.reshape((rows_here,) + received.shape[3:])

    residual, projected, lowered = [placed(received) for received in arrived]
    heads_here = projected.shape[1] // (2 * FEAT + HD)
    split_heads = jnp.transpose(
        projected.reshape(rows_here, heads_here, 2 * FEAT + HD).astype(jnp.float32), (1, 0, 2)
    )
    query_rows = split_heads[..., :FEAT]
    key_rows = split_heads[..., FEAT : 2 * FEAT]
    value_rows = split_heads[..., 2 * FEAT :]
    phi_query = features(query_rows, FEAT)
    phi_key = features(key_rows, FEAT)
    last_seg = segments[-1]
    member = (segments == last_seg).astype(jnp.float32)
    end_state = jnp.einsum(
        "hcp,hce->hpe", phi_key * member[None, :, None], value_rows, precision=PRECISE
    )
    end_totals = jnp.einsum("hcp,c->hp", phi_key, member, precision=PRECISE)
    end_tag = jnp.reshape(last_seg + 1, (1,)).astype(jnp.float32)
    got_state, got_totals, got_tag = (
        from_behind(end_state.astype(jnp.bfloat16), "group", 1).astype(end_state.dtype),
        from_behind(end_totals.astype(jnp.bfloat16), "group", 1).astype(end_totals.dtype),
        from_behind(end_tag.astype(jnp.bfloat16), "group", 1).astype(end_tag.dtype),
    )
    initial = (got_state, got_totals, got_tag[0].astype(jnp.int32) - 1)
    block_len = min(256, rows_here)
    blocks = rows_here // block_len

    def regroup(values):
        return jnp.transpose(
            values.reshape(values.shape[0], blocks, block_len, values.shape[-1]), (1, 0, 2, 3)
        )

    scan_inputs = (
        regroup(phi_query),
        regroup(phi_key),
        regroup(query_rows),
        regroup(key_rows),
        regroup(value_rows),
        segments.reshape(blocks, block_len),
    )

    def scan_step(state_carry, block_inputs):
        return block_step(state_carry, block_inputs, FEAT)

    _, (mixed_out, state_norm) = lax.scan(scan_step, initial, scan_inputs)
    attended = (
        jnp.transpose(mixed_out, (0, 2, 1, 3))
        .reshape(rows_here, heads_here * HD)
        .astype(jnp.bfloat16)
    )
    state_norms = jnp.transpose(state_norm, (1, 0, 2)).reshape(heads_here, rows_here)
    request_ids = jnp.arange(request_adapter.shape[0], dtype=jnp.int32)
    adapter_of = jnp.sum(
        jnp.where(segments[:, None] == request_ids[None, :], request_adapter[None, :], 0), axis=1
    )
    adapter_ids = jnp.arange(adapter_slot.shape[0], dtype=jnp.int32)
    slot_ids = jnp.sum(
        jnp.where(adapter_of[:, None] == adapter_ids[None, :], adapter_slot[None, :], 0), axis=1
    )
    column_slot = jnp.arange(lowered.shape[1], dtype=jnp.int32) // RANK
    local_slot = slot_ids - own_shard * (lowered.shape[1] // RANK)
    low_rank = jnp.where(
        local_slot[:, None] == column_slot[None, :], lowered, jnp.zeros_like(lowered)
    )
    partial_value = jnp.dot(attended, out_weight, preferred_element_type=jnp.float32)
    partial_value = partial_value + jnp.dot(
        low_rank, adapter_up, preferred_element_type=jnp.float32
    )
    summed = lax.psum_scatter(
        partial_value.astype(jnp.bfloat16), "mp", scatter_dimension=1, tiled=True
    )
    final_rows = (residual.astype(jnp.float32) + summed.astype(jnp.float32)).astype(jnp.bfloat16)
    own_rows = lax.all_to_all(final_rows, "mp", split_axis=0, concat_axis=1, tiled=True)
    max_logits = best_of(own_rows, lax.all_gather(vocab_rows, ("group", "mp"), axis=0, tiled=True))
    return (summed, state_norms, max_logits)


def solution(mesh):
    placed = (
        P("group", None),
        P(),
        P(None, "mp"),
        P("mp", None),
        P(None, "mp"),
        P("mp", None),
        P(("group", "mp"), None),
        P("group"),
        P(),
        P(),
        P(),
    )
    return jax.shard_map(
        on_device,
        mesh=mesh,
        in_specs=placed,
        out_specs=(P("group", "mp"), P("mp", "group"), P(("group", "mp"))),
        check_vma=False,
    )
```

profile of v0, /device:TPU:8, one launch (start us, length us, event | category | flops | bytes accessed | tf_op | source)
XLA Modules:
  0.0 275.7 jit_solution(12786450912121898422)
XLA Ops:
  8.0 1.4 slice.34
  10.1 2.7 collective-permute-start.2
  12.8 0.8 reshape.237
  13.7 1.0 sort.17
  14.9 0.8 gather_fusion.4
  16.1 1.9 gather_fusion
  18.0 2.0 fusion.49
  20.2 3.0 %fusion.59 = bf16[32,2,8,128]{3,2,1,0:T(8,128)(2,1)} fusion(bf16[32,2,8,1792]{3,2,1,0:T(8,128)(2,1)} %bitcast.226, f32[1792]{0:T(1024)S(1)} %copy-done.19, f32[32,2,8]{2,1,0:T(2,128)S(1)} %copy.95, bf16[1792,128]{1,0:T(8,128)(2,1)} %param.17), kind=kOutput, calls=%fused_computation.84 | convolution fusion | flops 238616576 | bytes 2434048 | tf_op jit(solution)/shard_map/abrd,dc->abrc/dot_general | solution.py:119
  23.2 8.4 %all-to-all-start.1 = ((bf16[32,2,8,128]{3,2,1,0:T(8,128)(2,1)}), bf16[32,2,8,128]{3,2,1,0:T(8,128)(2,1)S(1)}, u32[]{:S(2)}, u32[]{:S(2)}) async-start(bf16[32,2,8,128]{3,2,1,0:T(8,128)(2,1)} %fusion.59), calls=%async_computation.1 | async-start | bytes 262144 | tf_op jit(solution)/shard_map/all_to_all | solution.py:126
  32.4 3.4 %fusion.56 = bf16[32,2,8,288]{3,2,1,0:T(8,128)(2,1)} fusion(bf16[32,2,8,1792]{3,2,1,0:T(8,128)(2,1)} %bitcast.227, f32[1792]{0:T(1024)S(1)} %copy-done.19, f32[32,2,8]{2,1,0:T(2,128)S(1)} %copy.95, bf16[1792,288]{0,1:T(8,128)(2,1)S(1)} %copy-done.18), kind=kOutput, calls=%fused_computation.81 | convolution fusion | flops 532299776 | bytes 3171328 | tf_op jit(solution)/shard_map/abrd,dc->abrc/dot_general | solution.py:116
  37.2 1.1 all-to-all-done.1
  38.3 6.3 %all-to-all-start = ((bf16[32,2,8,288]{3,2,1,0:T(8,128)(2,1)}), bf16[32,2,8,288]{3,2,1,0:T(8,128)(2,1)S(1)}, u32[]{:S(2)}, u32[]{:S(2)}) async-start(bf16[32,2,8,288]{3,2,1,0:T(8,128)(2,1)} %fusion.56), calls=%async_computation | async-start | bytes 786432 | tf_op jit(solution)/shard_map/all_to_all | solution.py:125
  46.5 1.3 gather_fusion.2
  47.8 5.5 %all-to-all-done = bf16[32,2,8,288]{3,2,1,0:T(8,128)(2,1)S(1)} async-done(((bf16[32,2,8,288]{3,2,1,0:T(8,128)(2,1)}), bf16[32,2,8,288]{3,2,1,0:T(8,128)(2,1)S(1)}, u32[]{:S(2)}, u32[]{:S(2)}) %all-to-all-start) | async-done | bytes 294944 | tf_op jit(solution)/shard_map/all_to_all | solution.py:125
  54.6 0.8 copy-done.4
  55.7 1.3 pad_maximum_fusion.1
  57.0 1.3 convolution_convert_fusion
  58.3 2.4 collective-permute-start
  60.8 0.7 fusion.80
  61.5 0.8 copy.114
  62.3 2.7 collective-permute-start.1
  65.0 1.5 bitcast_bitcast_fusion.1
  66.5 1.7 reshape.241
  68.2 0.8 copy.135
  69.6 1.7 reshape.245
  71.3 0.9 convert_element_type.128
  72.2 0.9 convert_element_type.126
  73.1 48.3 %while.21 = (s32[]{:T(128)}, f32[2,273,112]{2,1,0:T(8,128)S(1)}, f32[2,273]{0,1:T(8,128)S(1)}, s32[]{:T(128)}, bf16[2,2,256,112]{2,3,1,0:T(8,128)(2,1)}, /*index...) while((s32[]{:T(128)}, f32[2,273,112]{2,1,0:T(8,128)S(1)}, ...), condition=%wide.region_10.11_spmd, body=%wide.region_4.10_spmd.sunk | while | flops 1377437056 | bytes 16456851 | solution.py:182
  73.8 2.5 constant_dynamic-slice_fusion.7
  76.4 1.5 fusion.142
  77.9 1.3 compare_convert_fusion.5
  79.1 1.3 dynamic-slice.2
  81.1 1.6 convolution_multiply_fusion.6
  83.3 1.7 convolution_add_fusion.3
  85.7 1.0 fusion.134
  87.0 0.8 fusion.135
  87.8 1.1 copy.152
  88.9 1.5 fusion.136
  90.9 0.7 fusion.138
  91.6 2.1 fusion.139
  98.0 2.5 constant_dynamic-slice_fusion.7
  100.5 1.5 fusion.142
  102.0 1.3 compare_convert_fusion.5
  103.3 1.3 dynamic-slice.2
  105.3 1.6 convolution_multiply_fusion.6
  107.5 1.7 convolution_add_fusion.3
  109.9 1.0 fusion.134
  111.1 0.8 fusion.135
  111.9 1.1 copy.152
  113.0 1.5 fusion.136
  115.0 0.7 fusion.138
  115.8 2.1 fusion.139
  118.4 0.7 convolution_multiply_fusion.7
  121.4 1.2 copy.102
  122.7 1.9 fusion.81
  124.6 2.0 add_convert_fusion
  127.3 1.1 constant_dynamic-slice_fusion.3
  128.4 13.8 %all_to_all.34 = bf16[32,2,8,224]{3,2,1,0:T(8,128)(2,1)S(1)} all-to-all(bf16[32,2,8,224]{3,2,1,0:T(8,128)(2,1)S(1)} %constant_dynamic-slice_fusion.3), channel_id=1, replica_groups=mesh['group'=32,'mp'=8] {'group'}, dimensions={0} | all-to-all | bytes 458752 | tf_op jit(solution)/shard_map/all_to_all | solution.py:124
  142.2 0.7 gather_fusion.3
  143.2 27.1 %reduce-scatter.2.cloned.1.call-done = bf16[512,224]{0,1:T(8,128)(2,1)} async-done(((bf16[512,1792]{0,1:T(8,128)(2,1)}), bf16[512,224]{0,1:T(8,128)(2,1)}) %reduce-scatter.2.cloned.1.call-update) | async-done | bytes 229392 | tf_op jit(solution)/shard_map/reduce_scatter | solution.py:206
  170.3 1.0 add_convert_fusion.1
  171.5 14.7 %all_to_all.35 = bf16[8,64,224]{2,1,0:T(8,128)(2,1)S(1)} all-to-all(bf16[8,64,224]{2,1,0:T(8,128)(2,1)S(1)} %bitcast.244), channel_id=1, replica_groups=mesh['group'=32,'mp'=8] {'mp'}, dimensions={0} | all-to-all | bytes 458752 | tf_op jit(solution)/shard_map/all_to_all | solution.py:210
  186.6 71.4 %all-gather.2.cloned.1.call-done = bf16[4096,1792]{1,0:T(8,128)(2,1)} async-done(((bf16[16,1792]{1,0:T(8,128)(2,1)}), bf16[4096,1792]{1,0:T(8,128)(2,1)}) %all-gather.2.cloned.1.call-update) | async-done | bytes 14680080 | tf_op jit(solution)/shard_map/all_gather | solution.py:211
  258.0 10.3 %convolution_reduce_fusion = f32[64]{0:T(128)} fusion(bf16[64,1792]{1,0:T(8,128)(2,1)S(1)} %all_to_all.29, bf16[4096,1792]{1,0:T(8,128)(2,1)} %all-gather.2.cloned.1.call-done), kind=kOutput, calls=%fused_computation.82 | convolution fusion | flops 939786176 | bytes 14909696 | tf_op jit(solution)/shard_map/rd,vd->rv/dot_general | solution.py:81
  (139 shorter events, 18.2 us)
Async XLA Ops:
  8.0 8.1 %copy-start = (bf16[512,1792]{1,0:T(8,128)(2,1)S(1)}, bf16[512,1792]{1,0:T(8,128)(2,1)}, u32[]{:S(2)}) copy-start(bf16[512,1792]{1,0:T(8,128)(2,1)} %param.13) | copy-start | bytes 5505028
  10.1 35.7 %collective-permute-start.2 = (bf16[1]{0:T(256)(128)(2,1)}, bf16[1]{0:T(256)(128)(2,1)}, u32[]{:S(2)}, u32[]{:S(2)}) collective-permute-start(bf16[1]{0:T(256)(128)(2,1)} %bitcast.30), channel_id=1, source_target_pairs={{0,8},{8,16},{16,24},{24,32},{32,40},{40,48},{48,56},{56,64},{64,7... | collective-permute-start | bytes 14 | tf_op jit(solution)/shard_map/ppermute | solution.py:18
  18.0 2.1 copy-start.19
  20.2 11.5 %copy-start.11 = (s32[512]{0:T(512)S(1)}, s32[512]{0:T(512)}, u32[]{:S(2)}) copy-start(s32[512]{0:T(512)} %param.20) | copy-start | bytes 6148
  20.2 12.1 %copy-start.18 = (bf16[1792,288]{0,1:T(8,128)(2,1)S(1)}, bf16[1792,288]{0,1:T(8,128)(2,1)}, u32[]{:S(2)}) copy-start(bf16[1792,288]{0,1:T(8,128)(2,1)} %param.15) | copy-start | bytes 3096580
  23.2 15.0 %all-to-all-start.1 = ((bf16[32,2,8,128]{3,2,1,0:T(8,128)(2,1)}), bf16[32,2,8,128]{3,2,1,0:T(8,128)(2,1)S(1)}, u32[]{:S(2)}, u32[]{:S(2)}) async-start(bf16[32,2,8,128]{3,2,1,0:T(8,128)(2,1)} %fusion.59), calls=%async_computation.1 | async-start | bytes 262144 | tf_op jit(solution)/shard_map/all_to_all | solution.py:126
  32.3 3.8 %copy-start.16 = (s32[128]{0:T(128)S(1)}, s32[128]{0:T(128)}, u32[]{:S(2)}) copy-start(s32[128]{0:T(128)} %param.21) | copy-start | bytes 1540
  32.3 4.7 %copy-start.17 = (s32[64]{0:T(128)S(1)}, s32[64]{0:T(128)}, u32[]{:S(2)}) copy-start(s32[64]{0:T(128)} %param.22) | copy-start | bytes 772
  36.4 18.2 %copy-start.14 = (s32[1024]{0:T(1024)}, s32[1024]{0:T(1024)S(1)}, u32[]{:S(2)}) copy-start(s32[1024]{0:T(1024)S(1)} %pad_clamp_fusion) | copy-start | bytes 12292
  38.3 15.0 %all-to-all-start = ((bf16[32,2,8,288]{3,2,1,0:T(8,128)(2,1)}), bf16[32,2,8,288]{3,2,1,0:T(8,128)(2,1)S(1)}, u32[]{:S(2)}, u32[]{:S(2)}) async-start(bf16[32,2,8,288]{3,2,1,0:T(8,128)(2,1)} %fusion.56), calls=%async_computation | async-start | bytes 786432 | tf_op jit(solution)/shard_map/all_to_all | solution.py:125
  44.6 125.8 %reduce-scatter.2.cloned.1.call-start = ((), (), s32[]{:S(2)}) async-start(), calls=%async_computation.5 | async-start | bytes 2064384 | tf_op jit(solution)/shard_map/reduce_scatter | solution.py:206
  54.6 0.8 copy-start.4
  54.6 2.4 copy-start.5
  58.3 13.9 %collective-permute-start = (bf16[2,273,112]{2,1,0:T(8,128)(2,1)}, bf16[2,273,112]{2,1,0:T(8,128)(2,1)}, u32[]{:S(2)}, u32[]{:S(2)}) collective-permute-start(bf16[2,273,112]{2,1,0:T(8,128)(2,1)} %convolution_convert_fusion), channel_id=1, source_target_pairs={{0,8},{8,16},{16,24},{24,32},{32,40},{40,48},{48,56},{56,64},{64,7... | collective-permute-start | bytes 366920 | tf_op jit(solution)/shard_map/ppermute | solution.py:18
  61.5 6.7 %slice-start = ((f32[2,512,144]{1,2,0:T(8,128)}), f32[2,512,112]{1,2,0:T(8,128)S(1)}, s32[]{:S(2)}) async-start(f32[2,512,144]{1,2,0:T(8,128)} %copy-done.4), calls=%async_computation.7 | async-start | bytes 917504 | tf_op jit(solution)/shard_map/slice | solution.py:146
  62.3 9.0 %collective-permute-start.1 = (bf16[2,273]{0,1:T(8,128)(2,1)}, bf16[2,273]{0,1:T(8,128)(2,1)}, u32[]{:S(2)}, u32[]{:S(2)}) collective-permute-start(bf16[2,273]{0,1:T(8,128)(2,1)} %bitcast.250), channel_id=1, source_target_pairs={{0,8},{8,16},{16,24},{24,32},{32,40},{40,48},{48,56},{56,64},{64,7... | collective-permute-start | bytes 3284 | tf_op jit(solution)/shard_map/ppermute | solution.py:18
  68.2 1.4 copy-start.3
  73.2 3.2 %copy-start.1 = (f32[2,2,256,112]{2,3,1,0:T(8,128)S(1)}, f32[2,2,256,112]{2,3,1,0:T(8,128)}, u32[]{:S(2)}) copy-start(f32[2,2,256,112]{2,3,1,0:T(8,128)} %get-tuple-element.408) | copy-start | bytes 1376260 | tf_op jit(solution)/shard_map/while
  86.8 4.8 %copy-start.2 = (f32[2,2,256,112]{2,3,1,0:T(8,128)S(1)}, f32[2,2,256,112]{2,3,1,0:T(8,128)}, u32[]{:S(2)}) copy-start(f32[2,2,256,112]{2,3,1,0:T(8,128)} %get-tuple-element.408) | copy-start | bytes 1376260 | tf_op jit(solution)/shard_map/while
  88.9 4.8 %copy-start.6 = (f32[2,2,256,16]{2,3,1,0:T(8,128)S(1)}, f32[2,2,256,16]{2,3,1,0:T(8,128)}, u32[]{:S(2)}) copy-start(f32[2,2,256,16]{2,3,1,0:T(8,128)} %get-tuple-element.410) | copy-start | bytes 196612 | tf_op jit(solution)/shard_map/while
  91.6 4.1 %copy-start.9 = (f32[1,256]{1,0:T(1,128)S(1)}, f32[1,256]{1,0:T(1,128)}, u32[]{:S(2)}) copy-start(f32[1,256]{1,0:T(1,128)} %get-tuple-element.369) | copy-start | bytes 3076 | tf_op jit(solution)/shard_map/while
  91.6 4.1 %copy-start.10 = (f32[2,256]{1,0:T(2,128)S(1)}, f32[2,256]{1,0:T(2,128)}, u32[]{:S(2)}) copy-start(f32[2,256]{1,0:T(2,128)} %fusion.142) | copy-start | bytes 6148 | tf_op jit(solution)/shard_map/while
  91.6 4.1 %copy-start.12 = (f32[2]{0:T(128)S(1)}, f32[2]{0:T(128)}, u32[]{:S(2)}) copy-start(f32[2]{0:T(128)} %multiply_reduce_fusion.2) | copy-start | bytes 28 | tf_op jit(solution)/shard_map/while
  91.6 4.1 %copy-start.20 = (f32[2,2,256]{2,1,0:T(2,128)S(1)}, f32[2,2,256]{2,1,0:T(2,128)}, u32[]{:S(2)}) copy-start(f32[2,2,256]{2,1,0:T(2,128)} %get-tuple-element.390) | copy-start | bytes 12292 | tf_op jit(solution)/shard_map/while
  91.6 4.1 %copy-start.22 = (f32[2]{0:T(128)S(1)}, f32[2]{0:T(128)}, u32[]{:S(2)}) copy-start(f32[2]{0:T(128)} %slice_bitcast_fusion.2) | copy-start | bytes 28 | tf_op jit(solution)/shard_map/while
  96.0 0.6 copy-start.21
  97.3 3.2 %copy-start.1 = (f32[2,2,256,112]{2,3,1,0:T(8,128)S(1)}, f32[2,2,256,112]{2,3,1,0:T(8,128)}, u32[]{:S(2)}) copy-start(f32[2,2,256,112]{2,3,1,0:T(8,128)} %get-tuple-element.408) | copy-start | bytes 1376260 | tf_op jit(solution)/shard_map/while
  110.9 4.8 %copy-start.2 = (f32[2,2,256,112]{2,3,1,0:T(8,128)S(1)}, f32[2,2,256,112]{2,3,1,0:T(8,128)}, u32[]{:S(2)}) copy-start(f32[2,2,256,112]{2,3,1,0:T(8,128)} %get-tuple-element.408) | copy-start | bytes 1376260 | tf_op jit(solution)/shard_map/while
  113.0 4.8 %copy-start.6 = (f32[2,2,256,16]{2,3,1,0:T(8,128)S(1)}, f32[2,2,256,16]{2,3,1,0:T(8,128)}, u32[]{:S(2)}) copy-start(f32[2,2,256,16]{2,3,1,0:T(8,128)} %get-tuple-element.410) | copy-start | bytes 196612 | tf_op jit(solution)/shard_map/while
  115.7 4.1 %copy-start.9 = (f32[1,256]{1,0:T(1,128)S(1)}, f32[1,256]{1,0:T(1,128)}, u32[]{:S(2)}) copy-start(f32[1,256]{1,0:T(1,128)} %get-tuple-element.369) | copy-start | bytes 3076 | tf_op jit(solution)/shard_map/while
  115.7 4.1 %copy-start.10 = (f32[2,256]{1,0:T(2,128)S(1)}, f32[2,256]{1,0:T(2,128)}, u32[]{:S(2)}) copy-start(f32[2,256]{1,0:T(2,128)} %fusion.142) | copy-start | bytes 6148 | tf_op jit(solution)/shard_map/while
  115.7 4.1 %copy-start.12 = (f32[2]{0:T(128)S(1)}, f32[2]{0:T(128)}, u32[]{:S(2)}) copy-start(f32[2]{0:T(128)} %multiply_reduce_fusion.2) | copy-start | bytes 28 | tf_op jit(solution)/shard_map/while
  115.7 4.1 %copy-start.20 = (f32[2,2,256]{2,1,0:T(2,128)S(1)}, f32[2,2,256]{2,1,0:T(2,128)}, u32[]{:S(2)}) copy-start(f32[2,2,256]{2,1,0:T(2,128)} %get-tuple-element.390) | copy-start | bytes 12292 | tf_op jit(solution)/shard_map/while
  115.7 4.1 %copy-start.22 = (f32[2]{0:T(128)S(1)}, f32[2]{0:T(128)}, u32[]{:S(2)}) copy-start(f32[2]{0:T(128)} %slice_bitcast_fusion.2) | copy-start | bytes 28 | tf_op jit(solution)/shard_map/while
  120.2 0.6 copy-start.21
  122.7 1.9 copy-start.7
  122.7 1.9 copy-start.8
  122.7 1.9 copy-start.13
  122.7 1.9 copy-start.15
  126.7 131.3 %all-gather.2.cloned.1.call-start = ((), (), s32[]{:S(2)}) async-start(), calls=%async_computation.6 | async-start | bytes 14737408 | tf_op jit(solution)/shard_map/all_gather | solution.py:211
Sparse Core Ops, SparseCore 0:
  126.8 43.4 reduce-scatter.1
Sparse Core Ops, SparseCore 1:
  130.7 127.2 all-gather.1
where the time goes:
time: 278 us; the launch traced here: 276 us
  waiting for transfers between devices  106 us (38%)
  matrix products  46.6 us (17%)
  local copies, waits for them, and re-layouts  33.4 us (12%)
  blocking collectives  28.5 us (10%)
  starting transfers between devices  22.7 us (8%)
  other arithmetic  18.6 us (7%)
  between operations  17.3 us (6%)
  loops' own time  2.95 us (1%)
    all_gather x1, waiting for transfers between devices, on_device(): lax.all_gather(vocab_rows, ('group', 'mp'), axis=0, tiled=True)  71.4 us
    reduce_scatter x1, waiting for transfers between devices, on_device(): lax.psum_scatter(partial_value.astype(jnp.bfloat16), 'mp', scatter_dimens...  27.1 us
    all_to_all x1, blocking collectives, on_device(): lax.all_to_all(final_rows, 'mp', split_axis=0, concat_axis=1, tiled=True)  14.7 us
    all_to_all x1, blocking collectives, on_device(): lax.all_to_all(kept_pages, 'group', split_axis=0, concat_axis=0, tiled=True)  13.8 us
    dot_general x1, matrix products, best_of(): jnp.einsum('rd,vd->rv', candidates, piece, preferred_element_type=jnp.flo...  10.3 us
    all_to_all x1, starting transfers between devices, on_device(): lax.all_to_all(lowered_pages, 'group', split_axis=0, concat_axis=0, tiled...  8.43 us
    ppermute x3, starting transfers between devices, from_behind(): return lax.ppermute(value, axis, pairs)  7.88 us
    all_to_all x1, starting transfers between devices, on_device(): lax.all_to_all(projected_pages, 'group', split_axis=0, concat_axis=0, til...  6.3 us
  transfers between devices with their start and end apart: 7, of which 4 were waited for; matrix products, arithmetic and copies ran while one was open for 11% of the time, Pallas kernels for 0%

commit v1 on v0

--- a/solution.py
+++ b/solution.py
@@ -137,6 +137,8 @@
         return gathered_rows.reshape((rows_here,) + received.shape[3:])
 
     residual, projected, lowered = [placed(received) for received in arrived]
+    group_vocab = lax.all_gather(vocab_rows, "group", axis=0, tiled=True)
+    group_vocab, projected = lax.optimization_barrier((group_vocab, projected))
     heads_here = projected.shape[1] // (2 * FEAT + HD)
     split_heads = jnp.transpose(
         projected.reshape(rows_here, heads_here, 2 * FEAT + HD).astype(jnp.float32), (1, 0, 2)
@@ -207,8 +209,11 @@
         partial_value.astype(jnp.bfloat16), "mp", scatter_dimension=1, tiled=True
     )
     final_rows = (residual.astype(jnp.float32) + summed.astype(jnp.float32)).astype(jnp.bfloat16)
-    own_rows = lax.all_to_all(final_rows, "mp", split_axis=0, concat_axis=1, tiled=True)
-    max_logits = best_of(own_rows, lax.all_gather(vocab_rows, ("group", "mp"), axis=0, tiled=True))
+    group_rows = lax.all_gather(final_rows, "mp", axis=1, tiled=True)
+    partial_best = best_of(group_rows, group_vocab)
+    max_logits = lax.dynamic_slice_in_dim(
+        lax.pmax(partial_best, "mp"), own_shard * (rows_here // shards), rows_here // shards
+    )
     return (summed, state_norms, max_logits)
 
 

time: 278 us -> 223 us (0.80)
  waiting for transfers between devices: 106 us -> 84.2 us
  matrix products: 46.6 us -> 31.4 us
  local copies, waits for them, and re-layouts: 33.4 us -> 23.3 us
  other arithmetic: 18.6 us -> 12.4 us
    all_gather x1 -> x2, waiting for transfers between devices: 71.4 us -> 48.6 us  [the longest x1 39.5 us: on_device(): group_rows = lax.all_gather(final_rows, 'mp', axis=1, tiled=True)]
    pmax x0 -> x1, blocking collectives: none -> 16.1 us  [on_device(): lax.pmax(partial_best, 'mp')]
    all_to_all x1 -> x0, blocking collectives: 14.7 us -> none  [on_device(): lax.all_to_all(final_rows, 'mp', split_axis=0, concat_axis=1, tiled=True)]
    dot_general x1, matrix products: 10.3 us -> 3.17 us  [best_of(): jnp.einsum('rd,vd->rv', candidates, piece, preferred_element_type=jnp.flo...]
    dot_general x2, matrix products: 4.11 us -> 0.91 us  [block_step(): jnp.einsum('hcd,hde->hce', weights, value_rows, precision=PRECISE)]
    dynamic_slice x2, local copies, waits for them, and re-layouts: 5.09 us -> 2.31 us  [on_device(): _, (mixed_out, state_norm) = lax.scan(scan_step, initial, scan_inputs)]
  transfers between devices with their start and end apart: 7 -> 8, of which waited for: 4 -> 5; matrix products, arithmetic and copies ran while one was open for 11% -> 13% of each run, Pallas kernels for 0% -> 0%
where the time goes in v1:
time: 223 us; the launch traced here: 222 us
  waiting for transfers between devices  84.2 us (38%)
  matrix products  31.4 us (14%)
  blocking collectives  30.3 us (14%)
  local copies, waits for them, and re-layouts  23.3 us (10%)
  starting transfers between devices  22.2 us (10%)
  between operations  15.5 us (7%)
  other arithmetic  12.4 us (6%)
  loops' own time  2.93 us (1%)
    all_gather x1, waiting for transfers between devices, on_device(): group_rows = lax.all_gather(final_rows, 'mp', axis=1, tiled=True)  39.5 us
    reduce_scatter x1, waiting for transfers between devices, on_device(): lax.psum_scatter(partial_value.astype(jnp.bfloat16), 'mp', scatter_dimens...  26.9 us
    pmax x1, blocking collectives, on_device(): lax.pmax(partial_best, 'mp')  16.1 us
    all_to_all x1, blocking collectives, on_device(): lax.all_to_all(kept_pages, 'group', split_axis=0, concat_axis=0, tiled=True)  14.2 us
    all_gather x1, waiting for transfers between devices, on_device(): group_vocab = lax.all_gather(vocab_rows, 'group', axis=0, tiled=True)  9.12 us
    all_to_all x1, starting transfers between devices, on_device(): lax.all_to_all(lowered_pages, 'group', split_axis=0, concat_axis=0, tiled...  8.42 us
    ppermute x3, starting transfers between devices, from_behind(): return lax.ppermute(value, axis, pairs)  8.02 us
    all_to_all x1, waiting for transfers between devices, on_device(): lax.all_to_all(projected_pages, 'group', split_axis=0, concat_axis=0, til...  6.2 us
  transfers between devices with their start and end apart: 8, of which 5 were waited for; matrix products, arithmetic and copies ran while one was open for 13% of the time, Pallas kernels for 0%

profile of v1, /device:TPU:8, one launch (start us, length us, event | category | flops | bytes accessed | tf_op | source)
XLA Modules:
  0.0 222.2 jit_solution(6068181078464134090)
XLA Ops:
  7.2 0.7 all-gather.3.cloned.1.call-update
  7.9 1.3 slice.34
  9.8 2.7 %collective-permute-start.2 = (bf16[1]{0:T(256)(128)(2,1)}, bf16[1]{0:T(256)(128)(2,1)}, u32[]{:S(2)}, u32[]{:S(2)}) collective-permute-start(bf16[1]{0:T(256)(128)(2,1)} %bitcast.33), channel_id=1, source_target_pairs={{0,8},{8,16},{16,24},{24,32},{32,40},{40,48},{48,56},{56,64},{64,7... | collective-permute-start | bytes 14 | tf_op jit(solution)/shard_map/ppermute | solution.py:18
  12.6 0.8 reshape.240
  13.4 1.0 sort.17
  14.7 0.8 gather_fusion.4
  15.9 1.9 gather_fusion
  17.8 2.0 fusion.49
  20.0 3.0 %fusion.59 = bf16[32,2,8,128]{3,2,1,0:T(8,128)(2,1)} fusion(bf16[32,2,8,1792]{3,2,1,0:T(8,128)(2,1)} %bitcast.226, f32[1792]{0:T(1024)S(1)} %copy-done.14, f32[32,2,8]{2,1,0:T(2,128)S(1)} %copy.89, bf16[1792,128]{1,0:T(8,128)(2,1)} %param.17), kind=kOutput, calls=%fused_computation.84 | convolution fusion | flops 238616576 | bytes 2434048 | tf_op jit(solution)/shard_map/abrd,dc->abrc/dot_general | solution.py:119
  23.0 8.4 %all-to-all-start.1 = ((bf16[32,2,8,128]{3,2,1,0:T(8,128)(2,1)}), bf16[32,2,8,128]{3,2,1,0:T(8,128)(2,1)S(1)}, u32[]{:S(2)}, u32[]{:S(2)}) async-start(bf16[32,2,8,128]{3,2,1,0:T(8,128)(2,1)} %fusion.59), calls=%async_computation.1 | async-start | bytes 262144 | tf_op jit(solution)/shard_map/all_to_all | solution.py:126
  32.1 0.7 fusion.78
  32.8 3.4 %fusion.56 = bf16[32,2,8,288]{3,2,1,0:T(8,128)(2,1)} fusion(bf16[32,2,8,1792]{3,2,1,0:T(8,128)(2,1)} %bitcast.227, f32[1792]{0:T(1024)S(1)} %copy-done.14, f32[32,2,8]{2,1,0:T(2,128)S(1)} %copy.89, bf16[1792,288]{0,1:T(8,128)(2,1)S(1)} %copy-done.13), kind=kOutput, calls=%fused_computation.81 | convolution fusion | flops 532299776 | bytes 3171328 | tf_op jit(solution)/shard_map/abrd,dc->abrc/dot_general | solution.py:116
  36.3 1.8 all-to-all-done.1
  38.1 5.6 %all-to-all-start = ((bf16[32,2,8,288]{3,2,1,0:T(8,128)(2,1)}), bf16[32,2,8,288]{3,2,1,0:T(8,128)(2,1)S(1)}, u32[]{:S(2)}, u32[]{:S(2)}) async-start(bf16[32,2,8,288]{3,2,1,0:T(8,128)(2,1)} %fusion.56), calls=%async_computation | async-start | bytes 786432 | tf_op jit(solution)/shard_map/all_to_all | solution.py:125
  45.0 1.3 gather_fusion.2
  46.3 6.2 %all-to-all-done = bf16[32,2,8,288]{3,2,1,0:T(8,128)(2,1)S(1)} async-done(((bf16[32,2,8,288]{3,2,1,0:T(8,128)(2,1)}), bf16[32,2,8,288]{3,2,1,0:T(8,128)(2,1)S(1)}, u32[]{:S(2)}, u32[]{:S(2)}) %all-to-all-start) | async-done | bytes 294944 | tf_op jit(solution)/shard_map/all_to_all | solution.py:125
  52.5 0.6 gather_fusion.1
  53.1 9.1 %all-gather.3.cloned.1.call-done = bf16[512,1792]{1,0:T(8,128)(2,1)} async-done(((bf16[16,1792]{1,0:T(8,128)(2,1)}), bf16[512,1792]{1,0:T(8,128)(2,1)}) %all-gather.3.cloned.1.call-update) | async-done | bytes 1835024 | tf_op jit(solution)/shard_map/all_gather | solution.py:140
  62.8 1.3 pad_maximum_fusion.1
  64.1 1.3 convolution_convert_fusion
  65.4 0.7 fusion.81
  66.3 2.2 collective-permute-start.1
  68.5 3.1 %collective-permute-start = (bf16[2,273,112]{2,1,0:T(8,128)(2,1)}, bf16[2,273,112]{2,1,0:T(8,128)(2,1)}, u32[]{:S(2)}, u32[]{:S(2)}) collective-permute-start(bf16[2,273,112]{2,1,0:T(8,128)(2,1)} %convolution_convert_fusion), channel_id=1, source_target_pairs={{0,8},{8,16},{16,24},{24,32},{32,40},{40,48},{48,56},{56,64},{64,7... | collective-permute-start | bytes 366920 | tf_op jit(solution)/shard_map/ppermute | solution.py:18
  71.6 0.6 bitcast_bitcast_fusion.1
  72.2 0.8 slice.50
  73.1 1.7 reshape.246
  74.8 1.1 copy.127
  75.9 3.0 %reshape.250 = f32[2,2,256,273]{2,1,3,0:T(2,128)} reshape(f32[2,512,273]{1,2,0:T(8,128)} %get-tuple-element.279) | data formatting | bytes 2236416 | tf_op jit(solution)/shard_map/reshape | solution.py:169
  78.9 0.9 convert_element_type.128
  79.8 0.9 convert_element_type.126
  80.7 25.4 %while.21 = (s32[]{:T(128)}, f32[2,273,112]{2,1,0:T(8,128)S(1)}, f32[2,273]{0,1:T(8,128)S(1)}, s32[]{:T(128)}, bf16[2,2,256,112]{2,3,1,0:T(8,128)(2,1)}, /*index...) while((s32[]{:T(128)}, f32[2,273,112]{2,1,0:T(8,128)S(1)}, ...), condition=%wide.region_10.11_spmd, body=%wide.region_4.10_spmd.sunk | while | flops 1377437056 | bytes 23302216 | solution.py:184
  80.7 0.6 dynamic-slice.2
  82.3 0.6 compare_convert_fusion.6
  83.4 0.6 fusion.141
  84.0 0.7 convolution_multiply_fusion.7
  85.2 0.7 fusion.137
  85.9 1.2 constant_dynamic-slice_fusion.7
  87.6 0.9 convolution_multiply_fusion.6
  88.9 0.9 fusion.143
  89.8 0.9 fusion.145
  90.8 1.0 fusion.135
  91.8 0.8 convolution_add_fusion.3
  93.4 0.6 dynamic-slice.2
  95.0 0.6 compare_convert_fusion.6
  96.1 0.6 fusion.141
  96.7 0.7 convolution_multiply_fusion.7
  97.9 0.7 fusion.137
  98.6 1.2 constant_dynamic-slice_fusion.7
  100.3 0.9 convolution_multiply_fusion.6
  101.6 0.9 fusion.143
  102.5 0.9 fusion.145
  103.4 1.0 fusion.135
  104.5 0.8 convolution_add_fusion.3
  106.1 1.2 copy.96
  107.4 1.9 fusion.82
  109.3 2.0 add_convert_fusion
  111.4 1.1 constant_dynamic-slice_fusion.3
  112.5 14.2 %all_to_all.15 = bf16[32,2,8,224]{3,2,1,0:T(8,128)(2,1)S(1)} all-to-all(bf16[32,2,8,224]{3,2,1,0:T(8,128)(2,1)S(1)} %constant_dynamic-slice_fusion.3), channel_id=1, replica_groups=mesh['group'=32,'mp'=8] {'group'}, dimensions={0} | all-to-all | bytes 458752 | tf_op jit(solution)/shard_map/all_to_all | solution.py:124
  126.7 0.7 gather_fusion.3
  127.7 26.9 %reduce-scatter.2.cloned.1.call-done = bf16[512,224]{0,1:T(8,128)(2,1)} async-done(((bf16[512,1792]{0,1:T(8,128)(2,1)}), bf16[512,224]{0,1:T(8,128)(2,1)}) %reduce-scatter.2.cloned.1.call-update) | async-done | bytes 229392 | tf_op jit(solution)/shard_map/reduce_scatter | solution.py:208
  154.6 1.7 add_convert_fusion.1
  156.3 39.5 %all-gather.5.cloned.1.call-done = bf16[512,1792]{0,1:T(8,128)(2,1)} async-done(((bf16[512,224]{0,1:T(8,128)(2,1)}), bf16[512,1792]{0,1:T(8,128)(2,1)}) %all-gather.5.cloned.1.call-update) | async-done | bytes 1835024 | tf_op jit(solution)/shard_map/all_gather | solution.py:212
  195.7 3.2 %convolution_reduce_fusion = f32[512]{0:T(512)S(1)} fusion(bf16[512,1792]{1,0:T(8,128)(2,1)} %all-gather.3.cloned.1.call-done, bf16[512,1792]{0,1:T(8,128)(2,1)} %all-gather.5.cloned.1.call-done), kind=kOutput, calls=%fused_computation.82 | convolution fusion | flops 939785728 | bytes 3672064 | tf_op jit(solution)/shard_map/rd,vd->rv/dot_general | solution.py:81
  198.9 16.1 %pmax.7 = f32[512]{0:T(512)S(1)} all-reduce(f32[512]{0:T(512)S(1)} %convolution_reduce_fusion), channel_id=1, replica_groups=mesh['group'=32,'mp'=8] {'mp'}, use_global_device_ids=true, to_apply=%region_15.16 | all-reduce | flops 512 | bytes 4096 | tf_op jit(solution)/shard_map/pmax | solution.py:215
  (113 shorter events, 8.5 us)
Async XLA Ops:
  7.2 8.7 %copy-start = (bf16[512,1792]{1,0:T(8,128)(2,1)S(1)}, bf16[512,1792]{1,0:T(8,128)(2,1)}, u32[]{:S(2)}) copy-start(bf16[512,1792]{1,0:T(8,128)(2,1)} %param.13) | copy-start | bytes 5505028
  7.2 55.1 %all-gather.3.cloned.1.call-start = ((), (), s32[]{:S(2)}) async-start(), calls=%async_computation.4 | async-start | bytes 1892352 | tf_op jit(solution)/shard_map/all_gather | solution.py:140
  9.8 34.5 %collective-permute-start.2 = (bf16[1]{0:T(256)(128)(2,1)}, bf16[1]{0:T(256)(128)(2,1)}, u32[]{:S(2)}, u32[]{:S(2)}) collective-permute-start(bf16[1]{0:T(256)(128)(2,1)} %bitcast.33), channel_id=1, source_target_pairs={{0,8},{8,16},{16,24},{24,32},{32,40},{40,48},{48,56},{56,64},{64,7... | collective-permute-start | bytes 14 | tf_op jit(solution)/shard_map/ppermute | solution.py:18
  17.8 2.1 copy-start.14
  20.0 11.8 %copy-start.8 = (s32[512]{0:T(512)S(1)}, s32[512]{0:T(512)}, u32[]{:S(2)}) copy-start(s32[512]{0:T(512)} %param.20) | copy-start | bytes 6148
  20.0 11.8 %copy-start.11 = (s32[128]{0:T(128)S(1)}, s32[128]{0:T(128)}, u32[]{:S(2)}) copy-start(s32[128]{0:T(128)} %param.21) | copy-start | bytes 1540
  20.0 12.8 %copy-start.13 = (bf16[1792,288]{0,1:T(8,128)(2,1)S(1)}, bf16[1792,288]{0,1:T(8,128)(2,1)}, u32[]{:S(2)}) copy-start(bf16[1792,288]{0,1:T(8,128)(2,1)} %param.15) | copy-start | bytes 3096580
  23.0 15.1 %all-to-all-start.1 = ((bf16[32,2,8,128]{3,2,1,0:T(8,128)(2,1)}), bf16[32,2,8,128]{3,2,1,0:T(8,128)(2,1)S(1)}, u32[]{:S(2)}, u32[]{:S(2)}) async-start(bf16[32,2,8,128]{3,2,1,0:T(8,128)(2,1)} %fusion.59), calls=%async_computation.1 | async-start | bytes 262144 | tf_op jit(solution)/shard_map/all_to_all | solution.py:126
  32.7 3.5 %copy-start.12 = (s32[64]{0:T(128)S(1)}, s32[64]{0:T(128)}, u32[]{:S(2)}) copy-start(s32[64]{0:T(128)} %param.22) | copy-start | bytes 772
  36.2 26.3 %copy-start.9 = (s32[1024]{0:T(1024)}, s32[1024]{0:T(1024)S(1)}, u32[]{:S(2)}) copy-start(s32[1024]{0:T(1024)S(1)} %pad_clamp_fusion) | copy-start | bytes 12292
  38.1 14.4 %all-to-all-start = ((bf16[32,2,8,288]{3,2,1,0:T(8,128)(2,1)}), bf16[32,2,8,288]{3,2,1,0:T(8,128)(2,1)S(1)}, u32[]{:S(2)}, u32[]{:S(2)}) async-start(bf16[32,2,8,288]{3,2,1,0:T(8,128)(2,1)} %fusion.56), calls=%async_computation | async-start | bytes 786432 | tf_op jit(solution)/shard_map/all_to_all | solution.py:125
  43.7 110.8 %reduce-scatter.2.cloned.1.call-start = ((), (), s32[]{:S(2)}) async-start(), calls=%async_computation.5 | async-start | bytes 2064384 | tf_op jit(solution)/shard_map/reduce_scatter | solution.py:208
  66.3 12.6 %collective-permute-start.1 = (bf16[2,273]{0,1:T(8,128)(2,1)S(1)}, bf16[2,273]{0,1:T(8,128)(2,1)}, u32[]{:S(2)}, u32[]{:S(2)}) collective-permute-start(bf16[2,273]{0,1:T(8,128)(2,1)S(1)} %bitcast.252), channel_id=1, source_target_pairs={{0,8},{8,16},{16,24},{24,32},{32,40},{40,48},{48,56},{56,64},{64,7... | collective-permute-start | bytes 3284 | tf_op jit(solution)/shard_map/ppermute | solution.py:18
  68.5 11.3 %collective-permute-start = (bf16[2,273,112]{2,1,0:T(8,128)(2,1)}, bf16[2,273,112]{2,1,0:T(8,128)(2,1)}, u32[]{:S(2)}, u32[]{:S(2)}) collective-permute-start(bf16[2,273,112]{2,1,0:T(8,128)(2,1)} %convolution_convert_fusion), channel_id=1, source_target_pairs={{0,8},{8,16},{16,24},{24,32},{32,40},{40,48},{48,56},{56,64},{64,7... | collective-permute-start | bytes 366920 | tf_op jit(solution)/shard_map/ppermute | solution.py:18
  74.8 5.9 %copy-start.7 = (f32[2,2,256,16]{2,3,1,0:T(8,128)S(1)}, f32[2,2,256,16]{2,3,1,0:T(8,128)}, u32[]{:S(2)}) copy-start(f32[2,2,256,16]{2,3,1,0:T(8,128)} %get-tuple-element.383) | copy-start | bytes 196612
  83.3 2.6 %copy-start.1 = (f32[2,2,256,273]{2,0,3,1:T(2,128)S(1)}, f32[2,2,256,273]{2,0,3,1:T(2,128)}, u32[]{:S(2)}) copy-start(f32[2,2,256,273]{2,0,3,1:T(2,128)} %get-tuple-element.411) | copy-start | bytes 3354628 | tf_op jit(solution)/shard_map/while
  83.4 2.6 %copy-start.2 = (f32[2,2,256,273]{2,0,3,1:T(2,128)S(1)}, f32[2,2,256,273]{2,0,3,1:T(2,128)}, u32[]{:S(2)}) copy-start(f32[2,2,256,273]{2,0,3,1:T(2,128)} %get-tuple-element.415) | copy-start | bytes 3354628 | tf_op jit(solution)/shard_map/while
  85.9 2.5 %copy-start.5 = (bf16[2,2,256,112]{2,3,1,0:T(8,128)(2,1)S(1)}, bf16[2,2,256,112]{2,3,1,0:T(8,128)(2,1)}, u32[]{:S(2)}) copy-start(bf16[2,2,256,112]{2,3,1,0:T(8,128)(2,1)} %get-tuple-element.393) | copy-start | bytes 688132 | tf_op jit(solution)/shard_map/while
  88.9 3.8 %copy-start.6 = (bf16[2,2,256,112]{2,3,1,0:T(8,128)(2,1)}, bf16[2,2,256,112]{2,3,1,0:T(8,128)(2,1)S(1)}, u32[]{:S(2)}) copy-start(bf16[2,2,256,112]{2,3,1,0:T(8,128)(2,1)S(1)} %fusion.140) | copy-start | bytes 688132 | tf_op jit(solution)/shard_map/while
  96.0 2.6 %copy-start.1 = (f32[2,2,256,273]{2,0,3,1:T(2,128)S(1)}, f32[2,2,256,273]{2,0,3,1:T(2,128)}, u32[]{:S(2)}) copy-start(f32[2,2,256,273]{2,0,3,1:T(2,128)} %get-tuple-element.411) | copy-start | bytes 3354628 | tf_op jit(solution)/shard_map/while
  96.0 2.6 %copy-start.2 = (f32[2,2,256,273]{2,0,3,1:T(2,128)S(1)}, f32[2,2,256,273]{2,0,3,1:T(2,128)}, u32[]{:S(2)}) copy-start(f32[2,2,256,273]{2,0,3,1:T(2,128)} %get-tuple-element.415) | copy-start | bytes 3354628 | tf_op jit(solution)/shard_map/while
  98.6 2.5 %copy-start.5 = (bf16[2,2,256,112]{2,3,1,0:T(8,128)(2,1)S(1)}, bf16[2,2,256,112]{2,3,1,0:T(8,128)(2,1)}, u32[]{:S(2)}) copy-start(bf16[2,2,256,112]{2,3,1,0:T(8,128)(2,1)} %get-tuple-element.393) | copy-start | bytes 688132 | tf_op jit(solution)/shard_map/while
  101.6 3.8 %copy-start.6 = (bf16[2,2,256,112]{2,3,1,0:T(8,128)(2,1)}, bf16[2,2,256,112]{2,3,1,0:T(8,128)(2,1)S(1)}, u32[]{:S(2)}) copy-start(bf16[2,2,256,112]{2,3,1,0:T(8,128)(2,1)S(1)} %fusion.140) | copy-start | bytes 688132 | tf_op jit(solution)/shard_map/while
  107.3 1.9 copy-start.3
  107.3 1.9 copy-start.4
  107.3 1.9 copy-start.10
  111.3 84.4 %all-gather.5.cloned.1.call-start = ((), (), s32[]{:S(2)}) async-start(), calls=%async_computation.6 | async-start | bytes 2064384 | tf_op jit(solution)/shard_map/all_gather | solution.py:212
Sparse Core Ops, SparseCore 0:
  10.6 51.6 all-gather.2
  111.4 43.0 reduce-scatter.1
  156.4 39.2 all-gather.4

commit v2 on v1

--- a/solution.py
+++ b/solution.py
@@ -120,10 +120,15 @@
         "abrd,dc->abrc", normed_pages, adapter_down, preferred_element_type=jnp.float32
     ).astype(jnp.bfloat16)
     kept_pages = lax.dynamic_slice_in_dim(outgoing, own_shard * slice_width, slice_width, 3)
+    widths = (kept_pages.shape[3], projected_pages.shape[3], lowered_pages.shape[3])
+    packed = lax.all_to_all(
+        jnp.concatenate([kept_pages, projected_pages, lowered_pages], axis=3),
+        "group", split_axis=0, concat_axis=0, tiled=True,
+    )
     arrived = (
-        lax.all_to_all(kept_pages, "group", split_axis=0, concat_axis=0, tiled=True),
-        lax.all_to_all(projected_pages, "group", split_axis=0, concat_axis=0, tiled=True),
-        lax.all_to_all(lowered_pages, "group", split_axis=0, concat_axis=0, tiled=True),
+        packed[..., : widths[0]],
+        packed[..., widths[0] : widths[0] + widths[1]],
+        packed[..., widths[0] + widths[1] :],
     )
     own_holders = lax.dynamic_index_in_dim(holders, own_group, 0, keepdims=False)
     onehot = (own_holders[:, None] == jnp.arange(groups, dtype=jnp.int32)[None, :]).astype(
@@ -138,7 +143,6 @@
 
     residual, projected, lowered = [placed(received) for received in arrived]
     group_vocab = lax.all_gather(vocab_rows, "group", axis=0, tiled=True)
-    group_vocab, projected = lax.optimization_barrier((group_vocab, projected))
     heads_here = projected.shape[1] // (2 * FEAT + HD)
     split_heads = jnp.transpose(
         projected.reshape(rows_here, heads_here, 2 * FEAT + HD).astype(jnp.float32), (1, 0, 2)
@@ -155,11 +159,17 @@
     )
     end_totals = jnp.einsum("hcp,c->hp", phi_key, member, precision=PRECISE)
     end_tag = jnp.reshape(last_seg + 1, (1,)).astype(jnp.float32)
-    got_state, got_totals, got_tag = (
-        from_behind(end_state.astype(jnp.bfloat16), "group", 1).astype(end_state.dtype),
-        from_behind(end_totals.astype(jnp.bfloat16), "group", 1).astype(end_totals.dtype),
-        from_behind(end_tag.astype(jnp.bfloat16), "group", 1).astype(end_tag.dtype),
-    )
+    state_size, totals_size = end_state.size, end_totals.size
+    handed = from_behind(
+        jnp.concatenate(
+            [end_state.reshape(-1), end_totals.reshape(-1), end_tag]
+        ).astype(jnp.bfloat16),
+        "group",
+        1,
+    ).astype(jnp.float32)
+    got_state = handed[:state_size].reshape(end_state.shape)
+    got_totals = handed[state_size : state_size + totals_size].reshape(end_totals.shape)
+    got_tag = handed[state_size + totals_size :]
     initial = (got_state, got_totals, got_tag[0].astype(jnp.int32) - 1)
     block_len = min(256, rows_here)
     blocks = rows_here // block_len
@@ -187,6 +197,7 @@
         .reshape(rows_here, heads_here * HD)
         .astype(jnp.bfloat16)
     )
+    group_vocab, attended = lax.optimization_barrier((group_vocab, attended))
     state_norms = jnp.transpose(state_norm, (1, 0, 2)).reshape(heads_here, rows_here)
     request_ids = jnp.arange(request_adapter.shape[0], dtype=jnp.int32)
     adapter_of = jnp.sum(

time: 223 us -> 209 us (0.937)
  blocking collectives: 30.3 us -> 16.1 us
  starting transfers between devices: 22.2 us -> 9.74 us
  waiting for transfers between devices: 84.2 us -> 93.8 us
  local copies, waits for them, and re-layouts: 23.3 us -> 29 us
  matrix products: 31.4 us -> 28.2 us
    all_to_all x1 -> x0, blocking collectives: 14.2 us -> none  [on_device(): lax.all_to_all(kept_pages, 'group', split_axis=0, concat_axis=0, tiled=True)]
    reduce_scatter x1, waiting for transfers between devices: 26.9 us -> 41 us  [on_device(): lax.psum_scatter(partial_value.astype(jnp.bfloat16), 'mp', scatter_dimens...]
    all_gather x1, waiting for transfers between devices: 9.12 us -> 0.02 us  [on_device(): group_vocab = lax.all_gather(vocab_rows, 'group', axis=0, tiled=True)]
    all_to_all x2 -> x1, starting transfers between devices: 14 us -> 7.54 us  [on_device(): lax.all_to_all(jnp.concatenate([kept_pages, projected_pages, lowered_page...]
    ppermute x3 -> x1, starting transfers between devices: 8.02 us -> 2.09 us  [from_behind(): return lax.ppermute(value, axis, pairs)]
    ppermute x3 -> x1, waiting for transfers between devices: 0.01 us -> 3.26 us  [from_behind(): return lax.ppermute(value, axis, pairs)]
    dot_general x1, matrix products: 3.4 us -> 1.16 us  [on_device(): jnp.einsum('abrd,dc->abrc', normed_pages, qkv_weight, preferred_element_t...]
    reshape x0 -> x4, local copies, waits for them, and re-layouts: none -> 2.24 us  [the longest x1 1.82 us: on_device(): end_state.reshape(-1)]
  transfers between devices with their start and end apart: 8 -> 5, of which waited for: 5 -> 4; matrix products, arithmetic and copies ran while one was open for 13% -> 29% of each run, Pallas kernels for 0% -> 0%
where the time goes in v2:
time: 209 us; the launch traced here: 208 us
  waiting for transfers between devices  93.8 us (45%)
  local copies, waits for them, and re-layouts  29 us (14%)
  matrix products  28.2 us (13%)
  blocking collectives  16.1 us (8%)
  between operations  15.6 us (7%)
  other arithmetic  12.8 us (6%)
  starting transfers between devices  9.74 us (5%)
  loops' own time  2.99 us (1%)
    reduce_scatter x1, waiting for transfers between devices, on_device(): lax.psum_scatter(partial_value.astype(jnp.bfloat16), 'mp', scatter_dimens...  41 us
    all_gather x1, waiting for transfers between devices, on_device(): group_rows = lax.all_gather(final_rows, 'mp', axis=1, tiled=True)  39.5 us
    pmax x1, blocking collectives, on_device(): lax.pmax(partial_best, 'mp')  16.1 us
    all_to_all x1, waiting for transfers between devices, on_device(): lax.all_to_all(jnp.concatenate([kept_pages, projected_pages, lowered_page...  9.31 us
    all_to_all x1, starting transfers between devices, on_device(): lax.all_to_all(jnp.concatenate([kept_pages, projected_pages, lowered_page...  7.54 us
    reshape x3, local copies, waits for them, and re-layouts, regroup(): values.reshape(values.shape[0], blocks, block_len, values.shape[-1])  4.7 us
  transfers between devices with their start and end apart: 5, of which 4 were waited for; matrix products, arithmetic and copies ran while one was open for 29% of the time, Pallas kernels for 0%

profile of v2, /device:TPU:8, one launch (start us, length us, event | category | flops | bytes accessed | tf_op | source)
XLA Modules:
  0.0 208.2 jit_solution(18308353681001285271)
XLA Ops:
  7.2 0.7 all-gather.3.cloned.1.call-update
  7.9 0.8 reshape.248
  8.8 1.0 sort.17
  10.0 0.8 gather_fusion.4
  11.3 1.9 gather_fusion
  13.2 2.0 fusion.49
  15.4 1.1 constant_dynamic-slice_fusion.4
  16.6 2.3 %fusion.59 = bf16[32,2,8,128]{3,2,1,0:T(8,128)(2,1)S(1)} fusion(bf16[32,2,8,1792]{3,2,1,0:T(8,128)(2,1)} %bitcast.225, f32[1792]{0:T(1024)S(1)} %copy-done.16, f32[32,2,8]{2,1,0:T(2,128)S(1)} %copy.93, bf16[1792,128]{1,0:T(8,128)(2,1)S(1)} %copy-done.15), kind=kOutput, calls=%fused_computation.84 | convolution fusion | flops 238616576 | bytes 2434048 | tf_op jit(solution)/shard_map/abrd,dc->abrc/dot_general | solution.py:119
  18.9 1.2 fusion.56
  20.1 1.1 pad_maximum_fusion.2
  21.3 7.5 %all-to-all-start = ((bf16[32,2,8,640]{3,2,1,0:T(8,128)(2,1)}), bf16[32,2,8,640]{3,2,1,0:T(8,128)(2,1)S(1)}, u32[]{:S(2)}, u32[]{:S(2)}) async-start(bf16[32,2,8,640]{3,2,1,0:T(8,128)(2,1)} %pad_maximum_fusion.2), calls=%async_computation | async-start | bytes 1310720 | tf_op jit(solution)/shard_map/all_to_all | solution.py:124
  28.9 0.6 slice.53
  29.5 0.6 fusion.78
  31.6 9.3 %all-to-all-done = bf16[32,2,8,640]{3,2,1,0:T(8,128)(2,1)S(1)} async-done(((bf16[32,2,8,640]{3,2,1,0:T(8,128)(2,1)}), bf16[32,2,8,640]{3,2,1,0:T(8,128)(2,1)S(1)}, u32[]{:S(2)}, u32[]{:S(2)}) %all-to-all-start) | async-done | bytes 655392 | tf_op jit(solution)/shard_map/all_to_all | solution.py:124
  41.1 1.4 gather_fusion.1
  42.5 1.2 reshape_reshape.3
  44.2 0.7 broadcast_multiply_fusion
  44.9 1.3 gather_fusion.2
  46.5 2.2 %pad_maximum_fusion.1 = (f32[2,512,273]{1,2,0:T(8,128)}, f32[2,512,273]{1,2,0:T(8,128)S(1)}) fusion(f32[2,512,256]{1,2,0:T(8,128)S(1)} %bitcast.227, f32[2,512,16]{1,2,0:T(8,128)} %get-tuple-element.273, f32[273]{0:T(512)S(1)} %pad.3.clone, f32[2,512,256]{1,2,0:T(8,128)S(1)} %bitcast.228, f32[2,512,16]{1,2,0:T(8,128)} %get-tuple-element.274), kind=kLoop, calls=%fused_computation.86 | loop fusion | flops 1118208 | bytes 4465732 | tf_op jit(solution)/shard_map/concatenate | solution.py:34
  48.7 1.7 reshape.256
  50.4 2.3 %convolution_convert_fusion = bf16[2,273,112]{2,1,0:T(8,128)(2,1)} fusion(f32[2,512,273]{1,2,0:T(8,128)S(1)} %get-tuple-element.280, f32[512]{0:T(512)S(1)} %get-tuple-element.265, bf16[2,512,144]{1,2,0:T(8,128)(2,1)} %bitcast.230), kind=kOutput, calls=%fused_computation.83 | convolution fusion | flops 376058592 | bytes 1471936 | tf_op jit(solution)/shard_map/hcp,hce->hpe/dot_general | solution.py:157
  52.7 1.8 reshape.251
  54.5 3.0 %reshape.260 = f32[2,2,256,273]{2,1,3,0:T(2,128)} reshape(f32[2,512,273]{1,2,0:T(8,128)} %get-tuple-element.279) | data formatting | bytes 2236416 | tf_op jit(solution)/shard_map/reshape | solution.py:179
  57.5 0.7 fusion.80
  58.3 2.1 concatenate.15
  60.3 2.1 %collective-permute-start = (bf16[61699]{0:T(1024)(128)(2,1)S(1)}, bf16[61699]{0:T(1024)(128)(2,1)S(1)}, u32[]{:S(2)}, u32[]{:S(2)}) collective-permute-start(bf16[61699]{0:T(1024)(128)(2,1)S(1)} %concatenate.15), channel_id=1, source_target_pairs={{0,8},{8,16},{16,24},{24,32},{32,40},{40,48},{48,56},{56,64},{64,7... | collective-permute-start | bytes 370202 | tf_op jit(solution)/shard_map/ppermute | solution.py:18
  62.4 0.8 bitcast_bitcast_fusion.1
  63.3 3.3 %collective-permute-done = bf16[61699]{0:T(1024)(128)(2,1)S(1)} collective-permute-done((bf16[61699]{0:T(1024)(128)(2,1)S(1)}, bf16[61699]{0:T(1024)(128)(2,1)S(1)}, u32[]{:S(2)}, u32[]{:S(2)}) %collective-permute-start) | collective-permute-done | bytes 123430 | tf_op jit(solution)/shard_map/ppermute | solution.py:18
  66.5 0.6 slice.77
  68.3 24.2 %while.21 = (s32[]{:T(128)}, f32[2,273,112]{2,1,0:T(8,128)S(1)}, f32[2,273]{0,1:T(8,128)S(1)}, s32[]{:T(128)}, bf16[2,2,256,112]{2,3,1,0:T(8,128)(2,1)}, /*index...) while((s32[]{:T(128)}, f32[2,273,112]{2,1,0:T(8,128)S(1)}, ...), condition=%wide.region_10.11_spmd, body=%wide.region_4.10_spmd.sunk | while | flops 1377437056 | bytes 23302216 | solution.py:194
  68.4 0.6 dynamic-slice.2
  69.9 0.7 compare_convert_fusion.6
  71.0 0.6 fusion.140
  71.6 0.7 convolution_multiply_fusion.7
  72.3 0.5 fusion.141
  72.8 0.7 fusion.136
  73.6 1.2 constant_dynamic-slice_fusion.7
  75.2 0.8 convolution_multiply_fusion.6
  76.5 0.9 fusion.142
  77.8 1.0 fusion.134
  78.8 0.8 convolution_add_fusion.3
  80.5 0.6 dynamic-slice.2
  82.0 0.7 compare_convert_fusion.6
  83.1 0.6 fusion.140
  83.7 0.7 convolution_multiply_fusion.7
  84.4 0.5 fusion.141
  84.9 0.7 fusion.136
  85.7 1.2 constant_dynamic-slice_fusion.7
  86.8 0.5 fusion.137
  87.3 0.8 convolution_multiply_fusion.6
  88.6 0.9 fusion.142
  89.9 1.0 fusion.134
  90.9 0.8 convolution_add_fusion.3
  92.6 1.2 copy.101
  93.8 1.9 fusion.81
  95.8 2.0 add_convert_fusion
  97.8 0.9 slice-done
  98.7 0.6 gather_fusion.3
  99.5 41.0 %reduce-scatter.2.cloned.1.call-done = bf16[512,224]{0,1:T(8,128)(2,1)} async-done(((bf16[512,1792]{0,1:T(8,128)(2,1)}), bf16[512,224]{0,1:T(8,128)(2,1)}) %reduce-scatter.2.cloned.1.call-update) | async-done | bytes 229392 | tf_op jit(solution)/shard_map/reduce_scatter | solution.py:219
  140.6 1.7 add_convert_fusion.1
  142.3 39.5 %all-gather.5.cloned.1.call-done = bf16[512,1792]{0,1:T(8,128)(2,1)} async-done(((bf16[512,224]{0,1:T(8,128)(2,1)}), bf16[512,1792]{0,1:T(8,128)(2,1)}) %all-gather.5.cloned.1.call-update) | async-done | bytes 1835024 | tf_op jit(solution)/shard_map/all_gather | solution.py:223
  181.8 3.2 %convolution_reduce_fusion = f32[512]{0:T(512)S(1)} fusion(bf16[512,1792]{1,0:T(8,128)(2,1)} %all-gather.3.cloned.1.call-done, bf16[512,1792]{0,1:T(8,128)(2,1)} %all-gather.5.cloned.1.call-done), kind=kOutput, calls=%fused_computation.82 | convolution fusion | flops 939785728 | bytes 3672064 | tf_op jit(solution)/shard_map/rd,vd->rv/dot_general | solution.py:81
  185.0 16.1 %pmax.7 = f32[512]{0:T(512)S(1)} all-reduce(f32[512]{0:T(512)S(1)} %convolution_reduce_fusion), channel_id=1, replica_groups=mesh['group'=32,'mp'=8] {'mp'}, use_global_device_ids=true, to_apply=%region_15.16 | all-reduce | flops 512 | bytes 4096 | tf_op jit(solution)/shard_map/pmax | solution.py:226
  201.1 0.6 dynamic_slice.58
  (124 shorter events, 7.6 us)
Async XLA Ops:
  7.2 4.1 %copy-start = (bf16[512,1792]{1,0:T(8,128)(2,1)S(1)}, bf16[512,1792]{1,0:T(8,128)(2,1)}, u32[]{:S(2)}) copy-start(bf16[512,1792]{1,0:T(8,128)(2,1)} %param.13) | copy-start | bytes 5505028
  7.2 86.6 %all-gather.3.cloned.1.call-start = ((), (), s32[]{:S(2)}) async-start(), calls=%async_computation.2 | async-start | bytes 1892352 | tf_op jit(solution)/shard_map/all_gather | solution.py:145
  13.2 3.3 %copy-start.15 = (bf16[1792,128]{1,0:T(8,128)(2,1)S(1)}, bf16[1792,128]{1,0:T(8,128)(2,1)}, u32[]{:S(2)}) copy-start(bf16[1792,128]{1,0:T(8,128)(2,1)} %param.17) | copy-start | bytes 1376260
  13.2 3.3 %copy-start.16 = (f32[1792]{0:T(1024)S(1)}, f32[1792]{0:T(1024)}, u32[]{:S(2)}) copy-start(f32[1792]{0:T(1024)} %param.14) | copy-start | bytes 21508
  16.5 2.4 %copy-start.3 = (bf16[64,8,1792]{2,1,0:T(8,128)(2,1)S(1)}, bf16[64,8,1792]{2,1,0:T(8,128)(2,1)}, u32[]{:S(2)}) copy-start(bf16[64,8,1792]{2,1,0:T(8,128)(2,1)} %gather_fusion) | copy-start | bytes 5505028
  16.5 2.4 %copy-start.14 = (bf16[1792,288]{0,1:T(8,128)(2,1)S(1)}, bf16[1792,288]{0,1:T(8,128)(2,1)}, u32[]{:S(2)}) copy-start(bf16[1792,288]{0,1:T(8,128)(2,1)} %param.15) | copy-start | bytes 3096580
  20.1 8.8 %copy-start.11 = (s32[512]{0:T(512)S(1)}, s32[512]{0:T(512)}, u32[]{:S(2)}) copy-start(s32[512]{0:T(512)} %param.20) | copy-start | bytes 6148
  20.1 11.1 %copy-start.12 = (s32[128]{0:T(128)S(1)}, s32[128]{0:T(128)}, u32[]{:S(2)}) copy-start(s32[128]{0:T(128)} %param.21) | copy-start | bytes 1540
  20.1 11.3 %copy-start.13 = (s32[64]{0:T(128)S(1)}, s32[64]{0:T(128)}, u32[]{:S(2)}) copy-start(s32[64]{0:T(128)} %param.22) | copy-start | bytes 772
  21.3 19.6 %all-to-all-start = ((bf16[32,2,8,640]{3,2,1,0:T(8,128)(2,1)}), bf16[32,2,8,640]{3,2,1,0:T(8,128)(2,1)S(1)}, u32[]{:S(2)}, u32[]{:S(2)}) async-start(bf16[32,2,8,640]{3,2,1,0:T(8,128)(2,1)} %pad_maximum_fusion.2), calls=%async_computation | async-start | bytes 1310720 | tf_op jit(solution)/shard_map/all_to_all | solution.py:124
  28.8 111.8 %reduce-scatter.2.cloned.1.call-start = ((), (), s32[]{:S(2)}) async-start(), calls=%async_computation.3 | async-start | bytes 2064384 | tf_op jit(solution)/shard_map/reduce_scatter | solution.py:219
  40.9 4.0 %copy-start.4 = (bf16[32,2,8,640]{3,2,1,0:T(8,128)(2,1)}, bf16[32,2,8,640]{3,2,1,0:T(8,128)(2,1)S(1)}, u32[]{:S(2)}) copy-start(bf16[32,2,8,640]{3,2,1,0:T(8,128)(2,1)S(1)} %all-to-all-done) | copy-start | bytes 1966084
  44.1 2.4 %copy-start.5 = (bf16[512,2,144]{0,2,1:T(8,128)(2,1)}, bf16[512,2,144]{0,2,1:T(8,128)(2,1)S(1)}, u32[]{:S(2)}) copy-start(bf16[512,2,144]{0,2,1:T(8,128)(2,1)S(1)} %copy.94) | copy-start | bytes 884740
  44.8 1.7 copy-start.6
  60.3 6.2 %collective-permute-start = (bf16[61699]{0:T(1024)(128)(2,1)S(1)}, bf16[61699]{0:T(1024)(128)(2,1)S(1)}, u32[]{:S(2)}, u32[]{:S(2)}) collective-permute-start(bf16[61699]{0:T(1024)(128)(2,1)S(1)} %concatenate.15), channel_id=1, source_target_pairs={{0,8},{8,16},{16,24},{24,32},{32,40},{40,48},{48,56},{56,64},{64,7... | collective-permute-start | bytes 370202 | tf_op jit(solution)/shard_map/ppermute | solution.py:18
  71.0 2.6 %copy-start.1 = (f32[2,2,256,273]{2,0,3,1:T(2,128)S(1)}, f32[2,2,256,273]{2,0,3,1:T(2,128)}, u32[]{:S(2)}) copy-start(f32[2,2,256,273]{2,0,3,1:T(2,128)} %get-tuple-element.411) | copy-start | bytes 3354628 | tf_op jit(solution)/shard_map/while
  71.0 2.6 %copy-start.2 = (f32[2,2,256,273]{2,0,3,1:T(2,128)S(1)}, f32[2,2,256,273]{2,0,3,1:T(2,128)}, u32[]{:S(2)}) copy-start(f32[2,2,256,273]{2,0,3,1:T(2,128)} %get-tuple-element.415) | copy-start | bytes 3354628 | tf_op jit(solution)/shard_map/while
  73.5 2.5 %copy-start.9 = (bf16[2,2,256,112]{2,3,1,0:T(8,128)(2,1)S(1)}, bf16[2,2,256,112]{2,3,1,0:T(8,128)(2,1)}, u32[]{:S(2)}) copy-start(bf16[2,2,256,112]{2,3,1,0:T(8,128)(2,1)} %get-tuple-element.393) | copy-start | bytes 688132 | tf_op jit(solution)/shard_map/while
  76.5 3.3 %copy-start.10 = (bf16[2,2,256,112]{2,3,1,0:T(8,128)(2,1)}, bf16[2,2,256,112]{2,3,1,0:T(8,128)(2,1)S(1)}, u32[]{:S(2)}) copy-start(bf16[2,2,256,112]{2,3,1,0:T(8,128)(2,1)S(1)} %fusion.139) | copy-start | bytes 688132 | tf_op jit(solution)/shard_map/while
  83.1 2.6 %copy-start.1 = (f32[2,2,256,273]{2,0,3,1:T(2,128)S(1)}, f32[2,2,256,273]{2,0,3,1:T(2,128)}, u32[]{:S(2)}) copy-start(f32[2,2,256,273]{2,0,3,1:T(2,128)} %get-tuple-element.411) | copy-start | bytes 3354628 | tf_op jit(solution)/shard_map/while
  83.1 2.6 %copy-start.2 = (f32[2,2,256,273]{2,0,3,1:T(2,128)S(1)}, f32[2,2,256,273]{2,0,3,1:T(2,128)}, u32[]{:S(2)}) copy-start(f32[2,2,256,273]{2,0,3,1:T(2,128)} %get-tuple-element.415) | copy-start | bytes 3354628 | tf_op jit(solution)/shard_map/while
  85.6 2.5 %copy-start.9 = (bf16[2,2,256,112]{2,3,1,0:T(8,128)(2,1)S(1)}, bf16[2,2,256,112]{2,3,1,0:T(8,128)(2,1)}, u32[]{:S(2)}) copy-start(bf16[2,2,256,112]{2,3,1,0:T(8,128)(2,1)} %get-tuple-element.393) | copy-start | bytes 688132 | tf_op jit(solution)/shard_map/while
  88.6 3.3 %copy-start.10 = (bf16[2,2,256,112]{2,3,1,0:T(8,128)(2,1)}, bf16[2,2,256,112]{2,3,1,0:T(8,128)(2,1)S(1)}, u32[]{:S(2)}) copy-start(bf16[2,2,256,112]{2,3,1,0:T(8,128)(2,1)S(1)} %fusion.139) | copy-start | bytes 688132 | tf_op jit(solution)/shard_map/while
  92.6 3.2 %copy-start.17 = (f32[2,2,256]{2,1,0:T(2,128)}, f32[2,2,256]{2,1,0:T(2,128)S(1)}, u32[]{:S(2)}) copy-start(f32[2,2,256]{2,1,0:T(2,128)S(1)} %get-tuple-element.189) | copy-start | bytes 12292
  93.8 1.9 copy-start.7
  93.8 1.9 copy-start.8
  97.8 0.9 slice-start
  97.8 84.0 %all-gather.5.cloned.1.call-start = ((), (), s32[]{:S(2)}) async-start(), calls=%async_computation.4 | async-start | bytes 2064384 | tf_op jit(solution)/shard_map/all_gather | solution.py:223
Sparse Core Ops, SparseCore 0:
  10.6 54.5 all-gather.2
  97.9 42.6 reduce-scatter.1
  142.4 39.3 all-gather.4

commit v3 on v2

--- a/solution.py
+++ b/solution.py
@@ -2,6 +2,8 @@
 import jax.numpy as jnp
 from jax import lax
 from jax.sharding import PartitionSpec as P
+from jax.experimental import pallas as pl
+from jax.experimental.pallas import tpu as pltpu
 
 FEAT = 16
 HD = 112
@@ -80,6 +82,107 @@
 def best_of(candidates, piece):
     logits = jnp.einsum("rd,vd->rv", candidates, piece, preferred_element_type=jnp.float32)
     return jnp.max(logits, axis=1)
+
+
+def exchange_kernel(
+    part_ref, resid_ref, vocab_ref, upd_ref, best_ref,
+    land, rows, tops, got, sems,
+):
+    n = part_ref.shape[0]
+    block_rows = best_ref.shape[0]
+    me = lax.axis_index("mp")
+    grp = lax.axis_index("group")
+    peers = [lax.rem(me + k, n) for k in range(1, n)]
+    mesh_id = pl.DeviceIdType.MESH
+
+    barrier = pltpu.get_barrier_semaphore()
+    for p in peers:
+        pl.semaphore_signal(barrier, inc=1, device_id=(grp, p), device_id_type=mesh_id)
+    pl.semaphore_wait(barrier, n - 1)
+
+    def send_all(phase, src_of, dst):
+        copies = []
+        for p in peers:
+            copy = pltpu.make_async_remote_copy(
+                src_ref=src_of(p),
+                dst_ref=dst.at[me],
+                send_sem=sems.at[phase, 0, p],
+                recv_sem=sems.at[phase, 1, me],
+                device_id=(grp, p),
+                device_id_type=mesh_id,
+            )
+            copy.start()
+            copies.append(copy)
+        return copies
+
+    def finish(phase, copies, src_of, dst):
+        for copy in copies:
+            copy.wait_send()
+        for q in peers:
+            pltpu.make_async_remote_copy(
+                src_ref=src_of(q),
+                dst_ref=dst.at[q],
+                send_sem=sems.at[phase, 0, q],
+                recv_sem=sems.at[phase, 1, q],
+                device_id=(grp, q),
+                device_id_type=mesh_id,
+            ).wait_recv()
+
+    part_of = lambda p: part_ref.at[p]
+    sent = send_all(0, part_of, land)
+    finish(0, sent, part_of, land)
+    total = part_ref[me].astype(jnp.float32)
+    for q in peers:
+        total = total + land[q].astype(jnp.float32)
+    update = total.astype(upd_ref.dtype)
+    upd_ref[...] = update
+    rows[me] = (resid_ref[...].astype(jnp.float32) + update.astype(jnp.float32)).astype(
+        rows.dtype
+    )
+
+    own_rows = lambda p: rows.at[me]
+    sent = send_all(1, own_rows, rows)
+    finish(1, sent, own_rows, rows)
+    scores = jnp.zeros((rows.shape[1], vocab_ref.shape[1]), jnp.float32)
+    for j in range(n):
+        scores = scores + lax.dot_general(
+            rows[j], vocab_ref[j], (((1,), (1,)), ((), ())),
+            preferred_element_type=jnp.float32,
+        )
+    for p in range(n):
+        piece = jnp.max(scores[p * block_rows : (p + 1) * block_rows], axis=1, keepdims=True)
+        tops[p] = jnp.broadcast_to(piece, tops.shape[1:])
+
+    top_of = lambda p: tops.at[p]
+    sent = send_all(2, top_of, got)
+    finish(2, sent, top_of, got)
+    best = tops[me]
+    for q in peers:
+        best = jnp.maximum(best, got[q])
+    best_ref[...] = best
+
+
+def mp_exchange(parts, residual, vocab_blocks):
+    n, rows_here, width = parts.shape
+    block_rows = rows_here // n
+    vmem = pl.BlockSpec(memory_space=pltpu.VMEM)
+    return pl.pallas_call(
+        exchange_kernel,
+        out_shape=(
+            jax.ShapeDtypeStruct((rows_here, width), jnp.bfloat16),
+            jax.ShapeDtypeStruct((block_rows, 128), jnp.float32),
+        ),
+        in_specs=[vmem] * 3,
+        out_specs=(vmem, vmem),
+        scratch_shapes=[
+            pltpu.VMEM((n, rows_here, width), jnp.bfloat16),
+            pltpu.VMEM((n, rows_here, width), jnp.bfloat16),
+            pltpu.VMEM((n, block_rows, 128), jnp.float32),
+            pltpu.VMEM((n, block_rows, 128), jnp.float32),
+            pltpu.SemaphoreType.DMA((3, 2, n)),
+        ],
+        compiler_params=pltpu.CompilerParams(collective_id=0, has_side_effects=True),
+    )(parts, residual, vocab_blocks)
 
 
 def on_device(
@@ -212,19 +315,16 @@
     low_rank = jnp.where(
         local_slot[:, None] == column_slot[None, :], lowered, jnp.zeros_like(lowered)
     )
-    partial_value = jnp.dot(attended, out_weight, preferred_element_type=jnp.float32)
-    partial_value = partial_value + jnp.dot(
-        low_rank, adapter_up, preferred_element_type=jnp.float32
-    )
-    summed = lax.psum_scatter(
-        partial_value.astype(jnp.bfloat16), "mp", scatter_dimension=1, tiled=True
-    )
-    final_rows = (residual.astype(jnp.float32) + summed.astype(jnp.float32)).astype(jnp.bfloat16)
-    group_rows = lax.all_gather(final_rows, "mp", axis=1, tiled=True)
-    partial_best = best_of(group_rows, group_vocab)
-    max_logits = lax.dynamic_slice_in_dim(
-        lax.pmax(partial_best, "mp"), own_shard * (rows_here // shards), rows_here // shards
-    )
+    out_blocks = out_weight.reshape(out_weight.shape[0], shards, slice_width)
+    up_blocks = adapter_up.reshape(adapter_up.shape[0], shards, slice_width)
+    partial_value = jnp.einsum(
+        "rk,kjc->jrc", attended, out_blocks, preferred_element_type=jnp.float32
+    ) + jnp.einsum("rk,kjc->jrc", low_rank, up_blocks, preferred_element_type=jnp.float32)
+    vocab_blocks = jnp.transpose(
+        group_vocab.reshape(group_vocab.shape[0], shards, slice_width), (1, 0, 2)
+    )
+    summed, best = mp_exchange(partial_value.astype(jnp.bfloat16), residual, vocab_blocks)
+    max_logits = best[:, 0]
     return (summed, state_norms, max_logits)
 
 

time: 209 us -> 243 us (1.16)
  Pallas kernels: 0 us -> 115 us
  waiting for transfers between devices: 93.8 us -> 8.8 us
  blocking collectives: 16.1 us -> 0 us
  local copies, waits for them, and re-layouts: 29 us -> 45 us
  other arithmetic: 12.8 us -> 18 us
  matrix products: 28.2 us -> 25.5 us
    pallas_call x0 -> x1, Pallas kernels: none -> 115 us  [mp_exchange(): pl.pallas_call(exchange_kernel, out_shape=(jax.ShapeDtypeStruct((rows_her...]
    reduce_scatter x1 -> x0, waiting for transfers between devices: 41 us -> none  [on_device(): lax.psum_scatter(partial_value.astype(jnp.bfloat16), 'mp', scatter_dimens...]
    all_gather x1 -> x0, waiting for transfers between devices: 39.5 us -> none  [on_device(): group_rows = lax.all_gather(final_rows, 'mp', axis=1, tiled=True)]
    pmax x1 -> x0, blocking collectives: 16.1 us -> none  [on_device(): lax.pmax(partial_best, 'mp')]
    dot_general x3 -> x0, matrix products: 7.05 us -> none  [the longest x1 3.17 us: best_of(): jnp.einsum('rd,vd->rv', candidates, piece, preferred_element_type=jnp.flo...]
    unnamed x0 -> x2, matrix products: none -> 4.35 us
    reshape x0 -> x1, local copies, waits for them, and re-layouts: none -> 3.89 us  [on_device(): group_vocab.reshape(group_vocab.shape[0], shards, slice_width)]
    optimization_barrier x0 -> x1, local copies, waits for them, and re-layouts: none -> 3.84 us  [on_device(): group_vocab, attended = lax.optimization_barrier((group_vocab, attended))]
  transfers between devices with their start and end apart: 5 -> 3, of which waited for: 4 -> 1; matrix products, arithmetic and copies ran while one was open for 29% -> 29% of each run, Pallas kernels for 0% -> 0%
where the time goes in v3:
time: 243 us; the launch traced here: 241 us
  Pallas kernels  115 us (47%)
  local copies, waits for them, and re-layouts  45 us (19%)
  matrix products  25.5 us (10%)
  other arithmetic  18 us (7%)
  between operations  15.8 us (7%)
  starting transfers between devices  9.62 us (4%)
  waiting for transfers between devices  8.8 us (4%)
  loops' own time  3.49 us (1%)
    pallas_call x1, Pallas kernels, mp_exchange(): pl.pallas_call(exchange_kernel, out_shape=(jax.ShapeDtypeStruct((rows_her...  115 us
    all_to_all x1, waiting for transfers between devices, on_device(): lax.all_to_all(jnp.concatenate([kept_pages, projected_pages, lowered_page...  8.1 us
    all_to_all x1, starting transfers between devices, on_device(): lax.all_to_all(jnp.concatenate([kept_pages, projected_pages, lowered_page...  7.53 us
  transfers between devices with their start and end apart: 3, of which 1 were waited for; matrix products, arithmetic and copies ran while one was open for 29% of the time, Pallas kernels for 0%

profile of v3, /device:TPU:8, one launch (start us, length us, event | category | flops | bytes accessed | tf_op | source)
XLA Modules:
  0.0 241.4 jit_solution(4934835924146689560)
XLA Ops:
  7.2 0.7 all-gather.2.cloned.1.call-update
  7.9 0.8 reshape.305
  8.8 1.0 sort.17
  10.0 0.8 gather_fusion.4
  11.3 1.9 gather_fusion
  13.2 2.0 fusion.49
  15.4 1.1 constant_dynamic-slice_fusion.4
  16.6 2.3 fusion.59
  18.9 1.2 fusion.56
  20.1 1.1 pad_maximum_fusion.2
  21.3 7.5 %all-to-all-start = ((bf16[32,2,8,640]{3,2,1,0:T(8,128)(2,1)}), bf16[32,2,8,640]{3,2,1,0:T(8,128)(2,1)S(1)}, u32[]{:S(2)}, u32[]{:S(2)}) async-start(bf16[32,2,8,640]{3,2,1,0:T(8,128)(2,1)} %pad_maximum_fusion.2), calls=%async_computation | async-start | bytes 1310720 | tf_op jit(solution)/shard_map/all_to_all | solution.py:227
  28.8 0.6 slice.56
  29.7 0.7 fusion.80
  31.3 0.7 sub.49
  32.9 8.1 %all-to-all-done = bf16[32,2,8,640]{3,2,1,0:T(8,128)(2,1)S(1)} async-done(((bf16[32,2,8,640]{3,2,1,0:T(8,128)(2,1)}), bf16[32,2,8,640]{3,2,1,0:T(8,128)(2,1)S(1)}, u32[]{:S(2)}, u32[]{:S(2)}) %all-to-all-start) | async-done | bytes 655392 | tf_op jit(solution)/shard_map/all_to_all | solution.py:227
  41.2 1.4 gather_fusion.1
  42.5 1.2 reshape_reshape.3
  44.2 0.7 broadcast_multiply_fusion
  45.0 1.3 gather_fusion.2
  46.3 1.3 gather_fusion.3
  47.6 1.2 multiply_multiply_fusion
  48.9 1.3 pad_maximum_fusion.1
  50.2 1.7 reshape.313
  51.9 2.3 convolution_convert_fusion
  54.2 1.8 reshape.308
  56.0 3.0 %reshape.317 = f32[2,2,256,273]{2,1,3,0:T(2,128)} reshape(f32[2,512,273]{1,2,0:T(8,128)} %get-tuple-element.313) | data formatting | bytes 2236416 | tf_op jit(solution)/shard_map/reshape | solution.py:282
  59.0 0.7 fusion.82
  59.8 2.1 concatenate.15
  61.9 2.0 collective-permute-start
  63.9 3.7 %fusion.68 = f32[512,1792]{0,1} fusion(bf16[128,1792]{1,0:T(8,128)(2,1)} %param.18, bf16[64,8,128]{2,1,0:T(8,128)(2,1)} %gather_fusion.2, s32[128]{0:T(128)} %and_select_fusion, s32[64,8]{1,0:T(8,128)} %sub.49), kind=kOutput, calls=%fused_computation.100 | convolution fusion | flops 235012096 | bytes 4262400
  67.6 0.6 bitcast_bitcast_fusion.1
  70.1 30.2 %while.21 = (s32[]{:T(128)}, f32[2,273,112]{2,1,0:T(8,128)S(1)}, f32[2,273]{0,1:T(8,128)S(1)}, s32[]{:T(128)}, bf16[2,2,256,112]{2,3,1,0:T(8,128)(2,1)S(1)}, /*i...) while((s32[]{:T(128)}, f32[2,273,112]{2,1,0:T(8,128)S(1)}, ...), condition=%wide.region_10.11_spmd, body=%wide.region_4.10_spmd.sunk | while | flops 1377437056 | bytes 21791080 | solution.py:297
  70.3 0.7 dynamic-slice.2
  72.1 0.6 multiply_reduce_fusion.2
  73.3 0.7 fusion.143
  74.0 1.2 compare_convert_fusion.6
  76.3 0.7 convolution_multiply_fusion.7
  77.5 0.7 fusion.136
  78.2 1.2 constant_dynamic-slice_fusion.7
  79.9 0.8 convolution_multiply_fusion.6
  81.2 0.9 fusion.142
  82.5 1.1 fusion.134
  83.6 0.8 convolution_add_fusion.3
  85.3 0.7 dynamic-slice.2
  87.2 0.6 multiply_reduce_fusion.2
  88.4 0.7 fusion.143
  89.1 1.2 compare_convert_fusion.6
  90.7 0.6 fusion.140
  91.3 0.7 convolution_multiply_fusion.7
  92.5 0.7 fusion.136
  93.3 1.2 constant_dynamic-slice_fusion.7
  94.9 0.8 convolution_multiply_fusion.6
  96.3 0.9 fusion.142
  97.5 1.1 fusion.134
  98.6 0.8 convolution_add_fusion.3
  100.6 3.8 %copy.151 = bf16[512,1792]{0,1:T(8,128)(2,1)} copy(bf16[512,1792]{1,0:T(8,128)(2,1)} %all-gather.2.cloned.1.call-done) | data formatting | bytes 3670016 | tf_op jit(solution)/shard_map/optimization_barrier | solution.py:303
  104.5 3.9 %copy.152 = bf16[512,8,224]{2,0,1:T(8,128)(2,1)} copy(bf16[512,8,224]{0,2,1:T(8,128)(2,1)} %bitcast.238) | data formatting | bytes 3670016 | tf_op jit(solution)/shard_map/reshape | solution.py:324
  108.4 0.7 fusion.83
  109.0 1.4 copy-done.1
  110.4 1.9 add.194
  112.3 3.8 %copy.150 = bf16[512,8,224]{2,0,1:T(8,128)(2,1)} copy(bf16[512,8,224]{0,2,1:T(8,128)(2,1)} %add.194) | data formatting | bytes 3670016 | tf_op jit(solution)/shard_map/add | solution.py:320
  116.1 115.2 %shard_map.130 = (bf16[512,224]{1,0:T(8,128)(2,1)}, f32[64,128]{1,0:T(8,128)}) custom-call(bf16[8,512,224]{2,1,0:T(8,128)(2,1)} %bitcast.237, bf16[512,224]{1,0:T(8,128)(2,1)} %bitcast.249, bf16[8,512,224]{2,1,0:T(8,128)(2,1)} %bitcast.236), custom_call_target="tpu_custom_call" | custom-call | tf_op jit(solution)/shard_map/pallas_call | solution.py:169
  231.4 1.8 copy.154
  233.2 1.4 slice_reduce_fusion
  (155 shorter events, 12.0 us)
Async XLA Ops:
  7.2 4.1 %copy-start = (bf16[512,1792]{1,0:T(8,128)(2,1)S(1)}, bf16[512,1792]{1,0:T(8,128)(2,1)}, u32[]{:S(2)}) copy-start(bf16[512,1792]{1,0:T(8,128)(2,1)} %param.13) | copy-start | bytes 5505028
  7.2 93.4 %all-gather.2.cloned.1.call-start = ((), (), s32[]{:S(2)}) async-start(), calls=%async_computation.1 | async-start | bytes 1892352 | tf_op jit(solution)/shard_map/all_gather | solution.py:248
  13.2 3.3 %copy-start.23 = (bf16[1792,128]{1,0:T(8,128)(2,1)S(1)}, bf16[1792,128]{1,0:T(8,128)(2,1)}, u32[]{:S(2)}) copy-start(bf16[1792,128]{1,0:T(8,128)(2,1)} %param.17) | copy-start | bytes 1376260
  13.2 3.3 %copy-start.24 = (f32[1792]{0:T(1024)S(1)}, f32[1792]{0:T(1024)}, u32[]{:S(2)}) copy-start(f32[1792]{0:T(1024)} %param.14) | copy-start | bytes 21508
  16.6 2.4 copy-start.4
  16.6 2.4 copy-start.22
  20.1 8.7 %copy-start.18 = (s32[512]{0:T(512)S(1)}, s32[512]{0:T(512)}, u32[]{:S(2)}) copy-start(s32[512]{0:T(512)} %param.20) | copy-start | bytes 6148
  20.1 9.4 %copy-start.20 = (s32[128]{0:T(128)S(1)}, s32[128]{0:T(128)}, u32[]{:S(2)}) copy-start(s32[128]{0:T(128)} %param.21) | copy-start | bytes 1540
  20.1 10.4 %copy-start.21 = (s32[64]{0:T(128)S(1)}, s32[64]{0:T(128)}, u32[]{:S(2)}) copy-start(s32[64]{0:T(128)} %param.22) | copy-start | bytes 772
  21.3 19.7 %all-to-all-start = ((bf16[32,2,8,640]{3,2,1,0:T(8,128)(2,1)}), bf16[32,2,8,640]{3,2,1,0:T(8,128)(2,1)S(1)}, u32[]{:S(2)}, u32[]{:S(2)}) async-start(bf16[32,2,8,640]{3,2,1,0:T(8,128)(2,1)} %pad_maximum_fusion.2), calls=%async_computation | async-start | bytes 1310720 | tf_op jit(solution)/shard_map/all_to_all | solution.py:227
  44.1 3.5 %copy-start.5 = (bf16[512,2,144]{0,2,1:T(8,128)(2,1)}, bf16[512,2,144]{0,2,1:T(8,128)(2,1)S(1)}, u32[]{:S(2)}) copy-start(bf16[512,2,144]{0,2,1:T(8,128)(2,1)S(1)} %copy.140) | copy-start | bytes 884740
  47.6 1.3 copy-start.9
  47.6 1.3 copy-start.10
  61.9 5.7 %copy-start.6 = (f32[2,512,16]{1,2,0:T(8,128)S(1)}, f32[2,512,16]{1,2,0:T(8,128)}, u32[]{:S(2)}) copy-start(f32[2,512,16]{1,2,0:T(8,128)} %get-tuple-element.309) | copy-start | bytes 196612
  61.9 5.7 %copy-start.7 = (f32[2,512,16]{1,2,0:T(8,128)S(1)}, f32[2,512,16]{1,2,0:T(8,128)}, u32[]{:S(2)}) copy-start(f32[2,512,16]{1,2,0:T(8,128)} %get-tuple-element.310) | copy-start | bytes 196612
  61.9 8.2 %copy-start.11 = (bf16[2,2,256,112]{2,3,1,0:T(8,128)(2,1)S(1)}, bf16[2,2,256,112]{2,3,1,0:T(8,128)(2,1)}, u32[]{:S(2)}) copy-start(bf16[2,2,256,112]{2,3,1,0:T(8,128)(2,1)} %custom-call.10) | copy-start | bytes 688132
  61.9 6.4 %collective-permute-start = (bf16[61699]{0:T(1024)(128)(2,1)S(1)}, bf16[61699]{0:T(1024)(128)(2,1)S(1)}, u32[]{:S(2)}, u32[]{:S(2)}) collective-permute-start(bf16[61699]{0:T(1024)(128)(2,1)S(1)} %concatenate.15), channel_id=1, source_target_pairs={{0,8},{8,16},{16,24},{24,32},{32,40},{40,48},{48,56},{56,64},{64,7... | collective-permute-start | bytes 370202 | tf_op jit(solution)/shard_map/ppermute | solution.py:20
  70.3 3.1 %copy-start.15 = (s32[2,256]{1,0:T(2,128)}, s32[2,256]{1,0:T(2,128)S(1)}, u32[]{:S(2)}) copy-start(s32[2,256]{1,0:T(2,128)S(1)} %get-tuple-element.444) | copy-start | bytes 6148 | tf_op jit(solution)/shard_map/while
  75.6 1.8 copy-start.14
  75.6 2.6 %copy-start.2 = (f32[2,2,256,273]{2,0,3,1:T(2,128)S(1)}, f32[2,2,256,273]{2,0,3,1:T(2,128)}, u32[]{:S(2)}) copy-start(f32[2,2,256,273]{2,0,3,1:T(2,128)} %get-tuple-element.445) | copy-start | bytes 3354628 | tf_op jit(solution)/shard_map/while
  75.6 2.6 %copy-start.3 = (f32[2,2,256,273]{2,0,3,1:T(2,128)S(1)}, f32[2,2,256,273]{2,0,3,1:T(2,128)}, u32[]{:S(2)}) copy-start(f32[2,2,256,273]{2,0,3,1:T(2,128)} %get-tuple-element.449) | copy-start | bytes 3354628 | tf_op jit(solution)/shard_map/while
  78.2 2.5 %copy-start.12 = (f32[1,256]{1,0:T(1,128)S(1)}, f32[1,256]{1,0:T(1,128)}, u32[]{:S(2)}) copy-start(f32[1,256]{1,0:T(1,128)} %get-tuple-element.407) | copy-start | bytes 3076 | tf_op jit(solution)/shard_map/while
  79.8 2.3 copy-start.17
  79.8 2.3 copy-start.19
  79.8 2.3 copy-start.25
  79.9 2.3 copy-start.27
  80.7 2.9 %copy-start.13 = (f32[256]{0:T(256)S(1)}, f32[256]{0:T(256)}, u32[]{:S(2)}) copy-start(f32[256]{0:T(256)} %get-tuple-element.402) | copy-start | bytes 3076 | tf_op jit(solution)/shard_map/while
  81.2 3.4 %copy-start.16 = (s32[2,256]{1,0:T(2,128)S(1)}, s32[2,256]{1,0:T(2,128)}, u32[]{:S(2)}) copy-start(s32[2,256]{1,0:T(2,128)} %copy-done.15) | copy-start | bytes 6148 | tf_op jit(solution)/shard_map/while
  82.5 2.1 copy-start.26
  85.3 3.1 %copy-start.15 = (s32[2,256]{1,0:T(2,128)}, s32[2,256]{1,0:T(2,128)S(1)}, u32[]{:S(2)}) copy-start(s32[2,256]{1,0:T(2,128)S(1)} %get-tuple-element.444) | copy-start | bytes 6148 | tf_op jit(solution)/shard_map/while
  90.6 1.8 copy-start.14
  90.7 2.6 %copy-start.2 = (f32[2,2,256,273]{2,0,3,1:T(2,128)S(1)}, f32[2,2,256,273]{2,0,3,1:T(2,128)}, u32[]{:S(2)}) copy-start(f32[2,2,256,273]{2,0,3,1:T(2,128)} %get-tuple-element.445) | copy-start | bytes 3354628 | tf_op jit(solution)/shard_map/while
  90.7 2.6 %copy-start.3 = (f32[2,2,256,273]{2,0,3,1:T(2,128)S(1)}, f32[2,2,256,273]{2,0,3,1:T(2,128)}, u32[]{:S(2)}) copy-start(f32[2,2,256,273]{2,0,3,1:T(2,128)} %get-tuple-element.449) | copy-start | bytes 3354628 | tf_op jit(solution)/shard_map/while
  93.2 2.5 %copy-start.12 = (f32[1,256]{1,0:T(1,128)S(1)}, f32[1,256]{1,0:T(1,128)}, u32[]{:S(2)}) copy-start(f32[1,256]{1,0:T(1,128)} %get-tuple-element.407) | copy-start | bytes 3076 | tf_op jit(solution)/shard_map/while
  94.9 2.3 copy-start.17
  94.9 2.3 copy-start.19
  94.9 2.3 copy-start.25
  94.9 2.3 copy-start.27
  95.8 2.9 %copy-start.13 = (f32[256]{0:T(256)S(1)}, f32[256]{0:T(256)}, u32[]{:S(2)}) copy-start(f32[256]{0:T(256)} %get-tuple-element.402) | copy-start | bytes 3076 | tf_op jit(solution)/shard_map/while
  96.2 3.4 %copy-start.16 = (s32[2,256]{1,0:T(2,128)S(1)}, s32[2,256]{1,0:T(2,128)}, u32[]{:S(2)}) copy-start(s32[2,256]{1,0:T(2,128)} %copy-done.15) | copy-start | bytes 6148 | tf_op jit(solution)/shard_map/while
  97.5 2.1 copy-start.26
  104.5 3.9 %copy-start.8 = (bf16[224,1792]{1,0:T(8,128)(2,1)S(1)}, bf16[224,1792]{1,0:T(8,128)(2,1)}, u32[]{:S(2)}) copy-start(bf16[224,1792]{1,0:T(8,128)(2,1)} %param.16) | copy-start | bytes 2408452
  108.4 2.0 copy-start.1
Sparse Core Ops, SparseCore 0:
  10.6 54.6 all-gather.1

commit v4 on v3

--- a/solution.py
+++ b/solution.py
@@ -86,63 +86,74 @@
 
 def exchange_kernel(
     part_ref, resid_ref, vocab_ref, upd_ref, best_ref,
-    land, rows, tops, got, sems,
+    land, acc, rows, tops, got, ring_sems, top_sems,
 ):
     n = part_ref.shape[0]
+    half = part_ref.shape[1] // 2
     block_rows = best_ref.shape[0]
     me = lax.axis_index("mp")
     grp = lax.axis_index("group")
     peers = [lax.rem(me + k, n) for k in range(1, n)]
     mesh_id = pl.DeviceIdType.MESH
+    towards = (lax.rem(me + 1, n), lax.rem(me + n - 1, n))
+    spans = (pl.ds(0, half), pl.ds(half, half))
 
     barrier = pltpu.get_barrier_semaphore()
     for p in peers:
         pl.semaphore_signal(barrier, inc=1, device_id=(grp, p), device_id_type=mesh_id)
     pl.semaphore_wait(barrier, n - 1)
 
-    def send_all(phase, src_of, dst):
+    def ring_copy(phase, way, step, src, dst):
+        return pltpu.make_async_remote_copy(
+            src_ref=src,
+            dst_ref=dst,
+            send_sem=ring_sems.at[phase, way, 0, step],
+            recv_sem=ring_sems.at[phase, way, 1, step],
+            device_id=(grp, towards[way]),
+            device_id_type=mesh_id,
+        )
+
+    def rs_chunk(way, step):
+        return lax.rem(me + (n - 1 - step if way == 0 else 1 + step) + n, n)
+
+    for step in range(n - 1):
         copies = []
-        for p in peers:
-            copy = pltpu.make_async_remote_copy(
-                src_ref=src_of(p),
-                dst_ref=dst.at[me],
-                send_sem=sems.at[phase, 0, p],
-                recv_sem=sems.at[phase, 1, me],
-                device_id=(grp, p),
-                device_id_type=mesh_id,
-            )
+        for way in range(2):
+            chunk = rs_chunk(way, step)
+            if step == 0:
+                src = part_ref.at[chunk, spans[way]]
+            else:
+                acc[way, step] = (
+                    land[way, step - 1].astype(jnp.float32)
+                    + part_ref[chunk, spans[way]].astype(jnp.float32)
+                ).astype(acc.dtype)
+                src = acc.at[way, step]
+            copy = ring_copy(0, way, step, src, land.at[way, step])
             copy.start()
             copies.append(copy)
-        return copies
-
-    def finish(phase, copies, src_of, dst):
         for copy in copies:
-            copy.wait_send()
-        for q in peers:
-            pltpu.make_async_remote_copy(
-                src_ref=src_of(q),
-                dst_ref=dst.at[q],
-                send_sem=sems.at[phase, 0, q],
-                recv_sem=sems.at[phase, 1, q],
-                device_id=(grp, q),
-                device_id_type=mesh_id,
-            ).wait_recv()
-
-    part_of = lambda p: part_ref.at[p]
-    sent = send_all(0, part_of, land)
-    finish(0, sent, part_of, land)
-    total = part_ref[me].astype(jnp.float32)
-    for q in peers:
-        total = total + land[q].astype(jnp.float32)
-    update = total.astype(upd_ref.dtype)
-    upd_ref[...] = update
-    rows[me] = (resid_ref[...].astype(jnp.float32) + update.astype(jnp.float32)).astype(
-        rows.dtype
-    )
-
-    own_rows = lambda p: rows.at[me]
-    sent = send_all(1, own_rows, rows)
-    finish(1, sent, own_rows, rows)
+            copy.wait()
+    for way in range(2):
+        total = land[way, n - 2].astype(jnp.float32) + part_ref[me, spans[way]].astype(
+            jnp.float32
+        )
+        update = total.astype(upd_ref.dtype)
+        upd_ref[spans[way]] = update
+        rows[me, spans[way]] = (
+            resid_ref[spans[way]].astype(jnp.float32) + update.astype(jnp.float32)
+        ).astype(rows.dtype)
+
+    for step in range(n - 1):
+        copies = []
+        for way in range(2):
+            chunk = lax.rem(me + (n - step if way == 0 else step), n)
+            view = rows.at[chunk, spans[way]]
+            copy = ring_copy(1, way, step, view, view)
+            copy.start()
+            copies.append(copy)
+        for copy in copies:
+            copy.wait()
+
     scores = jnp.zeros((rows.shape[1], vocab_ref.shape[1]), jnp.float32)
     for j in range(n):
         scores = scores + lax.dot_general(
@@ -153,9 +164,29 @@
         piece = jnp.max(scores[p * block_rows : (p + 1) * block_rows], axis=1, keepdims=True)
         tops[p] = jnp.broadcast_to(piece, tops.shape[1:])
 
-    top_of = lambda p: tops.at[p]
-    sent = send_all(2, top_of, got)
-    finish(2, sent, top_of, got)
+    sent = []
+    for p in peers:
+        copy = pltpu.make_async_remote_copy(
+            src_ref=tops.at[p],
+            dst_ref=got.at[me],
+            send_sem=top_sems.at[0, p],
+            recv_sem=top_sems.at[1, me],
+            device_id=(grp, p),
+            device_id_type=mesh_id,
+        )
+        copy.start()
+        sent.append(copy)
+    for copy in sent:
+        copy.wait_send()
+    for q in peers:
+        pltpu.make_async_remote_copy(
+            src_ref=tops.at[q],
+            dst_ref=got.at[q],
+            send_sem=top_sems.at[0, q],
+            recv_sem=top_sems.at[1, q],
+            device_id=(grp, q),
+            device_id_type=mesh_id,
+        ).wait_recv()
     best = tops[me]
     for q in peers:
         best = jnp.maximum(best, got[q])
@@ -175,11 +206,13 @@
         in_specs=[vmem] * 3,
         out_specs=(vmem, vmem),
         scratch_shapes=[
-            pltpu.VMEM((n, rows_here, width), jnp.bfloat16),
+            pltpu.VMEM((2, n - 1, rows_here // 2, width), jnp.bfloat16),
+            pltpu.VMEM((2, n - 1, rows_here // 2, width), jnp.bfloat16),
             pltpu.VMEM((n, rows_here, width), jnp.bfloat16),
             pltpu.VMEM((n, block_rows, 128), jnp.float32),
             pltpu.VMEM((n, block_rows, 128), jnp.float32),
-            pltpu.SemaphoreType.DMA((3, 2, n)),
+            pltpu.SemaphoreType.DMA((2, 2, 2, n - 1)),
+            pltpu.SemaphoreType.DMA((2, n)),
         ],
         compiler_params=pltpu.CompilerParams(collective_id=0, has_side_effects=True),
     )(parts, residual, vocab_blocks)

time: 243 us -> 220 us (0.905)
  Pallas kernels: 115 us -> 92.7 us
    pallas_call x1, Pallas kernels: 115 us -> 92.7 us  [mp_exchange(): pl.pallas_call(exchange_kernel, out_shape=(jax.ShapeDtypeStruct((rows_her...]
  transfers between devices with their start and end apart: 3 -> 3, of which waited for: 1 -> 1; matrix products, arithmetic and copies ran while one was open for 29% -> 32% of each run, Pallas kernels for 0% -> 0%
where the time goes in v4:
time: 220 us; the launch traced here: 219 us
  Pallas kernels  92.7 us (42%)
  local copies, waits for them, and re-layouts  45 us (20%)
  matrix products  25.5 us (12%)
  other arithmetic  18 us (8%)
  between operations  15.8 us (7%)
  starting transfers between devices  9.62 us (4%)
  waiting for transfers between devices  8.81 us (4%)
  loops' own time  3.49 us (2%)
    pallas_call x1, Pallas kernels, mp_exchange(): pl.pallas_call(exchange_kernel, out_shape=(jax.ShapeDtypeStruct((rows_her...  92.7 us
    all_to_all x1, waiting for transfers between devices, on_device(): lax.all_to_all(jnp.concatenate([kept_pages, projected_pages, lowered_page...  8.1 us
    all_to_all x1, starting transfers between devices, on_device(): lax.all_to_all(jnp.concatenate([kept_pages, projected_pages, lowered_page...  7.53 us
    reshape x3, local copies, waits for them, and re-layouts, regroup(): values.reshape(values.shape[0], blocks, block_len, values.shape[-1])  4.77 us
  transfers between devices with their start and end apart: 3, of which 1 were waited for; matrix products, arithmetic and copies ran while one was open for 32% of the time, Pallas kernels for 0%

profile of v4, /device:TPU:8, one launch (start us, length us, event | category | flops | bytes accessed | tf_op | source)
XLA Modules:
  0.0 218.9 jit_solution(11543971316110599347)
XLA Ops:
  7.2 0.7 all-gather.2.cloned.1.call-update
  7.9 0.8 reshape.305
  8.8 1.0 sort.17
  10.0 0.8 gather_fusion.4
  11.3 1.9 gather_fusion
  13.2 2.0 fusion.49
  15.4 1.1 constant_dynamic-slice_fusion.4
  16.6 2.3 %fusion.59 = bf16[32,2,8,128]{3,2,1,0:T(8,128)(2,1)S(1)} fusion(bf16[32,2,8,1792]{3,2,1,0:T(8,128)(2,1)} %bitcast.234, f32[1792]{0:T(1024)S(1)} %copy-done.24, f32[32,2,8]{2,1,0:T(2,128)S(1)} %copy.139, bf16[1792,128]{1,0:T(8,128)(2,1)S(1)} %copy-done.23), kind=kOutput, calls=%fused_computation.83 | convolution fusion | flops 238616576 | bytes 2434048 | tf_op jit(solution)/shard_map/abrd,dc->abrc/dot_general | solution.py:255
  18.9 1.2 fusion.56
  20.1 1.1 pad_maximum_fusion.2
  21.3 7.5 %all-to-all-start = ((bf16[32,2,8,640]{3,2,1,0:T(8,128)(2,1)}), bf16[32,2,8,640]{3,2,1,0:T(8,128)(2,1)S(1)}, u32[]{:S(2)}, u32[]{:S(2)}) async-start(bf16[32,2,8,640]{3,2,1,0:T(8,128)(2,1)} %pad_maximum_fusion.2), calls=%async_computation | async-start | bytes 1310720 | tf_op jit(solution)/shard_map/all_to_all | solution.py:260
  28.8 0.6 slice.56
  29.7 0.7 fusion.80
  31.3 0.7 sub.49
  32.9 8.1 %all-to-all-done = bf16[32,2,8,640]{3,2,1,0:T(8,128)(2,1)S(1)} async-done(((bf16[32,2,8,640]{3,2,1,0:T(8,128)(2,1)}), bf16[32,2,8,640]{3,2,1,0:T(8,128)(2,1)S(1)}, u32[]{:S(2)}, u32[]{:S(2)}) %all-to-all-start) | async-done | bytes 655392 | tf_op jit(solution)/shard_map/all_to_all | solution.py:260
  41.2 1.4 gather_fusion.1
  42.5 1.2 reshape_reshape.3
  44.2 0.7 broadcast_multiply_fusion
  45.0 1.3 gather_fusion.2
  46.3 1.3 gather_fusion.3
  47.6 1.2 multiply_multiply_fusion
  48.9 1.3 pad_maximum_fusion.1
  50.2 1.7 reshape.313
  51.9 2.3 %convolution_convert_fusion = bf16[2,273,112]{2,1,0:T(8,128)(2,1)} fusion(f32[2,512,273]{1,2,0:T(8,128)S(1)} %get-tuple-element.314, f32[512]{0:T(512)S(1)} %get-tuple-element.299, bf16[2,512,144]{1,2,0:T(8,128)(2,1)} %bitcast.241), kind=kOutput, calls=%fused_computation.82 | convolution fusion | flops 376058592 | bytes 1471936 | tf_op jit(solution)/shard_map/hcp,hce->hpe/dot_general | solution.py:293
  54.2 1.8 reshape.308
  56.0 3.0 %reshape.317 = f32[2,2,256,273]{2,1,3,0:T(2,128)} reshape(f32[2,512,273]{1,2,0:T(8,128)} %get-tuple-element.313) | data formatting | bytes 2236416 | tf_op jit(solution)/shard_map/reshape | solution.py:315
  59.0 0.7 fusion.82
  59.8 2.1 concatenate.15
  61.9 2.0 collective-permute-start
  63.9 3.7 %fusion.68 = f32[512,1792]{0,1} fusion(bf16[128,1792]{1,0:T(8,128)(2,1)} %param.18, bf16[64,8,128]{2,1,0:T(8,128)(2,1)} %gather_fusion.2, s32[128]{0:T(128)} %and_select_fusion, s32[64,8]{1,0:T(8,128)} %sub.49), kind=kOutput, calls=%fused_computation.100 | convolution fusion | flops 235012096 | bytes 4262400
  67.6 0.6 bitcast_bitcast_fusion.1
  70.1 30.3 %while.21 = (s32[]{:T(128)}, f32[2,273,112]{2,1,0:T(8,128)S(1)}, f32[2,273]{0,1:T(8,128)S(1)}, s32[]{:T(128)}, bf16[2,2,256,112]{2,3,1,0:T(8,128)(2,1)S(1)}, /*i...) while((s32[]{:T(128)}, f32[2,273,112]{2,1,0:T(8,128)S(1)}, ...), condition=%wide.region_10.11_spmd, body=%wide.region_4.10_spmd.sunk | while | flops 1377437056 | bytes 21791080 | solution.py:330
  70.3 0.7 dynamic-slice.2
  72.1 0.6 multiply_reduce_fusion.2
  73.4 0.7 fusion.143
  74.1 1.2 compare_convert_fusion.6
  76.3 0.7 convolution_multiply_fusion.7
  77.5 0.7 fusion.136
  78.2 1.2 constant_dynamic-slice_fusion.7
  79.9 0.8 convolution_multiply_fusion.6
  81.2 0.9 fusion.142
  82.5 1.1 fusion.134
  83.6 0.8 convolution_add_fusion.3
  85.3 0.7 dynamic-slice.2
  87.2 0.6 multiply_reduce_fusion.2
  88.4 0.7 fusion.143
  89.1 1.2 compare_convert_fusion.6
  90.7 0.6 fusion.140
  91.3 0.7 convolution_multiply_fusion.7
  92.5 0.7 fusion.136
  93.3 1.2 constant_dynamic-slice_fusion.7
  94.9 0.8 convolution_multiply_fusion.6
  96.3 0.9 fusion.142
  97.6 1.1 fusion.134
  98.6 0.8 convolution_add_fusion.3
  100.7 3.8 %copy.151 = bf16[512,1792]{0,1:T(8,128)(2,1)} copy(bf16[512,1792]{1,0:T(8,128)(2,1)} %all-gather.2.cloned.1.call-done) | data formatting | bytes 3670016 | tf_op jit(solution)/shard_map/optimization_barrier | solution.py:336
  104.5 3.9 %copy.152 = bf16[512,8,224]{2,0,1:T(8,128)(2,1)} copy(bf16[512,8,224]{0,2,1:T(8,128)(2,1)} %bitcast.238) | data formatting | bytes 3670016 | tf_op jit(solution)/shard_map/reshape | solution.py:357
  108.4 0.7 fusion.83
  109.1 1.4 copy-done.1
  110.4 1.9 add.194
  112.4 3.8 %copy.150 = bf16[512,8,224]{2,0,1:T(8,128)(2,1)} copy(bf16[512,8,224]{0,2,1:T(8,128)(2,1)} %add.194) | data formatting | bytes 3670016 | tf_op jit(solution)/shard_map/add | solution.py:353
  116.1 92.7 %shard_map.130 = (bf16[512,224]{1,0:T(8,128)(2,1)}, f32[64,128]{1,0:T(8,128)}) custom-call(bf16[8,512,224]{2,1,0:T(8,128)(2,1)} %bitcast.237, bf16[512,224]{1,0:T(8,128)(2,1)} %bitcast.249, bf16[8,512,224]{2,1,0:T(8,128)(2,1)} %bitcast.236), custom_call_target="tpu_custom_call" | custom-call | tf_op jit(solution)/shard_map/pallas_call | solution.py:200
  208.9 1.8 copy.154
  210.6 1.4 slice_reduce_fusion
  (155 shorter events, 12.0 us)
Async XLA Ops:
  7.2 4.1 %copy-start = (bf16[512,1792]{1,0:T(8,128)(2,1)S(1)}, bf16[512,1792]{1,0:T(8,128)(2,1)}, u32[]{:S(2)}) copy-start(bf16[512,1792]{1,0:T(8,128)(2,1)} %param.13) | copy-start | bytes 5505028
  7.2 93.5 %all-gather.2.cloned.1.call-start = ((), (), s32[]{:S(2)}) async-start(), calls=%async_computation.1 | async-start | bytes 1892352 | tf_op jit(solution)/shard_map/all_gather | solution.py:281
  13.2 3.3 %copy-start.23 = (bf16[1792,128]{1,0:T(8,128)(2,1)S(1)}, bf16[1792,128]{1,0:T(8,128)(2,1)}, u32[]{:S(2)}) copy-start(bf16[1792,128]{1,0:T(8,128)(2,1)} %param.17) | copy-start | bytes 1376260
  13.2 3.3 %copy-start.24 = (f32[1792]{0:T(1024)S(1)}, f32[1792]{0:T(1024)}, u32[]{:S(2)}) copy-start(f32[1792]{0:T(1024)} %param.14) | copy-start | bytes 21508
  16.6 2.4 %copy-start.4 = (bf16[64,8,1792]{2,1,0:T(8,128)(2,1)S(1)}, bf16[64,8,1792]{2,1,0:T(8,128)(2,1)}, u32[]{:S(2)}) copy-start(bf16[64,8,1792]{2,1,0:T(8,128)(2,1)} %gather_fusion) | copy-start | bytes 5505028
  16.6 2.4 %copy-start.22 = (bf16[1792,288]{0,1:T(8,128)(2,1)S(1)}, bf16[1792,288]{0,1:T(8,128)(2,1)}, u32[]{:S(2)}) copy-start(bf16[1792,288]{0,1:T(8,128)(2,1)} %param.15) | copy-start | bytes 3096580
  20.1 8.7 %copy-start.18 = (s32[512]{0:T(512)S(1)}, s32[512]{0:T(512)}, u32[]{:S(2)}) copy-start(s32[512]{0:T(512)} %param.20) | copy-start | bytes 6148
  20.1 9.4 %copy-start.20 = (s32[128]{0:T(128)S(1)}, s32[128]{0:T(128)}, u32[]{:S(2)}) copy-start(s32[128]{0:T(128)} %param.21) | copy-start | bytes 1540
  20.1 10.4 %copy-start.21 = (s32[64]{0:T(128)S(1)}, s32[64]{0:T(128)}, u32[]{:S(2)}) copy-start(s32[64]{0:T(128)} %param.22) | copy-start | bytes 772
  21.3 19.7 %all-to-all-start = ((bf16[32,2,8,640]{3,2,1,0:T(8,128)(2,1)}), bf16[32,2,8,640]{3,2,1,0:T(8,128)(2,1)S(1)}, u32[]{:S(2)}, u32[]{:S(2)}) async-start(bf16[32,2,8,640]{3,2,1,0:T(8,128)(2,1)} %pad_maximum_fusion.2), calls=%async_computation | async-start | bytes 1310720 | tf_op jit(solution)/shard_map/all_to_all | solution.py:260
  44.1 3.5 %copy-start.5 = (bf16[512,2,144]{0,2,1:T(8,128)(2,1)}, bf16[512,2,144]{0,2,1:T(8,128)(2,1)S(1)}, u32[]{:S(2)}) copy-start(bf16[512,2,144]{0,2,1:T(8,128)(2,1)S(1)} %copy.140) | copy-start | bytes 884740
  47.6 1.3 copy-start.9
  47.6 1.3 copy-start.10
  61.9 5.8 %copy-start.6 = (f32[2,512,16]{1,2,0:T(8,128)S(1)}, f32[2,512,16]{1,2,0:T(8,128)}, u32[]{:S(2)}) copy-start(f32[2,512,16]{1,2,0:T(8,128)} %get-tuple-element.309) | copy-start | bytes 196612
  61.9 5.8 %copy-start.7 = (f32[2,512,16]{1,2,0:T(8,128)S(1)}, f32[2,512,16]{1,2,0:T(8,128)}, u32[]{:S(2)}) copy-start(f32[2,512,16]{1,2,0:T(8,128)} %get-tuple-element.310) | copy-start | bytes 196612
  61.9 8.2 %copy-start.11 = (bf16[2,2,256,112]{2,3,1,0:T(8,128)(2,1)S(1)}, bf16[2,2,256,112]{2,3,1,0:T(8,128)(2,1)}, u32[]{:S(2)}) copy-start(bf16[2,2,256,112]{2,3,1,0:T(8,128)(2,1)} %custom-call.10) | copy-start | bytes 688132
  61.9 6.4 %collective-permute-start = (bf16[61699]{0:T(1024)(128)(2,1)S(1)}, bf16[61699]{0:T(1024)(128)(2,1)S(1)}, u32[]{:S(2)}, u32[]{:S(2)}) collective-permute-start(bf16[61699]{0:T(1024)(128)(2,1)S(1)} %concatenate.15), channel_id=1, source_target_pairs={{0,8},{8,16},{16,24},{24,32},{32,40},{40,48},{48,56},{56,64},{64,7... | collective-permute-start | bytes 370202 | tf_op jit(solution)/shard_map/ppermute | solution.py:20
  70.3 3.1 %copy-start.15 = (s32[2,256]{1,0:T(2,128)}, s32[2,256]{1,0:T(2,128)S(1)}, u32[]{:S(2)}) copy-start(s32[2,256]{1,0:T(2,128)S(1)} %get-tuple-element.444) | copy-start | bytes 6148 | tf_op jit(solution)/shard_map/while
  75.6 1.8 copy-start.14
  75.6 2.6 %copy-start.2 = (f32[2,2,256,273]{2,0,3,1:T(2,128)S(1)}, f32[2,2,256,273]{2,0,3,1:T(2,128)}, u32[]{:S(2)}) copy-start(f32[2,2,256,273]{2,0,3,1:T(2,128)} %get-tuple-element.445) | copy-start | bytes 3354628 | tf_op jit(solution)/shard_map/while
  75.6 2.6 %copy-start.3 = (f32[2,2,256,273]{2,0,3,1:T(2,128)S(1)}, f32[2,2,256,273]{2,0,3,1:T(2,128)}, u32[]{:S(2)}) copy-start(f32[2,2,256,273]{2,0,3,1:T(2,128)} %get-tuple-element.449) | copy-start | bytes 3354628 | tf_op jit(solution)/shard_map/while
  78.2 2.5 %copy-start.12 = (f32[1,256]{1,0:T(1,128)S(1)}, f32[1,256]{1,0:T(1,128)}, u32[]{:S(2)}) copy-start(f32[1,256]{1,0:T(1,128)} %get-tuple-element.407) | copy-start | bytes 3076 | tf_op jit(solution)/shard_map/while
  79.9 2.3 %copy-start.17 = (f32[256]{0:T(256)S(1)}, f32[256]{0:T(256)}, u32[]{:S(2)}) copy-start(f32[256]{0:T(256)} %fusion.143) | copy-start | bytes 3076 | tf_op jit(solution)/shard_map/while
  79.9 2.3 %copy-start.19 = (f32[2]{0:T(128)S(1)}, f32[2]{0:T(128)}, u32[]{:S(2)}) copy-start(f32[2]{0:T(128)} %multiply_reduce_fusion.2) | copy-start | bytes 28 | tf_op jit(solution)/shard_map/while
  79.9 2.3 %copy-start.25 = (f32[2,2,256]{2,1,0:T(2,128)S(1)}, f32[2,2,256]{2,1,0:T(2,128)}, u32[]{:S(2)}) copy-start(f32[2,2,256]{2,1,0:T(2,128)} %get-tuple-element.428) | copy-start | bytes 12292 | tf_op jit(solution)/shard_map/while
  79.9 2.3 %copy-start.27 = (f32[2]{0:T(128)S(1)}, f32[2]{0:T(128)}, u32[]{:S(2)}) copy-start(f32[2]{0:T(128)} %slice_bitcast_fusion.2) | copy-start | bytes 28 | tf_op jit(solution)/shard_map/while
  80.7 2.9 %copy-start.13 = (f32[256]{0:T(256)S(1)}, f32[256]{0:T(256)}, u32[]{:S(2)}) copy-start(f32[256]{0:T(256)} %get-tuple-element.402) | copy-start | bytes 3076 | tf_op jit(solution)/shard_map/while
  81.2 3.4 %copy-start.16 = (s32[2,256]{1,0:T(2,128)S(1)}, s32[2,256]{1,0:T(2,128)}, u32[]{:S(2)}) copy-start(s32[2,256]{1,0:T(2,128)} %copy-done.15) | copy-start | bytes 6148 | tf_op jit(solution)/shard_map/while
  82.5 2.1 copy-start.26
  85.3 3.1 %copy-start.15 = (s32[2,256]{1,0:T(2,128)}, s32[2,256]{1,0:T(2,128)S(1)}, u32[]{:S(2)}) copy-start(s32[2,256]{1,0:T(2,128)S(1)} %get-tuple-element.444) | copy-start | bytes 6148 | tf_op jit(solution)/shard_map/while
  90.7 1.8 copy-start.14
  90.7 2.6 %copy-start.2 = (f32[2,2,256,273]{2,0,3,1:T(2,128)S(1)}, f32[2,2,256,273]{2,0,3,1:T(2,128)}, u32[]{:S(2)}) copy-start(f32[2,2,256,273]{2,0,3,1:T(2,128)} %get-tuple-element.445) | copy-start | bytes 3354628 | tf_op jit(solution)/shard_map/while
  90.7 2.6 %copy-start.3 = (f32[2,2,256,273]{2,0,3,1:T(2,128)S(1)}, f32[2,2,256,273]{2,0,3,1:T(2,128)}, u32[]{:S(2)}) copy-start(f32[2,2,256,273]{2,0,3,1:T(2,128)} %get-tuple-element.449) | copy-start | bytes 3354628 | tf_op jit(solution)/shard_map/while
  93.3 2.5 %copy-start.12 = (f32[1,256]{1,0:T(1,128)S(1)}, f32[1,256]{1,0:T(1,128)}, u32[]{:S(2)}) copy-start(f32[1,256]{1,0:T(1,128)} %get-tuple-element.407) | copy-start | bytes 3076 | tf_op jit(solution)/shard_map/while
  94.9 2.3 %copy-start.17 = (f32[256]{0:T(256)S(1)}, f32[256]{0:T(256)}, u32[]{:S(2)}) copy-start(f32[256]{0:T(256)} %fusion.143) | copy-start | bytes 3076 | tf_op jit(solution)/shard_map/while
  94.9 2.3 %copy-start.19 = (f32[2]{0:T(128)S(1)}, f32[2]{0:T(128)}, u32[]{:S(2)}) copy-start(f32[2]{0:T(128)} %multiply_reduce_fusion.2) | copy-start | bytes 28 | tf_op jit(solution)/shard_map/while
  94.9 2.3 %copy-start.25 = (f32[2,2,256]{2,1,0:T(2,128)S(1)}, f32[2,2,256]{2,1,0:T(2,128)}, u32[]{:S(2)}) copy-start(f32[2,2,256]{2,1,0:T(2,128)} %get-tuple-element.428) | copy-start | bytes 12292 | tf_op jit(solution)/shard_map/while
  94.9 2.3 %copy-start.27 = (f32[2]{0:T(128)S(1)}, f32[2]{0:T(128)}, u32[]{:S(2)}) copy-start(f32[2]{0:T(128)} %slice_bitcast_fusion.2) | copy-start | bytes 28 | tf_op jit(solution)/shard_map/while
  95.8 2.9 %copy-start.13 = (f32[256]{0:T(256)S(1)}, f32[256]{0:T(256)}, u32[]{:S(2)}) copy-start(f32[256]{0:T(256)} %get-tuple-element.402) | copy-start | bytes 3076 | tf_op jit(solution)/shard_map/while
  96.3 3.4 %copy-start.16 = (s32[2,256]{1,0:T(2,128)S(1)}, s32[2,256]{1,0:T(2,128)}, u32[]{:S(2)}) copy-start(s32[2,256]{1,0:T(2,128)} %copy-done.15) | copy-start | bytes 6148 | tf_op jit(solution)/shard_map/while
  97.5 2.1 copy-start.26
  104.5 3.9 %copy-start.8 = (bf16[224,1792]{1,0:T(8,128)(2,1)S(1)}, bf16[224,1792]{1,0:T(8,128)(2,1)}, u32[]{:S(2)}) copy-start(bf16[224,1792]{1,0:T(8,128)(2,1)} %param.16) | copy-start | bytes 2408452
  108.4 2.0 copy-start.1
Sparse Core Ops, SparseCore 0:
  10.6 54.6 all-gather.1

commit v5 on v2

--- a/solution.py
+++ b/solution.py
@@ -2,6 +2,8 @@
 import jax.numpy as jnp
 from jax import lax
 from jax.sharding import PartitionSpec as P
+from jax.experimental import pallas as pl
+from jax.experimental.pallas import tpu as pltpu
 
 FEAT = 16
 HD = 112
@@ -57,8 +59,9 @@
     key_scores = jnp.einsum("hcf,hdf->hcd", key_rows, key_rows, precision=PRECISE) * scaling
     value_gram = jnp.einsum("hce,hde->hcd", value_rows, value_rows, precision=PRECISE)
     key_gram = (1.0 + key_scores + 0.5 * key_scores * key_scores) * value_gram
-    masked_gram = jnp.einsum("cd,hde->hce", allowed, key_gram, precision=PRECISE)
-    local_squares = jnp.sum(masked_gram * allowed[None], axis=-1)
+    diagonal = (position[:, None] == position[None, :]).astype(jnp.float32)
+    row_terms = jnp.sum(key_gram * (allowed * (2.0 - diagonal))[None], axis=-1)
+    local_squares = jnp.einsum("cd,hd->hc", allowed, row_terms, precision=PRECISE)
     along = jnp.sum(
         jnp.einsum("hcp,hpe->hce", phi_key, states, precision=PRECISE) * value_rows, axis=-1
     )
@@ -80,6 +83,63 @@
 def best_of(candidates, piece):
     logits = jnp.einsum("rd,vd->rv", candidates, piece, preferred_element_type=jnp.float32)
     return jnp.max(logits, axis=1)
+
+
+def top_kernel(tops, best_ref, got, sems):
+    n = tops.shape[0]
+    me = lax.axis_index("mp")
+    grp = lax.axis_index("group")
+    peers = [lax.rem(me + k, n) for k in range(1, n)]
+    mesh_id = pl.DeviceIdType.MESH
+    barrier = pltpu.get_barrier_semaphore()
+    for p in peers:
+        pl.semaphore_signal(barrier, inc=1, device_id=(grp, p), device_id_type=mesh_id)
+    pl.semaphore_wait(barrier, n - 1)
+    sent = []
+    for p in peers:
+        copy = pltpu.make_async_remote_copy(
+            src_ref=tops.at[p],
+            dst_ref=got.at[me],
+            send_sem=sems.at[0, p],
+            recv_sem=sems.at[1, me],
+            device_id=(grp, p),
+            device_id_type=mesh_id,
+        )
+        copy.start()
+        sent.append(copy)
+    for copy in sent:
+        copy.wait_send()
+    for q in peers:
+        pltpu.make_async_remote_copy(
+            src_ref=tops.at[q],
+            dst_ref=got.at[q],
+            send_sem=sems.at[0, q],
+            recv_sem=sems.at[1, q],
+            device_id=(grp, q),
+            device_id_type=mesh_id,
+        ).wait_recv()
+    best = tops[me]
+    for q in peers:
+        best = jnp.maximum(best, got[q])
+    best_ref[...] = best
+
+
+def mp_max(partial_best, shards):
+    block_rows = partial_best.shape[0] // shards
+    tops = jnp.broadcast_to(partial_best.reshape(shards, block_rows, 1), (shards, block_rows, 128))
+    vmem = pl.BlockSpec(memory_space=pltpu.VMEM)
+    best = pl.pallas_call(
+        top_kernel,
+        out_shape=jax.ShapeDtypeStruct((block_rows, 128), jnp.float32),
+        in_specs=[vmem],
+        out_specs=vmem,
+        scratch_shapes=[
+            pltpu.VMEM((shards, block_rows, 128), jnp.float32),
+            pltpu.SemaphoreType.DMA((2, shards)),
+        ],
+        compiler_params=pltpu.CompilerParams(collective_id=0, has_side_effects=True),
+    )(tops)
+    return best[:, 0]
 
 
 def on_device(
@@ -171,7 +231,7 @@
     got_totals = handed[state_size : state_size + totals_size].reshape(end_totals.shape)
     got_tag = handed[state_size + totals_size :]
     initial = (got_state, got_totals, got_tag[0].astype(jnp.int32) - 1)
-    block_len = min(256, rows_here)
+    block_len = rows_here
     blocks = rows_here // block_len
 
     def regroup(values):
@@ -222,9 +282,7 @@
     final_rows = (residual.astype(jnp.float32) + summed.astype(jnp.float32)).astype(jnp.bfloat16)
     group_rows = lax.all_gather(final_rows, "mp", axis=1, tiled=True)
     partial_best = best_of(group_rows, group_vocab)
-    max_logits = lax.dynamic_slice_in_dim(
-        lax.pmax(partial_best, "mp"), own_shard * (rows_here // shards), rows_here // shards
-    )
+    max_logits = mp_max(partial_best, shards)
     return (summed, state_norms, max_logits)
 
 

time: 209 us -> 176 us (0.84)
  blocking collectives: 16.1 us -> 0 us
  local copies, waits for them, and re-layouts: 29 us -> 17.6 us
  Pallas kernels: 0 us -> 11.2 us
  waiting for transfers between devices: 93.8 us -> 85.3 us
  loops' own time: 2.99 us -> 0 us
  other arithmetic: 12.8 us -> 10.3 us
  matrix products: 28.2 us -> 26 us
    pmax x1 -> x0, blocking collectives: 16.1 us -> none  [on_device(): lax.pmax(partial_best, 'mp')]
    pallas_call x0 -> x1, Pallas kernels: none -> 11.2 us  [mp_max(): pl.pallas_call(top_kernel, out_shape=jax.ShapeDtypeStruct((block_rows, 12...]
    all_gather x1, waiting for transfers between devices: 39.5 us -> 33.8 us  [on_device(): group_rows = lax.all_gather(final_rows, 'mp', axis=1, tiled=True)]
    reshape x4 -> x0, local copies, waits for them, and re-layouts: 4.72 us -> none  [the longest x3 4.7 us: regroup(): values.reshape(values.shape[0], blocks, block_len, values.shape[-1])]
    dot_general x6 -> x1, matrix products: 4.64 us -> 1.04 us  [block_step(): jnp.einsum('cd,hd->hc', allowed, row_terms, precision=PRECISE)]
    ppermute x1, waiting for transfers between devices: 3.26 us -> 0.01 us  [from_behind(): return lax.ppermute(value, axis, pairs)]
    another operation x1 -> x0, loops' own time: 2.99 us -> none  [on_device(): _, (mixed_out, state_norm) = lax.scan(scan_step, initial, scan_inputs)]
    dynamic_slice x3 -> x0, local copies, waits for them, and re-layouts: 2.89 us -> none  [the longest x2 2.31 us: on_device(): _, (mixed_out, state_norm) = lax.scan(scan_step, initial, scan_inputs)]
  transfers between devices with their start and end apart: 5 -> 5, of which waited for: 4 -> 4; matrix products, arithmetic and copies ran while one was open for 29% -> 23% of each run, Pallas kernels for 0% -> 0%
where the time goes in v5:
time: 176 us
  waiting for transfers between devices  85.3 us (48%)
  matrix products  26 us (15%)
  local copies, waits for them, and re-layouts  17.6 us (10%)
  between operations  15.6 us (9%)
  Pallas kernels  11.2 us (6%)
  other arithmetic  10.3 us (6%)
  starting transfers between devices  9.74 us (6%)
    reduce_scatter x1, waiting for transfers between devices, on_device(): lax.psum_scatter(partial_value.astype(jnp.bfloat16), 'mp', scatter_dimens...  41.2 us
    all_gather x1, waiting for transfers between devices, on_device(): group_rows = lax.all_gather(final_rows, 'mp', axis=1, tiled=True)  33.8 us
    pallas_call x1, Pallas kernels, mp_max(): pl.pallas_call(top_kernel, out_shape=jax.ShapeDtypeStruct((block_rows, 12...  11.2 us
    all_to_all x1, waiting for transfers between devices, on_device(): lax.all_to_all(jnp.concatenate([kept_pages, projected_pages, lowered_page...  8.12 us
    all_to_all x1, starting transfers between devices, on_device(): lax.all_to_all(jnp.concatenate([kept_pages, projected_pages, lowered_page...  7.53 us
  transfers between devices with their start and end apart: 5, of which 4 were waited for; matrix products, arithmetic and copies ran while one was open for 23% of the time, Pallas kernels for 0%

profile of v5, /device:TPU:8, one launch (start us, length us, event | category | flops | bytes accessed | tf_op | source)
XLA Modules:
  0.0 175.7 jit_solution(15924133240363035271)
XLA Ops:
  7.2 0.7 all-gather.3.cloned.1.call-update
  7.9 0.8 reshape.260
  8.8 1.0 sort.17
  9.9 0.1 reshape.304
  10.0 0.8 gather_fusion.4
  10.9 0.1 reshape.307
  11.1 0.1 reshape.274
  11.3 1.9 %gather_fusion = bf16[64,8,1792]{2,1,0:T(8,128)(2,1)} fusion(bf16[64,8,1792]{2,1,0:T(8,128)(2,1)S(1)} %bitcast.69, s32[1024]{0:T(1024)S(1)} %pad_clamp_fusion.1), kind=kCustom, calls=%fused_computation | custom fusion | bytes 3670272 | tf_op jit(solution)/shard_map/gather | solution.py:174
  13.2 2.0 %fusion = f32[32,2,8]{2,1,0:T(2,128)S(1)} fusion(bf16[32,2,8,1792]{3,2,1,0:T(8,128)(2,1)} %bitcast.70), kind=kLoop, calls=%fused_computation.7 | loop fusion | flops 2752000 | bytes 1837056 | tf_op jit(solution)/shard_map/reduce_sum | solution.py:25
  15.4 1.1 constant_dynamic-slice_fusion.1
  16.6 2.3 %fusion.14 = bf16[32,2,8,128]{3,2,1,0:T(8,128)(2,1)S(1)} fusion(bf16[32,2,8,1792]{3,2,1,0:T(8,128)(2,1)} %bitcast.72, f32[1792]{0:T(1024)S(1)} %copy-done.14, f32[32,2,8]{2,1,0:T(2,128)S(1)} %copy.53, bf16[1792,128]{1,0:T(8,128)(2,1)S(1)} %copy-done.13), kind=kOutput, calls=%fused_computation.24 | convolution fusion | flops 238616576 | bytes 2434048 | tf_op jit(solution)/shard_map/abrd,dc->abrc/dot_general | solution.py:179
  18.9 1.2 fusion.7
  20.1 1.1 pad_maximum_fusion.4
  21.3 7.5 %all-to-all-start = ((bf16[32,2,8,640]{3,2,1,0:T(8,128)(2,1)}), bf16[32,2,8,640]{3,2,1,0:T(8,128)(2,1)S(1)}, u32[]{:S(2)}, u32[]{:S(2)}) async-start(bf16[32,2,8,640]{3,2,1,0:T(8,128)(2,1)} %pad_maximum_fusion.4), calls=%async_computation | async-start | bytes 1310720 | tf_op jit(solution)/shard_map/all_to_all | solution.py:184
  28.9 0.6 slice.58
  29.5 0.2 select_reduce_fusion
  29.7 0.7 fusion.62
  30.4 0.1 reduce_window_sum.11
  30.5 0.2 select_reduce_fusion.2
  31.5 0.1 select_reduce_fusion.1
  31.6 1.2 fusion.34
  32.7 8.1 %all-to-all-done = bf16[32,2,8,640]{3,2,1,0:T(8,128)(2,1)S(1)} async-done(((bf16[32,2,8,640]{3,2,1,0:T(8,128)(2,1)}), bf16[32,2,8,640]{3,2,1,0:T(8,128)(2,1)S(1)}, u32[]{:S(2)}, u32[]{:S(2)}) %all-to-all-start) | async-done | bytes 655392 | tf_op jit(solution)/shard_map/all_to_all | solution.py:184
  40.9 0.2 slice.80
  41.1 1.4 gather_fusion.1
  42.5 1.2 reshape_reshape.3
  43.7 0.4 copy.54
  44.2 0.8 copy-done.3
  45.0 0.1 multiply_multiply_fusion.1
  45.1 1.0 copy-done.2
  46.1 0.8 fusion.25
  46.9 0.1 reshape.264
  47.0 2.1 %convolution_convert_fusion = bf16[2,273,112]{2,1,0:T(8,128)(2,1)S(1)} fusion(f32[2,512,256]{1,2,0:T(8,128)} %bitcast.81, f32[2,512,16]{1,2,0:T(8,128)S(1)} %get-tuple-element.48, f32[273]{0:T(512)S(1)} %pad.3.clone, f32[512]{0:T(512)S(1)} %get-tuple-element.33, bf16[2,512,144]{1,2,0:T(8,128)(2,1)S(1)} %bitcast.74), kind=kOutput, calls=%fused_computation.23 | convolution fusion | flops 376617696 | bytes 1469888 | tf_op jit(solution)/shard_map/hcp,hce->hpe/dot_general | solution.py:217
  49.1 0.3 reshape.263
  49.3 0.9 concatenate.15
  50.3 2.1 %collective-permute-start = (bf16[61699]{0:T(1024)(128)(2,1)S(1)}, bf16[61699]{0:T(1024)(128)(2,1)S(1)}, u32[]{:S(2)}, u32[]{:S(2)}) collective-permute-start(bf16[61699]{0:T(1024)(128)(2,1)S(1)} %concatenate.15), channel_id=1, source_target_pairs={{0,8},{8,16},{16,24},{24,32},{32,40},{40,48},{48,56},{56,64},{64,7... | collective-permute-start | bytes 370202 | tf_op jit(solution)/shard_map/ppermute | solution.py:20
  52.4 1.9 %fusion.63 = (f32[2,512]{1,0:T(2,128)S(1)}, f32[2,512,512]{1,2,0:T(8,128)S(1)}) fusion(f32[512,512]{0,1:T(8,128)} %fusion.34, bf16[2,512,144]{1,2,0:T(8,128)(2,1)S(1)} %bitcast.75), kind=kOutput, calls=%fused_computation.121 | convolution fusion | flops 20446208 | bytes 3215360 | tf_op jit(solution)/shard_map/while/body/eval_jaxpr/hcf,hdf->hcd/dot_general | solution.py:49
  54.3 1.6 fusion.39
  55.9 1.1 multiply_multiply_fusion
  57.1 0.6 gather_fusion.2
  57.7 0.6 slice.85
  59.1 0.3 reshape.265
  59.5 2.0 %fusion.24 = f32[2,1,512]{2,1,0:T(1,128)S(1)} fusion(bf16[2,273,1]{1,2,0:T(2,128)(2,1)S(1)} %reshape.324, f32[2,512,256]{1,2,0:T(8,128)} %bitcast.83, f32[2,512,16]{1,2,0:T(8,128)S(1)} %get-tuple-element.35, f32[273]{0:T(512)S(1)} %pad.3.clone), kind=kOutput, calls=%fused_computation.41 | convolution fusion | flops 3913728 | bytes 1120392 | tf_op jit(solution)/shard_map/while/body/eval_jaxpr/hcp,hp->hc/dot_general | solution.py:55
  61.5 2.2 %fusion.12 = bf16[2,512,112]{1,2,0:T(8,128)(2,1)S(1)} fusion(f32[2,512,112]{1,2,0:T(8,128)} %fusion.39, bf16[2,273,112]{2,1,0:T(8,128)(2,1)S(1)} %reshape.265, f32[2,512,256]{1,2,0:T(8,128)} %bitcast.84, f32[2,512,16]{1,2,0:T(8,128)S(1)} %get-tuple-element.35, f32[273]{0:T(512)S(1)} %pad.3.clone, f32[2,512]{1,0:T(2,128)S(1)} %fusion.52, ...), kind=kOutput, calls=%fused_computation.21 | convolution fusion | flops 376735744 | bytes 1931780 | tf_op jit(solution)/shard_map/while/body/eval_jaxpr/hcp,hpe->hce/dot_general | solution.py:52
  63.7 1.4 all-gather.3.cloned.1.call-done
  65.2 1.9 %fusion.64 = f32[512,1792]{0,1:T(8,128)S(1)} fusion(bf16[512,224]{0,1:T(8,128)(2,1)S(1)} %bitcast.87, bf16[224,1792]{1,0:T(8,128)(2,1)} %param.14), kind=kOutput, calls=%fused_computation.122 | convolution fusion | flops 411041792 | bytes 4702208 | tf_op jit(solution)/shard_map/dot_general | solution.py:275
  67.1 2.0 %add_convert_fusion = bf16[512,1792]{0,1:T(8,128)(2,1)} fusion(f32[512,1792]{0,1:T(8,128)S(1)} %fusion.64, bf16[128,1792]{1,0:T(8,128)(2,1)S(1)} %copy-done.5, bf16[64,8,128]{2,1,0:T(8,128)(2,1)S(1)} %gather_fusion.2, s32[128]{0:T(128)S(1)} %and_select_fusion, s32[512]{0:T(512)S(1)} %broadcast_subtract_fusion), kind=kOutput, calls=%fused_computation.10 | convolution fusion | flops 236847104 | bytes 6097408 | tf_op jit(solution)/shard_map/dot_general | solution.py:276
  69.2 0.6 gather_fusion.3
  69.8 0.2 copy.56
  70.0 41.2 %reduce-scatter.2.cloned.1.call-done = bf16[512,224]{0,1:T(8,128)(2,1)} async-done(((bf16[512,1792]{0,1:T(8,128)(2,1)}), bf16[512,224]{0,1:T(8,128)(2,1)}) %reduce-scatter.2.cloned.1.call-update) | async-done | bytes 229392 | tf_op jit(solution)/shard_map/reduce_scatter | solution.py:279
  111.2 1.7 add_convert_fusion.1
  112.9 0.3 fusion.36
  113.1 0.5 fusion.47
  113.6 0.7 multiply_reduce_fusion
  114.6 0.3 mul.257
  114.9 0.1 reduce_sum.94
  115.0 0.1 slice_reduce_fusion.1
  115.1 2.1 %fusion.13 = f32[2,512]{1,0:T(2,128)S(1)} fusion(bf16[2,273,112]{2,1,0:T(8,128)(2,1)} %copy-done.6, f32[2,512,256]{1,2,0:T(8,128)} %bitcast.82, f32[2,512,16]{1,2,0:T(8,128)S(1)} %copy-done.9, f32[273]{0:T(512)S(1)} %pad.3.clone, f32[2,512,144]{1,2,0:T(8,128)S(1)} %copy-done.4), kind=kOutput, calls=%fused_computation.22 | convolution fusion | flops 376505344 | bytes 1700356 | tf_op jit(solution)/shard_map/while/body/eval_jaxpr/hcp,hpe->hce/dot_general | solution.py:66
  117.2 0.4 fusion.21
  117.6 1.0 fusion.19
  118.7 33.8 %all-gather.5.cloned.1.call-done = bf16[512,1792]{0,1:T(8,128)(2,1)} async-done(((bf16[512,224]{0,1:T(8,128)(2,1)}), bf16[512,1792]{0,1:T(8,128)(2,1)}) %all-gather.5.cloned.1.call-update) | async-done | bytes 1835024 | tf_op jit(solution)/shard_map/all_gather | solution.py:283
  152.5 3.2 %convolution_reduce_fusion = f32[512]{0:T(512)S(1)} fusion(bf16[512,1792]{1,0:T(8,128)(2,1)} %all-gather.3.cloned.1.call-done, bf16[512,1792]{0,1:T(8,128)(2,1)} %all-gather.5.cloned.1.call-done), kind=kOutput, calls=%fused_computation.16 | convolution fusion | flops 939785728 | bytes 3672064 | tf_op jit(solution)/shard_map/rd,vd->rv/dot_general | solution.py:84
  155.7 0.8 broadcast_in_dim.90.tops
  156.6 11.2 %shard_map.130 = f32[64,128]{1,0:T(8,128)} custom-call(f32[8,64,128]{2,1,0:T(8,128)} %broadcast_in_dim.90.tops), custom_call_target="tpu_custom_call" | custom-call | tf_op jit(solution)/shard_map/pallas_call | solution.py:131
  167.8 1.4 slice_reduce_fusion
  (71 shorter events, 1.5 us)
Async XLA Ops:
  7.2 4.1 %copy-start = (bf16[512,1792]{1,0:T(8,128)(2,1)S(1)}, bf16[512,1792]{1,0:T(8,128)(2,1)}, u32[]{:S(2)}) copy-start(bf16[512,1792]{1,0:T(8,128)(2,1)} %param.11) | copy-start | bytes 5505028
  7.2 58.0 %all-gather.3.cloned.1.call-start = ((), (), s32[]{:S(2)}) async-start(), calls=%async_computation.2 | async-start | bytes 1892352 | tf_op jit(solution)/shard_map/all_gather | solution.py:205
  13.2 3.3 %copy-start.13 = (bf16[1792,128]{1,0:T(8,128)(2,1)S(1)}, bf16[1792,128]{1,0:T(8,128)(2,1)}, u32[]{:S(2)}) copy-start(bf16[1792,128]{1,0:T(8,128)(2,1)} %param.15) | copy-start | bytes 1376260
  13.2 3.3 %copy-start.14 = (f32[1792]{0:T(1024)S(1)}, f32[1792]{0:T(1024)}, u32[]{:S(2)}) copy-start(f32[1792]{0:T(1024)} %param.12) | copy-start | bytes 21508
  16.5 2.4 %copy-start.1 = (bf16[64,8,1792]{2,1,0:T(8,128)(2,1)S(1)}, bf16[64,8,1792]{2,1,0:T(8,128)(2,1)}, u32[]{:S(2)}) copy-start(bf16[64,8,1792]{2,1,0:T(8,128)(2,1)} %gather_fusion) | copy-start | bytes 5505028
  16.5 2.4 %copy-start.12 = (bf16[1792,288]{0,1:T(8,128)(2,1)S(1)}, bf16[1792,288]{0,1:T(8,128)(2,1)}, u32[]{:S(2)}) copy-start(bf16[1792,288]{0,1:T(8,128)(2,1)} %param.13) | copy-start | bytes 3096580
  20.1 8.8 %copy-start.7 = (s32[512]{0:T(512)S(1)}, s32[512]{0:T(512)}, u32[]{:S(2)}) copy-start(s32[512]{0:T(512)} %param.18) | copy-start | bytes 6148
  20.1 9.3 %copy-start.10 = (s32[128]{0:T(128)S(1)}, s32[128]{0:T(128)}, u32[]{:S(2)}) copy-start(s32[128]{0:T(128)} %param.19) | copy-start | bytes 1540
  20.1 11.3 %copy-start.11 = (s32[64]{0:T(128)S(1)}, s32[64]{0:T(128)}, u32[]{:S(2)}) copy-start(s32[64]{0:T(128)} %param.20) | copy-start | bytes 772
  21.3 19.6 %all-to-all-start = ((bf16[32,2,8,640]{3,2,1,0:T(8,128)(2,1)}), bf16[32,2,8,640]{3,2,1,0:T(8,128)(2,1)S(1)}, u32[]{:S(2)}, u32[]{:S(2)}) async-start(bf16[32,2,8,640]{3,2,1,0:T(8,128)(2,1)} %pad_maximum_fusion.4), calls=%async_computation | async-start | bytes 1310720 | tf_op jit(solution)/shard_map/all_to_all | solution.py:184
  28.8 82.4 %reduce-scatter.2.cloned.1.call-start = ((), (), s32[]{:S(2)}) async-start(), calls=%async_computation.3 | async-start | bytes 2064384 | tf_op jit(solution)/shard_map/reduce_scatter | solution.py:279
  44.1 0.8 copy-start.3
  45.0 2.0 %copy-start.8 = (f32[2,512,16]{1,2,0:T(8,128)}, f32[2,512,16]{1,2,0:T(8,128)S(1)}, u32[]{:S(2)}) copy-start(f32[2,512,16]{1,2,0:T(8,128)S(1)} %get-tuple-element.48) | copy-start | bytes 196612
  45.1 1.0 copy-start.2
  50.3 7.5 %collective-permute-start = (bf16[61699]{0:T(1024)(128)(2,1)S(1)}, bf16[61699]{0:T(1024)(128)(2,1)S(1)}, u32[]{:S(2)}, u32[]{:S(2)}) collective-permute-start(bf16[61699]{0:T(1024)(128)(2,1)S(1)} %concatenate.15), channel_id=1, source_target_pairs={{0,8},{8,16},{16,24},{24,32},{32,40},{40,48},{48,56},{56,64},{64,7... | collective-permute-start | bytes 370202 | tf_op jit(solution)/shard_map/ppermute | solution.py:20
  59.4 4.3 %copy-start.6 = (bf16[2,273,112]{2,1,0:T(8,128)(2,1)}, bf16[2,273,112]{2,1,0:T(8,128)(2,1)S(1)}, u32[]{:S(2)}) copy-start(bf16[2,273,112]{2,1,0:T(8,128)(2,1)S(1)} %reshape.265) | copy-start | bytes 366916
  65.2 1.9 %copy-start.5 = (bf16[128,1792]{1,0:T(8,128)(2,1)S(1)}, bf16[128,1792]{1,0:T(8,128)(2,1)}, u32[]{:S(2)}) copy-start(bf16[128,1792]{1,0:T(8,128)(2,1)} %param.16) | copy-start | bytes 1376260
  69.1 83.4 %all-gather.5.cloned.1.call-start = ((), (), s32[]{:S(2)}) async-start(), calls=%async_computation.4 | async-start | bytes 2064384 | tf_op jit(solution)/shard_map/all_gather | solution.py:283
  113.6 1.5 copy-start.4
  113.6 1.5 copy-start.9
Sparse Core Ops, SparseCore 0:
  10.6 54.5 all-gather.2
  69.2 41.9 reduce-scatter.1
  113.0 39.4 all-gather.4

commit v6 on v4

--- a/solution.py
+++ b/solution.py
@@ -59,8 +59,9 @@
     key_scores = jnp.einsum("hcf,hdf->hcd", key_rows, key_rows, precision=PRECISE) * scaling
     value_gram = jnp.einsum("hce,hde->hcd", value_rows, value_rows, precision=PRECISE)
     key_gram = (1.0 + key_scores + 0.5 * key_scores * key_scores) * value_gram
-    masked_gram = jnp.einsum("cd,hde->hce", allowed, key_gram, precision=PRECISE)
-    local_squares = jnp.sum(masked_gram * allowed[None], axis=-1)
+    diagonal = (position[:, None] == position[None, :]).astype(jnp.float32)
+    row_terms = jnp.sum(key_gram * (allowed * (2.0 - diagonal))[None], axis=-1)
+    local_squares = jnp.einsum("cd,hd->hc", allowed, row_terms, precision=PRECISE)
     along = jnp.sum(
         jnp.einsum("hcp,hpe->hce", phi_key, states, precision=PRECISE) * value_rows, axis=-1
     )
@@ -89,75 +90,78 @@
     land, acc, rows, tops, got, ring_sems, top_sems,
 ):
     n = part_ref.shape[0]
-    half = part_ref.shape[1] // 2
+    quarter = part_ref.shape[1] // 4
     block_rows = best_ref.shape[0]
     me = lax.axis_index("mp")
     grp = lax.axis_index("group")
     peers = [lax.rem(me + k, n) for k in range(1, n)]
     mesh_id = pl.DeviceIdType.MESH
     towards = (lax.rem(me + 1, n), lax.rem(me + n - 1, n))
-    spans = (pl.ds(0, half), pl.ds(half, half))
+    chains = [(0, 0), (1, 2), (0, 1), (1, 3)]
+    spans = [pl.ds(quarter * piece, quarter) for _, piece in chains]
 
     barrier = pltpu.get_barrier_semaphore()
     for p in peers:
         pl.semaphore_signal(barrier, inc=1, device_id=(grp, p), device_id_type=mesh_id)
     pl.semaphore_wait(barrier, n - 1)
 
-    def ring_copy(phase, way, step, src, dst):
+    def ring_copy(phase, chain, step, src, dst):
         return pltpu.make_async_remote_copy(
             src_ref=src,
             dst_ref=dst,
-            send_sem=ring_sems.at[phase, way, 0, step],
-            recv_sem=ring_sems.at[phase, way, 1, step],
-            device_id=(grp, towards[way]),
+            send_sem=ring_sems.at[phase, chain, 0, step],
+            recv_sem=ring_sems.at[phase, chain, 1, step],
+            device_id=(grp, towards[chains[chain][0]]),
             device_id_type=mesh_id,
         )
 
-    def rs_chunk(way, step):
+    def rs_chunk(chain, step):
+        way = chains[chain][0]
         return lax.rem(me + (n - 1 - step if way == 0 else 1 + step) + n, n)
 
+    pending = [None] * len(chains)
     for step in range(n - 1):
-        copies = []
-        for way in range(2):
-            chunk = rs_chunk(way, step)
+        for chain in range(len(chains)):
+            chunk = rs_chunk(chain, step)
             if step == 0:
-                src = part_ref.at[chunk, spans[way]]
+                src = part_ref.at[chunk, spans[chain]]
             else:
-                acc[way, step] = (
-                    land[way, step - 1].astype(jnp.float32)
-                    + part_ref[chunk, spans[way]].astype(jnp.float32)
+                pending[chain].wait()
+                acc[chain, step] = (
+                    land[chain, step - 1].astype(jnp.float32)
+                    + part_ref[chunk, spans[chain]].astype(jnp.float32)
                 ).astype(acc.dtype)
-                src = acc.at[way, step]
-            copy = ring_copy(0, way, step, src, land.at[way, step])
-            copy.start()
-            copies.append(copy)
-        for copy in copies:
-            copy.wait()
-    for way in range(2):
-        total = land[way, n - 2].astype(jnp.float32) + part_ref[me, spans[way]].astype(
-            jnp.float32
-        )
+                src = acc.at[chain, step]
+            pending[chain] = ring_copy(0, chain, step, src, land.at[chain, step])
+            pending[chain].start()
+    for chain in range(len(chains)):
+        pending[chain].wait()
+        total = land[chain, n - 2].astype(jnp.float32) + part_ref[
+            me, spans[chain]
+        ].astype(jnp.float32)
         update = total.astype(upd_ref.dtype)
-        upd_ref[spans[way]] = update
-        rows[me, spans[way]] = (
-            resid_ref[spans[way]].astype(jnp.float32) + update.astype(jnp.float32)
+        upd_ref[spans[chain]] = update
+        rows[me, spans[chain]] = (
+            resid_ref[spans[chain]].astype(jnp.float32) + update.astype(jnp.float32)
         ).astype(rows.dtype)
 
     for step in range(n - 1):
-        copies = []
-        for way in range(2):
+        for chain in range(len(chains)):
+            if step > 0:
+                pending[chain].wait()
+            way = chains[chain][0]
             chunk = lax.rem(me + (n - step if way == 0 else step), n)
-            view = rows.at[chunk, spans[way]]
-            copy = ring_copy(1, way, step, view, view)
-            copy.start()
-            copies.append(copy)
-        for copy in copies:
-            copy.wait()
-
-    scores = jnp.zeros((rows.shape[1], vocab_ref.shape[1]), jnp.float32)
+            view = rows.at[chunk, spans[chain]]
+            pending[chain] = ring_copy(1, chain, step, view, view)
+            pending[chain].start()
+    for chain in range(len(chains)):
+        pending[chain].wait()
+
+    scores = jnp.zeros((rows.shape[1], vocab_ref.shape[0] * vocab_ref.shape[2]), jnp.float32)
     for j in range(n):
+        block = vocab_ref[:, j].reshape(scores.shape[1], rows.shape[2])
         scores = scores + lax.dot_general(
-            rows[j], vocab_ref[j], (((1,), (1,)), ((), ())),
+            rows[j], block, (((1,), (1,)), ((), ())),
             preferred_element_type=jnp.float32,
         )
     for p in range(n):
@@ -196,6 +200,7 @@
 def mp_exchange(parts, residual, vocab_blocks):
     n, rows_here, width = parts.shape
     block_rows = rows_here // n
+    chains = 4
     vmem = pl.BlockSpec(memory_space=pltpu.VMEM)
     return pl.pallas_call(
         exchange_kernel,
@@ -206,12 +211,12 @@
         in_specs=[vmem] * 3,
         out_specs=(vmem, vmem),
         scratch_shapes=[
-            pltpu.VMEM((2, n - 1, rows_here // 2, width), jnp.bfloat16),
-            pltpu.VMEM((2, n - 1, rows_here // 2, width), jnp.bfloat16),
+            pltpu.VMEM((chains, n - 1, rows_here // chains, width), jnp.bfloat16),
+            pltpu.VMEM((chains, n - 1, rows_here // chains, width), jnp.bfloat16),
             pltpu.VMEM((n, rows_here, width), jnp.bfloat16),
             pltpu.VMEM((n, block_rows, 128), jnp.float32),
             pltpu.VMEM((n, block_rows, 128), jnp.float32),
-            pltpu.SemaphoreType.DMA((2, 2, 2, n - 1)),
+            pltpu.SemaphoreType.DMA((2, chains, 2, n - 1)),
             pltpu.SemaphoreType.DMA((2, n)),
         ],
         compiler_params=pltpu.CompilerParams(collective_id=0, has_side_effects=True),
@@ -278,7 +283,10 @@
         return gathered_rows.reshape((rows_here,) + received.shape[3:])
 
     residual, projected, lowered = [placed(received) for received in arrived]
-    group_vocab = lax.all_gather(vocab_rows, "group", axis=0, tiled=True)
+    vocab_pieces = jnp.transpose(
+        vocab_rows.reshape(vocab_rows.shape[0], shards, slice_width), (1, 0, 2)
+    )
+    group_vocab = lax.all_gather(vocab_pieces[None], "group", axis=0, tiled=True)
     heads_here = projected.shape[1] // (2 * FEAT + HD)
     split_heads = jnp.transpose(
         projected.reshape(rows_here, heads_here, 2 * FEAT + HD).astype(jnp.float32), (1, 0, 2)
@@ -307,7 +315,7 @@
     got_totals = handed[state_size : state_size + totals_size].reshape(end_totals.shape)
     got_tag = handed[state_size + totals_size :]
     initial = (got_state, got_totals, got_tag[0].astype(jnp.int32) - 1)
-    block_len = min(256, rows_here)
+    block_len = rows_here
     blocks = rows_here // block_len
 
     def regroup(values):
@@ -348,15 +356,12 @@
     low_rank = jnp.where(
         local_slot[:, None] == column_slot[None, :], lowered, jnp.zeros_like(lowered)
     )
-    out_blocks = out_weight.reshape(out_weight.shape[0], shards, slice_width)
-    up_blocks = adapter_up.reshape(adapter_up.shape[0], shards, slice_width)
+    out_blocks = jnp.transpose(out_weight.reshape(out_weight.shape[0], shards, slice_width), (1, 0, 2))
+    up_blocks = jnp.transpose(adapter_up.reshape(adapter_up.shape[0], shards, slice_width), (1, 0, 2))
     partial_value = jnp.einsum(
-        "rk,kjc->jrc", attended, out_blocks, preferred_element_type=jnp.float32
-    ) + jnp.einsum("rk,kjc->jrc", low_rank, up_blocks, preferred_element_type=jnp.float32)
-    vocab_blocks = jnp.transpose(
-        group_vocab.reshape(group_vocab.shape[0], shards, slice_width), (1, 0, 2)
-    )
-    summed, best = mp_exchange(partial_value.astype(jnp.bfloat16), residual, vocab_blocks)
+        "rk,jkc->jrc", attended, out_blocks, preferred_element_type=jnp.float32
+    ) + jnp.einsum("rk,jkc->jrc", low_rank, up_blocks, preferred_element_type=jnp.float32)
+    summed, best = mp_exchange(partial_value.astype(jnp.bfloat16), residual, group_vocab)
     max_logits = best[:, 0]
     return (summed, state_norms, max_logits)
 

time: 220 us -> 177 us (0.80)
  Pallas kernels: 92.7 us -> 77.5 us
  local copies, waits for them, and re-layouts: 45 us -> 32.9 us
  matrix products: 25.5 us -> 20.3 us
  other arithmetic: 18 us -> 13 us
  loops' own time: 3.49 us -> 0 us
  waiting for transfers between devices: 8.81 us -> 6.55 us
    pallas_call x1, Pallas kernels: 92.7 us -> 77.5 us  [mp_exchange(): pl.pallas_call(exchange_kernel, out_shape=(jax.ShapeDtypeStruct((rows_her...]
    reshape x5 -> x1, local copies, waits for them, and re-layouts: 8.68 us -> 1.08 us  [on_device(): vocab_rows.reshape(vocab_rows.shape[0], shards, slice_width)]
    optimization_barrier x1 -> x0, local copies, waits for them, and re-layouts: 3.84 us -> none  [on_device(): group_vocab, attended = lax.optimization_barrier((group_vocab, attended))]
    dot_general x6 -> x1, matrix products: 4.72 us -> 1.01 us  [block_step(): jnp.einsum('cd,hd->hc', allowed, row_terms, precision=PRECISE)]
    another operation x1 -> x0, loops' own time: 3.49 us -> none  [on_device(): _, (mixed_out, state_norm) = lax.scan(scan_step, initial, scan_inputs)]
    convert_element_type x2 -> x1, other arithmetic: 2.42 us -> 0.01 us  [block_step(): carried = (seg_ids == owner_seg).astype(jnp.float32)[None, :]]
    dynamic_slice x2 -> x0, local copies, waits for them, and re-layouts: 2.31 us -> none  [on_device(): _, (mixed_out, state_norm) = lax.scan(scan_step, initial, scan_inputs)]
    unnamed x34 -> x55, local copies, waits for them, and re-layouts: 3.24 us -> 4.65 us
  transfers between devices with their start and end apart: 3 -> 3, of which waited for: 1 -> 1; matrix products, arithmetic and copies ran while one was open for 32% -> 30% of each run, Pallas kernels for 0% -> 0%
where the time goes in v6:
time: 177 us; the launch traced here: 176 us
  Pallas kernels  77.5 us (44%)
  local copies, waits for them, and re-layouts  32.9 us (19%)
  matrix products  20.3 us (11%)
  between operations  15.9 us (9%)
  other arithmetic  13 us (7%)
  starting transfers between devices  9.91 us (6%)
  waiting for transfers between devices  6.55 us (4%)
    pallas_call x1, Pallas kernels, mp_exchange(): pl.pallas_call(exchange_kernel, out_shape=(jax.ShapeDtypeStruct((rows_her...  77.5 us
    all_to_all x1, starting transfers between devices, on_device(): lax.all_to_all(jnp.concatenate([kept_pages, projected_pages, lowered_page...  7.53 us
    all_to_all x1, waiting for transfers between devices, on_device(): lax.all_to_all(jnp.concatenate([kept_pages, projected_pages, lowered_page...  6.51 us
    unnamed x55, local copies, waits for them, and re-layouts  4.65 us
    gather x3, local copies, waits for them, and re-layouts, placed(): received.reshape((groups * per_peer,) + received.shape[2:])[source_rows]  4.27 us
    add x1, local copies, waits for them, and re-layouts, on_device(): jnp.einsum('rk,jkc->jrc', attended, out_blocks, preferred_element_type=jn...  3.82 us
  transfers between devices with their start and end apart: 3, of which 1 were waited for; matrix products, arithmetic and copies ran while one was open for 30% of the time, Pallas kernels for 0%

profile of v6, /device:TPU:8, one launch (start us, length us, event | category | flops | bytes accessed | tf_op | source)
XLA Modules:
  0.0 176.1 jit_solution(7921692659968239027)
XLA Ops:
  7.2 1.1 reshape.266
  8.3 0.6 copy.95
  9.0 0.8 reshape.268
  9.9 1.0 sort.17
  11.1 0.8 gather_fusion.4
  12.2 0.1 reshape.284
  12.3 1.9 %gather_fusion = bf16[64,8,1792]{2,1,0:T(8,128)(2,1)} fusion(bf16[64,8,1792]{2,1,0:T(8,128)(2,1)S(1)} %bitcast.86, s32[1024]{0:T(1024)S(1)} %pad_clamp_fusion.1), kind=kCustom, calls=%fused_computation | custom fusion | bytes 3670272 | tf_op jit(solution)/shard_map/gather | solution.py:255
  14.3 2.0 %fusion = f32[32,2,8]{2,1,0:T(2,128)S(1)} fusion(bf16[32,2,8,1792]{3,2,1,0:T(8,128)(2,1)} %bitcast.89), kind=kLoop, calls=%fused_computation.7 | loop fusion | flops 2752000 | bytes 1837056 | tf_op jit(solution)/shard_map/reduce_sum | solution.py:25
  16.4 1.1 constant_dynamic-slice_fusion.1
  17.6 2.3 %fusion.14 = bf16[32,2,8,128]{3,2,1,0:T(8,128)(2,1)S(1)} fusion(bf16[32,2,8,1792]{3,2,1,0:T(8,128)(2,1)} %bitcast.91, f32[1792]{0:T(1024)S(1)} %copy-done.25, f32[32,2,8]{2,1,0:T(2,128)S(1)} %copy.101, bf16[1792,128]{1,0:T(8,128)(2,1)S(1)} %copy-done.24), kind=kOutput, calls=%fused_computation.23 | convolution fusion | flops 238616576 | bytes 2434048 | tf_op jit(solution)/shard_map/abrd,dc->abrc/dot_general | solution.py:260
  20.0 1.2 fusion.7
  21.2 1.1 pad_maximum_fusion.4
  22.3 7.5 %all-to-all-start = ((bf16[32,2,8,640]{3,2,1,0:T(8,128)(2,1)}), bf16[32,2,8,640]{3,2,1,0:T(8,128)(2,1)S(1)}, u32[]{:S(2)}, u32[]{:S(2)}) async-start(bf16[32,2,8,640]{3,2,1,0:T(8,128)(2,1)} %pad_maximum_fusion.4), calls=%async_computation | async-start | bytes 1310720 | tf_op jit(solution)/shard_map/all_to_all | solution.py:265
  29.9 0.6 slice.58
  30.5 0.2 select_reduce_fusion
  30.7 0.7 fusion.63
  31.6 0.2 select_reduce_fusion.2
  32.6 1.2 fusion.34
  33.8 1.3 fusion.36
  35.0 6.5 %all-to-all-done = bf16[32,2,8,640]{3,2,1,0:T(8,128)(2,1)S(1)} async-done(((bf16[32,2,8,640]{3,2,1,0:T(8,128)(2,1)}), bf16[32,2,8,640]{3,2,1,0:T(8,128)(2,1)S(1)}, u32[]{:S(2)}, u32[]{:S(2)}) %all-to-all-start) | async-done | bytes 655392 | tf_op jit(solution)/shard_map/all_to_all | solution.py:265
  41.5 0.6 gather_fusion.2
  42.2 0.2 slice.80
  42.4 1.4 gather_fusion.1
  43.8 1.2 reshape_reshape.3
  45.0 0.4 copy.102
  45.4 0.7 broadcast_multiply_fusion
  46.1 0.2 copy-done.9
  46.3 0.1 multiply_multiply_fusion.1
  46.5 1.0 copy-done.4
  47.5 0.8 fusion.25
  48.4 1.8 %fusion.48 = f32[2,512,512]{1,2,0:T(8,128)} fusion(bf16[2,512,144]{1,2,0:T(8,128)(2,1)S(1)} %bitcast.94), kind=kOutput, calls=%fused_computation.74 | convolution fusion | flops 16777216 | bytes 2129920 | tf_op jit(solution)/shard_map/while/body/eval_jaxpr/hcf,hdf->hcd/dot_general | solution.py:59
  50.2 0.8 convolution_convert_fusion
  51.1 0.3 reshape.271
  51.3 2.9 %concatenate.15 = bf16[61699]{0:T(1024)(128)(2,1)} concatenate(bf16[61152]{0:T(1024)(128)(2,1)S(1)} %reshape.271, bf16[546]{0:T(1024)(128)(2,1)S(1)} %reshape.272, bf16[1]{0:T(256)(128)(2,1)} %bitcast.18), dimensions={0} | concatenate | bytes 246796 | tf_op jit(solution)/shard_map/concatenate | solution.py:308
  54.2 2.3 %collective-permute-start = (bf16[61699]{0:T(1024)(128)(2,1)}, bf16[61699]{0:T(1024)(128)(2,1)}, u32[]{:S(2)}, u32[]{:S(2)}) collective-permute-start(bf16[61699]{0:T(1024)(128)(2,1)} %concatenate.15), channel_id=1, source_target_pairs={{0,8},{8,16},{16,24},{24,32},{32,40},{40,48},{48,56},{56,64},{64,7... | collective-permute-start | bytes 370202 | tf_op jit(solution)/shard_map/ppermute | solution.py:20
  56.6 2.0 %fusion.64 = (f32[2,512]{1,0:T(2,128)S(1)}, f32[2,512,512]{1,2,0:T(8,128)S(1)}) fusion(f32[512,512]{0,1:T(8,128)} %fusion.34, bf16[2,512,144]{1,2,0:T(8,128)(2,1)S(1)} %bitcast.96), kind=kOutput, calls=%fused_computation.119 | convolution fusion | flops 20446208 | bytes 3215360 | tf_op jit(solution)/shard_map/while/body/eval_jaxpr/hcf,hdf->hcd/dot_general | solution.py:49
  58.7 1.7 fusion.39
  60.3 1.3 multiply_reduce_fusion
  61.7 2.6 %fusion.41 = f32[512,1792]{0,1} fusion(bf16[128,1792]{1,0:T(8,128)(2,1)S(1)} %copy-done.11, bf16[64,8,128]{2,1,0:T(8,128)(2,1)S(1)} %gather_fusion.2, s32[128]{0:T(128)S(1)} %and_select_fusion, s32[512]{0:T(512)S(1)} %broadcast_subtract_fusion), kind=kOutput, calls=%fused_computation.60 | convolution fusion | flops 235012096 | bytes 4262400
  64.2 1.1 multiply_multiply_fusion
  65.4 0.7 slice.90
  66.1 2.3 %gather_fusion.3 = bf16[64,8,224]{2,1,0:T(8,128)(2,1)} fusion(bf16[64,8,224]{2,1,0:T(8,128)(2,1)} %bitcast.107, s32[1024]{0:T(1024)S(1)} %pad_clamp_fusion), kind=kCustom, calls=%fused_computation.3 | custom fusion | bytes 459008 | tf_op jit(solution)/shard_map/gather | solution.py:282
  68.4 1.3 slice.85
  70.3 0.7 slice.88
  71.1 0.7 slice.93
  71.9 0.9 slice.87
  72.8 0.9 reshape.273
  73.8 1.0 convert_element_type.83
  74.8 0.3 mul.257
  75.0 0.1 reduce_sum.94
  75.2 0.1 slice_reduce_fusion.1
  75.3 2.1 %fusion.13 = f32[2,512]{1,0:T(2,128)S(1)} fusion(bf16[2,273,112]{2,1,0:T(8,128)(2,1)} %reshape.273, f32[2,512,256]{1,2,0:T(8,128)S(1)} %bitcast.104, f32[2,512,16]{1,2,0:T(8,128)} %copy-done.17, f32[273]{0:T(512)S(1)} %copy-done.19, f32[2,512,144]{1,2,0:T(8,128)} %copy-done.9), kind=kOutput, calls=%fused_computation.21 | convolution fusion | flops 376505344 | bytes 1700356 | tf_op jit(solution)/shard_map/while/body/eval_jaxpr/hcp,hpe->hce/dot_general | solution.py:66
  77.5 0.7 fusion.24
  78.2 0.4 fusion.21
  78.6 1.0 fusion.19
  79.6 0.9 fusion.12
  80.5 0.2 copy-done.10
  80.8 0.7 fusion.65
  81.4 1.4 copy-done.1
  82.8 1.9 %add.154 = bf16[512,8,224]{0,2,1:T(8,128)(2,1)} add(f32[512,8,224]{0,2,1:T(8,128)S(1)} %bitcast.87, f32[512,8,224]{0,2,1:T(8,128)S(1)} %bitcast.88) | non-fusion elementwise | flops 917504 | bytes 9175040 | tf_op jit(solution)/shard_map/add | solution.py:361
  84.7 3.8 %copy.106 = bf16[512,8,224]{2,0,1:T(8,128)(2,1)} copy(bf16[512,8,224]{0,2,1:T(8,128)(2,1)} %add.154) | data formatting | bytes 3670016 | tf_op jit(solution)/shard_map/add | solution.py:361
  88.5 77.5 %shard_map.130 = (bf16[512,224]{1,0:T(8,128)(2,1)}, f32[64,128]{1,0:T(8,128)}) custom-call(bf16[8,512,224]{2,1,0:T(8,128)(2,1)} %bitcast.93, bf16[512,224]{1,0:T(8,128)(2,1)} %bitcast.101, bf16[32,8,16,224]{3,2,1,0:T(8,128)(2,1)} %bitcast.99), custom_call_target="tpu_custom_call" | custom-call | tf_op jit(solution)/shard_map/pallas_call | solution.py:205
  166.1 1.8 %copy.107 = bf16[512,224]{0,1:T(8,128)(2,1)} copy(bf16[512,224]{1,0:T(8,128)(2,1)} %get-tuple-element.70) | data formatting | bytes 458752
  167.8 1.4 slice_reduce_fusion
  (88 shorter events, 1.7 us)
Async XLA Ops:
  7.2 5.2 %copy-start = (bf16[512,1792]{1,0:T(8,128)(2,1)S(1)}, bf16[512,1792]{1,0:T(8,128)(2,1)}, u32[]{:S(2)}) copy-start(bf16[512,1792]{1,0:T(8,128)(2,1)} %param.11) | copy-start | bytes 5505028
  7.2 73.4 %all-gather.3.cloned.1.call-start = ((), (), s32[]{:S(2)}) async-start(), calls=%async_computation.1 | async-start | bytes 2162688 | tf_op jit(solution)/shard_map/all_gather | solution.py:289
  14.3 3.3 %copy-start.24 = (bf16[1792,128]{1,0:T(8,128)(2,1)S(1)}, bf16[1792,128]{1,0:T(8,128)(2,1)}, u32[]{:S(2)}) copy-start(bf16[1792,128]{1,0:T(8,128)(2,1)} %param.15) | copy-start | bytes 1376260
  14.3 3.3 %copy-start.25 = (f32[1792]{0:T(1024)S(1)}, f32[1792]{0:T(1024)}, u32[]{:S(2)}) copy-start(f32[1792]{0:T(1024)} %param.12) | copy-start | bytes 21508
  17.6 2.4 %copy-start.2 = (bf16[64,8,1792]{2,1,0:T(8,128)(2,1)S(1)}, bf16[64,8,1792]{2,1,0:T(8,128)(2,1)}, u32[]{:S(2)}) copy-start(bf16[64,8,1792]{2,1,0:T(8,128)(2,1)} %gather_fusion) | copy-start | bytes 5505028
  17.6 2.4 %copy-start.23 = (bf16[1792,288]{0,1:T(8,128)(2,1)S(1)}, bf16[1792,288]{0,1:T(8,128)(2,1)}, u32[]{:S(2)}) copy-start(bf16[1792,288]{0,1:T(8,128)(2,1)} %param.13) | copy-start | bytes 3096580
  21.2 8.7 %copy-start.14 = (s32[512]{0:T(512)S(1)}, s32[512]{0:T(512)}, u32[]{:S(2)}) copy-start(s32[512]{0:T(512)} %param.18) | copy-start | bytes 6148
  21.2 9.3 %copy-start.21 = (s32[128]{0:T(128)S(1)}, s32[128]{0:T(128)}, u32[]{:S(2)}) copy-start(s32[128]{0:T(128)} %param.19) | copy-start | bytes 1540
  21.2 10.6 %copy-start.22 = (s32[64]{0:T(128)S(1)}, s32[64]{0:T(128)}, u32[]{:S(2)}) copy-start(s32[64]{0:T(128)} %param.20) | copy-start | bytes 772
  22.3 19.2 %all-to-all-start = ((bf16[32,2,8,640]{3,2,1,0:T(8,128)(2,1)}), bf16[32,2,8,640]{3,2,1,0:T(8,128)(2,1)S(1)}, u32[]{:S(2)}, u32[]{:S(2)}) async-start(bf16[32,2,8,640]{3,2,1,0:T(8,128)(2,1)} %pad_maximum_fusion.4), calls=%async_computation | async-start | bytes 1310720 | tf_op jit(solution)/shard_map/all_to_all | solution.py:265
  32.6 17.7 %copy-start.18 = (f32[273]{0:T(512)}, f32[273]{0:T(512)S(1)}, u32[]{:S(2)}) copy-start(f32[273]{0:T(512)S(1)} %pad.3.clone) | copy-start | bytes 3280
  45.4 0.9 copy-start.9
  46.3 3.9 %copy-start.17 = (f32[2,512,16]{1,2,0:T(8,128)}, f32[2,512,16]{1,2,0:T(8,128)S(1)}, u32[]{:S(2)}) copy-start(f32[2,512,16]{1,2,0:T(8,128)S(1)} %get-tuple-element.76) | copy-start | bytes 196612
  46.5 1.0 copy-start.4
  48.4 1.9 %copy-start.5 = (f32[2,512,16,16]{1,3,2,0:T(8,128)S(1)}, f32[2,512,16,16]{1,3,2,0:T(8,128)}, u32[]{:S(2)}) copy-start(f32[2,512,16,16]{1,3,2,0:T(8,128)} %copy-done.4) | copy-start | bytes 3145732
  54.2 14.1 %collective-permute-start = (bf16[61699]{0:T(1024)(128)(2,1)}, bf16[61699]{0:T(1024)(128)(2,1)}, u32[]{:S(2)}, u32[]{:S(2)}) collective-permute-start(bf16[61699]{0:T(1024)(128)(2,1)} %concatenate.15), channel_id=1, source_target_pairs={{0,8},{8,16},{16,24},{24,32},{32,40},{40,48},{48,56},{56,64},{64,7... | collective-permute-start | bytes 370202 | tf_op jit(solution)/shard_map/ppermute | solution.py:20
  56.6 3.7 %copy-start.8 = (f32[512,512]{0,1:T(8,128)S(1)}, f32[512,512]{0,1:T(8,128)}, u32[]{:S(2)}) copy-start(f32[512,512]{0,1:T(8,128)} %get-tuple-element.82) | copy-start | bytes 3145732
  58.7 1.7 copy-start.3
  60.3 1.3 copy-start.11
  65.4 9.9 %copy-start.6 = (f32[2,512,16,16]{1,3,2,0:T(8,128)S(1)}, f32[2,512,16,16]{1,3,2,0:T(8,128)}, u32[]{:S(2)}) copy-start(f32[2,512,16,16]{1,3,2,0:T(8,128)} %copy-done.4) | copy-start | bytes 3145732
  66.1 9.2 %copy-start.19 = (f32[273]{0:T(512)S(1)}, f32[273]{0:T(512)}, u32[]{:S(2)}) copy-start(f32[273]{0:T(512)} %copy-done.18) | copy-start | bytes 3280
  73.8 3.7 %copy-start.15 = (f32[2,512,16]{1,2,0:T(8,128)S(1)}, f32[2,512,16]{1,2,0:T(8,128)}, u32[]{:S(2)}) copy-start(f32[2,512,16]{1,2,0:T(8,128)} %get-tuple-element.75) | copy-start | bytes 196612
  75.2 2.3 %copy-start.7 = (f32[2,512,16,16]{1,3,2,0:T(8,128)S(1)}, f32[2,512,16,16]{1,3,2,0:T(8,128)}, u32[]{:S(2)}) copy-start(f32[2,512,16,16]{1,3,2,0:T(8,128)} %multiply_multiply_fusion) | copy-start | bytes 3145732
  75.3 3.3 %copy-start.26 = (f32[2,512]{1,0:T(2,128)S(1)}, f32[2,512]{1,0:T(2,128)}, u32[]{:S(2)}) copy-start(f32[2,512]{1,0:T(2,128)} %multiply_reduce_fusion) | copy-start | bytes 12292
  77.4 2.2 %copy-start.12 = (f32[2,512,112]{1,2,0:T(8,128)S(1)}, f32[2,512,112]{1,2,0:T(8,128)}, u32[]{:S(2)}) copy-start(f32[2,512,112]{1,2,0:T(8,128)} %fusion.39) | copy-start | bytes 1376260
  77.4 2.2 %copy-start.13 = (bf16[2,273,112]{2,1,0:T(8,128)(2,1)S(1)}, bf16[2,273,112]{2,1,0:T(8,128)(2,1)}, u32[]{:S(2)}) copy-start(bf16[2,273,112]{2,1,0:T(8,128)(2,1)} %reshape.273) | copy-start | bytes 366916
  77.4 2.2 %copy-start.16 = (f32[2,512,16]{1,2,0:T(8,128)S(1)}, f32[2,512,16]{1,2,0:T(8,128)}, u32[]{:S(2)}) copy-start(f32[2,512,16]{1,2,0:T(8,128)} %get-tuple-element.75) | copy-start | bytes 196612
  77.4 2.2 %copy-start.20 = (f32[273]{0:T(512)S(1)}, f32[273]{0:T(512)}, u32[]{:S(2)}) copy-start(f32[273]{0:T(512)} %copy-done.18) | copy-start | bytes 3280
  79.6 1.1 copy-start.10
  80.8 2.0 %copy-start.1 = (f32[512,1792]{0,1:S(1)}, f32[512,1792]{0,1}, u32[]{:S(2)}) copy-start(f32[512,1792]{0,1} %fusion.41) | copy-start | bytes 11010052
Sparse Core Ops, SparseCore 0:
  10.6 53.0 all-gather.2

commit v7 on v6

--- a/solution.py
+++ b/solution.py
@@ -356,12 +356,14 @@
     low_rank = jnp.where(
         local_slot[:, None] == column_slot[None, :], lowered, jnp.zeros_like(lowered)
     )
-    out_blocks = jnp.transpose(out_weight.reshape(out_weight.shape[0], shards, slice_width), (1, 0, 2))
-    up_blocks = jnp.transpose(adapter_up.reshape(adapter_up.shape[0], shards, slice_width), (1, 0, 2))
-    partial_value = jnp.einsum(
-        "rk,jkc->jrc", attended, out_blocks, preferred_element_type=jnp.float32
-    ) + jnp.einsum("rk,jkc->jrc", low_rank, up_blocks, preferred_element_type=jnp.float32)
-    summed, best = mp_exchange(partial_value.astype(jnp.bfloat16), residual, group_vocab)
+    partial_value = jnp.dot(attended, out_weight, preferred_element_type=jnp.float32)
+    partial_value = partial_value + jnp.dot(
+        low_rank, adapter_up, preferred_element_type=jnp.float32
+    )
+    partial_value = jnp.transpose(
+        partial_value.astype(jnp.bfloat16).reshape(rows_here, shards, slice_width), (1, 0, 2)
+    )
+    summed, best = mp_exchange(partial_value, residual, group_vocab)
     max_logits = best[:, 0]
     return (summed, state_norms, max_logits)
 

time: 177 us -> 180 us (1.017)
  local copies, waits for them, and re-layouts: 32.9 us -> 38 us
    convert_element_type x0 -> x1, local copies, waits for them, and re-layouts: none -> 3.86 us  [on_device(): partial_value.astype(jnp.bfloat16).reshape(rows_here, shards, slice_width)]
    reshape x0 -> x1, local copies, waits for them, and re-layouts: none -> 3.82 us  [on_device(): partial_value.astype(jnp.bfloat16).reshape(rows_here, shards, slice_width)]
    add x1 -> x0, local copies, waits for them, and re-layouts: 3.82 us -> none  [on_device(): jnp.einsum('rk,jkc->jrc', attended, out_blocks, preferred_element_type=jn...]
    unnamed x2 -> x0, matrix products: 3.23 us -> none
    dot_general x0 -> x2, matrix products: none -> 2.61 us  [the longest x1 1.93 us: on_device(): jnp.dot(low_rank, adapter_up, preferred_element_type=jnp.float32)]
    add x1 -> x0, other arithmetic: 1.9 us -> none  [on_device(): jnp.einsum('rk,jkc->jrc', attended, out_blocks, preferred_element_type=jn...]
    unnamed x55 -> x59, local copies, waits for them, and re-layouts: 4.65 us -> 3.7 us
  transfers between devices with their start and end apart: 3 -> 3, of which waited for: 1 -> 1; matrix products, arithmetic and copies ran while one was open for 30% -> 29% of each run, Pallas kernels for 0% -> 0%
where the time goes in v7:
time: 180 us; the launch traced here: 179 us
  Pallas kernels  78.1 us (43%)
  local copies, waits for them, and re-layouts  38 us (21%)
  matrix products  19.6 us (11%)
  between operations  15.9 us (9%)
  other arithmetic  12.3 us (7%)
  starting transfers between devices  9.92 us (6%)
  waiting for transfers between devices  5.39 us (3%)
    pallas_call x1, Pallas kernels, mp_exchange(): pl.pallas_call(exchange_kernel, out_shape=(jax.ShapeDtypeStruct((rows_her...  78.1 us
    all_to_all x1, starting transfers between devices, on_device(): lax.all_to_all(jnp.concatenate([kept_pages, projected_pages, lowered_page...  7.53 us
    gather x3, local copies, waits for them, and re-layouts, placed(): received.reshape((groups * per_peer,) + received.shape[2:])[source_rows]  5.89 us
    all_to_all x1, waiting for transfers between devices, on_device(): lax.all_to_all(jnp.concatenate([kept_pages, projected_pages, lowered_page...  5.35 us
    convert_element_type x1, local copies, waits for them, and re-layouts, on_device(): partial_value.astype(jnp.bfloat16).reshape(rows_here, shards, slice_width)  3.86 us
    reshape x1, local copies, waits for them, and re-layouts, on_device(): partial_value.astype(jnp.bfloat16).reshape(rows_here, shards, slice_width)  3.82 us
    unnamed x59, local copies, waits for them, and re-layouts  3.7 us
  transfers between devices with their start and end apart: 3, of which 1 were waited for; matrix products, arithmetic and copies ran while one was open for 29% of the time, Pallas kernels for 0%

profile of v7, /device:TPU:8, one launch (start us, length us, event | category | flops | bytes accessed | tf_op | source)
XLA Modules:
  0.0 179.2 jit_solution(10182418527997558862)
XLA Ops:
  7.2 1.1 reshape.263
  8.3 0.6 copy.80
  9.0 0.8 reshape.265
  9.9 1.0 sort.17
  11.1 0.8 gather_fusion.4
  12.3 1.9 %gather_fusion = bf16[64,8,1792]{2,1,0:T(8,128)(2,1)} fusion(bf16[64,8,1792]{2,1,0:T(8,128)(2,1)S(1)} %bitcast.69, s32[1024]{0:T(1024)S(1)} %pad_clamp_fusion.1), kind=kCustom, calls=%fused_computation | custom fusion | bytes 3670272 | tf_op jit(solution)/shard_map/gather | solution.py:255
  14.2 2.0 %fusion = f32[32,2,8]{2,1,0:T(2,128)S(1)} fusion(bf16[32,2,8,1792]{3,2,1,0:T(8,128)(2,1)} %bitcast.70), kind=kLoop, calls=%fused_computation.7 | loop fusion | flops 2752000 | bytes 1837056 | tf_op jit(solution)/shard_map/reduce_sum | solution.py:25
  16.4 1.1 constant_dynamic-slice_fusion.1
  17.6 2.3 %fusion.14 = bf16[32,2,8,128]{3,2,1,0:T(8,128)(2,1)S(1)} fusion(bf16[32,2,8,1792]{3,2,1,0:T(8,128)(2,1)} %bitcast.72, f32[1792]{0:T(1024)S(1)} %copy-done.27, f32[32,2,8]{2,1,0:T(2,128)S(1)} %copy.86, bf16[1792,128]{1,0:T(8,128)(2,1)S(1)} %copy-done.26), kind=kOutput, calls=%fused_computation.23 | convolution fusion | flops 238616576 | bytes 2434048 | tf_op jit(solution)/shard_map/abrd,dc->abrc/dot_general | solution.py:260
  20.0 1.2 fusion.7
  21.2 1.1 pad_maximum_fusion.4
  22.3 7.5 %all-to-all-start = ((bf16[32,2,8,640]{3,2,1,0:T(8,128)(2,1)}), bf16[32,2,8,640]{3,2,1,0:T(8,128)(2,1)S(1)}, u32[]{:S(2)}, u32[]{:S(2)}) async-start(bf16[32,2,8,640]{3,2,1,0:T(8,128)(2,1)} %pad_maximum_fusion.4), calls=%async_computation | async-start | bytes 1310720 | tf_op jit(solution)/shard_map/all_to_all | solution.py:265
  29.9 0.6 slice.58
  30.5 0.2 select_reduce_fusion
  30.7 0.7 fusion.62
  31.5 0.2 select_reduce_fusion.2
  31.9 0.5 and_select_fusion
  33.1 1.2 fusion.34
  34.3 1.9 %fusion.36 = (f32[512]{0:T(512)}, f32[512,512]{0,1:T(8,128)}) fusion(s32[512]{0:T(512)S(1)} %copy-done.14), kind=kLoop, calls=%fused_computation.51 | loop fusion | flops 2358784 | bytes 1052672 | tf_op jit(solution)/shard_map/while/body/eval_jaxpr/reduce_sum | solution.py:71
  36.2 5.3 %all-to-all-done = bf16[32,2,8,640]{3,2,1,0:T(8,128)(2,1)S(1)} async-done(((bf16[32,2,8,640]{3,2,1,0:T(8,128)(2,1)}), bf16[32,2,8,640]{3,2,1,0:T(8,128)(2,1)S(1)}, u32[]{:S(2)}, u32[]{:S(2)}) %all-to-all-start) | async-done | bytes 655392 | tf_op jit(solution)/shard_map/all_to_all | solution.py:265
  41.5 0.2 slice.80
  41.7 1.4 gather_fusion.1
  43.1 1.2 reshape_reshape.3
  44.3 0.4 copy.87
  44.8 0.7 broadcast_multiply_fusion
  45.5 0.1 copy-done.8
  45.8 1.0 copy-done.3
  46.7 0.8 fusion.25
  47.6 1.8 fusion.47
  49.4 0.8 convolution_convert_fusion
  50.3 0.3 reshape.268
  50.5 2.9 %concatenate.15 = bf16[61699]{0:T(1024)(128)(2,1)} concatenate(bf16[61152]{0:T(1024)(128)(2,1)S(1)} %reshape.268, bf16[546]{0:T(1024)(128)(2,1)S(1)} %reshape.269, bf16[1]{0:T(256)(128)(2,1)} %bitcast.18), dimensions={0} | concatenate | bytes 246796 | tf_op jit(solution)/shard_map/concatenate | solution.py:308
  53.5 2.3 %collective-permute-start = (bf16[61699]{0:T(1024)(128)(2,1)}, bf16[61699]{0:T(1024)(128)(2,1)}, u32[]{:S(2)}, u32[]{:S(2)}) collective-permute-start(bf16[61699]{0:T(1024)(128)(2,1)} %concatenate.15), channel_id=1, source_target_pairs={{0,8},{8,16},{16,24},{24,32},{32,40},{40,48},{48,56},{56,64},{64,7... | collective-permute-start | bytes 370202 | tf_op jit(solution)/shard_map/ppermute | solution.py:20
  55.8 2.0 %fusion.63 = (f32[2,512]{1,0:T(2,128)S(1)}, f32[2,512,512]{1,2,0:T(8,128)S(1)}) fusion(f32[512,512]{0,1:T(8,128)} %fusion.34, bf16[2,512,144]{1,2,0:T(8,128)(2,1)S(1)} %bitcast.78), kind=kOutput, calls=%fused_computation.118 | convolution fusion | flops 20446208 | bytes 3215360 | tf_op jit(solution)/shard_map/while/body/eval_jaxpr/hcf,hdf->hcd/dot_general | solution.py:49
  57.9 1.6 fusion.39
  59.6 1.3 multiply_reduce_fusion
  60.9 1.1 multiply_multiply_fusion
  62.0 0.7 slice.89
  62.7 2.2 %gather_fusion.2 = bf16[64,8,128]{2,1,0:T(8,128)(2,1)} fusion(bf16[64,8,128]{2,1,0:T(8,128)(2,1)} %bitcast.90, s32[1024]{0:T(1024)S(1)} %pad_clamp_fusion), kind=kCustom, calls=%fused_computation.2 | custom fusion | bytes 262400 | tf_op jit(solution)/shard_map/gather | solution.py:282
  65.0 0.7 slice.90
  65.7 2.3 %gather_fusion.3 = bf16[64,8,224]{2,1,0:T(8,128)(2,1)} fusion(bf16[64,8,224]{2,1,0:T(8,128)(2,1)} %bitcast.89, s32[1024]{0:T(1024)S(1)} %pad_clamp_fusion), kind=kCustom, calls=%fused_computation.3 | custom fusion | bytes 459008 | tf_op jit(solution)/shard_map/gather | solution.py:282
  67.9 1.3 slice.85
  69.8 0.8 slice.88
  70.7 0.8 slice.93
  71.5 0.9 slice.87
  72.4 0.9 reshape.270
  73.4 1.0 convert_element_type.81
  74.4 0.3 mul.257
  74.6 0.1 reduce_sum.94
  74.9 2.1 %fusion.13 = f32[2,512]{1,0:T(2,128)S(1)} fusion(bf16[2,273,112]{2,1,0:T(8,128)(2,1)} %reshape.270, f32[2,512,256]{1,2,0:T(8,128)S(1)} %bitcast.86, f32[2,512,16]{1,2,0:T(8,128)} %copy-done.17, f32[273]{0:T(512)} %copy-done.19, f32[2,512,144]{1,2,0:T(8,128)} %copy-done.8), kind=kOutput, calls=%fused_computation.21 | convolution fusion | flops 376505344 | bytes 1700356 | tf_op jit(solution)/shard_map/while/body/eval_jaxpr/hcp,hpe->hce/dot_general | solution.py:66
  77.1 0.7 fusion.24
  77.8 0.4 fusion.21
  78.2 1.0 fusion.19
  79.2 0.9 fusion.12
  80.2 0.2 copy-done.9
  80.4 0.7 fusion.64
  81.1 0.2 copy-done.10
  81.3 0.2 copy-done.11
  81.5 1.9 %add_convert_fusion = bf16[512,1792]{1,0:T(8,128)(2,1)} fusion(f32[512,1792]{1,0:T(8,128)S(1)} %fusion.64, bf16[128,1792]{1,0:T(8,128)(2,1)S(1)} %copy-done.11, bf16[64,8,128]{2,1,0:T(8,128)(2,1)S(1)} %copy-done.10, s32[128]{0:T(128)S(1)} %copy-done.22, s32[512]{0:T(512)S(1)} %broadcast_subtract_fusion), kind=kOutput, calls=%fused_computation.10 | convolution fusion | flops 236847104 | bytes 6097408 | tf_op jit(solution)/shard_map/dot_general | solution.py:360
  83.4 3.9 %copy.89 = bf16[512,1792]{0,1:T(8,128)(2,1)} copy(bf16[512,1792]{1,0:T(8,128)(2,1)} %add_convert_fusion) | data formatting | bytes 3670016 | tf_op jit(solution)/shard_map/convert_element_type | solution.py:364
  87.3 3.8 %copy.90 = bf16[512,8,224]{2,0,1:T(8,128)(2,1)} copy(bf16[512,8,224]{0,2,1:T(8,128)(2,1)} %bitcast.75) | data formatting | bytes 3670016 | tf_op jit(solution)/shard_map/reshape | solution.py:364
  91.1 78.1 %shard_map.130 = (bf16[512,224]{1,0:T(8,128)(2,1)}, f32[64,128]{1,0:T(8,128)}) custom-call(bf16[8,512,224]{2,1,0:T(8,128)(2,1)} %bitcast.74, bf16[512,224]{1,0:T(8,128)(2,1)} %bitcast.83, bf16[32,8,16,224]{3,2,1,0:T(8,128)(2,1)} %bitcast.81), custom_call_target="tpu_custom_call" | custom-call | tf_op jit(solution)/shard_map/pallas_call | solution.py:205
  169.2 1.8 copy.91
  171.0 1.4 slice_reduce_fusion
  (92 shorter events, 2.1 us)
Async XLA Ops:
  7.2 5.2 %copy-start = (bf16[512,1792]{1,0:T(8,128)(2,1)S(1)}, bf16[512,1792]{1,0:T(8,128)(2,1)}, u32[]{:S(2)}) copy-start(bf16[512,1792]{1,0:T(8,128)(2,1)} %param.11) | copy-start | bytes 5505028
  7.2 73.0 %all-gather.3.cloned.1.call-start = ((), (), s32[]{:S(2)}) async-start(), calls=%async_computation.1 | async-start | bytes 2162688 | tf_op jit(solution)/shard_map/all_gather | solution.py:289
  14.2 3.3 %copy-start.26 = (bf16[1792,128]{1,0:T(8,128)(2,1)S(1)}, bf16[1792,128]{1,0:T(8,128)(2,1)}, u32[]{:S(2)}) copy-start(bf16[1792,128]{1,0:T(8,128)(2,1)} %param.15) | copy-start | bytes 1376260
  14.2 3.3 %copy-start.27 = (f32[1792]{0:T(1024)S(1)}, f32[1792]{0:T(1024)}, u32[]{:S(2)}) copy-start(f32[1792]{0:T(1024)} %param.12) | copy-start | bytes 21508
  17.6 2.4 %copy-start.1 = (bf16[64,8,1792]{2,1,0:T(8,128)(2,1)S(1)}, bf16[64,8,1792]{2,1,0:T(8,128)(2,1)}, u32[]{:S(2)}) copy-start(bf16[64,8,1792]{2,1,0:T(8,128)(2,1)} %gather_fusion) | copy-start | bytes 5505028
  17.6 2.4 %copy-start.25 = (bf16[1792,288]{0,1:T(8,128)(2,1)S(1)}, bf16[1792,288]{0,1:T(8,128)(2,1)}, u32[]{:S(2)}) copy-start(bf16[1792,288]{0,1:T(8,128)(2,1)} %param.13) | copy-start | bytes 3096580
  21.2 8.7 %copy-start.14 = (s32[512]{0:T(512)S(1)}, s32[512]{0:T(512)}, u32[]{:S(2)}) copy-start(s32[512]{0:T(512)} %param.18) | copy-start | bytes 6148
  21.2 9.3 %copy-start.23 = (s32[128]{0:T(128)S(1)}, s32[128]{0:T(128)}, u32[]{:S(2)}) copy-start(s32[128]{0:T(128)} %param.19) | copy-start | bytes 1540
  21.2 10.6 %copy-start.24 = (s32[64]{0:T(128)S(1)}, s32[64]{0:T(128)}, u32[]{:S(2)}) copy-start(s32[64]{0:T(128)} %param.20) | copy-start | bytes 772
  22.3 19.2 %all-to-all-start = ((bf16[32,2,8,640]{3,2,1,0:T(8,128)(2,1)}), bf16[32,2,8,640]{3,2,1,0:T(8,128)(2,1)S(1)}, u32[]{:S(2)}, u32[]{:S(2)}) async-start(bf16[32,2,8,640]{3,2,1,0:T(8,128)(2,1)} %pad_maximum_fusion.4), calls=%async_computation | async-start | bytes 1310720 | tf_op jit(solution)/shard_map/all_to_all | solution.py:265
  33.1 16.4 %copy-start.19 = (f32[273]{0:T(512)}, f32[273]{0:T(512)S(1)}, u32[]{:S(2)}) copy-start(f32[273]{0:T(512)S(1)} %pad.3.clone) | copy-start | bytes 3280
  44.8 0.8 copy-start.8
  45.6 3.8 %copy-start.17 = (f32[2,512,16]{1,2,0:T(8,128)}, f32[2,512,16]{1,2,0:T(8,128)S(1)}, u32[]{:S(2)}) copy-start(f32[2,512,16]{1,2,0:T(8,128)S(1)} %get-tuple-element.76) | copy-start | bytes 196612
  45.7 1.0 copy-start.3
  47.6 1.8 %copy-start.4 = (f32[2,512,16,16]{1,3,2,0:T(8,128)S(1)}, f32[2,512,16,16]{1,3,2,0:T(8,128)}, u32[]{:S(2)}) copy-start(f32[2,512,16,16]{1,3,2,0:T(8,128)} %copy-done.3) | copy-start | bytes 3145732
  53.5 14.5 %collective-permute-start = (bf16[61699]{0:T(1024)(128)(2,1)}, bf16[61699]{0:T(1024)(128)(2,1)}, u32[]{:S(2)}, u32[]{:S(2)}) collective-permute-start(bf16[61699]{0:T(1024)(128)(2,1)} %concatenate.15), channel_id=1, source_target_pairs={{0,8},{8,16},{16,24},{24,32},{32,40},{40,48},{48,56},{56,64},{64,7... | collective-permute-start | bytes 370202 | tf_op jit(solution)/shard_map/ppermute | solution.py:20
  55.8 3.7 %copy-start.7 = (f32[512,512]{0,1:T(8,128)S(1)}, f32[512,512]{0,1:T(8,128)}, u32[]{:S(2)}) copy-start(f32[512,512]{0,1:T(8,128)} %get-tuple-element.82) | copy-start | bytes 3145732
  57.8 1.7 copy-start.2
  62.7 12.2 %copy-start.5 = (f32[2,512,16,16]{1,3,2,0:T(8,128)S(1)}, f32[2,512,16,16]{1,3,2,0:T(8,128)}, u32[]{:S(2)}) copy-start(f32[2,512,16,16]{1,3,2,0:T(8,128)} %copy-done.3) | copy-start | bytes 3145732
  73.4 3.7 %copy-start.15 = (f32[2,512,16]{1,2,0:T(8,128)S(1)}, f32[2,512,16]{1,2,0:T(8,128)}, u32[]{:S(2)}) copy-start(f32[2,512,16]{1,2,0:T(8,128)} %get-tuple-element.75) | copy-start | bytes 196612
  73.4 3.7 %copy-start.20 = (f32[273]{0:T(512)S(1)}, f32[273]{0:T(512)}, u32[]{:S(2)}) copy-start(f32[273]{0:T(512)} %copy-done.19) | copy-start | bytes 3280
  74.8 2.3 %copy-start.6 = (f32[2,512,16,16]{1,3,2,0:T(8,128)S(1)}, f32[2,512,16,16]{1,3,2,0:T(8,128)}, u32[]{:S(2)}) copy-start(f32[2,512,16,16]{1,3,2,0:T(8,128)} %multiply_multiply_fusion) | copy-start | bytes 3145732
  74.9 3.3 %copy-start.18 = (f32[512]{0:T(512)S(1)}, f32[512]{0:T(512)}, u32[]{:S(2)}) copy-start(f32[512]{0:T(512)} %get-tuple-element.81) | copy-start | bytes 6148
  74.9 3.3 %copy-start.28 = (f32[2,512]{1,0:T(2,128)S(1)}, f32[2,512]{1,0:T(2,128)}, u32[]{:S(2)}) copy-start(f32[2,512]{1,0:T(2,128)} %multiply_reduce_fusion) | copy-start | bytes 12292
  77.0 2.2 %copy-start.12 = (f32[2,512,112]{1,2,0:T(8,128)S(1)}, f32[2,512,112]{1,2,0:T(8,128)}, u32[]{:S(2)}) copy-start(f32[2,512,112]{1,2,0:T(8,128)} %fusion.39) | copy-start | bytes 1376260
  77.0 2.2 %copy-start.13 = (bf16[2,273,112]{2,1,0:T(8,128)(2,1)S(1)}, bf16[2,273,112]{2,1,0:T(8,128)(2,1)}, u32[]{:S(2)}) copy-start(bf16[2,273,112]{2,1,0:T(8,128)(2,1)} %reshape.270) | copy-start | bytes 366916
  77.0 2.2 %copy-start.16 = (f32[2,512,16]{1,2,0:T(8,128)S(1)}, f32[2,512,16]{1,2,0:T(8,128)}, u32[]{:S(2)}) copy-start(f32[2,512,16]{1,2,0:T(8,128)} %get-tuple-element.75) | copy-start | bytes 196612
  77.0 2.2 %copy-start.21 = (f32[273]{0:T(512)S(1)}, f32[273]{0:T(512)}, u32[]{:S(2)}) copy-start(f32[273]{0:T(512)} %copy-done.19) | copy-start | bytes 3280
  79.2 1.1 copy-start.9
  80.4 0.9 copy-start.10
  80.4 1.1 copy-start.11
  80.4 1.1 copy-start.22
Sparse Core Ops, SparseCore 0:
  10.6 53.7 all-gather.2

commit v8 on v7

--- a/solution.py
+++ b/solution.py
@@ -86,11 +86,11 @@
 
 
 def exchange_kernel(
-    part_ref, resid_ref, vocab_ref, upd_ref, best_ref,
+    att_ref, low_ref, w_ref, u_ref, resid_ref, vocab_ref, upd_ref, best_ref,
     land, acc, rows, tops, got, ring_sems, top_sems,
 ):
-    n = part_ref.shape[0]
-    quarter = part_ref.shape[1] // 4
+    n = w_ref.shape[0]
+    quarter = att_ref.shape[0] // 4
     block_rows = best_ref.shape[0]
     me = lax.axis_index("mp")
     grp = lax.axis_index("group")
@@ -119,26 +119,28 @@
         way = chains[chain][0]
         return lax.rem(me + (n - 1 - step if way == 0 else 1 + step) + n, n)
 
+    def part(chunk, span):
+        value = jnp.dot(att_ref[span], w_ref[chunk], preferred_element_type=jnp.float32)
+        value = value + jnp.dot(low_ref[span], u_ref[chunk], preferred_element_type=jnp.float32)
+        return value.astype(jnp.bfloat16).astype(jnp.float32)
+
     pending = [None] * len(chains)
     for step in range(n - 1):
         for chain in range(len(chains)):
             chunk = rs_chunk(chain, step)
             if step == 0:
-                src = part_ref.at[chunk, spans[chain]]
+                acc[chain, step] = part(chunk, spans[chain]).astype(acc.dtype)
             else:
                 pending[chain].wait()
                 acc[chain, step] = (
-                    land[chain, step - 1].astype(jnp.float32)
-                    + part_ref[chunk, spans[chain]].astype(jnp.float32)
+                    land[chain, step - 1].astype(jnp.float32) + part(chunk, spans[chain])
                 ).astype(acc.dtype)
-                src = acc.at[chain, step]
+            src = acc.at[chain, step]
             pending[chain] = ring_copy(0, chain, step, src, land.at[chain, step])
             pending[chain].start()
     for chain in range(len(chains)):
         pending[chain].wait()
-        total = land[chain, n - 2].astype(jnp.float32) + part_ref[
-            me, spans[chain]
-        ].astype(jnp.float32)
+        total = land[chain, n - 2].astype(jnp.float32) + part(me, spans[chain])
         update = total.astype(upd_ref.dtype)
         upd_ref[spans[chain]] = update
         rows[me, spans[chain]] = (
@@ -197,8 +199,9 @@
     best_ref[...] = best
 
 
-def mp_exchange(parts, residual, vocab_blocks):
-    n, rows_here, width = parts.shape
+def mp_exchange(attended, low_rank, out_blocks, up_blocks, residual, vocab_blocks):
+    n, _, width = out_blocks.shape
+    rows_here = attended.shape[0]
     block_rows = rows_here // n
     chains = 4
     vmem = pl.BlockSpec(memory_space=pltpu.VMEM)
@@ -208,7 +211,7 @@
             jax.ShapeDtypeStruct((rows_here, width), jnp.bfloat16),
             jax.ShapeDtypeStruct((block_rows, 128), jnp.float32),
         ),
-        in_specs=[vmem] * 3,
+        in_specs=[vmem] * 6,
         out_specs=(vmem, vmem),
         scratch_shapes=[
             pltpu.VMEM((chains, n - 1, rows_here // chains, width), jnp.bfloat16),
@@ -220,7 +223,7 @@
             pltpu.SemaphoreType.DMA((2, n)),
         ],
         compiler_params=pltpu.CompilerParams(collective_id=0, has_side_effects=True),
-    )(parts, residual, vocab_blocks)
+    )(attended, low_rank, out_blocks, up_blocks, residual, vocab_blocks)
 
 
 def on_device(
@@ -356,14 +359,13 @@
     low_rank = jnp.where(
         local_slot[:, None] == column_slot[None, :], lowered, jnp.zeros_like(lowered)
     )
-    partial_value = jnp.dot(attended, out_weight, preferred_element_type=jnp.float32)
-    partial_value = partial_value + jnp.dot(
-        low_rank, adapter_up, preferred_element_type=jnp.float32
-    )
-    partial_value = jnp.transpose(
-        partial_value.astype(jnp.bfloat16).reshape(rows_here, shards, slice_width), (1, 0, 2)
-    )
-    summed, best = mp_exchange(partial_value, residual, group_vocab)
+    out_blocks = jnp.transpose(
+        out_weight.reshape(out_weight.shape[0], shards, slice_width), (1, 0, 2)
+    )
+    up_blocks = jnp.transpose(
+        adapter_up.reshape(adapter_up.shape[0], shards, slice_width), (1, 0, 2)
+    )
+    summed, best = mp_exchange(attended, low_rank, out_blocks, up_blocks, residual, group_vocab)
     max_logits = best[:, 0]
     return (summed, state_norms, max_logits)
 

time: 180 us -> 173 us (0.961)
  local copies, waits for them, and re-layouts: 38 us -> 33.9 us
  waiting for transfers between devices: 5.39 us -> 2.3 us
    all_to_all x1, waiting for transfers between devices: 5.35 us -> 0.01 us  [on_device(): lax.all_to_all(jnp.concatenate([kept_pages, projected_pages, lowered_page...]
    convert_element_type x1 -> x0, local copies, waits for them, and re-layouts: 3.86 us -> none  [on_device(): partial_value.astype(jnp.bfloat16).reshape(rows_here, shards, slice_width)]
    dot_general x2 -> x0, matrix products: 2.61 us -> none  [the longest x1 1.93 us: on_device(): jnp.dot(low_rank, adapter_up, preferred_element_type=jnp.float32)]
    all_gather x1, waiting for transfers between devices: 0.02 us -> 2.27 us  [on_device(): lax.all_gather(vocab_pieces[None], 'group', axis=0, tiled=True)]
    dot_general x1, matrix products: 1.16 us -> 3.07 us  [on_device(): jnp.einsum('abrd,dc->abrc', normed_pages, qkv_weight, preferred_element_t...]
    dot_general x1, matrix products: 1.34 us -> 3.2 us  [block_step(): jnp.einsum('hce,hde->hcd', value_rows, value_rows, precision=PRECISE)]
    reshape x1 -> x3, local copies, waits for them, and re-layouts: 3.82 us -> 4.65 us  [the longest x2 3.63 us: on_device(): out_weight.reshape(out_weight.shape[0], shards, slice_width)]
    unnamed x59 -> x48, local copies, waits for them, and re-layouts: 3.7 us -> 4.31 us
  transfers between devices with their start and end apart: 3 -> 3, of which waited for: 1 -> 1; matrix products, arithmetic and copies ran while one was open for 29% -> 27% of each run, Pallas kernels for 0% -> 0%
where the time goes in v8:
time: 173 us
  Pallas kernels  78.7 us (45%)
  local copies, waits for them, and re-layouts  33.9 us (20%)
  matrix products  19 us (11%)
  between operations  15.8 us (9%)
  other arithmetic  13 us (8%)
  starting transfers between devices  9.81 us (6%)
  waiting for transfers between devices  2.3 us (1%)
    pallas_call x1, Pallas kernels, mp_exchange(): pl.pallas_call(exchange_kernel, out_shape=(jax.ShapeDtypeStruct((rows_her...  78.7 us
    all_to_all x1, starting transfers between devices, on_device(): lax.all_to_all(jnp.concatenate([kept_pages, projected_pages, lowered_page...  7.54 us
    gather x3, local copies, waits for them, and re-layouts, placed(): received.reshape((groups * per_peer,) + received.shape[2:])[source_rows]  4.91 us
    unnamed x48, local copies, waits for them, and re-layouts  4.31 us
    reshape x2, local copies, waits for them, and re-layouts, on_device(): out_weight.reshape(out_weight.shape[0], shards, slice_width)  3.63 us
  transfers between devices with their start and end apart: 3, of which 1 were waited for; matrix products, arithmetic and copies ran while one was open for 27% of the time, Pallas kernels for 0%

profile of v8, /device:TPU:8, one launch (start us, length us, event | category | flops | bytes accessed | tf_op | source)
XLA Modules:
  0.0 172.6 jit_solution(17277187755021525768)
XLA Ops:
  7.2 0.9 reshape.268
  8.2 1.0 sort.17
  9.4 0.8 gather_fusion.4
  10.5 0.1 reshape.284
  10.7 1.9 %gather_fusion = bf16[64,8,1792]{2,1,0:T(8,128)(2,1)} fusion(bf16[64,8,1792]{2,1,0:T(8,128)(2,1)S(1)} %bitcast.66, s32[1024]{0:T(1024)S(1)} %pad_clamp_fusion.1), kind=kCustom, calls=%fused_computation | custom fusion | bytes 3670272 | tf_op jit(solution)/shard_map/gather | solution.py:258
  12.6 2.0 %fusion = f32[32,2,8]{2,1,0:T(2,128)S(1)} fusion(bf16[32,2,8,1792]{3,2,1,0:T(8,128)(2,1)} %bitcast.67), kind=kLoop, calls=%fused_computation.7 | loop fusion | flops 2752000 | bytes 1837056 | tf_op jit(solution)/shard_map/reduce_sum | solution.py:25
  14.8 3.1 %fusion.7 = bf16[32,2,8,288]{3,2,1,0:T(8,128)(2,1)S(1)} fusion(bf16[32,2,8,1792]{3,2,1,0:T(8,128)(2,1)} %bitcast.68, f32[1792]{0:T(1024)S(1)} %copy-done.21, f32[32,2,8]{2,1,0:T(2,128)S(1)} %copy.99, bf16[1792,288]{0,1:T(8,128)(2,1)} %param.13), kind=kOutput, calls=%fused_computation.14 | convolution fusion | flops 532299776 | bytes 3171328 | tf_op jit(solution)/shard_map/abrd,dc->abrc/dot_general | solution.py:260
  17.9 0.7 fusion.14
  18.6 1.2 constant_dynamic-slice_fusion.1
  19.8 1.1 pad_maximum_fusion.4
  20.9 7.5 %all-to-all-start = ((bf16[32,2,8,640]{3,2,1,0:T(8,128)(2,1)}), bf16[32,2,8,640]{3,2,1,0:T(8,128)(2,1)S(1)}, u32[]{:S(2)}, u32[]{:S(2)}) async-start(bf16[32,2,8,640]{3,2,1,0:T(8,128)(2,1)} %pad_maximum_fusion.4), calls=%async_computation | async-start | bytes 1310720 | tf_op jit(solution)/shard_map/all_to_all | solution.py:268
  28.5 0.1 reshape.266
  28.7 0.6 copy.93
  29.5 0.2 select_reduce_fusion.2
  29.7 0.6 slice.58
  30.3 0.6 fusion.57
  31.0 0.2 select_reduce_fusion
  31.3 0.6 and_select_fusion
  32.6 2.5 %reshape.277 = bf16[224,8,224]{2,1,0:T(8,128)(2,1)S(1)} reshape(bf16[224,1792]{1,0:T(8,128)(2,1)} %param.14) | data formatting | bytes 1605632 | tf_op jit(solution)/shard_map/reshape | solution.py:363
  35.1 1.2 copy.116
  36.2 1.3 copy.103
  37.5 1.0 copy.104
  38.5 1.9 %fusion.36 = (f32[512]{0:T(512)}, f32[512,512]{0,1:T(8,128)}) fusion(s32[512]{0:T(512)S(1)} %copy-done.10), kind=kLoop, calls=%fused_computation.51 | loop fusion | flops 2358784 | bytes 1052672 | tf_op jit(solution)/shard_map/while/body/eval_jaxpr/reduce_sum | solution.py:71
  40.4 1.2 fusion.34
  41.6 0.2 slice.80
  41.8 1.4 gather_fusion.1
  43.2 1.2 reshape_reshape.3
  44.4 0.4 copy.100
  44.8 0.7 broadcast_multiply_fusion
  45.6 0.1 copy-done.6
  45.7 0.1 multiply_multiply_fusion.1
  45.8 1.0 copy-done.2
  46.9 0.8 fusion.25
  47.8 1.8 %fusion.43 = f32[2,512,512]{1,2,0:T(8,128)} fusion(bf16[2,512,144]{1,2,0:T(8,128)(2,1)S(1)} %bitcast.72), kind=kOutput, calls=%fused_computation.69 | convolution fusion | flops 16777216 | bytes 2129920 | tf_op jit(solution)/shard_map/while/body/eval_jaxpr/hcf,hdf->hcd/dot_general | solution.py:59
  49.6 0.8 convolution_convert_fusion
  50.4 0.3 reshape.271
  50.7 2.8 %concatenate.15 = bf16[61699]{0:T(1024)(128)(2,1)} concatenate(bf16[61152]{0:T(1024)(128)(2,1)S(1)} %reshape.271, bf16[546]{0:T(1024)(128)(2,1)S(1)} %reshape.272, bf16[1]{0:T(256)(128)(2,1)} %bitcast.18), dimensions={0} | concatenate | bytes 246796 | tf_op jit(solution)/shard_map/concatenate | solution.py:311
  53.5 2.2 %collective-permute-start = (bf16[61699]{0:T(1024)(128)(2,1)}, bf16[61699]{0:T(1024)(128)(2,1)}, u32[]{:S(2)}, u32[]{:S(2)}) collective-permute-start(bf16[61699]{0:T(1024)(128)(2,1)} %concatenate.15), channel_id=1, source_target_pairs={{0,8},{8,16},{16,24},{24,32},{32,40},{40,48},{48,56},{56,64},{64,7... | collective-permute-start | bytes 370202 | tf_op jit(solution)/shard_map/ppermute | solution.py:20
  55.7 1.1 multiply_multiply_fusion
  56.8 1.9 %fusion.58 = (f32[2,512]{1,0:T(2,128)S(1)}, f32[2,512,512]{1,2,0:T(8,128)S(1)}) fusion(f32[512,512]{0,1:T(8,128)} %fusion.34, bf16[2,512,144]{1,2,0:T(8,128)(2,1)S(1)} %bitcast.74), kind=kOutput, calls=%fused_computation.113 | convolution fusion | flops 20446208 | bytes 3215360 | tf_op jit(solution)/shard_map/while/body/eval_jaxpr/hcf,hdf->hcd/dot_general | solution.py:49
  58.8 1.6 fusion.39
  60.4 1.3 gather_fusion.2
  61.7 3.2 %multiply_reduce_fusion = f32[2,512]{1,0:T(2,128)} fusion(f32[2,512,512]{1,2,0:T(8,128)} %fusion.43, f32[512,512]{0,1:T(8,128)} %get-tuple-element.82, bf16[2,512,144]{1,2,0:T(8,128)(2,1)S(1)} %bitcast.76), kind=kOutput, calls=%fused_computation.10 | convolution fusion | flops 121633792 | bytes 3379200 | tf_op jit(solution)/shard_map/while/body/eval_jaxpr/hce,hde->hcd/dot_general | solution.py:60
  64.9 0.8 compare_select_fusion.low_ref
  65.7 0.7 slice.90
  66.4 2.2 %gather_fusion.3 = bf16[64,8,224]{2,1,0:T(8,128)(2,1)} fusion(bf16[64,8,224]{2,1,0:T(8,128)(2,1)} %bitcast.87, s32[1024]{0:T(1024)S(1)} %pad_clamp_fusion), kind=kCustom, calls=%fused_computation.3 | custom fusion | bytes 459008 | tf_op jit(solution)/shard_map/gather | solution.py:285
  68.6 0.9 slice.87
  69.5 0.9 reshape.273
  70.5 1.0 convert_element_type.78
  71.5 0.3 mul.257
  71.7 1.3 slice.85
  73.6 0.8 slice.93
  74.5 0.8 slice.88
  75.3 0.1 reduce_sum.94
  75.6 2.1 %fusion.13 = f32[2,512]{1,0:T(2,128)S(1)} fusion(bf16[2,273,112]{2,1,0:T(8,128)(2,1)} %reshape.273, f32[2,512,256]{1,2,0:T(8,128)S(1)} %bitcast.84, f32[2,512,16]{1,2,0:T(8,128)} %copy-done.12, f32[273]{0:T(512)} %copy-done.15, f32[2,512,144]{1,2,0:T(8,128)} %copy-done.6), kind=kOutput, calls=%fused_computation.20 | convolution fusion | flops 376505344 | bytes 1700356 | tf_op jit(solution)/shard_map/while/body/eval_jaxpr/hcp,hpe->hce/dot_general | solution.py:66
  77.8 0.7 fusion.24
  78.5 0.4 fusion.21
  78.9 1.0 fusion.19
  79.9 0.9 fusion.12
  80.8 2.3 %all-gather.3.cloned.1.call-done = bf16[256,16,224]{2,1,0:T(8,128)(2,1)} async-done(((bf16[8,16,224]{2,1,0:T(8,128)(2,1)}), bf16[256,16,224]{2,1,0:T(8,128)(2,1)}) %all-gather.3.cloned.1.call-update) | async-done | bytes 1835024 | tf_op jit(solution)/shard_map/all_gather | solution.py:292
  83.1 0.8 copy.105.att_ref
  83.9 78.7 %shard_map.130 = (bf16[512,224]{1,0:T(8,128)(2,1)}, f32[64,128]{1,0:T(8,128)}) custom-call(bf16[512,224]{1,0:T(8,128)(2,1)} %copy.105.att_ref, bf16[512,128]{1,0:T(8,128)(2,1)} %compare_select_fusion.low_ref, bf16[8,224,224]{2,1,0:T(8,128)(2,1)} %bitcast.71, bf16[8,128,224]{2,1,0:T(8,128)(2,1)} %bitcast.78, bf16[512,224]{1,0:T(8,128)(2,1)} %bitcast.81, ...), custom_call_target="tpu_custom_call" | custom-call | tf_op jit(solution)/shard_map/pallas_call | solution.py:208
  162.6 1.8 %copy.106 = bf16[512,224]{0,1:T(8,128)(2,1)} copy(bf16[512,224]{1,0:T(8,128)(2,1)} %get-tuple-element.70) | data formatting | bytes 458752
  164.4 1.4 slice_reduce_fusion
  (82 shorter events, 1.7 us)
Async XLA Ops:
  7.2 3.5 %copy-start = (bf16[512,1792]{1,0:T(8,128)(2,1)S(1)}, bf16[512,1792]{1,0:T(8,128)(2,1)}, u32[]{:S(2)}) copy-start(bf16[512,1792]{1,0:T(8,128)(2,1)} %param.11) | copy-start | bytes 5505028
  12.6 2.1 %copy-start.21 = (f32[1792]{0:T(1024)S(1)}, f32[1792]{0:T(1024)}, u32[]{:S(2)}) copy-start(f32[1792]{0:T(1024)} %param.12) | copy-start | bytes 21508
  14.7 3.1 %copy-start.1 = (bf16[64,8,1792]{2,1,0:T(8,128)(2,1)S(1)}, bf16[64,8,1792]{2,1,0:T(8,128)(2,1)}, u32[]{:S(2)}) copy-start(bf16[64,8,1792]{2,1,0:T(8,128)(2,1)} %gather_fusion) | copy-start | bytes 5505028
  14.8 3.1 %copy-start.20 = (bf16[1792,128]{1,0:T(8,128)(2,1)S(1)}, bf16[1792,128]{1,0:T(8,128)(2,1)}, u32[]{:S(2)}) copy-start(bf16[1792,128]{1,0:T(8,128)(2,1)} %param.15) | copy-start | bytes 1376260
  18.6 9.9 %copy-start.13 = (bf16[16,1792]{1,0:T(8,128)(2,1)S(1)}, bf16[16,1792]{1,0:T(8,128)(2,1)}, u32[]{:S(2)}) copy-start(bf16[16,1792]{1,0:T(8,128)(2,1)} %param.17) | copy-start | bytes 172036
  18.6 11.1 %copy-start.10 = (s32[512]{0:T(512)S(1)}, s32[512]{0:T(512)}, u32[]{:S(2)}) copy-start(s32[512]{0:T(512)} %param.18) | copy-start | bytes 6148
  18.6 12.4 %copy-start.18 = (s32[128]{0:T(128)S(1)}, s32[128]{0:T(128)}, u32[]{:S(2)}) copy-start(s32[128]{0:T(128)} %param.19) | copy-start | bytes 1540
  18.6 12.6 %copy-start.19 = (s32[64]{0:T(128)S(1)}, s32[64]{0:T(128)}, u32[]{:S(2)}) copy-start(s32[64]{0:T(128)} %param.20) | copy-start | bytes 772
  20.9 20.6 %all-to-all-start = ((bf16[32,2,8,640]{3,2,1,0:T(8,128)(2,1)}), bf16[32,2,8,640]{3,2,1,0:T(8,128)(2,1)S(1)}, u32[]{:S(2)}, u32[]{:S(2)}) async-start(bf16[32,2,8,640]{3,2,1,0:T(8,128)(2,1)} %pad_maximum_fusion.4), calls=%async_computation | async-start | bytes 1310720 | tf_op jit(solution)/shard_map/all_to_all | solution.py:268
  28.5 54.6 %all-gather.3.cloned.1.call-start = ((), (), s32[]{:S(2)}) async-start(), calls=%async_computation.1 | async-start | bytes 2162688 | tf_op jit(solution)/shard_map/all_gather | solution.py:292
  38.5 11.0 %copy-start.15 = (f32[273]{0:T(512)}, f32[273]{0:T(512)S(1)}, u32[]{:S(2)}) copy-start(f32[273]{0:T(512)S(1)} %pad.3.clone) | copy-start | bytes 3280
  44.8 0.9 copy-start.6
  45.7 3.9 %copy-start.12 = (f32[2,512,16]{1,2,0:T(8,128)}, f32[2,512,16]{1,2,0:T(8,128)S(1)}, u32[]{:S(2)}) copy-start(f32[2,512,16]{1,2,0:T(8,128)S(1)} %get-tuple-element.76) | copy-start | bytes 196612
  45.8 1.0 copy-start.2
  47.8 1.8 %copy-start.3 = (f32[2,512,16,16]{1,3,2,0:T(8,128)S(1)}, f32[2,512,16,16]{1,3,2,0:T(8,128)}, u32[]{:S(2)}) copy-start(f32[2,512,16,16]{1,3,2,0:T(8,128)} %copy-done.2) | copy-start | bytes 3145732
  53.5 15.2 %collective-permute-start = (bf16[61699]{0:T(1024)(128)(2,1)}, bf16[61699]{0:T(1024)(128)(2,1)}, u32[]{:S(2)}, u32[]{:S(2)}) collective-permute-start(bf16[61699]{0:T(1024)(128)(2,1)} %concatenate.15), channel_id=1, source_target_pairs={{0,8},{8,16},{16,24},{24,32},{32,40},{40,48},{48,56},{56,64},{64,7... | collective-permute-start | bytes 370202 | tf_op jit(solution)/shard_map/ppermute | solution.py:20
  61.7 3.2 %copy-start.7 = (bf16[64,8,128]{2,1,0:T(8,128)(2,1)S(1)}, bf16[64,8,128]{2,1,0:T(8,128)(2,1)}, u32[]{:S(2)}) copy-start(bf16[64,8,128]{2,1,0:T(8,128)(2,1)} %gather_fusion.2) | copy-start | bytes 393220
  61.7 3.2 %copy-start.17 = (s32[128]{0:T(128)S(1)}, s32[128]{0:T(128)}, u32[]{:S(2)}) copy-start(s32[128]{0:T(128)} %and_select_fusion) | copy-start | bytes 1540
  64.9 10.7 %copy-start.4 = (f32[2,512,16,16]{1,3,2,0:T(8,128)S(1)}, f32[2,512,16,16]{1,3,2,0:T(8,128)}, u32[]{:S(2)}) copy-start(f32[2,512,16,16]{1,3,2,0:T(8,128)} %copy-done.2) | copy-start | bytes 3145732
  70.5 7.3 %copy-start.11 = (f32[2,512,16]{1,2,0:T(8,128)S(1)}, f32[2,512,16]{1,2,0:T(8,128)}, u32[]{:S(2)}) copy-start(f32[2,512,16]{1,2,0:T(8,128)} %get-tuple-element.75) | copy-start | bytes 196612
  70.5 7.3 %copy-start.16 = (f32[273]{0:T(512)S(1)}, f32[273]{0:T(512)}, u32[]{:S(2)}) copy-start(f32[273]{0:T(512)} %copy-done.15) | copy-start | bytes 3280
  75.5 2.3 %copy-start.5 = (f32[2,512,16,16]{1,3,2,0:T(8,128)S(1)}, f32[2,512,16,16]{1,3,2,0:T(8,128)}, u32[]{:S(2)}) copy-start(f32[2,512,16,16]{1,3,2,0:T(8,128)} %multiply_multiply_fusion) | copy-start | bytes 3145732
  75.6 3.3 %copy-start.14 = (f32[512]{0:T(512)S(1)}, f32[512]{0:T(512)}, u32[]{:S(2)}) copy-start(f32[512]{0:T(512)} %get-tuple-element.81) | copy-start | bytes 6148
  75.6 3.3 %copy-start.22 = (f32[2,512]{1,0:T(2,128)S(1)}, f32[2,512]{1,0:T(2,128)}, u32[]{:S(2)}) copy-start(f32[2,512]{1,0:T(2,128)} %multiply_reduce_fusion) | copy-start | bytes 12292
  77.7 2.2 %copy-start.8 = (f32[2,512,112]{1,2,0:T(8,128)S(1)}, f32[2,512,112]{1,2,0:T(8,128)}, u32[]{:S(2)}) copy-start(f32[2,512,112]{1,2,0:T(8,128)} %fusion.39) | copy-start | bytes 1376260
  77.7 2.2 %copy-start.9 = (bf16[2,273,112]{2,1,0:T(8,128)(2,1)S(1)}, bf16[2,273,112]{2,1,0:T(8,128)(2,1)}, u32[]{:S(2)}) copy-start(bf16[2,273,112]{2,1,0:T(8,128)(2,1)} %reshape.273) | copy-start | bytes 366916
Sparse Core Ops, SparseCore 0:
  31.9 51.1 all-gather.2

commit v9 on v8

--- a/solution.py
+++ b/solution.py
@@ -90,14 +90,14 @@
     land, acc, rows, tops, got, ring_sems, top_sems,
 ):
     n = w_ref.shape[0]
-    quarter = att_ref.shape[0] // 4
+    quarter = att_ref.shape[0] // 8
     block_rows = best_ref.shape[0]
     me = lax.axis_index("mp")
     grp = lax.axis_index("group")
     peers = [lax.rem(me + k, n) for k in range(1, n)]
     mesh_id = pl.DeviceIdType.MESH
     towards = (lax.rem(me + 1, n), lax.rem(me + n - 1, n))
-    chains = [(0, 0), (1, 2), (0, 1), (1, 3)]
+    chains = [(0, 0), (1, 4), (0, 1), (1, 5), (0, 2), (1, 6), (0, 3), (1, 7)]
     spans = [pl.ds(quarter * piece, quarter) for _, piece in chains]
 
     barrier = pltpu.get_barrier_semaphore()
@@ -203,7 +203,7 @@
     n, _, width = out_blocks.shape
     rows_here = attended.shape[0]
     block_rows = rows_here // n
-    chains = 4
+    chains = 8
     vmem = pl.BlockSpec(memory_space=pltpu.VMEM)
     return pl.pallas_call(
         exchange_kernel,

time: 173 us -> 169 us (0.977)
  Pallas kernels: 78.7 us -> 73.7 us
    pallas_call x1, Pallas kernels: 78.7 us -> 73.7 us  [mp_exchange(): pl.pallas_call(exchange_kernel, out_shape=(jax.ShapeDtypeStruct((rows_her...]
  transfers between devices with their start and end apart: 3 -> 3, of which waited for: 1 -> 1; matrix products, arithmetic and copies ran while one was open for 27% -> 28% of each run, Pallas kernels for 0% -> 0%
where the time goes in v9:
time: 169 us; the launch traced here: 168 us
  Pallas kernels  73.7 us (44%)
  local copies, waits for them, and re-layouts  33.9 us (20%)
  matrix products  19 us (11%)
  between operations  15.8 us (9%)
  other arithmetic  13 us (8%)
  starting transfers between devices  9.8 us (6%)
  waiting for transfers between devices  2.3 us (1%)
    pallas_call x1, Pallas kernels, mp_exchange(): pl.pallas_call(exchange_kernel, out_shape=(jax.ShapeDtypeStruct((rows_her...  73.7 us
    all_to_all x1, starting transfers between devices, on_device(): lax.all_to_all(jnp.concatenate([kept_pages, projected_pages, lowered_page...  7.54 us
    gather x3, local copies, waits for them, and re-layouts, placed(): received.reshape((groups * per_peer,) + received.shape[2:])[source_rows]  4.91 us
    unnamed x48, local copies, waits for them, and re-layouts  4.31 us
    reshape x2, local copies, waits for them, and re-layouts, on_device(): out_weight.reshape(out_weight.shape[0], shards, slice_width)  3.63 us
  transfers between devices with their start and end apart: 3, of which 1 were waited for; matrix products, arithmetic and copies ran while one was open for 28% of the time, Pallas kernels for 0%

profile of v9, /device:TPU:8, one launch (start us, length us, event | category | flops | bytes accessed | tf_op | source)
XLA Modules:
  0.0 167.6 jit_solution(8550571601110376223)
XLA Ops:
  7.2 0.9 reshape.268
  8.2 1.0 sort.17
  9.4 0.8 gather_fusion.4
  10.5 0.1 reshape.284
  10.7 1.9 %gather_fusion = bf16[64,8,1792]{2,1,0:T(8,128)(2,1)} fusion(bf16[64,8,1792]{2,1,0:T(8,128)(2,1)S(1)} %bitcast.66, s32[1024]{0:T(1024)S(1)} %pad_clamp_fusion.1), kind=kCustom, calls=%fused_computation | custom fusion | bytes 3670272 | tf_op jit(solution)/shard_map/gather | solution.py:258
  12.6 2.0 %fusion = f32[32,2,8]{2,1,0:T(2,128)S(1)} fusion(bf16[32,2,8,1792]{3,2,1,0:T(8,128)(2,1)} %bitcast.67), kind=kLoop, calls=%fused_computation.7 | loop fusion | flops 2752000 | bytes 1837056 | tf_op jit(solution)/shard_map/reduce_sum | solution.py:25
  14.8 3.1 %fusion.7 = bf16[32,2,8,288]{3,2,1,0:T(8,128)(2,1)S(1)} fusion(bf16[32,2,8,1792]{3,2,1,0:T(8,128)(2,1)} %bitcast.68, f32[1792]{0:T(1024)S(1)} %copy-done.21, f32[32,2,8]{2,1,0:T(2,128)S(1)} %copy.99, bf16[1792,288]{0,1:T(8,128)(2,1)} %param.13), kind=kOutput, calls=%fused_computation.14 | convolution fusion | flops 532299776 | bytes 3171328 | tf_op jit(solution)/shard_map/abrd,dc->abrc/dot_general | solution.py:260
  17.9 0.7 fusion.14
  18.6 1.2 constant_dynamic-slice_fusion.1
  19.8 1.1 pad_maximum_fusion.4
  20.9 7.5 %all-to-all-start = ((bf16[32,2,8,640]{3,2,1,0:T(8,128)(2,1)}), bf16[32,2,8,640]{3,2,1,0:T(8,128)(2,1)S(1)}, u32[]{:S(2)}, u32[]{:S(2)}) async-start(bf16[32,2,8,640]{3,2,1,0:T(8,128)(2,1)} %pad_maximum_fusion.4), calls=%async_computation | async-start | bytes 1310720 | tf_op jit(solution)/shard_map/all_to_all | solution.py:268
  28.5 0.1 reshape.266
  28.7 0.6 copy.93
  29.5 0.2 select_reduce_fusion.2
  29.7 0.6 slice.58
  30.3 0.6 fusion.57
  31.0 0.2 select_reduce_fusion
  31.3 0.6 and_select_fusion
  32.6 2.5 %reshape.277 = bf16[224,8,224]{2,1,0:T(8,128)(2,1)S(1)} reshape(bf16[224,1792]{1,0:T(8,128)(2,1)} %param.14) | data formatting | bytes 1605632 | tf_op jit(solution)/shard_map/reshape | solution.py:363
  35.1 1.2 copy.116
  36.2 1.3 copy.103
  37.5 1.0 copy.104
  38.5 1.9 %fusion.36 = (f32[512]{0:T(512)}, f32[512,512]{0,1:T(8,128)}) fusion(s32[512]{0:T(512)S(1)} %copy-done.10), kind=kLoop, calls=%fused_computation.51 | loop fusion | flops 2358784 | bytes 1052672 | tf_op jit(solution)/shard_map/while/body/eval_jaxpr/reduce_sum | solution.py:71
  40.4 1.2 fusion.34
  41.6 0.2 slice.80
  41.8 1.4 gather_fusion.1
  43.2 1.2 reshape_reshape.3
  44.4 0.4 copy.100
  44.8 0.7 broadcast_multiply_fusion
  45.5 0.1 copy-done.6
  45.7 0.1 multiply_multiply_fusion.1
  45.8 1.0 copy-done.2
  46.9 0.8 fusion.25
  47.8 1.8 %fusion.43 = f32[2,512,512]{1,2,0:T(8,128)} fusion(bf16[2,512,144]{1,2,0:T(8,128)(2,1)S(1)} %bitcast.72), kind=kOutput, calls=%fused_computation.69 | convolution fusion | flops 16777216 | bytes 2129920 | tf_op jit(solution)/shard_map/while/body/eval_jaxpr/hcf,hdf->hcd/dot_general | solution.py:59
  49.6 0.8 convolution_convert_fusion
  50.4 0.3 reshape.271
  50.7 2.8 %concatenate.15 = bf16[61699]{0:T(1024)(128)(2,1)} concatenate(bf16[61152]{0:T(1024)(128)(2,1)S(1)} %reshape.271, bf16[546]{0:T(1024)(128)(2,1)S(1)} %reshape.272, bf16[1]{0:T(256)(128)(2,1)} %bitcast.18), dimensions={0} | concatenate | bytes 246796 | tf_op jit(solution)/shard_map/concatenate | solution.py:311
  53.5 2.2 %collective-permute-start = (bf16[61699]{0:T(1024)(128)(2,1)}, bf16[61699]{0:T(1024)(128)(2,1)}, u32[]{:S(2)}, u32[]{:S(2)}) collective-permute-start(bf16[61699]{0:T(1024)(128)(2,1)} %concatenate.15), channel_id=1, source_target_pairs={{0,8},{8,16},{16,24},{24,32},{32,40},{40,48},{48,56},{56,64},{64,7... | collective-permute-start | bytes 370202 | tf_op jit(solution)/shard_map/ppermute | solution.py:20
  55.7 1.1 multiply_multiply_fusion
  56.8 1.9 %fusion.58 = (f32[2,512]{1,0:T(2,128)S(1)}, f32[2,512,512]{1,2,0:T(8,128)S(1)}) fusion(f32[512,512]{0,1:T(8,128)} %fusion.34, bf16[2,512,144]{1,2,0:T(8,128)(2,1)S(1)} %bitcast.74), kind=kOutput, calls=%fused_computation.113 | convolution fusion | flops 20446208 | bytes 3215360 | tf_op jit(solution)/shard_map/while/body/eval_jaxpr/hcf,hdf->hcd/dot_general | solution.py:49
  58.8 1.6 fusion.39
  60.4 1.3 gather_fusion.2
  61.7 3.2 %multiply_reduce_fusion = f32[2,512]{1,0:T(2,128)} fusion(f32[2,512,512]{1,2,0:T(8,128)} %fusion.43, f32[512,512]{0,1:T(8,128)} %get-tuple-element.82, bf16[2,512,144]{1,2,0:T(8,128)(2,1)S(1)} %bitcast.76), kind=kOutput, calls=%fused_computation.10 | convolution fusion | flops 121633792 | bytes 3379200 | tf_op jit(solution)/shard_map/while/body/eval_jaxpr/hce,hde->hcd/dot_general | solution.py:60
  64.9 0.8 compare_select_fusion.low_ref
  65.7 0.7 slice.90
  66.4 2.2 %gather_fusion.3 = bf16[64,8,224]{2,1,0:T(8,128)(2,1)} fusion(bf16[64,8,224]{2,1,0:T(8,128)(2,1)} %bitcast.87, s32[1024]{0:T(1024)S(1)} %pad_clamp_fusion), kind=kCustom, calls=%fused_computation.3 | custom fusion | bytes 459008 | tf_op jit(solution)/shard_map/gather | solution.py:285
  68.6 0.9 slice.87
  69.5 0.9 reshape.273
  70.5 1.0 convert_element_type.78
  71.5 0.3 mul.257
  71.7 1.3 slice.85
  73.6 0.8 slice.93
  74.5 0.8 slice.88
  75.3 0.1 reduce_sum.94
  75.6 2.1 %fusion.13 = f32[2,512]{1,0:T(2,128)S(1)} fusion(bf16[2,273,112]{2,1,0:T(8,128)(2,1)} %reshape.273, f32[2,512,256]{1,2,0:T(8,128)S(1)} %bitcast.84, f32[2,512,16]{1,2,0:T(8,128)} %copy-done.12, f32[273]{0:T(512)} %copy-done.15, f32[2,512,144]{1,2,0:T(8,128)} %copy-done.6), kind=kOutput, calls=%fused_computation.20 | convolution fusion | flops 376505344 | bytes 1700356 | tf_op jit(solution)/shard_map/while/body/eval_jaxpr/hcp,hpe->hce/dot_general | solution.py:66
  77.8 0.7 fusion.24
  78.5 0.4 fusion.21
  78.9 1.0 fusion.19
  79.9 0.9 fusion.12
  80.8 2.3 %all-gather.3.cloned.1.call-done = bf16[256,16,224]{2,1,0:T(8,128)(2,1)} async-done(((bf16[8,16,224]{2,1,0:T(8,128)(2,1)}), bf16[256,16,224]{2,1,0:T(8,128)(2,1)}) %all-gather.3.cloned.1.call-update) | async-done | bytes 1835024 | tf_op jit(solution)/shard_map/all_gather | solution.py:292
  83.1 0.8 copy.105.att_ref
  83.9 73.7 %shard_map.130 = (bf16[512,224]{1,0:T(8,128)(2,1)}, f32[64,128]{1,0:T(8,128)}) custom-call(bf16[512,224]{1,0:T(8,128)(2,1)} %copy.105.att_ref, bf16[512,128]{1,0:T(8,128)(2,1)} %compare_select_fusion.low_ref, bf16[8,224,224]{2,1,0:T(8,128)(2,1)} %bitcast.71, bf16[8,128,224]{2,1,0:T(8,128)(2,1)} %bitcast.78, bf16[512,224]{1,0:T(8,128)(2,1)} %bitcast.81, ...), custom_call_target="tpu_custom_call" | custom-call | tf_op jit(solution)/shard_map/pallas_call | solution.py:208
  157.6 1.8 %copy.106 = bf16[512,224]{0,1:T(8,128)(2,1)} copy(bf16[512,224]{1,0:T(8,128)(2,1)} %get-tuple-element.70) | data formatting | bytes 458752
  159.3 1.4 slice_reduce_fusion
  (82 shorter events, 1.7 us)
Async XLA Ops:
  7.2 3.5 %copy-start = (bf16[512,1792]{1,0:T(8,128)(2,1)S(1)}, bf16[512,1792]{1,0:T(8,128)(2,1)}, u32[]{:S(2)}) copy-start(bf16[512,1792]{1,0:T(8,128)(2,1)} %param.11) | copy-start | bytes 5505028
  12.6 2.1 %copy-start.21 = (f32[1792]{0:T(1024)S(1)}, f32[1792]{0:T(1024)}, u32[]{:S(2)}) copy-start(f32[1792]{0:T(1024)} %param.12) | copy-start | bytes 21508
  14.7 3.1 %copy-start.1 = (bf16[64,8,1792]{2,1,0:T(8,128)(2,1)S(1)}, bf16[64,8,1792]{2,1,0:T(8,128)(2,1)}, u32[]{:S(2)}) copy-start(bf16[64,8,1792]{2,1,0:T(8,128)(2,1)} %gather_fusion) | copy-start | bytes 5505028
  14.8 3.1 %copy-start.20 = (bf16[1792,128]{1,0:T(8,128)(2,1)S(1)}, bf16[1792,128]{1,0:T(8,128)(2,1)}, u32[]{:S(2)}) copy-start(bf16[1792,128]{1,0:T(8,128)(2,1)} %param.15) | copy-start | bytes 1376260
  18.6 9.9 %copy-start.13 = (bf16[16,1792]{1,0:T(8,128)(2,1)S(1)}, bf16[16,1792]{1,0:T(8,128)(2,1)}, u32[]{:S(2)}) copy-start(bf16[16,1792]{1,0:T(8,128)(2,1)} %param.17) | copy-start | bytes 172036
  18.6 11.1 %copy-start.10 = (s32[512]{0:T(512)S(1)}, s32[512]{0:T(512)}, u32[]{:S(2)}) copy-start(s32[512]{0:T(512)} %param.18) | copy-start | bytes 6148
  18.6 12.4 %copy-start.18 = (s32[128]{0:T(128)S(1)}, s32[128]{0:T(128)}, u32[]{:S(2)}) copy-start(s32[128]{0:T(128)} %param.19) | copy-start | bytes 1540
  18.6 12.6 %copy-start.19 = (s32[64]{0:T(128)S(1)}, s32[64]{0:T(128)}, u32[]{:S(2)}) copy-start(s32[64]{0:T(128)} %param.20) | copy-start | bytes 772
  20.9 20.6 %all-to-all-start = ((bf16[32,2,8,640]{3,2,1,0:T(8,128)(2,1)}), bf16[32,2,8,640]{3,2,1,0:T(8,128)(2,1)S(1)}, u32[]{:S(2)}, u32[]{:S(2)}) async-start(bf16[32,2,8,640]{3,2,1,0:T(8,128)(2,1)} %pad_maximum_fusion.4), calls=%async_computation | async-start | bytes 1310720 | tf_op jit(solution)/shard_map/all_to_all | solution.py:268
  28.5 54.6 %all-gather.3.cloned.1.call-start = ((), (), s32[]{:S(2)}) async-start(), calls=%async_computation.1 | async-start | bytes 2162688 | tf_op jit(solution)/shard_map/all_gather | solution.py:292
  38.5 11.0 %copy-start.15 = (f32[273]{0:T(512)}, f32[273]{0:T(512)S(1)}, u32[]{:S(2)}) copy-start(f32[273]{0:T(512)S(1)} %pad.3.clone) | copy-start | bytes 3280
  44.8 0.9 copy-start.6
  45.7 3.9 %copy-start.12 = (f32[2,512,16]{1,2,0:T(8,128)}, f32[2,512,16]{1,2,0:T(8,128)S(1)}, u32[]{:S(2)}) copy-start(f32[2,512,16]{1,2,0:T(8,128)S(1)} %get-tuple-element.76) | copy-start | bytes 196612
  45.8 1.0 copy-start.2
  47.8 1.8 %copy-start.3 = (f32[2,512,16,16]{1,3,2,0:T(8,128)S(1)}, f32[2,512,16,16]{1,3,2,0:T(8,128)}, u32[]{:S(2)}) copy-start(f32[2,512,16,16]{1,3,2,0:T(8,128)} %copy-done.2) | copy-start | bytes 3145732
  53.5 15.2 %collective-permute-start = (bf16[61699]{0:T(1024)(128)(2,1)}, bf16[61699]{0:T(1024)(128)(2,1)}, u32[]{:S(2)}, u32[]{:S(2)}) collective-permute-start(bf16[61699]{0:T(1024)(128)(2,1)} %concatenate.15), channel_id=1, source_target_pairs={{0,8},{8,16},{16,24},{24,32},{32,40},{40,48},{48,56},{56,64},{64,7... | collective-permute-start | bytes 370202 | tf_op jit(solution)/shard_map/ppermute | solution.py:20
  61.7 3.2 %copy-start.7 = (bf16[64,8,128]{2,1,0:T(8,128)(2,1)S(1)}, bf16[64,8,128]{2,1,0:T(8,128)(2,1)}, u32[]{:S(2)}) copy-start(bf16[64,8,128]{2,1,0:T(8,128)(2,1)} %gather_fusion.2) | copy-start | bytes 393220
  61.7 3.2 %copy-start.17 = (s32[128]{0:T(128)S(1)}, s32[128]{0:T(128)}, u32[]{:S(2)}) copy-start(s32[128]{0:T(128)} %and_select_fusion) | copy-start | bytes 1540
  64.9 10.7 %copy-start.4 = (f32[2,512,16,16]{1,3,2,0:T(8,128)S(1)}, f32[2,512,16,16]{1,3,2,0:T(8,128)}, u32[]{:S(2)}) copy-start(f32[2,512,16,16]{1,3,2,0:T(8,128)} %copy-done.2) | copy-start | bytes 3145732
  70.5 7.3 %copy-start.11 = (f32[2,512,16]{1,2,0:T(8,128)S(1)}, f32[2,512,16]{1,2,0:T(8,128)}, u32[]{:S(2)}) copy-start(f32[2,512,16]{1,2,0:T(8,128)} %get-tuple-element.75) | copy-start | bytes 196612
  70.5 7.3 %copy-start.16 = (f32[273]{0:T(512)S(1)}, f32[273]{0:T(512)}, u32[]{:S(2)}) copy-start(f32[273]{0:T(512)} %copy-done.15) | copy-start | bytes 3280
  75.5 2.3 %copy-start.5 = (f32[2,512,16,16]{1,3,2,0:T(8,128)S(1)}, f32[2,512,16,16]{1,3,2,0:T(8,128)}, u32[]{:S(2)}) copy-start(f32[2,512,16,16]{1,3,2,0:T(8,128)} %multiply_multiply_fusion) | copy-start | bytes 3145732
  75.6 3.3 %copy-start.14 = (f32[512]{0:T(512)S(1)}, f32[512]{0:T(512)}, u32[]{:S(2)}) copy-start(f32[512]{0:T(512)} %get-tuple-element.81) | copy-start | bytes 6148
  75.6 3.3 %copy-start.22 = (f32[2,512]{1,0:T(2,128)S(1)}, f32[2,512]{1,0:T(2,128)}, u32[]{:S(2)}) copy-start(f32[2,512]{1,0:T(2,128)} %multiply_reduce_fusion) | copy-start | bytes 12292
  77.7 2.2 %copy-start.8 = (f32[2,512,112]{1,2,0:T(8,128)S(1)}, f32[2,512,112]{1,2,0:T(8,128)}, u32[]{:S(2)}) copy-start(f32[2,512,112]{1,2,0:T(8,128)} %fusion.39) | copy-start | bytes 1376260
  77.7 2.2 %copy-start.9 = (bf16[2,273,112]{2,1,0:T(8,128)(2,1)S(1)}, bf16[2,273,112]{2,1,0:T(8,128)(2,1)}, u32[]{:S(2)}) copy-start(bf16[2,273,112]{2,1,0:T(8,128)(2,1)} %reshape.273) | copy-start | bytes 366916
Sparse Core Ops, SparseCore 0:
  31.9 51.1 all-gather.2

commit v10 on v9

--- a/solution.py
+++ b/solution.py
@@ -87,7 +87,7 @@
 
 def exchange_kernel(
     att_ref, low_ref, w_ref, u_ref, resid_ref, vocab_ref, upd_ref, best_ref,
-    land, acc, rows, tops, got, ring_sems, top_sems,
+    land, acc, rows, tops, got, parts, ring_sems, top_sems,
 ):
     n = w_ref.shape[0]
     quarter = att_ref.shape[0] // 8
@@ -100,6 +100,11 @@
     chains = [(0, 0), (1, 4), (0, 1), (1, 5), (0, 2), (1, 6), (0, 3), (1, 7)]
     spans = [pl.ds(quarter * piece, quarter) for _, piece in chains]
 
+    for c in range(n):
+        value = jnp.dot(att_ref[...], w_ref[c], preferred_element_type=jnp.float32)
+        value = value + jnp.dot(low_ref[...], u_ref[c], preferred_element_type=jnp.float32)
+        parts[c] = value.astype(parts.dtype)
+
     barrier = pltpu.get_barrier_semaphore()
     for p in peers:
         pl.semaphore_signal(barrier, inc=1, device_id=(grp, p), device_id_type=mesh_id)
@@ -120,9 +125,7 @@
         return lax.rem(me + (n - 1 - step if way == 0 else 1 + step) + n, n)
 
     def part(chunk, span):
-        value = jnp.dot(att_ref[span], w_ref[chunk], preferred_element_type=jnp.float32)
-        value = value + jnp.dot(low_ref[span], u_ref[chunk], preferred_element_type=jnp.float32)
-        return value.astype(jnp.bfloat16).astype(jnp.float32)
+        return parts[chunk, span].astype(jnp.float32)
 
     pending = [None] * len(chains)
     for step in range(n - 1):
@@ -146,11 +149,13 @@
         rows[me, spans[chain]] = (
             resid_ref[spans[chain]].astype(jnp.float32) + update.astype(jnp.float32)
         ).astype(rows.dtype)
-
-    for step in range(n - 1):
+        view = rows.at[me, spans[chain]]
+        pending[chain] = ring_copy(1, chain, 0, view, view)
+        pending[chain].start()
+
+    for step in range(1, n - 1):
         for chain in range(len(chains)):
-            if step > 0:
-                pending[chain].wait()
+            pending[chain].wait()
             way = chains[chain][0]
             chunk = lax.rem(me + (n - step if way == 0 else step), n)
             view = rows.at[chunk, spans[chain]]
@@ -219,6 +224,7 @@
             pltpu.VMEM((n, rows_here, width), jnp.bfloat16),
             pltpu.VMEM((n, block_rows, 128), jnp.float32),
             pltpu.VMEM((n, block_rows, 128), jnp.float32),
+            pltpu.VMEM((n, rows_here, width), jnp.bfloat16),
             pltpu.SemaphoreType.DMA((2, chains, 2, n - 1)),
             pltpu.SemaphoreType.DMA((2, n)),
         ],

time: 169 us -> 165 us (0.976)
  Pallas kernels: 73.7 us -> 69.5 us
    pallas_call x1, Pallas kernels: 73.7 us -> 69.5 us  [mp_exchange(): pl.pallas_call(exchange_kernel, out_shape=(jax.ShapeDtypeStruct((rows_her...]
  transfers between devices with their start and end apart: 3 -> 3, of which waited for: 1 -> 1; matrix products, arithmetic and copies ran while one was open for 28% -> 29% of each run, Pallas kernels for 0% -> 0%
where the time goes in v10:
time: 165 us; the launch traced here: 163 us
  Pallas kernels  69.5 us (42%)
  local copies, waits for them, and re-layouts  33.9 us (21%)
  matrix products  19 us (12%)
  between operations  15.8 us (10%)
  other arithmetic  13 us (8%)
  starting transfers between devices  9.81 us (6%)
  waiting for transfers between devices  2.3 us (1%)
    pallas_call x1, Pallas kernels, mp_exchange(): pl.pallas_call(exchange_kernel, out_shape=(jax.ShapeDtypeStruct((rows_her...  69.5 us
    all_to_all x1, starting transfers between devices, on_device(): lax.all_to_all(jnp.concatenate([kept_pages, projected_pages, lowered_page...  7.54 us
    gather x3, local copies, waits for them, and re-layouts, placed(): received.reshape((groups * per_peer,) + received.shape[2:])[source_rows]  4.91 us
    unnamed x48, local copies, waits for them, and re-layouts  4.31 us
    reshape x2, local copies, waits for them, and re-layouts, on_device(): out_weight.reshape(out_weight.shape[0], shards, slice_width)  3.63 us
  transfers between devices with their start and end apart: 3, of which 1 were waited for; matrix products, arithmetic and copies ran while one was open for 29% of the time, Pallas kernels for 0%

profile of v10, /device:TPU:8, one launch (start us, length us, event | category | flops | bytes accessed | tf_op | source)
XLA Modules:
  0.0 163.4 jit_solution(7648017686256973698)
XLA Ops:
  7.2 0.9 reshape.268
  8.2 1.0 sort.17
  9.4 0.8 gather_fusion.4
  10.5 0.1 reshape.284
  10.7 1.9 %gather_fusion = bf16[64,8,1792]{2,1,0:T(8,128)(2,1)} fusion(bf16[64,8,1792]{2,1,0:T(8,128)(2,1)S(1)} %bitcast.66, s32[1024]{0:T(1024)S(1)} %pad_clamp_fusion.1), kind=kCustom, calls=%fused_computation | custom fusion | bytes 3670272 | tf_op jit(solution)/shard_map/gather | solution.py:264
  12.6 2.0 %fusion = f32[32,2,8]{2,1,0:T(2,128)S(1)} fusion(bf16[32,2,8,1792]{3,2,1,0:T(8,128)(2,1)} %bitcast.67), kind=kLoop, calls=%fused_computation.7 | loop fusion | flops 2752000 | bytes 1837056 | tf_op jit(solution)/shard_map/reduce_sum | solution.py:25
  14.8 3.1 %fusion.7 = bf16[32,2,8,288]{3,2,1,0:T(8,128)(2,1)S(1)} fusion(bf16[32,2,8,1792]{3,2,1,0:T(8,128)(2,1)} %bitcast.68, f32[1792]{0:T(1024)S(1)} %copy-done.21, f32[32,2,8]{2,1,0:T(2,128)S(1)} %copy.99, bf16[1792,288]{0,1:T(8,128)(2,1)} %param.13), kind=kOutput, calls=%fused_computation.14 | convolution fusion | flops 532299776 | bytes 3171328 | tf_op jit(solution)/shard_map/abrd,dc->abrc/dot_general | solution.py:266
  17.9 0.7 fusion.14
  18.6 1.2 constant_dynamic-slice_fusion.1
  19.8 1.1 pad_maximum_fusion.4
  20.9 7.5 %all-to-all-start = ((bf16[32,2,8,640]{3,2,1,0:T(8,128)(2,1)}), bf16[32,2,8,640]{3,2,1,0:T(8,128)(2,1)S(1)}, u32[]{:S(2)}, u32[]{:S(2)}) async-start(bf16[32,2,8,640]{3,2,1,0:T(8,128)(2,1)} %pad_maximum_fusion.4), calls=%async_computation | async-start | bytes 1310720 | tf_op jit(solution)/shard_map/all_to_all | solution.py:274
  28.5 0.1 reshape.266
  28.7 0.6 copy.93
  29.5 0.2 select_reduce_fusion.2
  29.7 0.6 slice.58
  30.3 0.6 fusion.57
  31.0 0.2 select_reduce_fusion
  31.3 0.6 and_select_fusion
  32.6 2.5 %reshape.277 = bf16[224,8,224]{2,1,0:T(8,128)(2,1)S(1)} reshape(bf16[224,1792]{1,0:T(8,128)(2,1)} %param.14) | data formatting | bytes 1605632 | tf_op jit(solution)/shard_map/reshape | solution.py:369
  35.1 1.2 copy.116
  36.2 1.3 copy.103
  37.5 1.0 copy.104
  38.5 1.9 %fusion.36 = (f32[512]{0:T(512)}, f32[512,512]{0,1:T(8,128)}) fusion(s32[512]{0:T(512)S(1)} %copy-done.10), kind=kLoop, calls=%fused_computation.51 | loop fusion | flops 2358784 | bytes 1052672 | tf_op jit(solution)/shard_map/while/body/eval_jaxpr/reduce_sum | solution.py:71
  40.4 1.2 fusion.34
  41.6 0.2 slice.80
  41.8 1.4 gather_fusion.1
  43.2 1.2 reshape_reshape.3
  44.4 0.4 copy.100
  44.8 0.7 broadcast_multiply_fusion
  45.5 0.1 copy-done.6
  45.7 0.1 multiply_multiply_fusion.1
  45.8 1.0 copy-done.2
  46.9 0.8 fusion.25
  47.8 1.8 %fusion.43 = f32[2,512,512]{1,2,0:T(8,128)} fusion(bf16[2,512,144]{1,2,0:T(8,128)(2,1)S(1)} %bitcast.72), kind=kOutput, calls=%fused_computation.69 | convolution fusion | flops 16777216 | bytes 2129920 | tf_op jit(solution)/shard_map/while/body/eval_jaxpr/hcf,hdf->hcd/dot_general | solution.py:59
  49.6 0.8 convolution_convert_fusion
  50.4 0.3 reshape.271
  50.7 2.8 %concatenate.15 = bf16[61699]{0:T(1024)(128)(2,1)} concatenate(bf16[61152]{0:T(1024)(128)(2,1)S(1)} %reshape.271, bf16[546]{0:T(1024)(128)(2,1)S(1)} %reshape.272, bf16[1]{0:T(256)(128)(2,1)} %bitcast.18), dimensions={0} | concatenate | bytes 246796 | tf_op jit(solution)/shard_map/concatenate | solution.py:317
  53.5 2.2 %collective-permute-start = (bf16[61699]{0:T(1024)(128)(2,1)}, bf16[61699]{0:T(1024)(128)(2,1)}, u32[]{:S(2)}, u32[]{:S(2)}) collective-permute-start(bf16[61699]{0:T(1024)(128)(2,1)} %concatenate.15), channel_id=1, source_target_pairs={{0,8},{8,16},{16,24},{24,32},{32,40},{40,48},{48,56},{56,64},{64,7... | collective-permute-start | bytes 370202 | tf_op jit(solution)/shard_map/ppermute | solution.py:20
  55.7 1.1 multiply_multiply_fusion
  56.8 1.9 %fusion.58 = (f32[2,512]{1,0:T(2,128)S(1)}, f32[2,512,512]{1,2,0:T(8,128)S(1)}) fusion(f32[512,512]{0,1:T(8,128)} %fusion.34, bf16[2,512,144]{1,2,0:T(8,128)(2,1)S(1)} %bitcast.74), kind=kOutput, calls=%fused_computation.113 | convolution fusion | flops 20446208 | bytes 3215360 | tf_op jit(solution)/shard_map/while/body/eval_jaxpr/hcf,hdf->hcd/dot_general | solution.py:49
  58.8 1.6 fusion.39
  60.4 1.3 gather_fusion.2
  61.7 3.2 %multiply_reduce_fusion = f32[2,512]{1,0:T(2,128)} fusion(f32[2,512,512]{1,2,0:T(8,128)} %fusion.43, f32[512,512]{0,1:T(8,128)} %get-tuple-element.82, bf16[2,512,144]{1,2,0:T(8,128)(2,1)S(1)} %bitcast.76), kind=kOutput, calls=%fused_computation.10 | convolution fusion | flops 121633792 | bytes 3379200 | tf_op jit(solution)/shard_map/while/body/eval_jaxpr/hce,hde->hcd/dot_general | solution.py:60
  64.9 0.8 compare_select_fusion.low_ref
  65.7 0.7 slice.90
  66.4 2.2 %gather_fusion.3 = bf16[64,8,224]{2,1,0:T(8,128)(2,1)} fusion(bf16[64,8,224]{2,1,0:T(8,128)(2,1)} %bitcast.87, s32[1024]{0:T(1024)S(1)} %pad_clamp_fusion), kind=kCustom, calls=%fused_computation.3 | custom fusion | bytes 459008 | tf_op jit(solution)/shard_map/gather | solution.py:291
  68.6 0.9 slice.87
  69.5 0.9 reshape.273
  70.5 1.0 convert_element_type.78
  71.5 0.3 mul.257
  71.7 1.3 slice.85
  73.6 0.8 slice.93
  74.5 0.8 slice.88
  75.3 0.1 reduce_sum.94
  75.6 2.1 %fusion.13 = f32[2,512]{1,0:T(2,128)S(1)} fusion(bf16[2,273,112]{2,1,0:T(8,128)(2,1)} %reshape.273, f32[2,512,256]{1,2,0:T(8,128)S(1)} %bitcast.84, f32[2,512,16]{1,2,0:T(8,128)} %copy-done.12, f32[273]{0:T(512)} %copy-done.15, f32[2,512,144]{1,2,0:T(8,128)} %copy-done.6), kind=kOutput, calls=%fused_computation.20 | convolution fusion | flops 376505344 | bytes 1700356 | tf_op jit(solution)/shard_map/while/body/eval_jaxpr/hcp,hpe->hce/dot_general | solution.py:66
  77.8 0.7 fusion.24
  78.5 0.4 fusion.21
  78.9 1.0 fusion.19
  79.9 0.9 fusion.12
  80.8 2.3 %all-gather.3.cloned.1.call-done = bf16[256,16,224]{2,1,0:T(8,128)(2,1)} async-done(((bf16[8,16,224]{2,1,0:T(8,128)(2,1)}), bf16[256,16,224]{2,1,0:T(8,128)(2,1)}) %all-gather.3.cloned.1.call-update) | async-done | bytes 1835024 | tf_op jit(solution)/shard_map/all_gather | solution.py:298
  83.1 0.8 copy.105.att_ref
  83.9 69.5 %shard_map.130 = (bf16[512,224]{1,0:T(8,128)(2,1)}, f32[64,128]{1,0:T(8,128)}) custom-call(bf16[512,224]{1,0:T(8,128)(2,1)} %copy.105.att_ref, bf16[512,128]{1,0:T(8,128)(2,1)} %compare_select_fusion.low_ref, bf16[8,224,224]{2,1,0:T(8,128)(2,1)} %bitcast.71, bf16[8,128,224]{2,1,0:T(8,128)(2,1)} %bitcast.78, bf16[512,224]{1,0:T(8,128)(2,1)} %bitcast.81, ...), custom_call_target="tpu_custom_call" | custom-call | tf_op jit(solution)/shard_map/pallas_call | solution.py:213
  153.4 1.8 %copy.106 = bf16[512,224]{0,1:T(8,128)(2,1)} copy(bf16[512,224]{1,0:T(8,128)(2,1)} %get-tuple-element.70) | data formatting | bytes 458752
  155.2 1.4 slice_reduce_fusion
  (82 shorter events, 1.7 us)
Async XLA Ops:
  7.2 3.5 %copy-start = (bf16[512,1792]{1,0:T(8,128)(2,1)S(1)}, bf16[512,1792]{1,0:T(8,128)(2,1)}, u32[]{:S(2)}) copy-start(bf16[512,1792]{1,0:T(8,128)(2,1)} %param.11) | copy-start | bytes 5505028
  12.6 2.1 %copy-start.21 = (f32[1792]{0:T(1024)S(1)}, f32[1792]{0:T(1024)}, u32[]{:S(2)}) copy-start(f32[1792]{0:T(1024)} %param.12) | copy-start | bytes 21508
  14.7 3.1 %copy-start.1 = (bf16[64,8,1792]{2,1,0:T(8,128)(2,1)S(1)}, bf16[64,8,1792]{2,1,0:T(8,128)(2,1)}, u32[]{:S(2)}) copy-start(bf16[64,8,1792]{2,1,0:T(8,128)(2,1)} %gather_fusion) | copy-start | bytes 5505028
  14.8 3.1 %copy-start.20 = (bf16[1792,128]{1,0:T(8,128)(2,1)S(1)}, bf16[1792,128]{1,0:T(8,128)(2,1)}, u32[]{:S(2)}) copy-start(bf16[1792,128]{1,0:T(8,128)(2,1)} %param.15) | copy-start | bytes 1376260
  18.6 9.9 %copy-start.13 = (bf16[16,1792]{1,0:T(8,128)(2,1)S(1)}, bf16[16,1792]{1,0:T(8,128)(2,1)}, u32[]{:S(2)}) copy-start(bf16[16,1792]{1,0:T(8,128)(2,1)} %param.17) | copy-start | bytes 172036
  18.6 11.1 %copy-start.10 = (s32[512]{0:T(512)S(1)}, s32[512]{0:T(512)}, u32[]{:S(2)}) copy-start(s32[512]{0:T(512)} %param.18) | copy-start | bytes 6148
  18.6 12.4 %copy-start.18 = (s32[128]{0:T(128)S(1)}, s32[128]{0:T(128)}, u32[]{:S(2)}) copy-start(s32[128]{0:T(128)} %param.19) | copy-start | bytes 1540
  18.6 12.6 %copy-start.19 = (s32[64]{0:T(128)S(1)}, s32[64]{0:T(128)}, u32[]{:S(2)}) copy-start(s32[64]{0:T(128)} %param.20) | copy-start | bytes 772
  20.9 20.6 %all-to-all-start = ((bf16[32,2,8,640]{3,2,1,0:T(8,128)(2,1)}), bf16[32,2,8,640]{3,2,1,0:T(8,128)(2,1)S(1)}, u32[]{:S(2)}, u32[]{:S(2)}) async-start(bf16[32,2,8,640]{3,2,1,0:T(8,128)(2,1)} %pad_maximum_fusion.4), calls=%async_computation | async-start | bytes 1310720 | tf_op jit(solution)/shard_map/all_to_all | solution.py:274
  28.5 54.6 %all-gather.3.cloned.1.call-start = ((), (), s32[]{:S(2)}) async-start(), calls=%async_computation.1 | async-start | bytes 2162688 | tf_op jit(solution)/shard_map/all_gather | solution.py:298
  38.5 11.0 %copy-start.15 = (f32[273]{0:T(512)}, f32[273]{0:T(512)S(1)}, u32[]{:S(2)}) copy-start(f32[273]{0:T(512)S(1)} %pad.3.clone) | copy-start | bytes 3280
  44.8 0.9 copy-start.6
  45.7 3.9 %copy-start.12 = (f32[2,512,16]{1,2,0:T(8,128)}, f32[2,512,16]{1,2,0:T(8,128)S(1)}, u32[]{:S(2)}) copy-start(f32[2,512,16]{1,2,0:T(8,128)S(1)} %get-tuple-element.76) | copy-start | bytes 196612
  45.8 1.0 copy-start.2
  47.8 1.8 %copy-start.3 = (f32[2,512,16,16]{1,3,2,0:T(8,128)S(1)}, f32[2,512,16,16]{1,3,2,0:T(8,128)}, u32[]{:S(2)}) copy-start(f32[2,512,16,16]{1,3,2,0:T(8,128)} %copy-done.2) | copy-start | bytes 3145732
  53.5 15.2 %collective-permute-start = (bf16[61699]{0:T(1024)(128)(2,1)}, bf16[61699]{0:T(1024)(128)(2,1)}, u32[]{:S(2)}, u32[]{:S(2)}) collective-permute-start(bf16[61699]{0:T(1024)(128)(2,1)} %concatenate.15), channel_id=1, source_target_pairs={{0,8},{8,16},{16,24},{24,32},{32,40},{40,48},{48,56},{56,64},{64,7... | collective-permute-start | bytes 370202 | tf_op jit(solution)/shard_map/ppermute | solution.py:20
  61.7 3.2 %copy-start.7 = (bf16[64,8,128]{2,1,0:T(8,128)(2,1)S(1)}, bf16[64,8,128]{2,1,0:T(8,128)(2,1)}, u32[]{:S(2)}) copy-start(bf16[64,8,128]{2,1,0:T(8,128)(2,1)} %gather_fusion.2) | copy-start | bytes 393220
  61.7 3.2 %copy-start.17 = (s32[128]{0:T(128)S(1)}, s32[128]{0:T(128)}, u32[]{:S(2)}) copy-start(s32[128]{0:T(128)} %and_select_fusion) | copy-start | bytes 1540
  64.9 10.7 %copy-start.4 = (f32[2,512,16,16]{1,3,2,0:T(8,128)S(1)}, f32[2,512,16,16]{1,3,2,0:T(8,128)}, u32[]{:S(2)}) copy-start(f32[2,512,16,16]{1,3,2,0:T(8,128)} %copy-done.2) | copy-start | bytes 3145732
  70.5 7.2 %copy-start.11 = (f32[2,512,16]{1,2,0:T(8,128)S(1)}, f32[2,512,16]{1,2,0:T(8,128)}, u32[]{:S(2)}) copy-start(f32[2,512,16]{1,2,0:T(8,128)} %get-tuple-element.75) | copy-start | bytes 196612
  70.5 7.3 %copy-start.16 = (f32[273]{0:T(512)S(1)}, f32[273]{0:T(512)}, u32[]{:S(2)}) copy-start(f32[273]{0:T(512)} %copy-done.15) | copy-start | bytes 3280
  75.5 2.3 %copy-start.5 = (f32[2,512,16,16]{1,3,2,0:T(8,128)S(1)}, f32[2,512,16,16]{1,3,2,0:T(8,128)}, u32[]{:S(2)}) copy-start(f32[2,512,16,16]{1,3,2,0:T(8,128)} %multiply_multiply_fusion) | copy-start | bytes 3145732
  75.6 3.3 %copy-start.14 = (f32[512]{0:T(512)S(1)}, f32[512]{0:T(512)}, u32[]{:S(2)}) copy-start(f32[512]{0:T(512)} %get-tuple-element.81) | copy-start | bytes 6148
  75.6 3.3 %copy-start.22 = (f32[2,512]{1,0:T(2,128)S(1)}, f32[2,512]{1,0:T(2,128)}, u32[]{:S(2)}) copy-start(f32[2,512]{1,0:T(2,128)} %multiply_reduce_fusion) | copy-start | bytes 12292
  77.7 2.2 %copy-start.8 = (f32[2,512,112]{1,2,0:T(8,128)S(1)}, f32[2,512,112]{1,2,0:T(8,128)}, u32[]{:S(2)}) copy-start(f32[2,512,112]{1,2,0:T(8,128)} %fusion.39) | copy-start | bytes 1376260
  77.7 2.2 %copy-start.9 = (bf16[2,273,112]{2,1,0:T(8,128)(2,1)S(1)}, bf16[2,273,112]{2,1,0:T(8,128)(2,1)}, u32[]{:S(2)}) copy-start(bf16[2,273,112]{2,1,0:T(8,128)(2,1)} %reshape.273) | copy-start | bytes 366916
Sparse Core Ops, SparseCore 0:
  31.9 51.1 all-gather.2

commit v11 on v10

--- a/solution.py
+++ b/solution.py
@@ -275,11 +275,6 @@
         jnp.concatenate([kept_pages, projected_pages, lowered_pages], axis=3),
         "group", split_axis=0, concat_axis=0, tiled=True,
     )
-    arrived = (
-        packed[..., : widths[0]],
-        packed[..., widths[0] : widths[0] + widths[1]],
-        packed[..., widths[0] + widths[1] :],
-    )
     own_holders = lax.dynamic_index_in_dim(holders, own_group, 0, keepdims=False)
     onehot = (own_holders[:, None] == jnp.arange(groups, dtype=jnp.int32)[None, :]).astype(
         jnp.int32
@@ -291,7 +286,10 @@
         gathered_rows = received.reshape((groups * per_peer,) + received.shape[2:])[source_rows]
         return gathered_rows.reshape((rows_here,) + received.shape[3:])
 
-    residual, projected, lowered = [placed(received) for received in arrived]
+    all_rows = placed(packed)
+    residual = all_rows[:, : widths[0]]
+    projected = all_rows[:, widths[0] : widths[0] + widths[1]]
+    lowered = all_rows[:, widths[0] + widths[1] :]
     vocab_pieces = jnp.transpose(
         vocab_rows.reshape(vocab_rows.shape[0], shards, slice_width), (1, 0, 2)
     )
@@ -307,22 +305,18 @@
     phi_key = features(key_rows, FEAT)
     last_seg = segments[-1]
     member = (segments == last_seg).astype(jnp.float32)
-    end_state = jnp.einsum(
-        "hcp,hce->hpe", phi_key * member[None, :, None], value_rows, precision=PRECISE
-    )
-    end_totals = jnp.einsum("hcp,c->hp", phi_key, member, precision=PRECISE)
-    end_tag = jnp.reshape(last_seg + 1, (1,)).astype(jnp.float32)
-    state_size, totals_size = end_state.size, end_totals.size
-    handed = from_behind(
-        jnp.concatenate(
-            [end_state.reshape(-1), end_totals.reshape(-1), end_tag]
-        ).astype(jnp.bfloat16),
-        "group",
-        1,
-    ).astype(jnp.float32)
-    got_state = handed[:state_size].reshape(end_state.shape)
-    got_totals = handed[state_size : state_size + totals_size].reshape(end_totals.shape)
-    got_tag = handed[state_size + totals_size :]
+    value_ones = jnp.concatenate(
+        [value_rows, jnp.ones(value_rows.shape[:-1] + (1,), value_rows.dtype)], axis=-1
+    )
+    end_both = jnp.einsum(
+        "hcp,hce->hpe", phi_key * member[None, :, None], value_ones, precision=PRECISE
+    )
+    end_both = jnp.pad(end_both, ((0, 0), (0, 1), (0, 0)))
+    end_both = end_both.at[0, -1, 0].set((last_seg + 1).astype(jnp.float32))
+    handed = from_behind(end_both.astype(jnp.bfloat16), "group", 1).astype(jnp.float32)
+    got_state = handed[:, :-1, :-1]
+    got_totals = handed[:, :-1, -1]
+    got_tag = handed[0, -1, :1]
     initial = (got_state, got_totals, got_tag[0].astype(jnp.int32) - 1)
     block_len = rows_here
     blocks = rows_here // block_len

time: 165 us -> 165 us (level)
  waiting for transfers between devices: 2.3 us -> 24 us
  local copies, waits for them, and re-layouts: 33.9 us -> 23.2 us
  matrix products: 19 us -> 11.8 us
  other arithmetic: 13 us -> 9.26 us
    all_gather x1, waiting for transfers between devices: 2.28 us -> 23.5 us  [on_device(): lax.all_gather(vocab_pieces[None], 'group', axis=0, tiled=True)]
    gather x3 -> x1, local copies, waits for them, and re-layouts: 4.91 us -> 0.67 us  [placed(): received.reshape((groups * per_peer,) + received.shape[2:])[source_rows]]
    concatenate x1 -> x0, local copies, waits for them, and re-layouts: 2.8 us -> none  [on_device(): jnp.concatenate([end_state.reshape(-1), end_totals.reshape(-1), end_tag])]
    dot_general x1, matrix products: 3.2 us -> 0.76 us  [block_step(): jnp.einsum('hce,hde->hcd', value_rows, value_rows, precision=PRECISE)]
    slice x7 -> x8, local copies, waits for them, and re-layouts: 4.61 us -> 2.2 us  [the longest x1 0.73 us: on_device(): residual = all_rows[:, :widths[0]]]
    unnamed x48 -> x30, local copies, waits for them, and re-layouts: 4.31 us -> 4.41 us
  transfers between devices with their start and end apart: 3 -> 3, of which waited for: 1 -> 2; matrix products, arithmetic and copies ran while one was open for 29% -> 15% of each run, Pallas kernels for 0% -> 0%
where the time goes in v11:
time: 165 us; the launch traced here: 164 us
  Pallas kernels  69.8 us (42%)
  waiting for transfers between devices  24 us (15%)
  local copies, waits for them, and re-layouts  23.2 us (14%)
  between operations  15.8 us (10%)
  matrix products  11.8 us (7%)
  starting transfers between devices  9.94 us (6%)
  other arithmetic  9.26 us (6%)
    pallas_call x1, Pallas kernels, mp_exchange(): pl.pallas_call(exchange_kernel, out_shape=(jax.ShapeDtypeStruct((rows_her...  69.8 us
    all_gather x1, waiting for transfers between devices, on_device(): lax.all_gather(vocab_pieces[None], 'group', axis=0, tiled=True)  23.5 us
    all_to_all x1, starting transfers between devices, on_device(): lax.all_to_all(jnp.concatenate([kept_pages, projected_pages, lowered_page...  7.54 us
    unnamed x30, local copies, waits for them, and re-layouts  4.41 us
    reshape x2, local copies, waits for them, and re-layouts, on_device(): out_weight.reshape(out_weight.shape[0], shards, slice_width)  3.58 us
  transfers between devices with their start and end apart: 3, of which 2 were waited for; matrix products, arithmetic and copies ran while one was open for 15% of the time, Pallas kernels for 0%

profile of v11, /device:TPU:8, one launch (start us, length us, event | category | flops | bytes accessed | tf_op | source)
XLA Modules:
  0.0 163.7 jit_solution(11412910568028139007)
XLA Ops:
  7.2 0.9 reshape.277
  8.1 0.1 copy.82
  8.2 1.0 sort.17
  9.2 0.1 copy.83
  9.3 0.1 reshape.301
  9.4 0.8 gather_fusion.2
  10.2 0.1 reshape.304
  10.4 0.1 copy.85
  10.5 0.1 reshape.287
  10.7 1.9 %gather_fusion = bf16[64,8,1792]{2,1,0:T(8,128)(2,1)} fusion(bf16[64,8,1792]{2,1,0:T(8,128)(2,1)S(1)} %bitcast.57, s32[1024]{0:T(1024)S(1)} %pad_clamp_fusion.1), kind=kCustom, calls=%fused_computation | custom fusion | bytes 3670272 | tf_op jit(solution)/shard_map/gather | solution.py:264
  12.6 2.0 %fusion = f32[32,2,8]{2,1,0:T(2,128)S(1)} fusion(bf16[32,2,8,1792]{3,2,1,0:T(8,128)(2,1)} %bitcast.58), kind=kLoop, calls=%fused_computation.5 | loop fusion | flops 2752000 | bytes 1837056 | tf_op jit(solution)/shard_map/reduce_sum | solution.py:25
  14.6 0.1 copy.87
  14.8 3.1 %fusion.7 = bf16[32,2,8,288]{3,2,1,0:T(8,128)(2,1)S(1)} fusion(bf16[32,2,8,1792]{3,2,1,0:T(8,128)(2,1)} %bitcast.59, f32[1792]{0:T(1024)S(1)} %copy-done.13, f32[32,2,8]{2,1,0:T(2,128)S(1)} %copy.87, bf16[1792,288]{0,1:T(8,128)(2,1)} %param.15), kind=kOutput, calls=%fused_computation.12 | convolution fusion | flops 532299776 | bytes 3171328 | tf_op jit(solution)/shard_map/abrd,dc->abrc/dot_general | solution.py:266
  17.9 0.7 fusion.14
  18.6 1.2 constant_dynamic-slice_fusion.1
  19.8 1.1 pad_maximum_fusion.6
  20.9 7.5 %all-to-all-start = ((bf16[32,2,8,640]{3,2,1,0:T(8,128)(2,1)}), bf16[32,2,8,640]{3,2,1,0:T(8,128)(2,1)S(1)}, u32[]{:S(2)}, u32[]{:S(2)}) async-start(bf16[32,2,8,640]{3,2,1,0:T(8,128)(2,1)} %pad_maximum_fusion.6), calls=%async_computation | async-start | bytes 1310720 | tf_op jit(solution)/shard_map/all_to_all | solution.py:274
  28.5 0.1 reshape.275
  28.7 0.6 copy.81
  29.4 0.1 reduce_window_sum.11
  29.5 0.2 select_reduce_fusion.2
  29.7 0.6 slice.83
  30.3 0.6 compare_convert_fusion.1
  31.0 0.2 select_reduce_fusion
  31.2 0.1 select_reduce_fusion.1
  32.0 2.5 %reshape.283 = bf16[224,8,224]{2,1,0:T(8,128)(2,1)S(1)} reshape(bf16[224,1792]{1,0:T(8,128)(2,1)} %param.16) | data formatting | bytes 1605632 | tf_op jit(solution)/shard_map/reshape | solution.py:363
  34.5 1.1 copy.102
  35.6 1.3 copy.91
  36.9 1.0 copy.92
  37.9 1.3 fusion.34
  39.2 1.2 fusion.31
  40.4 0.7 gather_fusion.1
  41.0 0.2 slice.101
  41.2 0.2 copy.88
  41.5 0.7 slice.112.resid_ref
  42.3 0.1 multiply_multiply_fusion.1
  42.5 0.9 copy-done.2
  43.4 1.3 fusion.17
  44.7 0.7 pad.9
  45.4 1.3 scatter.4
  46.7 2.4 %collective-permute-start = (bf16[2,274,113]{2,1,0:T(8,128)(2,1)}, bf16[2,274,113]{2,1,0:T(8,128)(2,1)S(1)}, u32[]{:S(2)}, u32[]{:S(2)}) collective-permute-start(bf16[2,274,113]{2,1,0:T(8,128)(2,1)} %scatter.4), channel_id=1, source_target_pairs={{0,8},{8,16},{16,24},{24,32},{32,40},{40,48},{48,56},{56,64},{64,7... | collective-permute-start | bytes 371552 | tf_op jit(solution)/shard_map/ppermute | solution.py:20
  49.0 0.1 multiply_multiply_fusion
  49.2 0.5 fusion.43
  49.7 0.7 fusion.58
  50.4 0.9 fusion.37
  51.3 0.4 copy-done.4
  51.6 0.8 multiply_reduce_fusion
  52.4 0.8 compare_select_fusion.low_ref
  53.2 0.4 collective-permute-done
  53.6 0.5 slice.107
  54.8 0.3 slice_reduce_fusion.1
  55.1 0.3 slice_reduce_fusion
  55.4 0.1 slice_reduce_fusion.3
  55.5 0.1 fusion.35
  55.6 0.9 fusion.13
  56.5 0.7 fusion.23
  57.2 0.4 convolution_multiply_fusion.2
  57.6 1.0 fusion.20
  58.6 0.9 fusion.12
  59.5 23.5 %all-gather.3.cloned.1.call-done = bf16[256,16,224]{2,1,0:T(8,128)(2,1)} async-done(((bf16[8,16,224]{2,1,0:T(8,128)(2,1)}), bf16[256,16,224]{2,1,0:T(8,128)(2,1)}) %all-gather.3.cloned.1.call-update) | async-done | bytes 1835024 | tf_op jit(solution)/shard_map/all_gather | solution.py:296
  83.0 0.9 copy.93.att_ref
  83.9 69.8 %shard_map.130 = (bf16[512,224]{1,0:T(8,128)(2,1)}, f32[64,128]{1,0:T(8,128)}) custom-call(bf16[512,224]{1,0:T(8,128)(2,1)} %copy.93.att_ref, bf16[512,128]{1,0:T(8,128)(2,1)} %compare_select_fusion.low_ref, bf16[8,224,224]{2,1,0:T(8,128)(2,1)} %bitcast.69, bf16[8,128,224]{2,1,0:T(8,128)(2,1)} %bitcast.75, bf16[512,224]{1,0:T(8,128)(2,1)} %slice.112.resid_ref, ...), custom_call_target="tpu_custom_call" | custom-call | tf_op jit(solution)/shard_map/pallas_call | solution.py:213
  153.7 1.8 %copy.94 = bf16[512,224]{0,1:T(8,128)(2,1)} copy(bf16[512,224]{1,0:T(8,128)(2,1)} %get-tuple-element.79) | data formatting | bytes 458752
  155.5 1.4 slice_reduce_fusion.2
  (53 shorter events, 0.7 us)
Async XLA Ops:
  7.2 3.5 %copy-start = (bf16[512,1792]{1,0:T(8,128)(2,1)S(1)}, bf16[512,1792]{1,0:T(8,128)(2,1)}, u32[]{:S(2)}) copy-start(bf16[512,1792]{1,0:T(8,128)(2,1)} %param.13) | copy-start | bytes 5505028
  12.6 2.1 %copy-start.13 = (f32[1792]{0:T(1024)S(1)}, f32[1792]{0:T(1024)}, u32[]{:S(2)}) copy-start(f32[1792]{0:T(1024)} %param.14) | copy-start | bytes 21508
  14.7 3.1 %copy-start.1 = (bf16[64,8,1792]{2,1,0:T(8,128)(2,1)S(1)}, bf16[64,8,1792]{2,1,0:T(8,128)(2,1)}, u32[]{:S(2)}) copy-start(bf16[64,8,1792]{2,1,0:T(8,128)(2,1)} %gather_fusion) | copy-start | bytes 5505028
  14.8 3.1 %copy-start.12 = (bf16[1792,128]{1,0:T(8,128)(2,1)S(1)}, bf16[1792,128]{1,0:T(8,128)(2,1)}, u32[]{:S(2)}) copy-start(bf16[1792,128]{1,0:T(8,128)(2,1)} %param.17) | copy-start | bytes 1376260
  18.6 9.9 %copy-start.9 = (bf16[16,1792]{1,0:T(8,128)(2,1)S(1)}, bf16[16,1792]{1,0:T(8,128)(2,1)}, u32[]{:S(2)}) copy-start(bf16[16,1792]{1,0:T(8,128)(2,1)} %param.19) | copy-start | bytes 172036
  18.6 11.1 %copy-start.6 = (s32[512]{0:T(512)S(1)}, s32[512]{0:T(512)}, u32[]{:S(2)}) copy-start(s32[512]{0:T(512)} %param.20) | copy-start | bytes 6148
  18.6 12.4 %copy-start.10 = (s32[128]{0:T(128)S(1)}, s32[128]{0:T(128)}, u32[]{:S(2)}) copy-start(s32[128]{0:T(128)} %param.21) | copy-start | bytes 1540
  18.6 12.6 %copy-start.11 = (s32[64]{0:T(128)S(1)}, s32[64]{0:T(128)}, u32[]{:S(2)}) copy-start(s32[64]{0:T(128)} %param.22) | copy-start | bytes 772
  20.9 19.4 %all-to-all-start = ((bf16[32,2,8,640]{3,2,1,0:T(8,128)(2,1)}), bf16[32,2,8,640]{3,2,1,0:T(8,128)(2,1)S(1)}, u32[]{:S(2)}, u32[]{:S(2)}) async-start(bf16[32,2,8,640]{3,2,1,0:T(8,128)(2,1)} %pad_maximum_fusion.6), calls=%async_computation | async-start | bytes 1310720 | tf_op jit(solution)/shard_map/all_to_all | solution.py:274
  28.5 54.6 %all-gather.3.cloned.1.call-start = ((), (), s32[]{:S(2)}) async-start(), calls=%async_computation.1 | async-start | bytes 2162688 | tf_op jit(solution)/shard_map/all_gather | solution.py:296
  42.4 1.0 copy-start.2
  42.4 2.9 %copy-start.7 = (f32[2,512,16]{1,2,0:T(8,128)}, f32[2,512,16]{1,2,0:T(8,128)S(1)}, u32[]{:S(2)}) copy-start(f32[2,512,16]{1,2,0:T(8,128)S(1)} %get-tuple-element.82) | copy-start | bytes 196612
  46.7 3.0 %copy-start.5 = (f32[512,512]{0,1:T(8,128)S(1)}, f32[512,512]{0,1:T(8,128)}, u32[]{:S(2)}) copy-start(f32[512,512]{0,1:T(8,128)} %fusion.31) | copy-start | bytes 3145732
  46.7 6.9 %collective-permute-start = (bf16[2,274,113]{2,1,0:T(8,128)(2,1)}, bf16[2,274,113]{2,1,0:T(8,128)(2,1)S(1)}, u32[]{:S(2)}, u32[]{:S(2)}) collective-permute-start(bf16[2,274,113]{2,1,0:T(8,128)(2,1)} %scatter.4), channel_id=1, source_target_pairs={{0,8},{8,16},{16,24},{24,32},{32,40},{40,48},{48,56},{56,64},{64,7... | collective-permute-start | bytes 371552 | tf_op jit(solution)/shard_map/ppermute | solution.py:20
  50.4 1.2 copy-start.4
  51.6 4.0 %copy-start.3 = (f32[2,512,16,16]{1,3,2,0:T(8,128)S(1)}, f32[2,512,16,16]{1,3,2,0:T(8,128)}, u32[]{:S(2)}) copy-start(f32[2,512,16,16]{1,3,2,0:T(8,128)} %copy-done.2) | copy-start | bytes 3145732
  51.6 4.0 %copy-start.8 = (f32[2,512,16]{1,2,0:T(8,128)S(1)}, f32[2,512,16]{1,2,0:T(8,128)}, u32[]{:S(2)}) copy-start(f32[2,512,16]{1,2,0:T(8,128)} %copy-done.7) | copy-start | bytes 196612
Sparse Core Ops, SparseCore 0:
  31.9 51.1 all-gather.2

commit v12 on v11

--- a/solution.py
+++ b/solution.py
@@ -86,8 +86,8 @@
 
 
 def exchange_kernel(
-    att_ref, low_ref, w_ref, u_ref, resid_ref, vocab_ref, upd_ref, best_ref,
-    land, acc, rows, tops, got, parts, ring_sems, top_sems,
+    att_ref, low_ref, w_ref, u_ref, resid_ref, vocab_in, upd_ref, best_ref,
+    land, acc, rows, tops, got, parts, vocab_ref, ring_sems, top_sems, vocab_sems,
 ):
     n = w_ref.shape[0]
     quarter = att_ref.shape[0] // 8
@@ -105,10 +105,29 @@
         value = value + jnp.dot(low_ref[...], u_ref[c], preferred_element_type=jnp.float32)
         parts[c] = value.astype(parts.dtype)
 
+    groups = vocab_ref.shape[0]
+    holders = [lax.rem(grp + k, groups) for k in range(1, groups)]
     barrier = pltpu.get_barrier_semaphore()
     for p in peers:
         pl.semaphore_signal(barrier, inc=1, device_id=(grp, p), device_id_type=mesh_id)
-    pl.semaphore_wait(barrier, n - 1)
+    for h in holders:
+        pl.semaphore_signal(barrier, inc=1, device_id=(h, me), device_id_type=mesh_id)
+    pl.semaphore_wait(barrier, n - 1 + groups - 1)
+
+    own_vocab = pltpu.make_async_copy(vocab_in, vocab_ref.at[grp], vocab_sems.at[2, 0])
+    own_vocab.start()
+    vocab_sent = []
+    for h in holders:
+        copy = pltpu.make_async_remote_copy(
+            src_ref=vocab_in,
+            dst_ref=vocab_ref.at[grp],
+            send_sem=vocab_sems.at[0, h],
+            recv_sem=vocab_sems.at[1, grp],
+            device_id=(h, me),
+            device_id_type=mesh_id,
+        )
+        copy.start()
+        vocab_sent.append(copy)
 
     def ring_copy(phase, chain, step, src, dst):
         return pltpu.make_async_remote_copy(
@@ -163,6 +182,19 @@
             pending[chain].start()
     for chain in range(len(chains)):
         pending[chain].wait()
+
+    own_vocab.wait()
+    for copy in vocab_sent:
+        copy.wait_send()
+    for h in holders:
+        pltpu.make_async_remote_copy(
+            src_ref=vocab_in,
+            dst_ref=vocab_ref.at[h],
+            send_sem=vocab_sems.at[0, h],
+            recv_sem=vocab_sems.at[1, h],
+            device_id=(h, me),
+            device_id_type=mesh_id,
+        ).wait_recv()
 
     scores = jnp.zeros((rows.shape[1], vocab_ref.shape[0] * vocab_ref.shape[2]), jnp.float32)
     for j in range(n):
@@ -204,7 +236,7 @@
     best_ref[...] = best
 
 
-def mp_exchange(attended, low_rank, out_blocks, up_blocks, residual, vocab_blocks):
+def mp_exchange(attended, low_rank, out_blocks, up_blocks, residual, vocab_blocks, groups):
     n, _, width = out_blocks.shape
     rows_here = attended.shape[0]
     block_rows = rows_here // n
@@ -225,8 +257,10 @@
             pltpu.VMEM((n, block_rows, 128), jnp.float32),
             pltpu.VMEM((n, block_rows, 128), jnp.float32),
             pltpu.VMEM((n, rows_here, width), jnp.bfloat16),
+            pltpu.VMEM((groups,) + vocab_blocks.shape, jnp.bfloat16),
             pltpu.SemaphoreType.DMA((2, chains, 2, n - 1)),
             pltpu.SemaphoreType.DMA((2, n)),
+            pltpu.SemaphoreType.DMA((3, groups)),
         ],
         compiler_params=pltpu.CompilerParams(collective_id=0, has_side_effects=True),
     )(attended, low_rank, out_blocks, up_blocks, residual, vocab_blocks)
@@ -290,10 +324,9 @@
     residual = all_rows[:, : widths[0]]
     projected = all_rows[:, widths[0] : widths[0] + widths[1]]
     lowered = all_rows[:, widths[0] + widths[1] :]
-    vocab_pieces = jnp.transpose(
+    vocab_blocks = jnp.transpose(
         vocab_rows.reshape(vocab_rows.shape[0], shards, slice_width), (1, 0, 2)
     )
-    group_vocab = lax.all_gather(vocab_pieces[None], "group", axis=0, tiled=True)
     heads_here = projected.shape[1] // (2 * FEAT + HD)
     split_heads = jnp.transpose(
         projected.reshape(rows_here, heads_here, 2 * FEAT + HD).astype(jnp.float32), (1, 0, 2)
@@ -344,7 +377,6 @@
         .reshape(rows_here, heads_here * HD)
         .astype(jnp.bfloat16)
     )
-    group_vocab, attended = lax.optimization_barrier((group_vocab, attended))
     state_norms = jnp.transpose(state_norm, (1, 0, 2)).reshape(heads_here, rows_here)
     request_ids = jnp.arange(request_adapter.shape[0], dtype=jnp.int32)
     adapter_of = jnp.sum(
@@ -365,7 +397,9 @@
     up_blocks = jnp.transpose(
         adapter_up.reshape(adapter_up.shape[0], shards, slice_width), (1, 0, 2)
     )
-    summed, best = mp_exchange(attended, low_rank, out_blocks, up_blocks, residual, group_vocab)
+    summed, best = mp_exchange(
+        attended, low_rank, out_blocks, up_blocks, residual, vocab_blocks, groups
+    )
     max_logits = best[:, 0]
     return (summed, state_norms, max_logits)
 

time: 165 us -> 134 us (0.81)
  waiting for transfers between devices: 24 us -> 0.01 us
  between operations: 15.8 us -> 2.42 us
  Pallas kernels: 69.8 us -> 74.5 us
  matrix products: 11.8 us -> 14.4 us
    all_gather x1 -> x0, waiting for transfers between devices: 23.5 us -> none  [on_device(): lax.all_gather(vocab_pieces[None], 'group', axis=0, tiled=True)]
    pallas_call x1, Pallas kernels: 69.8 us -> 74.5 us  [mp_exchange(): pl.pallas_call(exchange_kernel, out_shape=(jax.ShapeDtypeStruct((rows_her...]
    unnamed x30 -> x34, local copies, waits for them, and re-layouts: 4.41 us -> 4.78 us
  transfers between devices with their start and end apart: 3 -> 2, of which waited for: 2 -> 0; matrix products, arithmetic and copies ran while one was open for 15% -> 13% of each run, Pallas kernels for 0% -> 0%
where the time goes in v12:
time: 134 us; the launch traced here: 133 us
  Pallas kernels  74.5 us (56%)
  local copies, waits for them, and re-layouts  21.7 us (16%)
  matrix products  14.4 us (11%)
  other arithmetic  10.3 us (8%)
  starting transfers between devices  9.78 us (7%)
  between operations  2.42 us (2%)
    pallas_call x1, Pallas kernels, mp_exchange(): pl.pallas_call(exchange_kernel, out_shape=(jax.ShapeDtypeStruct((rows_her...  74.5 us
    all_to_all x1, starting transfers between devices, on_device(): lax.all_to_all(jnp.concatenate([kept_pages, projected_pages, lowered_page...  7.54 us
    unnamed x34, local copies, waits for them, and re-layouts  4.78 us
    reshape x2, local copies, waits for them, and re-layouts, on_device(): out_weight.reshape(out_weight.shape[0], shards, slice_width)  3.58 us
    dot_general x1, matrix products, on_device(): jnp.einsum('abrd,dc->abrc', normed_pages, qkv_weight, preferred_element_t...  3.08 us
  transfers between devices with their start and end apart: 2, of which 0 were waited for; matrix products, arithmetic and copies ran while one was open for 13% of the time, Pallas kernels for 0%

profile of v12, /device:TPU:8, one launch (start us, length us, event | category | flops | bytes accessed | tf_op | source)
XLA Modules:
  0.0 133.1 jit_solution(17334869897097925531)
XLA Ops:
  0.7 0.9 reshape.276
  1.6 0.1 copy.57
  1.7 1.0 sort.17
  2.7 0.1 copy.58
  2.8 0.1 reshape.301
  2.9 0.8 gather_fusion.2
  3.7 0.1 reshape.304
  3.8 0.1 copy.59
  3.9 0.1 copy.60
  4.0 0.1 reshape.287
  4.1 1.9 %gather_fusion = bf16[64,8,1792]{2,1,0:T(8,128)(2,1)} fusion(bf16[64,8,1792]{2,1,0:T(8,128)(2,1)S(1)} %bitcast.58, s32[1024]{0:T(1024)S(1)} %pad_clamp_fusion.1), kind=kCustom, calls=%fused_computation | custom fusion | bytes 3670272 | tf_op jit(solution)/shard_map/gather | solution.py:298
  6.1 2.0 %fusion = f32[32,2,8]{2,1,0:T(2,128)S(1)} fusion(bf16[32,2,8,1792]{3,2,1,0:T(8,128)(2,1)} %bitcast.59), kind=kLoop, calls=%fused_computation.5 | loop fusion | flops 2752000 | bytes 1837056 | tf_op jit(solution)/shard_map/reduce_sum | solution.py:25
  8.0 0.1 copy.61
  8.1 0.1 copy.62
  8.2 3.1 %fusion.7 = bf16[32,2,8,288]{3,2,1,0:T(8,128)(2,1)S(1)} fusion(bf16[32,2,8,1792]{3,2,1,0:T(8,128)(2,1)} %bitcast.60, f32[1792]{0:T(1024)S(1)} %copy-done.15, f32[32,2,8]{2,1,0:T(2,128)S(1)} %copy.62, bf16[1792,288]{0,1:T(8,128)(2,1)} %param.15), kind=kOutput, calls=%fused_computation.12 | convolution fusion | flops 532299776 | bytes 3171328 | tf_op jit(solution)/shard_map/abrd,dc->abrc/dot_general | solution.py:300
  11.3 0.7 fusion.14
  12.1 1.1 constant_dynamic-slice_fusion.1
  13.2 1.1 pad_maximum_fusion.6
  14.4 7.5 %all-to-all-start = ((bf16[32,2,8,640]{3,2,1,0:T(8,128)(2,1)}), bf16[32,2,8,640]{3,2,1,0:T(8,128)(2,1)S(1)}, u32[]{:S(2)}, u32[]{:S(2)}) async-start(bf16[32,2,8,640]{3,2,1,0:T(8,128)(2,1)} %pad_maximum_fusion.6), calls=%async_computation | async-start | bytes 1310720 | tf_op jit(solution)/shard_map/all_to_all | solution.py:308
  21.9 0.1 fusion.42
  22.0 0.1 reduce_window_sum.11
  22.1 0.2 select_reduce_fusion.2
  22.3 0.6 slice.83
  22.9 1.2 compare_convert_fusion.1
  24.1 0.2 select_reduce_fusion
  24.4 0.1 select_reduce_fusion.1
  24.5 0.5 and_select_fusion
  25.6 2.5 %reshape.282 = bf16[224,8,224]{2,1,0:T(8,128)(2,1)S(1)} reshape(bf16[224,1792]{1,0:T(8,128)(2,1)} %param.16) | data formatting | bytes 1605632 | tf_op jit(solution)/shard_map/reshape | solution.py:395
  28.1 1.1 copy.79
  29.3 1.3 copy.66
  30.5 1.0 copy.67
  31.6 0.1 reshape.284
  31.7 0.6 copy.80
  32.3 1.3 fusion.34
  33.6 1.2 fusion.31
  34.8 0.7 gather_fusion.1
  35.4 0.2 slice.101
  35.7 0.2 copy.63
  36.0 1.8 %fusion.43 = f32[2,512,512]{1,2,0:T(8,128)} fusion(bf16[2,512,144]{1,2,0:T(8,128)(2,1)S(1)} %bitcast.66), kind=kOutput, calls=%fused_computation.69 | convolution fusion | flops 16777216 | bytes 2129920 | tf_op jit(solution)/shard_map/while/body/eval_jaxpr/hcf,hdf->hcd/dot_general | solution.py:59
  37.8 0.7 slice.112.resid_ref
  38.5 0.1 multiply_multiply_fusion.1
  38.7 0.9 copy-done.3
  39.7 1.3 fusion.17
  41.1 2.2 %collective-permute-start = (bf16[2,274,113]{2,1,0:T(8,128)(2,1)S(1)}, bf16[2,274,113]{2,1,0:T(8,128)(2,1)S(1)}, u32[]{:S(2)}, u32[]{:S(2)}) collective-permute-start(bf16[2,274,113]{2,1,0:T(8,128)(2,1)S(1)} %scatter.4), channel_id=1, source_target_pairs={{0,8},{8,16},{16,24},{24,32},{32,40},{40,48},{48,56},{56,64},{64,7... | collective-permute-start | bytes 371552 | tf_op jit(solution)/shard_map/ppermute | solution.py:20
  43.3 0.1 multiply_multiply_fusion
  43.5 2.0 %fusion.58 = (f32[2,512]{1,0:T(2,128)S(1)}, f32[2,512,512]{1,2,0:T(8,128)S(1)}) fusion(f32[512,512]{0,1:T(8,128)} %fusion.31, bf16[2,512,144]{1,2,0:T(8,128)(2,1)S(1)} %bitcast.67), kind=kOutput, calls=%fused_computation.111 | convolution fusion | flops 20446208 | bytes 3215360 | tf_op jit(solution)/shard_map/while/body/eval_jaxpr/hcf,hdf->hcd/dot_general | solution.py:49
  45.5 0.8 fusion.37
  46.4 0.7 copy-done.2
  47.1 0.8 multiply_reduce_fusion
  47.9 0.8 compare_select_fusion.low_ref
  48.7 0.3 slice_reduce_fusion
  49.0 0.1 fusion.35
  49.1 0.9 fusion.13
  50.0 0.4 convolution_multiply_fusion.2
  50.4 0.1 slice_reduce_fusion.3
  50.6 0.5 slice.107
  51.7 0.3 slice_reduce_fusion.1
  52.0 0.7 fusion.23
  52.7 0.9 fusion.12
  53.6 0.8 copy.69.att_ref
  54.4 74.5 %shard_map.130 = (bf16[512,224]{1,0:T(8,128)(2,1)}, f32[64,128]{1,0:T(8,128)}) custom-call(bf16[512,224]{1,0:T(8,128)(2,1)} %copy.69.att_ref, bf16[512,128]{1,0:T(8,128)(2,1)} %compare_select_fusion.low_ref, bf16[8,224,224]{2,1,0:T(8,128)(2,1)} %bitcast.70, bf16[8,128,224]{2,1,0:T(8,128)(2,1)} %bitcast.75, bf16[512,224]{1,0:T(8,128)(2,1)} %slice.112.resid_ref, ...), custom_call_target="tpu_custom_call" | custom-call | tf_op jit(solution)/shard_map/pallas_call | solution.py:245
  128.9 1.8 %copy.70 = bf16[512,224]{0,1:T(8,128)(2,1)} copy(bf16[512,224]{1,0:T(8,128)(2,1)} %get-tuple-element.69) | data formatting | bytes 458752
  130.7 1.4 %slice_reduce_fusion.2 = f32[64]{0:T(128)} fusion(f32[64,128]{1,0:T(8,128)} %get-tuple-element.56), kind=kLoop, calls=%fused_computation.63 | loop fusion | bytes 512 | tf_op jit(solution)/shard_map/slice | solution.py:403
  132.1 1.0 fusion.20
  (54 shorter events, 0.4 us)
Async XLA Ops:
  0.6 3.5 %copy-start = (bf16[512,1792]{1,0:T(8,128)(2,1)S(1)}, bf16[512,1792]{1,0:T(8,128)(2,1)}, u32[]{:S(2)}) copy-start(bf16[512,1792]{1,0:T(8,128)(2,1)} %param.13) | copy-start | bytes 5505028
  6.1 2.1 %copy-start.15 = (f32[1792]{0:T(1024)S(1)}, f32[1792]{0:T(1024)}, u32[]{:S(2)}) copy-start(f32[1792]{0:T(1024)} %param.14) | copy-start | bytes 21508
  8.2 3.1 %copy-start.1 = (bf16[64,8,1792]{2,1,0:T(8,128)(2,1)S(1)}, bf16[64,8,1792]{2,1,0:T(8,128)(2,1)}, u32[]{:S(2)}) copy-start(bf16[64,8,1792]{2,1,0:T(8,128)(2,1)} %gather_fusion) | copy-start | bytes 5505028
  8.2 3.1 %copy-start.14 = (bf16[1792,128]{1,0:T(8,128)(2,1)S(1)}, bf16[1792,128]{1,0:T(8,128)(2,1)}, u32[]{:S(2)}) copy-start(bf16[1792,128]{1,0:T(8,128)(2,1)} %param.17) | copy-start | bytes 1376260
  12.0 10.3 %copy-start.8 = (s32[512]{0:T(512)S(1)}, s32[512]{0:T(512)}, u32[]{:S(2)}) copy-start(s32[512]{0:T(512)} %param.20) | copy-start | bytes 6148
  12.1 12.1 %copy-start.12 = (s32[128]{0:T(128)S(1)}, s32[128]{0:T(128)}, u32[]{:S(2)}) copy-start(s32[128]{0:T(128)} %param.21) | copy-start | bytes 1540
  12.1 12.3 %copy-start.13 = (s32[64]{0:T(128)S(1)}, s32[64]{0:T(128)}, u32[]{:S(2)}) copy-start(s32[64]{0:T(128)} %param.22) | copy-start | bytes 772
  14.4 20.4 %all-to-all-start = ((bf16[32,2,8,640]{3,2,1,0:T(8,128)(2,1)}), bf16[32,2,8,640]{3,2,1,0:T(8,128)(2,1)S(1)}, u32[]{:S(2)}, u32[]{:S(2)}) async-start(bf16[32,2,8,640]{3,2,1,0:T(8,128)(2,1)} %pad_maximum_fusion.6), calls=%async_computation | async-start | bytes 1310720 | tf_op jit(solution)/shard_map/all_to_all | solution.py:308
  28.1 3.4 %copy-start.9 = (bf16[16,1792]{1,0:T(8,128)(2,1)S(1)}, bf16[16,1792]{1,0:T(8,128)(2,1)}, u32[]{:S(2)}) copy-start(bf16[16,1792]{1,0:T(8,128)(2,1)} %param.19) | copy-start | bytes 172036
  35.9 2.8 %copy-start.6 = (f32[2,512,144]{1,2,0:T(8,128)}, f32[2,512,144]{1,2,0:T(8,128)S(1)}, u32[]{:S(2)}) copy-start(f32[2,512,144]{1,2,0:T(8,128)S(1)} %transpose.52) | copy-start | bytes 1769476
  36.0 3.7 %copy-start.10 = (f32[512]{0:T(512)S(1)}, f32[512]{0:T(512)}, u32[]{:S(2)}) copy-start(f32[512]{0:T(512)} %compare_convert_fusion.1) | copy-start | bytes 6148
  38.7 1.0 copy-start.3
  41.1 7.6 %collective-permute-start = (bf16[2,274,113]{2,1,0:T(8,128)(2,1)S(1)}, bf16[2,274,113]{2,1,0:T(8,128)(2,1)S(1)}, u32[]{:S(2)}, u32[]{:S(2)}) collective-permute-start(bf16[2,274,113]{2,1,0:T(8,128)(2,1)S(1)} %scatter.4), channel_id=1, source_target_pairs={{0,8},{8,16},{16,24},{24,32},{32,40},{40,48},{48,56},{56,64},{64,7... | collective-permute-start | bytes 371552 | tf_op jit(solution)/shard_map/ppermute | solution.py:20
  43.5 2.9 %copy-start.5 = (f32[512,512]{0,1:T(8,128)S(1)}, f32[512,512]{0,1:T(8,128)}, u32[]{:S(2)}) copy-start(f32[512,512]{0,1:T(8,128)} %get-tuple-element.79) | copy-start | bytes 3145732
  45.5 1.6 %copy-start.2 = (f32[2,512,512]{1,2,0:T(8,128)S(1)}, f32[2,512,512]{1,2,0:T(8,128)}, u32[]{:S(2)}) copy-start(f32[2,512,512]{1,2,0:T(8,128)} %fusion.43) | copy-start | bytes 6291460
  47.1 0.8 copy-start.11
  47.1 2.0 %copy-start.4 = (f32[2,512,16,16]{1,3,2,0:T(8,128)S(1)}, f32[2,512,16,16]{1,3,2,0:T(8,128)}, u32[]{:S(2)}) copy-start(f32[2,512,16,16]{1,3,2,0:T(8,128)} %copy-done.3) | copy-start | bytes 3145732
  47.1 2.0 %copy-start.7 = (f32[2,512,144]{1,2,0:T(8,128)S(1)}, f32[2,512,144]{1,2,0:T(8,128)}, u32[]{:S(2)}) copy-start(f32[2,512,144]{1,2,0:T(8,128)} %copy-done.6) | copy-start | bytes 1769476

commit v13 on v12

--- a/solution.py
+++ b/solution.py
@@ -91,7 +91,7 @@
 ):
     n = w_ref.shape[0]
     quarter = att_ref.shape[0] // 8
-    block_rows = best_ref.shape[0]
+    block_rows = best_ref.shape[1]
     me = lax.axis_index("mp")
     grp = lax.axis_index("group")
     peers = [lax.rem(me + k, n) for k in range(1, n)]
@@ -196,16 +196,16 @@
             device_id_type=mesh_id,
         ).wait_recv()
 
-    scores = jnp.zeros((rows.shape[1], vocab_ref.shape[0] * vocab_ref.shape[2]), jnp.float32)
+    scores = jnp.zeros((vocab_ref.shape[0] * vocab_ref.shape[2], rows.shape[1]), jnp.float32)
     for j in range(n):
-        block = vocab_ref[:, j].reshape(scores.shape[1], rows.shape[2])
+        block = vocab_ref[:, j].reshape(scores.shape[0], rows.shape[2])
         scores = scores + lax.dot_general(
-            rows[j], block, (((1,), (1,)), ((), ())),
+            block, rows[j], (((1,), (1,)), ((), ())),
             preferred_element_type=jnp.float32,
         )
+    column_best = jnp.max(scores, axis=0, keepdims=True)
     for p in range(n):
-        piece = jnp.max(scores[p * block_rows : (p + 1) * block_rows], axis=1, keepdims=True)
-        tops[p] = jnp.broadcast_to(piece, tops.shape[1:])
+        tops[p] = column_best[:, p * block_rows : (p + 1) * block_rows]
 
     sent = []
     for p in peers:
@@ -246,7 +246,7 @@
         exchange_kernel,
         out_shape=(
             jax.ShapeDtypeStruct((rows_here, width), jnp.bfloat16),
-            jax.ShapeDtypeStruct((block_rows, 128), jnp.float32),
+            jax.ShapeDtypeStruct((1, block_rows), jnp.float32),
         ),
         in_specs=[vmem] * 6,
         out_specs=(vmem, vmem),
@@ -254,8 +254,8 @@
             pltpu.VMEM((chains, n - 1, rows_here // chains, width), jnp.bfloat16),
             pltpu.VMEM((chains, n - 1, rows_here // chains, width), jnp.bfloat16),
             pltpu.VMEM((n, rows_here, width), jnp.bfloat16),
-            pltpu.VMEM((n, block_rows, 128), jnp.float32),
-            pltpu.VMEM((n, block_rows, 128), jnp.float32),
+            pltpu.VMEM((n, 1, block_rows), jnp.float32),
+            pltpu.VMEM((n, 1, block_rows), jnp.float32),
             pltpu.VMEM((n, rows_here, width), jnp.bfloat16),
             pltpu.VMEM((groups,) + vocab_blocks.shape, jnp.bfloat16),
             pltpu.SemaphoreType.DMA((2, chains, 2, n - 1)),
@@ -400,7 +400,7 @@
     summed, best = mp_exchange(
         attended, low_rank, out_blocks, up_blocks, residual, vocab_blocks, groups
     )
-    max_logits = best[:, 0]
+    max_logits = best[0]
     return (summed, state_norms, max_logits)
 
 

time: 134 us -> 130 us (0.970)
  Pallas kernels: 74.5 us -> 71.1 us
    pallas_call x1, Pallas kernels: 74.5 us -> 71.1 us  [mp_exchange(): pl.pallas_call(exchange_kernel, out_shape=(jax.ShapeDtypeStruct((rows_her...]
    slice x1 -> x0, local copies, waits for them, and re-layouts: 1.38 us -> none  [on_device(): max_logits = best[:, 0]]
    unnamed x34 -> x35, local copies, waits for them, and re-layouts: 4.78 us -> 5.97 us
where the time goes in v13:
time: 130 us; the launch traced here: 129 us
  Pallas kernels  71.1 us (55%)
  local copies, waits for them, and re-layouts  21.5 us (17%)
  matrix products  14.4 us (11%)
  other arithmetic  10.3 us (8%)
  starting transfers between devices  9.77 us (8%)
  between operations  2.42 us (2%)
    pallas_call x1, Pallas kernels, mp_exchange(): pl.pallas_call(exchange_kernel, out_shape=(jax.ShapeDtypeStruct((rows_her...  71.1 us
    all_to_all x1, starting transfers between devices, on_device(): lax.all_to_all(jnp.concatenate([kept_pages, projected_pages, lowered_page...  7.54 us
    unnamed x35, local copies, waits for them, and re-layouts  5.97 us
    reshape x2, local copies, waits for them, and re-layouts, on_device(): out_weight.reshape(out_weight.shape[0], shards, slice_width)  3.58 us
    dot_general x1, matrix products, on_device(): jnp.einsum('abrd,dc->abrc', normed_pages, qkv_weight, preferred_element_t...  3.07 us
  transfers between devices with their start and end apart: 2, of which 0 were waited for; matrix products, arithmetic and copies ran while one was open for 13% of the time, Pallas kernels for 0%

profile of v13, /device:TPU:8, one launch (start us, length us, event | category | flops | bytes accessed | tf_op | source)
XLA Modules:
  0.0 129.5 jit_solution(4759887480264099570)
XLA Ops:
  0.7 0.9 reshape.276
  1.6 0.1 copy.57
  1.7 1.0 sort.17
  2.7 0.1 copy.58
  2.8 0.1 reshape.301
  2.9 0.8 gather_fusion.2
  3.7 0.1 reshape.304
  3.8 0.1 copy.59
  3.9 0.1 copy.60
  4.0 0.1 reshape.287
  4.1 1.9 %gather_fusion = bf16[64,8,1792]{2,1,0:T(8,128)(2,1)} fusion(bf16[64,8,1792]{2,1,0:T(8,128)(2,1)S(1)} %bitcast.59, s32[1024]{0:T(1024)S(1)} %pad_clamp_fusion.1), kind=kCustom, calls=%fused_computation | custom fusion | bytes 3670272 | tf_op jit(solution)/shard_map/gather | solution.py:298
  6.1 2.0 %fusion = f32[32,2,8]{2,1,0:T(2,128)S(1)} fusion(bf16[32,2,8,1792]{3,2,1,0:T(8,128)(2,1)} %bitcast.60), kind=kLoop, calls=%fused_computation.5 | loop fusion | flops 2752000 | bytes 1837056 | tf_op jit(solution)/shard_map/reduce_sum | solution.py:25
  8.0 0.1 copy.61
  8.1 0.1 copy.62
  8.2 3.1 %fusion.7 = bf16[32,2,8,288]{3,2,1,0:T(8,128)(2,1)S(1)} fusion(bf16[32,2,8,1792]{3,2,1,0:T(8,128)(2,1)} %bitcast.61, f32[1792]{0:T(1024)S(1)} %copy-done.15, f32[32,2,8]{2,1,0:T(2,128)S(1)} %copy.62, bf16[1792,288]{0,1:T(8,128)(2,1)} %param.15), kind=kOutput, calls=%fused_computation.12 | convolution fusion | flops 532299776 | bytes 3171328 | tf_op jit(solution)/shard_map/abrd,dc->abrc/dot_general | solution.py:300
  11.3 0.7 fusion.14
  12.1 1.1 constant_dynamic-slice_fusion.1
  13.2 1.1 pad_maximum_fusion.6
  14.4 7.5 %all-to-all-start = ((bf16[32,2,8,640]{3,2,1,0:T(8,128)(2,1)}), bf16[32,2,8,640]{3,2,1,0:T(8,128)(2,1)S(1)}, u32[]{:S(2)}, u32[]{:S(2)}) async-start(bf16[32,2,8,640]{3,2,1,0:T(8,128)(2,1)} %pad_maximum_fusion.6), calls=%async_computation | async-start | bytes 1310720 | tf_op jit(solution)/shard_map/all_to_all | solution.py:308
  21.9 0.1 fusion.42
  22.0 0.1 reduce_window_sum.11
  22.1 0.2 select_reduce_fusion.2
  22.3 0.6 slice.80
  22.9 1.2 compare_convert_fusion.1
  24.1 0.2 select_reduce_fusion
  24.4 0.1 select_reduce_fusion.1
  24.5 0.5 and_select_fusion
  25.6 2.5 %reshape.282 = bf16[224,8,224]{2,1,0:T(8,128)(2,1)S(1)} reshape(bf16[224,1792]{1,0:T(8,128)(2,1)} %param.16) | data formatting | bytes 1605632 | tf_op jit(solution)/shard_map/reshape | solution.py:395
  28.1 1.1 copy.79
  29.3 1.3 copy.66
  30.5 1.0 copy.67
  31.6 0.1 reshape.284
  31.7 0.6 copy.80
  32.3 1.3 fusion.34
  33.6 1.2 fusion.31
  34.8 0.7 gather_fusion.1
  35.4 0.2 slice.97
  35.7 0.2 copy.63
  36.0 1.8 %fusion.43 = f32[2,512,512]{1,2,0:T(8,128)} fusion(bf16[2,512,144]{1,2,0:T(8,128)(2,1)S(1)} %bitcast.67), kind=kOutput, calls=%fused_computation.68 | convolution fusion | flops 16777216 | bytes 2129920 | tf_op jit(solution)/shard_map/while/body/eval_jaxpr/hcf,hdf->hcd/dot_general | solution.py:59
  37.8 0.7 slice.108.resid_ref
  38.5 0.1 multiply_multiply_fusion.1
  38.7 0.9 copy-done.3
  39.7 1.3 fusion.17
  41.1 2.2 %collective-permute-start = (bf16[2,274,113]{2,1,0:T(8,128)(2,1)S(1)}, bf16[2,274,113]{2,1,0:T(8,128)(2,1)S(1)}, u32[]{:S(2)}, u32[]{:S(2)}) collective-permute-start(bf16[2,274,113]{2,1,0:T(8,128)(2,1)S(1)} %scatter.4), channel_id=1, source_target_pairs={{0,8},{8,16},{16,24},{24,32},{32,40},{40,48},{48,56},{56,64},{64,7... | collective-permute-start | bytes 371552 | tf_op jit(solution)/shard_map/ppermute | solution.py:20
  43.3 0.1 multiply_multiply_fusion
  43.5 2.0 %fusion.58 = (f32[2,512]{1,0:T(2,128)S(1)}, f32[2,512,512]{1,2,0:T(8,128)S(1)}) fusion(f32[512,512]{0,1:T(8,128)} %fusion.31, bf16[2,512,144]{1,2,0:T(8,128)(2,1)S(1)} %bitcast.68), kind=kOutput, calls=%fused_computation.110 | convolution fusion | flops 20446208 | bytes 3215360 | tf_op jit(solution)/shard_map/while/body/eval_jaxpr/hcf,hdf->hcd/dot_general | solution.py:49
  45.5 0.9 fusion.37
  46.4 0.7 copy-done.2
  47.1 0.8 multiply_reduce_fusion
  47.9 0.8 compare_select_fusion.low_ref
  48.7 0.3 slice_reduce_fusion
  49.0 0.1 fusion.35
  49.1 0.9 fusion.13
  50.0 0.4 convolution_multiply_fusion.2
  50.4 0.1 slice_reduce_fusion.2
  50.5 0.5 slice.103
  51.7 0.3 slice_reduce_fusion.1
  52.0 0.7 fusion.23
  52.7 0.9 fusion.12
  53.6 0.8 copy.69.att_ref
  54.4 71.1 %shard_map.130 = (bf16[512,224]{1,0:T(8,128)(2,1)}, f32[1,64]{1,0:T(1,128)}) custom-call(bf16[512,224]{1,0:T(8,128)(2,1)} %copy.69.att_ref, bf16[512,128]{1,0:T(8,128)(2,1)} %compare_select_fusion.low_ref, bf16[8,224,224]{2,1,0:T(8,128)(2,1)} %bitcast.71, bf16[8,128,224]{2,1,0:T(8,128)(2,1)} %bitcast.76, bf16[512,224]{1,0:T(8,128)(2,1)} %slice.108.resid_ref, ...), custom_call_target="tpu_custom_call" | custom-call | tf_op jit(solution)/shard_map/pallas_call | solution.py:245
  125.5 1.8 %copy.70 = bf16[512,224]{0,1:T(8,128)(2,1)} copy(bf16[512,224]{1,0:T(8,128)(2,1)} %get-tuple-element.69) | data formatting | bytes 458752
  127.3 1.0 fusion.20
  128.3 1.2 copy.83
  (54 shorter events, 0.4 us)
Async XLA Ops:
  0.6 3.5 %copy-start = (bf16[512,1792]{1,0:T(8,128)(2,1)S(1)}, bf16[512,1792]{1,0:T(8,128)(2,1)}, u32[]{:S(2)}) copy-start(bf16[512,1792]{1,0:T(8,128)(2,1)} %param.13) | copy-start | bytes 5505028
  6.1 2.1 %copy-start.15 = (f32[1792]{0:T(1024)S(1)}, f32[1792]{0:T(1024)}, u32[]{:S(2)}) copy-start(f32[1792]{0:T(1024)} %param.14) | copy-start | bytes 21508
  8.2 3.1 %copy-start.1 = (bf16[64,8,1792]{2,1,0:T(8,128)(2,1)S(1)}, bf16[64,8,1792]{2,1,0:T(8,128)(2,1)}, u32[]{:S(2)}) copy-start(bf16[64,8,1792]{2,1,0:T(8,128)(2,1)} %gather_fusion) | copy-start | bytes 5505028
  8.2 3.1 %copy-start.14 = (bf16[1792,128]{1,0:T(8,128)(2,1)S(1)}, bf16[1792,128]{1,0:T(8,128)(2,1)}, u32[]{:S(2)}) copy-start(bf16[1792,128]{1,0:T(8,128)(2,1)} %param.17) | copy-start | bytes 1376260
  12.0 10.3 %copy-start.8 = (s32[512]{0:T(512)S(1)}, s32[512]{0:T(512)}, u32[]{:S(2)}) copy-start(s32[512]{0:T(512)} %param.20) | copy-start | bytes 6148
  12.1 12.1 %copy-start.12 = (s32[128]{0:T(128)S(1)}, s32[128]{0:T(128)}, u32[]{:S(2)}) copy-start(s32[128]{0:T(128)} %param.21) | copy-start | bytes 1540
  12.1 12.3 %copy-start.13 = (s32[64]{0:T(128)S(1)}, s32[64]{0:T(128)}, u32[]{:S(2)}) copy-start(s32[64]{0:T(128)} %param.22) | copy-start | bytes 772
  14.4 20.4 %all-to-all-start = ((bf16[32,2,8,640]{3,2,1,0:T(8,128)(2,1)}), bf16[32,2,8,640]{3,2,1,0:T(8,128)(2,1)S(1)}, u32[]{:S(2)}, u32[]{:S(2)}) async-start(bf16[32,2,8,640]{3,2,1,0:T(8,128)(2,1)} %pad_maximum_fusion.6), calls=%async_computation | async-start | bytes 1310720 | tf_op jit(solution)/shard_map/all_to_all | solution.py:308
  28.1 3.4 %copy-start.9 = (bf16[16,1792]{1,0:T(8,128)(2,1)S(1)}, bf16[16,1792]{1,0:T(8,128)(2,1)}, u32[]{:S(2)}) copy-start(bf16[16,1792]{1,0:T(8,128)(2,1)} %param.19) | copy-start | bytes 172036
  35.9 2.8 %copy-start.6 = (f32[2,512,144]{1,2,0:T(8,128)}, f32[2,512,144]{1,2,0:T(8,128)S(1)}, u32[]{:S(2)}) copy-start(f32[2,512,144]{1,2,0:T(8,128)S(1)} %transpose.52) | copy-start | bytes 1769476
  36.0 3.7 %copy-start.10 = (f32[512]{0:T(512)S(1)}, f32[512]{0:T(512)}, u32[]{:S(2)}) copy-start(f32[512]{0:T(512)} %compare_convert_fusion.1) | copy-start | bytes 6148
  38.7 1.0 copy-start.3
  41.1 7.6 %collective-permute-start = (bf16[2,274,113]{2,1,0:T(8,128)(2,1)S(1)}, bf16[2,274,113]{2,1,0:T(8,128)(2,1)S(1)}, u32[]{:S(2)}, u32[]{:S(2)}) collective-permute-start(bf16[2,274,113]{2,1,0:T(8,128)(2,1)S(1)} %scatter.4), channel_id=1, source_target_pairs={{0,8},{8,16},{16,24},{24,32},{32,40},{40,48},{48,56},{56,64},{64,7... | collective-permute-start | bytes 371552 | tf_op jit(solution)/shard_map/ppermute | solution.py:20
  43.5 2.9 %copy-start.5 = (f32[512,512]{0,1:T(8,128)S(1)}, f32[512,512]{0,1:T(8,128)}, u32[]{:S(2)}) copy-start(f32[512,512]{0,1:T(8,128)} %get-tuple-element.79) | copy-start | bytes 3145732
  45.5 1.6 %copy-start.2 = (f32[2,512,512]{1,2,0:T(8,128)S(1)}, f32[2,512,512]{1,2,0:T(8,128)}, u32[]{:S(2)}) copy-start(f32[2,512,512]{1,2,0:T(8,128)} %fusion.43) | copy-start | bytes 6291460
  47.1 0.8 copy-start.11
  47.1 2.0 %copy-start.4 = (f32[2,512,16,16]{1,3,2,0:T(8,128)S(1)}, f32[2,512,16,16]{1,3,2,0:T(8,128)}, u32[]{:S(2)}) copy-start(f32[2,512,16,16]{1,3,2,0:T(8,128)} %copy-done.3) | copy-start | bytes 3145732
  47.1 2.0 %copy-start.7 = (f32[2,512,144]{1,2,0:T(8,128)S(1)}, f32[2,512,144]{1,2,0:T(8,128)}, u32[]{:S(2)}) copy-start(f32[2,512,144]{1,2,0:T(8,128)} %copy-done.6) | copy-start | bytes 1769476

commit v14 on v13

--- a/solution.py
+++ b/solution.py
@@ -89,7 +89,7 @@
     att_ref, low_ref, w_ref, u_ref, resid_ref, vocab_in, upd_ref, best_ref,
     land, acc, rows, tops, got, parts, vocab_ref, ring_sems, top_sems, vocab_sems,
 ):
-    n = w_ref.shape[0]
+    n = rows.shape[0]
     quarter = att_ref.shape[0] // 8
     block_rows = best_ref.shape[1]
     me = lax.axis_index("mp")
@@ -100,9 +100,11 @@
     chains = [(0, 0), (1, 4), (0, 1), (1, 5), (0, 2), (1, 6), (0, 3), (1, 7)]
     spans = [pl.ds(quarter * piece, quarter) for _, piece in chains]
 
+    width = parts.shape[2]
     for c in range(n):
-        value = jnp.dot(att_ref[...], w_ref[c], preferred_element_type=jnp.float32)
-        value = value + jnp.dot(low_ref[...], u_ref[c], preferred_element_type=jnp.float32)
+        cols = slice(c * width, (c + 1) * width)
+        value = jnp.dot(att_ref[...], w_ref[:, cols], preferred_element_type=jnp.float32)
+        value = value + jnp.dot(low_ref[...], u_ref[:, cols], preferred_element_type=jnp.float32)
         parts[c] = value.astype(parts.dtype)
 
     groups = vocab_ref.shape[0]
@@ -237,7 +239,8 @@
 
 
 def mp_exchange(attended, low_rank, out_blocks, up_blocks, residual, vocab_blocks, groups):
-    n, _, width = out_blocks.shape
+    n = vocab_blocks.shape[0]
+    width = out_blocks.shape[1] // n
     rows_here = attended.shape[0]
     block_rows = rows_here // n
     chains = 8
@@ -391,12 +394,7 @@
     low_rank = jnp.where(
         local_slot[:, None] == column_slot[None, :], lowered, jnp.zeros_like(lowered)
     )
-    out_blocks = jnp.transpose(
-        out_weight.reshape(out_weight.shape[0], shards, slice_width), (1, 0, 2)
-    )
-    up_blocks = jnp.transpose(
-        adapter_up.reshape(adapter_up.shape[0], shards, slice_width), (1, 0, 2)
-    )
+    out_blocks, up_blocks = out_weight, adapter_up
     summed, best = mp_exchange(
         attended, low_rank, out_blocks, up_blocks, residual, vocab_blocks, groups
     )

time: 130 us -> 128 us (0.985)
  local copies, waits for them, and re-layouts: 21.5 us -> 15.6 us
  waiting for transfers between devices: 0.01 us -> 4.46 us
    reshape x3 -> x0, local copies, waits for them, and re-layouts: 4.61 us -> none  [the longest x2 3.58 us: on_device(): out_weight.reshape(out_weight.shape[0], shards, slice_width)]
    all_to_all x1, waiting for transfers between devices: 0.01 us -> 4.46 us  [on_device(): lax.all_to_all(jnp.concatenate([kept_pages, projected_pages, lowered_page...]
    unnamed x35 -> x34, local copies, waits for them, and re-layouts: 5.97 us -> 4.7 us
  transfers between devices with their start and end apart: 2 -> 2, of which waited for: 0 -> 1; matrix products, arithmetic and copies ran while one was open for 13% -> 8% of each run, Pallas kernels for 0% -> 0%
where the time goes in v14:
time: 128 us; the launch traced here: 127 us
  Pallas kernels  70.4 us (55%)
  local copies, waits for them, and re-layouts  15.6 us (12%)
  matrix products  14.4 us (11%)
  other arithmetic  10.3 us (8%)
  starting transfers between devices  9.8 us (8%)
  waiting for transfers between devices  4.46 us (3%)
  between operations  2.41 us (2%)
    pallas_call x1, Pallas kernels, mp_exchange(): pl.pallas_call(exchange_kernel, out_shape=(jax.ShapeDtypeStruct((rows_her...  70.4 us
    all_to_all x1, starting transfers between devices, on_device(): lax.all_to_all(jnp.concatenate([kept_pages, projected_pages, lowered_page...  7.54 us
    unnamed x34, local copies, waits for them, and re-layouts  4.7 us
    all_to_all x1, waiting for transfers between devices, on_device(): lax.all_to_all(jnp.concatenate([kept_pages, projected_pages, lowered_page...  4.46 us
    dot_general x1, matrix products, on_device(): jnp.einsum('abrd,dc->abrc', normed_pages, qkv_weight, preferred_element_t...  3.08 us
  transfers between devices with their start and end apart: 2, of which 1 were waited for; matrix products, arithmetic and copies ran while one was open for 8% of the time, Pallas kernels for 0%

profile of v14, /device:TPU:8, one launch (start us, length us, event | category | flops | bytes accessed | tf_op | source)
XLA Modules:
  0.0 127.3 jit_solution(2653334514892148244)
XLA Ops:
  0.6 0.0 copy-start
  0.7 0.9 reshape.270
  1.6 0.1 copy.48
  1.7 1.0 sort.17
  2.7 0.1 copy.49
  2.8 0.1 reshape.293
  2.9 0.8 gather_fusion.2
  3.7 0.1 reshape.296
  3.8 0.1 copy.50
  3.9 0.1 copy.51
  4.0 0.1 reshape.279
  4.1 1.9 %gather_fusion = bf16[64,8,1792]{2,1,0:T(8,128)(2,1)} fusion(bf16[64,8,1792]{2,1,0:T(8,128)(2,1)S(1)} %bitcast.54, s32[1024]{0:T(1024)S(1)} %pad_clamp_fusion.1), kind=kCustom, calls=%fused_computation | custom fusion | bytes 3670272 | tf_op jit(solution)/shard_map/gather | solution.py:301
  6.1 2.0 %fusion = f32[32,2,8]{2,1,0:T(2,128)S(1)} fusion(bf16[32,2,8,1792]{3,2,1,0:T(8,128)(2,1)} %bitcast.55), kind=kLoop, calls=%fused_computation.5 | loop fusion | flops 2752000 | bytes 1837056 | tf_op jit(solution)/shard_map/reduce_sum | solution.py:25
  8.0 0.1 copy.52
  8.1 0.1 copy.53
  8.2 0.0 copy-start.14
  8.2 3.1 %fusion.7 = bf16[32,2,8,288]{3,2,1,0:T(8,128)(2,1)S(1)} fusion(bf16[32,2,8,1792]{3,2,1,0:T(8,128)(2,1)} %bitcast.56, f32[1792]{0:T(1024)S(1)} %copy-done.15, f32[32,2,8]{2,1,0:T(2,128)S(1)} %copy.53, bf16[1792,288]{0,1:T(8,128)(2,1)} %param.15), kind=kOutput, calls=%fused_computation.12 | convolution fusion | flops 532299776 | bytes 3171328 | tf_op jit(solution)/shard_map/abrd,dc->abrc/dot_general | solution.py:303
  11.3 0.7 fusion.14
  12.1 1.2 constant_dynamic-slice_fusion.1
  13.3 1.1 pad_maximum_fusion.6
  14.4 7.5 %all-to-all-start = ((bf16[32,2,8,640]{3,2,1,0:T(8,128)(2,1)}), bf16[32,2,8,640]{3,2,1,0:T(8,128)(2,1)S(1)}, u32[]{:S(2)}, u32[]{:S(2)}) async-start(bf16[32,2,8,640]{3,2,1,0:T(8,128)(2,1)} %pad_maximum_fusion.6), calls=%async_computation | async-start | bytes 1310720 | tf_op jit(solution)/shard_map/all_to_all | solution.py:311
  22.0 0.1 fusion.42
  22.0 0.1 reduce_window_sum.11
  22.1 0.2 select_reduce_fusion.2
  22.3 0.6 slice.80
  22.9 1.2 compare_convert_fusion.1
  24.1 0.2 select_reduce_fusion
  24.4 0.1 select_reduce_fusion.1
  24.5 0.5 and_select_fusion
  25.7 0.1 reshape.276
  25.8 0.6 copy.66
  26.5 1.3 fusion.34
  27.7 1.2 fusion.31
  28.9 4.5 %all-to-all-done = bf16[32,2,8,640]{3,2,1,0:T(8,128)(2,1)S(1)} async-done(((bf16[32,2,8,640]{3,2,1,0:T(8,128)(2,1)}), bf16[32,2,8,640]{3,2,1,0:T(8,128)(2,1)S(1)}, u32[]{:S(2)}, u32[]{:S(2)}) %all-to-all-start) | async-done | bytes 655392 | tf_op jit(solution)/shard_map/all_to_all | solution.py:311
  33.4 0.7 gather_fusion.1
  34.0 0.2 slice.97
  34.2 0.2 copy.54
  34.4 0.1 transpose.46
  34.6 1.8 %fusion.43 = f32[2,512,512]{1,2,0:T(8,128)} fusion(bf16[2,512,144]{1,2,0:T(8,128)(2,1)S(1)} %bitcast.62), kind=kOutput, calls=%fused_computation.67 | convolution fusion | flops 16777216 | bytes 2129920 | tf_op jit(solution)/shard_map/while/body/eval_jaxpr/hcf,hdf->hcd/dot_general | solution.py:59
  36.4 0.7 slice.108.resid_ref
  37.1 0.1 multiply_multiply_fusion.1
  37.3 0.9 copy-done.3
  38.2 1.3 %fusion.17 = bf16[2,273,113]{2,1,0:T(8,128)(2,1)S(1)} fusion(f32[2,512,256]{1,2,0:T(8,128)S(1)} %bitcast.72, f32[2,512,16]{1,2,0:T(8,128)S(1)} %get-tuple-element.72, f32[273]{0:T(512)S(1)} %pad.13.clone, f32[512]{0:T(512)S(1)} %copy-done.10, f32[2,512,112]{1,2,0:T(8,128)S(1)} %slice.102), kind=kOutput, calls=%fused_computation.22 | convolution fusion | flops 379911168 | bytes 1699400 | tf_op jit(solution)/shard_map/hcp,hce->hpe/dot_general | solution.py:347
  39.6 2.3 %collective-permute-start = (bf16[2,274,113]{2,1,0:T(8,128)(2,1)S(1)}, bf16[2,274,113]{2,1,0:T(8,128)(2,1)S(1)}, u32[]{:S(2)}, u32[]{:S(2)}) collective-permute-start(bf16[2,274,113]{2,1,0:T(8,128)(2,1)S(1)} %scatter.4), channel_id=1, source_target_pairs={{0,8},{8,16},{16,24},{24,32},{32,40},{40,48},{48,56},{56,64},{64,7... | collective-permute-start | bytes 371552 | tf_op jit(solution)/shard_map/ppermute | solution.py:20
  41.9 0.1 multiply_multiply_fusion
  42.1 2.0 %fusion.58 = (f32[2,512]{1,0:T(2,128)S(1)}, f32[2,512,512]{1,2,0:T(8,128)S(1)}) fusion(f32[512,512]{0,1:T(8,128)} %fusion.31, bf16[2,512,144]{1,2,0:T(8,128)(2,1)S(1)} %bitcast.63), kind=kOutput, calls=%fused_computation.109 | convolution fusion | flops 20446208 | bytes 3215360 | tf_op jit(solution)/shard_map/while/body/eval_jaxpr/hcf,hdf->hcd/dot_general | solution.py:49
  44.1 0.9 fusion.37
  45.0 0.7 copy-done.2
  45.7 0.7 multiply_reduce_fusion
  46.5 0.8 compare_select_fusion.low_ref
  47.3 0.3 slice_reduce_fusion
  47.6 0.1 fusion.35
  47.7 0.9 fusion.13
  48.6 0.4 convolution_multiply_fusion.2
  49.0 0.1 slice_reduce_fusion.2
  49.1 0.5 slice.103
  50.3 0.3 slice_reduce_fusion.1
  50.6 0.7 fusion.23
  51.3 0.9 fusion.12
  52.2 0.8 copy.57.att_ref
  53.0 70.4 %shard_map.130 = (bf16[512,224]{1,0:T(8,128)(2,1)}, f32[1,64]{1,0:T(1,128)}) custom-call(bf16[512,224]{1,0:T(8,128)(2,1)} %copy.57.att_ref, bf16[512,128]{1,0:T(8,128)(2,1)} %compare_select_fusion.low_ref, bf16[224,1792]{1,0:T(8,128)(2,1)} %w_ref.1, bf16[128,1792]{1,0:T(8,128)(2,1)} %u_ref.1, bf16[512,224]{1,0:T(8,128)(2,1)} %slice.108.resid_ref, ...), custom_call_target="tpu_custom_call" | custom-call | tf_op jit(solution)/shard_map/pallas_call | solution.py:248
  123.4 1.8 %copy.58 = bf16[512,224]{0,1:T(8,128)(2,1)} copy(bf16[512,224]{1,0:T(8,128)(2,1)} %get-tuple-element.69) | data formatting | bytes 458752
  125.1 1.0 fusion.20
  126.1 1.2 copy.69
  (50 shorter events, 0.4 us)
Async XLA Ops:
  0.6 3.5 %copy-start = (bf16[512,1792]{1,0:T(8,128)(2,1)S(1)}, bf16[512,1792]{1,0:T(8,128)(2,1)}, u32[]{:S(2)}) copy-start(bf16[512,1792]{1,0:T(8,128)(2,1)} %param.13) | copy-start | bytes 5505028
  6.1 2.1 %copy-start.15 = (f32[1792]{0:T(1024)S(1)}, f32[1792]{0:T(1024)}, u32[]{:S(2)}) copy-start(f32[1792]{0:T(1024)} %param.14) | copy-start | bytes 21508
  8.2 3.1 %copy-start.1 = (bf16[64,8,1792]{2,1,0:T(8,128)(2,1)S(1)}, bf16[64,8,1792]{2,1,0:T(8,128)(2,1)}, u32[]{:S(2)}) copy-start(bf16[64,8,1792]{2,1,0:T(8,128)(2,1)} %gather_fusion) | copy-start | bytes 5505028
  8.2 3.1 %copy-start.14 = (bf16[1792,128]{1,0:T(8,128)(2,1)S(1)}, bf16[1792,128]{1,0:T(8,128)(2,1)}, u32[]{:S(2)}) copy-start(bf16[1792,128]{1,0:T(8,128)(2,1)} %param.17) | copy-start | bytes 1376260
  12.0 10.3 %copy-start.8 = (s32[512]{0:T(512)S(1)}, s32[512]{0:T(512)}, u32[]{:S(2)}) copy-start(s32[512]{0:T(512)} %param.20) | copy-start | bytes 6148
  12.1 12.1 %copy-start.12 = (s32[128]{0:T(128)S(1)}, s32[128]{0:T(128)}, u32[]{:S(2)}) copy-start(s32[128]{0:T(128)} %param.21) | copy-start | bytes 1540
  12.1 12.3 %copy-start.13 = (s32[64]{0:T(128)S(1)}, s32[64]{0:T(128)}, u32[]{:S(2)}) copy-start(s32[64]{0:T(128)} %param.22) | copy-start | bytes 772
  12.1 13.6 %copy-start.9 = (bf16[16,1792]{1,0:T(8,128)(2,1)S(1)}, bf16[16,1792]{1,0:T(8,128)(2,1)}, u32[]{:S(2)}) copy-start(bf16[16,1792]{1,0:T(8,128)(2,1)} %param.19) | copy-start | bytes 172036
  14.4 19.0 %all-to-all-start = ((bf16[32,2,8,640]{3,2,1,0:T(8,128)(2,1)}), bf16[32,2,8,640]{3,2,1,0:T(8,128)(2,1)S(1)}, u32[]{:S(2)}, u32[]{:S(2)}) async-start(bf16[32,2,8,640]{3,2,1,0:T(8,128)(2,1)} %pad_maximum_fusion.6), calls=%async_computation | async-start | bytes 1310720 | tf_op jit(solution)/shard_map/all_to_all | solution.py:311
  34.5 2.8 %copy-start.6 = (f32[2,512,144]{1,2,0:T(8,128)}, f32[2,512,144]{1,2,0:T(8,128)S(1)}, u32[]{:S(2)}) copy-start(f32[2,512,144]{1,2,0:T(8,128)S(1)} %transpose.46) | copy-start | bytes 1769476
  34.5 3.7 %copy-start.10 = (f32[512]{0:T(512)S(1)}, f32[512]{0:T(512)}, u32[]{:S(2)}) copy-start(f32[512]{0:T(512)} %compare_convert_fusion.1) | copy-start | bytes 6148
  37.3 1.0 copy-start.3
  39.6 7.6 %collective-permute-start = (bf16[2,274,113]{2,1,0:T(8,128)(2,1)S(1)}, bf16[2,274,113]{2,1,0:T(8,128)(2,1)S(1)}, u32[]{:S(2)}, u32[]{:S(2)}) collective-permute-start(bf16[2,274,113]{2,1,0:T(8,128)(2,1)S(1)} %scatter.4), channel_id=1, source_target_pairs={{0,8},{8,16},{16,24},{24,32},{32,40},{40,48},{48,56},{56,64},{64,7... | collective-permute-start | bytes 371552 | tf_op jit(solution)/shard_map/ppermute | solution.py:20
  42.1 2.9 %copy-start.5 = (f32[512,512]{0,1:T(8,128)S(1)}, f32[512,512]{0,1:T(8,128)}, u32[]{:S(2)}) copy-start(f32[512,512]{0,1:T(8,128)} %get-tuple-element.79) | copy-start | bytes 3145732
  44.1 1.6 %copy-start.2 = (f32[2,512,512]{1,2,0:T(8,128)S(1)}, f32[2,512,512]{1,2,0:T(8,128)}, u32[]{:S(2)}) copy-start(f32[2,512,512]{1,2,0:T(8,128)} %fusion.43) | copy-start | bytes 6291460
  45.7 0.8 copy-start.11
  45.7 2.0 %copy-start.4 = (f32[2,512,16,16]{1,3,2,0:T(8,128)S(1)}, f32[2,512,16,16]{1,3,2,0:T(8,128)}, u32[]{:S(2)}) copy-start(f32[2,512,16,16]{1,3,2,0:T(8,128)} %copy-done.3) | copy-start | bytes 3145732
  45.7 2.0 %copy-start.7 = (f32[2,512,144]{1,2,0:T(8,128)S(1)}, f32[2,512,144]{1,2,0:T(8,128)}, u32[]{:S(2)}) copy-start(f32[2,512,144]{1,2,0:T(8,128)} %copy-done.6) | copy-start | bytes 1769476

commit v15 on v14

--- a/solution.py
+++ b/solution.py
@@ -90,14 +90,14 @@
     land, acc, rows, tops, got, parts, vocab_ref, ring_sems, top_sems, vocab_sems,
 ):
     n = rows.shape[0]
-    quarter = att_ref.shape[0] // 8
+    quarter = att_ref.shape[0] // 16
     block_rows = best_ref.shape[1]
     me = lax.axis_index("mp")
     grp = lax.axis_index("group")
     peers = [lax.rem(me + k, n) for k in range(1, n)]
     mesh_id = pl.DeviceIdType.MESH
     towards = (lax.rem(me + 1, n), lax.rem(me + n - 1, n))
-    chains = [(0, 0), (1, 4), (0, 1), (1, 5), (0, 2), (1, 6), (0, 3), (1, 7)]
+    chains = [(way, piece + 8 * way) for piece in range(8) for way in range(2)]
     spans = [pl.ds(quarter * piece, quarter) for _, piece in chains]
 
     width = parts.shape[2]
@@ -243,7 +243,7 @@
     width = out_blocks.shape[1] // n
     rows_here = attended.shape[0]
     block_rows = rows_here // n
-    chains = 8
+    chains = 16
     vmem = pl.BlockSpec(memory_space=pltpu.VMEM)
     return pl.pallas_call(
         exchange_kernel,

time: 128 us -> 129 us (level)
  no operation moved by 1% of the time
where the time goes in v15:
time: 129 us; the launch traced here: 128 us
  Pallas kernels  71.2 us (55%)
  local copies, waits for them, and re-layouts  15.6 us (12%)
  matrix products  14.4 us (11%)
  other arithmetic  10.3 us (8%)
  starting transfers between devices  9.81 us (8%)
  waiting for transfers between devices  4.46 us (3%)
  between operations  2.41 us (2%)
    pallas_call x1, Pallas kernels, mp_exchange(): pl.pallas_call(exchange_kernel, out_shape=(jax.ShapeDtypeStruct((rows_her...  71.2 us
    all_to_all x1, starting transfers between devices, on_device(): lax.all_to_all(jnp.concatenate([kept_pages, projected_pages, lowered_page...  7.54 us
    unnamed x34, local copies, waits for them, and re-layouts  4.7 us
    all_to_all x1, waiting for transfers between devices, on_device(): lax.all_to_all(jnp.concatenate([kept_pages, projected_pages, lowered_page...  4.46 us
    dot_general x1, matrix products, on_device(): jnp.einsum('abrd,dc->abrc', normed_pages, qkv_weight, preferred_element_t...  3.08 us
  transfers between devices with their start and end apart: 2, of which 1 were waited for; matrix products, arithmetic and copies ran while one was open for 8% of the time, Pallas kernels for 0%

profile of v15, /device:TPU:8, one launch (start us, length us, event | category | flops | bytes accessed | tf_op | source)
XLA Modules:
  0.0 128.2 jit_solution(17396784799794577490)
XLA Ops:
  0.6 0.0 copy-start
  0.7 0.9 reshape.270
  1.6 0.1 copy.48
  1.7 1.0 sort.17
  2.7 0.1 copy.49
  2.8 0.1 reshape.293
  2.9 0.8 gather_fusion.2
  3.7 0.1 reshape.296
  3.8 0.1 copy.50
  3.9 0.1 copy.51
  4.0 0.1 reshape.279
  4.1 1.9 %gather_fusion = bf16[64,8,1792]{2,1,0:T(8,128)(2,1)} fusion(bf16[64,8,1792]{2,1,0:T(8,128)(2,1)S(1)} %bitcast.54, s32[1024]{0:T(1024)S(1)} %pad_clamp_fusion.1), kind=kCustom, calls=%fused_computation | custom fusion | bytes 3670272 | tf_op jit(solution)/shard_map/gather | solution.py:301
  6.1 2.0 %fusion = f32[32,2,8]{2,1,0:T(2,128)S(1)} fusion(bf16[32,2,8,1792]{3,2,1,0:T(8,128)(2,1)} %bitcast.55), kind=kLoop, calls=%fused_computation.5 | loop fusion | flops 2752000 | bytes 1837056 | tf_op jit(solution)/shard_map/reduce_sum | solution.py:25
  8.0 0.1 copy.52
  8.1 0.1 copy.53
  8.2 0.0 copy-start.14
  8.2 3.1 %fusion.7 = bf16[32,2,8,288]{3,2,1,0:T(8,128)(2,1)S(1)} fusion(bf16[32,2,8,1792]{3,2,1,0:T(8,128)(2,1)} %bitcast.56, f32[1792]{0:T(1024)S(1)} %copy-done.15, f32[32,2,8]{2,1,0:T(2,128)S(1)} %copy.53, bf16[1792,288]{0,1:T(8,128)(2,1)} %param.15), kind=kOutput, calls=%fused_computation.12 | convolution fusion | flops 532299776 | bytes 3171328 | tf_op jit(solution)/shard_map/abrd,dc->abrc/dot_general | solution.py:303
  11.3 0.7 fusion.14
  12.1 1.2 constant_dynamic-slice_fusion.1
  13.3 1.1 pad_maximum_fusion.6
  14.4 7.5 %all-to-all-start = ((bf16[32,2,8,640]{3,2,1,0:T(8,128)(2,1)}), bf16[32,2,8,640]{3,2,1,0:T(8,128)(2,1)S(1)}, u32[]{:S(2)}, u32[]{:S(2)}) async-start(bf16[32,2,8,640]{3,2,1,0:T(8,128)(2,1)} %pad_maximum_fusion.6), calls=%async_computation | async-start | bytes 1310720 | tf_op jit(solution)/shard_map/all_to_all | solution.py:311
  22.0 0.1 fusion.42
  22.0 0.1 reduce_window_sum.11
  22.1 0.2 select_reduce_fusion.2
  22.3 0.6 slice.80
  22.9 1.2 compare_convert_fusion.1
  24.1 0.2 select_reduce_fusion
  24.4 0.1 select_reduce_fusion.1
  24.5 0.5 and_select_fusion
  25.7 0.1 reshape.276
  25.8 0.6 copy.66
  26.5 1.3 fusion.34
  27.7 1.2 fusion.31
  28.9 4.5 %all-to-all-done = bf16[32,2,8,640]{3,2,1,0:T(8,128)(2,1)S(1)} async-done(((bf16[32,2,8,640]{3,2,1,0:T(8,128)(2,1)}), bf16[32,2,8,640]{3,2,1,0:T(8,128)(2,1)S(1)}, u32[]{:S(2)}, u32[]{:S(2)}) %all-to-all-start) | async-done | bytes 655392 | tf_op jit(solution)/shard_map/all_to_all | solution.py:311
  33.4 0.7 gather_fusion.1
  34.0 0.2 slice.97
  34.2 0.2 copy.54
  34.4 0.1 transpose.46
  34.6 1.8 %fusion.43 = f32[2,512,512]{1,2,0:T(8,128)} fusion(bf16[2,512,144]{1,2,0:T(8,128)(2,1)S(1)} %bitcast.62), kind=kOutput, calls=%fused_computation.67 | convolution fusion | flops 16777216 | bytes 2129920 | tf_op jit(solution)/shard_map/while/body/eval_jaxpr/hcf,hdf->hcd/dot_general | solution.py:59
  36.4 0.7 slice.108.resid_ref
  37.1 0.1 multiply_multiply_fusion.1
  37.3 0.9 copy-done.3
  38.2 1.3 %fusion.17 = bf16[2,273,113]{2,1,0:T(8,128)(2,1)S(1)} fusion(f32[2,512,256]{1,2,0:T(8,128)S(1)} %bitcast.72, f32[2,512,16]{1,2,0:T(8,128)S(1)} %get-tuple-element.72, f32[273]{0:T(512)S(1)} %pad.13.clone, f32[512]{0:T(512)S(1)} %copy-done.10, f32[2,512,112]{1,2,0:T(8,128)S(1)} %slice.102), kind=kOutput, calls=%fused_computation.22 | convolution fusion | flops 379911168 | bytes 1699400 | tf_op jit(solution)/shard_map/hcp,hce->hpe/dot_general | solution.py:347
  39.6 2.3 %collective-permute-start = (bf16[2,274,113]{2,1,0:T(8,128)(2,1)S(1)}, bf16[2,274,113]{2,1,0:T(8,128)(2,1)S(1)}, u32[]{:S(2)}, u32[]{:S(2)}) collective-permute-start(bf16[2,274,113]{2,1,0:T(8,128)(2,1)S(1)} %scatter.4), channel_id=1, source_target_pairs={{0,8},{8,16},{16,24},{24,32},{32,40},{40,48},{48,56},{56,64},{64,7... | collective-permute-start | bytes 371552 | tf_op jit(solution)/shard_map/ppermute | solution.py:20
  41.9 0.1 multiply_multiply_fusion
  42.1 2.0 %fusion.58 = (f32[2,512]{1,0:T(2,128)S(1)}, f32[2,512,512]{1,2,0:T(8,128)S(1)}) fusion(f32[512,512]{0,1:T(8,128)} %fusion.31, bf16[2,512,144]{1,2,0:T(8,128)(2,1)S(1)} %bitcast.63), kind=kOutput, calls=%fused_computation.109 | convolution fusion | flops 20446208 | bytes 3215360 | tf_op jit(solution)/shard_map/while/body/eval_jaxpr/hcf,hdf->hcd/dot_general | solution.py:49
  44.1 0.9 fusion.37
  45.0 0.7 copy-done.2
  45.7 0.7 multiply_reduce_fusion
  46.5 0.8 compare_select_fusion.low_ref
  47.3 0.3 slice_reduce_fusion
  47.6 0.1 fusion.35
  47.7 0.9 fusion.13
  48.6 0.4 convolution_multiply_fusion.2
  49.0 0.1 slice_reduce_fusion.2
  49.1 0.5 slice.103
  50.3 0.3 slice_reduce_fusion.1
  50.6 0.7 fusion.23
  51.3 0.9 fusion.12
  52.2 0.8 copy.57.att_ref
  53.0 71.2 %shard_map.130 = (bf16[512,224]{1,0:T(8,128)(2,1)}, f32[1,64]{1,0:T(1,128)}) custom-call(bf16[512,224]{1,0:T(8,128)(2,1)} %copy.57.att_ref, bf16[512,128]{1,0:T(8,128)(2,1)} %compare_select_fusion.low_ref, bf16[224,1792]{1,0:T(8,128)(2,1)} %w_ref.1, bf16[128,1792]{1,0:T(8,128)(2,1)} %u_ref.1, bf16[512,224]{1,0:T(8,128)(2,1)} %slice.108.resid_ref, ...), custom_call_target="tpu_custom_call" | custom-call | tf_op jit(solution)/shard_map/pallas_call | solution.py:248
  124.3 1.8 %copy.58 = bf16[512,224]{0,1:T(8,128)(2,1)} copy(bf16[512,224]{1,0:T(8,128)(2,1)} %get-tuple-element.69) | data formatting | bytes 458752
  126.0 1.0 fusion.20
  127.0 1.2 copy.69
  (50 shorter events, 0.4 us)
Async XLA Ops:
  0.6 3.5 %copy-start = (bf16[512,1792]{1,0:T(8,128)(2,1)S(1)}, bf16[512,1792]{1,0:T(8,128)(2,1)}, u32[]{:S(2)}) copy-start(bf16[512,1792]{1,0:T(8,128)(2,1)} %param.13) | copy-start | bytes 5505028
  6.1 2.1 %copy-start.15 = (f32[1792]{0:T(1024)S(1)}, f32[1792]{0:T(1024)}, u32[]{:S(2)}) copy-start(f32[1792]{0:T(1024)} %param.14) | copy-start | bytes 21508
  8.2 3.1 %copy-start.1 = (bf16[64,8,1792]{2,1,0:T(8,128)(2,1)S(1)}, bf16[64,8,1792]{2,1,0:T(8,128)(2,1)}, u32[]{:S(2)}) copy-start(bf16[64,8,1792]{2,1,0:T(8,128)(2,1)} %gather_fusion) | copy-start | bytes 5505028
  8.2 3.1 %copy-start.14 = (bf16[1792,128]{1,0:T(8,128)(2,1)S(1)}, bf16[1792,128]{1,0:T(8,128)(2,1)}, u32[]{:S(2)}) copy-start(bf16[1792,128]{1,0:T(8,128)(2,1)} %param.17) | copy-start | bytes 1376260
  12.0 10.3 %copy-start.8 = (s32[512]{0:T(512)S(1)}, s32[512]{0:T(512)}, u32[]{:S(2)}) copy-start(s32[512]{0:T(512)} %param.20) | copy-start | bytes 6148
  12.1 12.1 %copy-start.12 = (s32[128]{0:T(128)S(1)}, s32[128]{0:T(128)}, u32[]{:S(2)}) copy-start(s32[128]{0:T(128)} %param.21) | copy-start | bytes 1540
  12.1 12.3 %copy-start.13 = (s32[64]{0:T(128)S(1)}, s32[64]{0:T(128)}, u32[]{:S(2)}) copy-start(s32[64]{0:T(128)} %param.22) | copy-start | bytes 772
  12.1 13.6 %copy-start.9 = (bf16[16,1792]{1,0:T(8,128)(2,1)S(1)}, bf16[16,1792]{1,0:T(8,128)(2,1)}, u32[]{:S(2)}) copy-start(bf16[16,1792]{1,0:T(8,128)(2,1)} %param.19) | copy-start | bytes 172036
  14.4 19.0 %all-to-all-start = ((bf16[32,2,8,640]{3,2,1,0:T(8,128)(2,1)}), bf16[32,2,8,640]{3,2,1,0:T(8,128)(2,1)S(1)}, u32[]{:S(2)}, u32[]{:S(2)}) async-start(bf16[32,2,8,640]{3,2,1,0:T(8,128)(2,1)} %pad_maximum_fusion.6), calls=%async_computation | async-start | bytes 1310720 | tf_op jit(solution)/shard_map/all_to_all | solution.py:311
  34.5 2.8 %copy-start.6 = (f32[2,512,144]{1,2,0:T(8,128)}, f32[2,512,144]{1,2,0:T(8,128)S(1)}, u32[]{:S(2)}) copy-start(f32[2,512,144]{1,2,0:T(8,128)S(1)} %transpose.46) | copy-start | bytes 1769476
  34.6 3.7 %copy-start.10 = (f32[512]{0:T(512)S(1)}, f32[512]{0:T(512)}, u32[]{:S(2)}) copy-start(f32[512]{0:T(512)} %compare_convert_fusion.1) | copy-start | bytes 6148
  37.3 1.0 copy-start.3
  39.6 7.6 %collective-permute-start = (bf16[2,274,113]{2,1,0:T(8,128)(2,1)S(1)}, bf16[2,274,113]{2,1,0:T(8,128)(2,1)S(1)}, u32[]{:S(2)}, u32[]{:S(2)}) collective-permute-start(bf16[2,274,113]{2,1,0:T(8,128)(2,1)S(1)} %scatter.4), channel_id=1, source_target_pairs={{0,8},{8,16},{16,24},{24,32},{32,40},{40,48},{48,56},{56,64},{64,7... | collective-permute-start | bytes 371552 | tf_op jit(solution)/shard_map/ppermute | solution.py:20
  42.1 2.9 %copy-start.5 = (f32[512,512]{0,1:T(8,128)S(1)}, f32[512,512]{0,1:T(8,128)}, u32[]{:S(2)}) copy-start(f32[512,512]{0,1:T(8,128)} %get-tuple-element.79) | copy-start | bytes 3145732
  44.1 1.6 %copy-start.2 = (f32[2,512,512]{1,2,0:T(8,128)S(1)}, f32[2,512,512]{1,2,0:T(8,128)}, u32[]{:S(2)}) copy-start(f32[2,512,512]{1,2,0:T(8,128)} %fusion.43) | copy-start | bytes 6291460
  45.7 0.8 copy-start.11
  45.7 2.0 %copy-start.4 = (f32[2,512,16,16]{1,3,2,0:T(8,128)S(1)}, f32[2,512,16,16]{1,3,2,0:T(8,128)}, u32[]{:S(2)}) copy-start(f32[2,512,16,16]{1,3,2,0:T(8,128)} %copy-done.3) | copy-start | bytes 3145732
  45.7 2.0 %copy-start.7 = (f32[2,512,144]{1,2,0:T(8,128)S(1)}, f32[2,512,144]{1,2,0:T(8,128)}, u32[]{:S(2)}) copy-start(f32[2,512,144]{1,2,0:T(8,128)} %copy-done.6) | copy-start | bytes 1769476

commit v16 on v14

--- a/solution.py
+++ b/solution.py
@@ -46,7 +46,10 @@
         (position[:, None] >= position[None, :]) & (seg_ids[:, None] == seg_ids[None, :])
     ).astype(jnp.float32)
     carried = (seg_ids == owner_seg).astype(jnp.float32)[None, :]
-    scores = jnp.einsum("hcf,hdf->hcd", query_rows, key_rows, precision=PRECISE) * scaling
+    narrow = lambda values: values.astype(jnp.bfloat16)
+    scores = jnp.einsum(
+        "hcf,hdf->hcd", narrow(query_rows), narrow(key_rows), preferred_element_type=jnp.float32
+    ) * scaling
     weights = (1.0 + scores + 0.5 * scores * scores) * allowed[None]
     numerator = jnp.einsum("hcd,hde->hce", weights, value_rows, precision=PRECISE)
     numerator = numerator + carried[..., None] * jnp.einsum(
@@ -56,8 +59,12 @@
         "hcp,hp->hc", phi_query, totals, precision=PRECISE
     )
     mixed_out = numerator / denominator[..., None]
-    key_scores = jnp.einsum("hcf,hdf->hcd", key_rows, key_rows, precision=PRECISE) * scaling
-    value_gram = jnp.einsum("hce,hde->hcd", value_rows, value_rows, precision=PRECISE)
+    key_scores = jnp.einsum(
+        "hcf,hdf->hcd", narrow(key_rows), narrow(key_rows), preferred_element_type=jnp.float32
+    ) * scaling
+    value_gram = jnp.einsum(
+        "hce,hde->hcd", narrow(value_rows), narrow(value_rows), preferred_element_type=jnp.float32
+    )
     key_gram = (1.0 + key_scores + 0.5 * key_scores * key_scores) * value_gram
     diagonal = (position[:, None] == position[None, :]).astype(jnp.float32)
     row_terms = jnp.sum(key_gram * (allowed * (2.0 - diagonal))[None], axis=-1)

time: 128 us -> 133 us (1.039)
  matrix products: 14.4 us -> 18.4 us
  other arithmetic: 10.3 us -> 12 us
    dot_general x1, matrix products: 3.08 us -> 1.16 us  [on_device(): jnp.einsum('abrd,dc->abrc', normed_pages, qkv_weight, preferred_element_t...]
    dot_general x1, matrix products: 0.71 us -> 2.34 us  [on_device(): jnp.einsum('abrd,dc->abrc', normed_pages, adapter_down, preferred_element...]
    unnamed x34 -> x48, local copies, waits for them, and re-layouts: 4.7 us -> 3.36 us
  transfers between devices with their start and end apart: 2 -> 2, of which waited for: 1 -> 2; matrix products, arithmetic and copies ran while one was open for 8% -> 8% of each run, Pallas kernels for 0% -> 0%
where the time goes in v16:
time: 133 us
  Pallas kernels  70.3 us (53%)
  matrix products  18.4 us (14%)
  local copies, waits for them, and re-layouts  15.3 us (12%)
  other arithmetic  12 us (9%)
  starting transfers between devices  9.8 us (7%)
  waiting for transfers between devices  4.49 us (3%)
  between operations  2.42 us (2%)
    pallas_call x1, Pallas kernels, mp_exchange(): pl.pallas_call(exchange_kernel, out_shape=(jax.ShapeDtypeStruct((rows_her...  70.3 us
    all_to_all x1, starting transfers between devices, on_device(): lax.all_to_all(jnp.concatenate([kept_pages, projected_pages, lowered_page...  7.53 us
    all_to_all x1, waiting for transfers between devices, on_device(): lax.all_to_all(jnp.concatenate([kept_pages, projected_pages, lowered_page...  4.42 us
    unnamed x48, local copies, waits for them, and re-layouts  3.36 us
    dot_general x1, matrix products, block_step(): jnp.einsum('hce,hde->hcd', narrow(value_rows), narrow(value_rows), prefer...  3.24 us
  transfers between devices with their start and end apart: 2, of which 2 were waited for; matrix products, arithmetic and copies ran while one was open for 8% of the time, Pallas kernels for 0%

profile of v16, /device:TPU:8, one launch (start us, length us, event | category | flops | bytes accessed | tf_op | source)
XLA Modules:
  0.0 132.7 jit_solution(6525841835405897406)
XLA Ops:
  0.6 0.0 copy-start
  0.7 0.9 reshape.270
  1.6 0.1 copy.48
  1.7 1.0 sort.17
  2.7 0.1 copy.49
  2.8 0.1 reshape.293
  2.9 0.8 gather_fusion.2
  3.7 0.1 reshape.296
  3.8 0.1 copy.50
  3.9 0.1 copy.51
  4.0 0.1 reshape.279
  4.1 1.9 %gather_fusion = bf16[64,8,1792]{2,1,0:T(8,128)(2,1)} fusion(bf16[64,8,1792]{2,1,0:T(8,128)(2,1)S(1)} %bitcast.54, s32[1024]{0:T(1024)S(1)} %pad_clamp_fusion.1), kind=kCustom, calls=%fused_computation | custom fusion | bytes 3670272 | tf_op jit(solution)/shard_map/gather | solution.py:308
  6.1 2.0 %fusion = f32[32,2,8]{2,1,0:T(2,128)S(1)} fusion(bf16[32,2,8,1792]{3,2,1,0:T(8,128)(2,1)} %bitcast.55), kind=kLoop, calls=%fused_computation.5 | loop fusion | flops 2752000 | bytes 1837056 | tf_op jit(solution)/shard_map/reduce_sum | solution.py:25
  8.1 0.1 copy.52
  8.2 0.1 copy.53
  8.3 0.0 copy-start.19
  8.3 2.3 %fusion.14 = bf16[32,2,8,128]{3,2,1,0:T(8,128)(2,1)S(1)} fusion(bf16[32,2,8,1792]{3,2,1,0:T(8,128)(2,1)} %bitcast.56, f32[1792]{0:T(1024)S(1)} %copy-done.21, f32[32,2,8]{2,1,0:T(2,128)S(1)} %copy.53, bf16[1792,128]{1,0:T(8,128)(2,1)S(1)} %copy-done.20), kind=kOutput, calls=%fused_computation.19 | convolution fusion | flops 238616576 | bytes 2434048 | tf_op jit(solution)/shard_map/abrd,dc->abrc/dot_general | solution.py:313
  10.7 1.2 fusion.7
  11.9 1.2 constant_dynamic-slice_fusion.1
  13.0 1.1 pad_maximum_fusion.6
  14.2 7.5 %all-to-all-start = ((bf16[32,2,8,640]{3,2,1,0:T(8,128)(2,1)}), bf16[32,2,8,640]{3,2,1,0:T(8,128)(2,1)S(1)}, u32[]{:S(2)}, u32[]{:S(2)}) async-start(bf16[32,2,8,640]{3,2,1,0:T(8,128)(2,1)} %pad_maximum_fusion.6), calls=%async_computation | async-start | bytes 1310720 | tf_op jit(solution)/shard_map/all_to_all | solution.py:318
  21.7 0.1 fusion.42
  21.8 0.1 reduce_window_sum.11
  21.9 0.2 select_reduce_fusion.2
  22.1 0.6 slice.75
  22.7 1.2 compare_convert_fusion.1
  23.9 0.2 select_reduce_fusion
  24.2 0.1 select_reduce_fusion.1
  24.3 0.5 and_select_fusion
  25.5 0.1 reshape.276
  25.6 0.6 copy.66
  26.3 1.2 fusion.31
  27.4 1.2 fusion.34
  28.7 4.4 %all-to-all-done = bf16[32,2,8,640]{3,2,1,0:T(8,128)(2,1)S(1)} async-done(((bf16[32,2,8,640]{3,2,1,0:T(8,128)(2,1)}), bf16[32,2,8,640]{3,2,1,0:T(8,128)(2,1)S(1)}, u32[]{:S(2)}, u32[]{:S(2)}) %all-to-all-start) | async-done | bytes 655392 | tf_op jit(solution)/shard_map/all_to_all | solution.py:318
  33.1 0.7 gather_fusion.1
  33.8 0.2 slice.91
  34.0 0.2 copy.54
  34.2 0.1 transpose.46
  34.3 0.7 slice.100.resid_ref
  35.1 1.8 %fusion.44 = f32[2,512,512]{1,2,0:T(8,128)} fusion(f32[2,512,144]{1,2,0:T(8,128)S(1)} %transpose.46), kind=kOutput, calls=%fused_computation.72 | convolution fusion | flops 16777216 | bytes 2129920 | tf_op jit(solution)/shard_map/while/body/eval_jaxpr/hcf,hdf->hcd/dot_general | solution.py:62
  36.9 0.7 fusion.62
  37.6 1.6 %fusion.36 = f32[2,512,112]{1,2,0:T(8,128)} fusion(f32[2,512,512]{1,2,0:T(8,128)S(1)} %get-tuple-element.81, bf16[2,512,144]{1,2,0:T(8,128)(2,1)S(1)} %bitcast.62), kind=kOutput, calls=%fused_computation.52 | convolution fusion | flops 704643072 | bytes 2785280 | tf_op jit(solution)/shard_map/while/body/eval_jaxpr/hcd,hde->hce/dot_general | solution.py:54
  39.2 1.1 multiply_multiply_fusion
  40.4 0.1 multiply_multiply_fusion.1
  40.5 1.0 copy-done.2
  41.5 1.3 fusion.17
  42.9 2.3 %collective-permute-start = (bf16[2,274,113]{2,1,0:T(8,128)(2,1)S(1)}, bf16[2,274,113]{2,1,0:T(8,128)(2,1)S(1)}, u32[]{:S(2)}, u32[]{:S(2)}) collective-permute-start(bf16[2,274,113]{2,1,0:T(8,128)(2,1)S(1)} %scatter.4), channel_id=1, source_target_pairs={{0,8},{8,16},{16,24},{24,32},{32,40},{40,48},{48,56},{56,64},{64,7... | collective-permute-start | bytes 371552 | tf_op jit(solution)/shard_map/ppermute | solution.py:20
  45.2 3.2 %multiply_reduce_fusion = f32[2,512]{1,0:T(2,128)} fusion(f32[2,512,512]{1,2,0:T(8,128)} %fusion.44, f32[512,512]{0,1:T(8,128)} %get-tuple-element.79, f32[2,512,144]{1,2,0:T(8,128)S(1)} %copy-done.6), kind=kOutput, calls=%fused_computation.8 | convolution fusion | flops 121633792 | bytes 3379200 | tf_op jit(solution)/shard_map/while/body/eval_jaxpr/hce,hde->hcd/dot_general | solution.py:65
  48.5 0.8 compare_select_fusion.low_ref
  49.2 0.1 collective-permute-done
  49.3 0.7 fusion.35
  50.1 0.3 slice_reduce_fusion
  50.4 0.3 slice_reduce_fusion.1
  50.6 0.5 slice.96
  51.8 0.7 fusion.23
  52.5 1.6 %fusion.12 = bf16[2,512,112]{1,2,0:T(8,128)(2,1)} fusion(f32[2,512,112]{1,2,0:T(8,128)S(1)} %copy-done.10, f32[2,512,256]{1,2,0:T(8,128)S(1)} %bitcast.70, f32[2,512,16]{1,2,0:T(8,128)S(1)} %get-tuple-element.73, f32[273]{0:T(512)S(1)} %copy-done.14, f32[2,512]{1,0:T(2,128)S(1)} %fusion.48, f32[512]{0:T(512)S(1)} %compare_convert_fusion, ...), kind=kOutput, calls=%fused_computation.17 | convolution fusion | flops 376735744 | bytes 1933324 | tf_op jit(solution)/shard_map/while/body/eval_jaxpr/hcp,hpe->hce/dot_general | solution.py:55
  54.1 1.9 %copy.57.att_ref = bf16[512,224]{1,0:T(8,128)(2,1)} copy(bf16[512,224]{0,1:T(8,128)(2,1)} %bitcast.72) | data formatting | bytes 458752 | tf_op jit(solution)/shard_map/convert_element_type | solution.py:388
  56.0 70.3 %shard_map.130 = (bf16[512,224]{1,0:T(8,128)(2,1)}, f32[1,64]{1,0:T(1,128)}) custom-call(bf16[512,224]{1,0:T(8,128)(2,1)} %copy.57.att_ref, bf16[512,128]{1,0:T(8,128)(2,1)} %compare_select_fusion.low_ref, bf16[224,1792]{1,0:T(8,128)(2,1)} %w_ref.1, bf16[128,1792]{1,0:T(8,128)(2,1)} %u_ref.1, bf16[512,224]{1,0:T(8,128)(2,1)} %slice.100.resid_ref, ...), custom_call_target="tpu_custom_call" | custom-call | tf_op jit(solution)/shard_map/pallas_call | solution.py:255
  126.4 1.8 %copy.58 = bf16[512,224]{0,1:T(8,128)(2,1)} copy(bf16[512,224]{1,0:T(8,128)(2,1)} %get-tuple-element.69) | data formatting | bytes 458752
  128.1 1.8 %fusion.13 = f32[2,512]{1,0:T(2,128)S(1)} fusion(f32[2,512,256]{1,2,0:T(8,128)S(1)} %bitcast.68, f32[2,512,16]{1,2,0:T(8,128)S(1)} %get-tuple-element.72, f32[273]{0:T(512)} %copy-done.13, bf16[2,274,113]{2,1,0:T(8,128)(2,1)} %copy-done.9, f32[2,512,144]{1,2,0:T(8,128)S(1)} %copy-done.7), kind=kOutput, calls=%fused_computation.18 | convolution fusion | flops 376505344 | bytes 1701900 | tf_op jit(solution)/shard_map/while/body/eval_jaxpr/hcp,hpe->hce/dot_general | solution.py:73
  130.0 0.4 convolution_multiply_fusion.2
  130.3 0.1 slice_reduce_fusion.2
  130.5 1.7 %fusion.20 = f32[2,512]{1,0:T(2,128)} fusion(f32[2,512]{1,0:T(2,128)} %multiply_reduce_fusion, s32[512]{0:T(512)S(1)} %copy-done.11, f32[2,512]{1,0:T(2,128)S(1)} %convolution_multiply_fusion.2, f32[2]{0:T(128)} %fusion.35, f32[512]{0:T(512)S(1)} %get-tuple-element.78, f32[512]{0:T(512)S(1)} %compare_convert_fusion, f32[2]{0:T(128)S(1)} %slice_reduce_fusion.2), kind=kOutput, calls=%fused_computation.26 | convolution fusion | flops 7085056 | bytes 18448 | tf_op jit(solution)/shard_map/while/body/eval_jaxpr/cd,hd->hc/dot_general | solution.py:71
  132.2 0.5 copy.69
  (64 shorter events, 0.4 us)
Async XLA Ops:
  0.6 3.5 %copy-start = (bf16[512,1792]{1,0:T(8,128)(2,1)S(1)}, bf16[512,1792]{1,0:T(8,128)(2,1)}, u32[]{:S(2)}) copy-start(bf16[512,1792]{1,0:T(8,128)(2,1)} %param.13) | copy-start | bytes 5505028
  6.1 2.2 %copy-start.20 = (bf16[1792,128]{1,0:T(8,128)(2,1)S(1)}, bf16[1792,128]{1,0:T(8,128)(2,1)}, u32[]{:S(2)}) copy-start(bf16[1792,128]{1,0:T(8,128)(2,1)} %param.17) | copy-start | bytes 1376260
  6.1 2.2 %copy-start.21 = (f32[1792]{0:T(1024)S(1)}, f32[1792]{0:T(1024)}, u32[]{:S(2)}) copy-start(f32[1792]{0:T(1024)} %param.14) | copy-start | bytes 21508
  8.3 2.4 %copy-start.1 = (bf16[64,8,1792]{2,1,0:T(8,128)(2,1)S(1)}, bf16[64,8,1792]{2,1,0:T(8,128)(2,1)}, u32[]{:S(2)}) copy-start(bf16[64,8,1792]{2,1,0:T(8,128)(2,1)} %gather_fusion) | copy-start | bytes 5505028
  8.3 2.4 %copy-start.19 = (bf16[1792,288]{0,1:T(8,128)(2,1)S(1)}, bf16[1792,288]{0,1:T(8,128)(2,1)}, u32[]{:S(2)}) copy-start(bf16[1792,288]{0,1:T(8,128)(2,1)} %param.15) | copy-start | bytes 3096580
  11.8 10.3 %copy-start.11 = (s32[512]{0:T(512)S(1)}, s32[512]{0:T(512)}, u32[]{:S(2)}) copy-start(s32[512]{0:T(512)} %param.20) | copy-start | bytes 6148
  11.8 12.1 %copy-start.17 = (s32[128]{0:T(128)S(1)}, s32[128]{0:T(128)}, u32[]{:S(2)}) copy-start(s32[128]{0:T(128)} %param.21) | copy-start | bytes 1540
  11.8 12.3 %copy-start.18 = (s32[64]{0:T(128)S(1)}, s32[64]{0:T(128)}, u32[]{:S(2)}) copy-start(s32[64]{0:T(128)} %param.22) | copy-start | bytes 772
  11.9 13.6 %copy-start.12 = (bf16[16,1792]{1,0:T(8,128)(2,1)S(1)}, bf16[16,1792]{1,0:T(8,128)(2,1)}, u32[]{:S(2)}) copy-start(bf16[16,1792]{1,0:T(8,128)(2,1)} %param.19) | copy-start | bytes 172036
  14.2 19.0 %all-to-all-start = ((bf16[32,2,8,640]{3,2,1,0:T(8,128)(2,1)}), bf16[32,2,8,640]{3,2,1,0:T(8,128)(2,1)S(1)}, u32[]{:S(2)}, u32[]{:S(2)}) async-start(bf16[32,2,8,640]{3,2,1,0:T(8,128)(2,1)} %pad_maximum_fusion.6), calls=%async_computation | async-start | bytes 1310720 | tf_op jit(solution)/shard_map/all_to_all | solution.py:318
  26.3 14.3 %copy-start.13 = (f32[273]{0:T(512)}, f32[273]{0:T(512)S(1)}, u32[]{:S(2)}) copy-start(f32[273]{0:T(512)S(1)} %pad.13.clone) | copy-start | bytes 3280
  34.2 2.7 %copy-start.5 = (f32[2,512,144]{1,2,0:T(8,128)}, f32[2,512,144]{1,2,0:T(8,128)S(1)}, u32[]{:S(2)}) copy-start(f32[2,512,144]{1,2,0:T(8,128)S(1)} %transpose.46) | copy-start | bytes 1769476
  34.3 2.6 %copy-start.8 = (f32[512,512]{0,1:T(8,128)S(1)}, f32[512,512]{0,1:T(8,128)}, u32[]{:S(2)}) copy-start(f32[512,512]{0,1:T(8,128)} %fusion.31) | copy-start | bytes 3145732
  39.2 2.3 %copy-start.15 = (f32[512]{0:T(512)S(1)}, f32[512]{0:T(512)}, u32[]{:S(2)}) copy-start(f32[512]{0:T(512)} %compare_convert_fusion.1) | copy-start | bytes 6148
  40.4 4.8 %copy-start.6 = (f32[2,512,144]{1,2,0:T(8,128)S(1)}, f32[2,512,144]{1,2,0:T(8,128)}, u32[]{:S(2)}) copy-start(f32[2,512,144]{1,2,0:T(8,128)} %copy-done.5) | copy-start | bytes 1769476
  40.5 1.0 copy-start.2
  42.9 6.4 %collective-permute-start = (bf16[2,274,113]{2,1,0:T(8,128)(2,1)S(1)}, bf16[2,274,113]{2,1,0:T(8,128)(2,1)S(1)}, u32[]{:S(2)}, u32[]{:S(2)}) collective-permute-start(bf16[2,274,113]{2,1,0:T(8,128)(2,1)S(1)} %scatter.4), channel_id=1, source_target_pairs={{0,8},{8,16},{16,24},{24,32},{32,40},{40,48},{48,56},{56,64},{64,7... | collective-permute-start | bytes 371552 | tf_op jit(solution)/shard_map/ppermute | solution.py:20
  45.2 3.3 %copy-start.16 = (s32[128]{0:T(128)S(1)}, s32[128]{0:T(128)}, u32[]{:S(2)}) copy-start(s32[128]{0:T(128)} %and_select_fusion) | copy-start | bytes 1540
  45.2 6.6 %copy-start.4 = (f32[2,512,16,16]{1,3,2,0:T(8,128)S(1)}, f32[2,512,16,16]{1,3,2,0:T(8,128)}, u32[]{:S(2)}) copy-start(f32[2,512,16,16]{1,3,2,0:T(8,128)} %multiply_multiply_fusion) | copy-start | bytes 3145732
  45.2 6.6 %copy-start.14 = (f32[273]{0:T(512)S(1)}, f32[273]{0:T(512)}, u32[]{:S(2)}) copy-start(f32[273]{0:T(512)} %copy-done.13) | copy-start | bytes 3280
  48.5 4.1 %copy-start.10 = (f32[2,512,112]{1,2,0:T(8,128)S(1)}, f32[2,512,112]{1,2,0:T(8,128)}, u32[]{:S(2)}) copy-start(f32[2,512,112]{1,2,0:T(8,128)} %fusion.36) | copy-start | bytes 1376260
  49.3 4.8 %copy-start.9 = (bf16[2,274,113]{2,1,0:T(8,128)(2,1)}, bf16[2,274,113]{2,1,0:T(8,128)(2,1)S(1)}, u32[]{:S(2)}) copy-start(bf16[2,274,113]{2,1,0:T(8,128)(2,1)S(1)} %collective-permute-done) | copy-start | bytes 371548
  54.1 74.0 %copy-start.3 = (f32[2,512,16,16]{1,3,2,0:T(8,128)S(1)}, f32[2,512,16,16]{1,3,2,0:T(8,128)}, u32[]{:S(2)}) copy-start(f32[2,512,16,16]{1,3,2,0:T(8,128)} %copy-done.2) | copy-start | bytes 3145732
  54.1 74.0 %copy-start.7 = (f32[2,512,144]{1,2,0:T(8,128)S(1)}, f32[2,512,144]{1,2,0:T(8,128)}, u32[]{:S(2)}) copy-start(f32[2,512,144]{1,2,0:T(8,128)} %copy-done.5) | copy-start | bytes 1769476
  128.1 4.1 %copy-start.22 = (f32[1,64]{1,0:T(1,128)S(1)}, f32[1,64]{1,0:T(1,128)}, u32[]{:S(2)}) copy-start(f32[1,64]{1,0:T(1,128)} %get-tuple-element.56) | copy-start | bytes 772

commit v17 on v14

--- a/solution.py
+++ b/solution.py
@@ -198,9 +198,10 @@
             device_id_type=mesh_id,
         ).wait_recv()
 
-    scores = jnp.zeros((vocab_ref.shape[0] * vocab_ref.shape[2], rows.shape[1]), jnp.float32)
+    scores = jnp.zeros((vocab_ref.shape[0] * vocab_ref.shape[1], rows.shape[1]), jnp.float32)
     for j in range(n):
-        block = vocab_ref[:, j].reshape(scores.shape[0], rows.shape[2])
+        cut = slice(j * rows.shape[2], (j + 1) * rows.shape[2])
+        block = vocab_ref[:, :, cut].reshape(scores.shape[0], rows.shape[2])
         scores = scores + lax.dot_general(
             block, rows[j], (((1,), (1,)), ((), ())),
             preferred_element_type=jnp.float32,
@@ -239,8 +240,8 @@
 
 
 def mp_exchange(attended, low_rank, out_blocks, up_blocks, residual, vocab_blocks, groups):
-    n = vocab_blocks.shape[0]
-    width = out_blocks.shape[1] // n
+    width = residual.shape[1]
+    n = out_blocks.shape[1] // width
     rows_here = attended.shape[0]
     block_rows = rows_here // n
     chains = 8
@@ -327,9 +328,7 @@
     residual = all_rows[:, : widths[0]]
     projected = all_rows[:, widths[0] : widths[0] + widths[1]]
     lowered = all_rows[:, widths[0] + widths[1] :]
-    vocab_blocks = jnp.transpose(
-        vocab_rows.reshape(vocab_rows.shape[0], shards, slice_width), (1, 0, 2)
-    )
+    vocab_blocks = vocab_rows
     heads_here = projected.shape[1] // (2 * FEAT + HD)
     split_heads = jnp.transpose(
         projected.reshape(rows_here, heads_here, 2 * FEAT + HD).astype(jnp.float32), (1, 0, 2)

time: 128 us -> 129 us (level)
  waiting for transfers between devices: 4.46 us -> 6.3 us
    all_to_all x1, waiting for transfers between devices: 4.46 us -> 6.3 us  [on_device(): lax.all_to_all(jnp.concatenate([kept_pages, projected_pages, lowered_page...]
    unnamed x34 -> x30, local copies, waits for them, and re-layouts: 4.7 us -> 4.61 us
  transfers between devices with their start and end apart: 2 -> 2, of which waited for: 1 -> 1; matrix products, arithmetic and copies ran while one was open for 8% -> 7% of each run, Pallas kernels for 0% -> 0%
where the time goes in v17:
time: 129 us
  Pallas kernels  70.3 us (54%)
  local copies, waits for them, and re-layouts  16.6 us (13%)
  matrix products  14.1 us (11%)
  starting transfers between devices  9.79 us (8%)
  other arithmetic  9.32 us (7%)
  waiting for transfers between devices  6.3 us (5%)
  between operations  2.4 us (2%)
    pallas_call x1, Pallas kernels, mp_exchange(): pl.pallas_call(exchange_kernel, out_shape=(jax.ShapeDtypeStruct((rows_her...  70.3 us
    all_to_all x1, starting transfers between devices, on_device(): lax.all_to_all(jnp.concatenate([kept_pages, projected_pages, lowered_page...  7.53 us
    all_to_all x1, waiting for transfers between devices, on_device(): lax.all_to_all(jnp.concatenate([kept_pages, projected_pages, lowered_page...  6.3 us
    unnamed x30, local copies, waits for them, and re-layouts  4.61 us
    dot_general x1, matrix products, on_device(): jnp.einsum('abrd,dc->abrc', normed_pages, qkv_weight, preferred_element_t...  2.8 us
  transfers between devices with their start and end apart: 2, of which 1 were waited for; matrix products, arithmetic and copies ran while one was open for 7% of the time, Pallas kernels for 0%

profile of v17, /device:TPU:8, one launch (start us, length us, event | category | flops | bytes accessed | tf_op | source)
XLA Modules:
  0.0 128.9 jit_solution(10461941938418082542)
XLA Ops:
  0.6 0.0 copy-start
  0.7 0.9 reshape.267
  1.6 0.1 copy.45
  1.7 1.0 sort.17
  2.7 0.1 copy.46
  2.8 0.1 reshape.289
  2.9 0.8 gather_fusion.2
  3.7 0.1 reshape.292
  3.8 0.1 copy.47
  3.9 0.1 copy.48
  4.0 0.1 reshape.275
  4.1 1.9 %gather_fusion = bf16[64,8,1792]{2,1,0:T(8,128)(2,1)} fusion(bf16[64,8,1792]{2,1,0:T(8,128)(2,1)S(1)} %bitcast.51, s32[1024]{0:T(1024)S(1)} %pad_clamp_fusion.1), kind=kCustom, calls=%fused_computation | custom fusion | bytes 3670272 | tf_op jit(solution)/shard_map/gather | solution.py:302
  6.1 2.0 %fusion = f32[32,2,8]{2,1,0:T(2,128)S(1)} fusion(bf16[32,2,8,1792]{3,2,1,0:T(8,128)(2,1)} %bitcast.52), kind=kLoop, calls=%fused_computation.5 | loop fusion | flops 2752000 | bytes 1837056 | tf_op jit(solution)/shard_map/reduce_sum | solution.py:25
  8.1 0.1 copy.49
  8.2 0.1 copy.50
  8.3 2.8 %fusion.7 = bf16[32,2,8,288]{3,2,1,0:T(8,128)(2,1)S(1)} fusion(bf16[32,2,8,1792]{3,2,1,0:T(8,128)(2,1)} %bitcast.53, f32[1792]{0:T(1024)S(1)} %copy-done.13, f32[32,2,8]{2,1,0:T(2,128)S(1)} %copy.50, bf16[1792,288]{0,1:T(8,128)(2,1)S(1)} %copy-done.11), kind=kOutput, calls=%fused_computation.12 | convolution fusion | flops 532299776 | bytes 3171328 | tf_op jit(solution)/shard_map/abrd,dc->abrc/dot_general | solution.py:304
  11.2 0.7 fusion.14
  11.9 0.0 copy-start.9
  11.9 0.0 copy-start.10
  11.9 1.1 constant_dynamic-slice_fusion.1
  13.1 1.1 pad_maximum_fusion.6
  14.2 7.5 %all-to-all-start = ((bf16[32,2,8,640]{3,2,1,0:T(8,128)(2,1)}), bf16[32,2,8,640]{3,2,1,0:T(8,128)(2,1)S(1)}, u32[]{:S(2)}, u32[]{:S(2)}) async-start(bf16[32,2,8,640]{3,2,1,0:T(8,128)(2,1)} %pad_maximum_fusion.6), calls=%async_computation | async-start | bytes 1310720 | tf_op jit(solution)/shard_map/all_to_all | solution.py:312
  21.7 0.1 fusion.42
  21.8 0.1 reduce_window_sum.11
  21.9 0.2 select_reduce_fusion.2
  22.1 0.6 slice.80
  22.7 0.6 compare_convert_fusion.1
  23.4 0.2 select_reduce_fusion
  23.6 0.1 select_reduce_fusion.1
  24.4 1.3 fusion.34
  25.7 1.2 fusion.31
  26.8 6.3 %all-to-all-done = bf16[32,2,8,640]{3,2,1,0:T(8,128)(2,1)S(1)} async-done(((bf16[32,2,8,640]{3,2,1,0:T(8,128)(2,1)}), bf16[32,2,8,640]{3,2,1,0:T(8,128)(2,1)S(1)}, u32[]{:S(2)}, u32[]{:S(2)}) %all-to-all-start) | async-done | bytes 655392 | tf_op jit(solution)/shard_map/all_to_all | solution.py:312
  33.1 0.7 gather_fusion.1
  33.8 0.2 slice.97
  34.0 0.2 copy.51
  34.2 0.1 transpose.43
  34.3 1.8 %fusion.43 = f32[2,512,512]{1,2,0:T(8,128)} fusion(bf16[2,512,144]{1,2,0:T(8,128)(2,1)S(1)} %bitcast.59), kind=kOutput, calls=%fused_computation.66 | convolution fusion | flops 16777216 | bytes 2129920 | tf_op jit(solution)/shard_map/while/body/eval_jaxpr/hcf,hdf->hcd/dot_general | solution.py:59
  36.2 0.7 slice.108.resid_ref
  36.9 0.1 multiply_multiply_fusion.1
  37.1 0.9 copy-done.3
  38.0 1.3 %fusion.17 = bf16[2,273,113]{2,1,0:T(8,128)(2,1)S(1)} fusion(f32[2,512,256]{1,2,0:T(8,128)S(1)} %bitcast.69, f32[2,512,16]{1,2,0:T(8,128)S(1)} %get-tuple-element.72, f32[273]{0:T(512)S(1)} %pad.13.clone, f32[512]{0:T(512)S(1)} %compare_convert_fusion.1, f32[2,512,112]{1,2,0:T(8,128)S(1)} %slice.102), kind=kOutput, calls=%fused_computation.22 | convolution fusion | flops 379911168 | bytes 1699400 | tf_op jit(solution)/shard_map/hcp,hce->hpe/dot_general | solution.py:346
  39.3 0.7 pad.9
  40.0 1.3 scatter.4
  41.3 2.3 %collective-permute-start = (bf16[2,274,113]{2,1,0:T(8,128)(2,1)}, bf16[2,274,113]{2,1,0:T(8,128)(2,1)S(1)}, u32[]{:S(2)}, u32[]{:S(2)}) collective-permute-start(bf16[2,274,113]{2,1,0:T(8,128)(2,1)} %scatter.4), channel_id=1, source_target_pairs={{0,8},{8,16},{16,24},{24,32},{32,40},{40,48},{48,56},{56,64},{64,7... | collective-permute-start | bytes 371552 | tf_op jit(solution)/shard_map/ppermute | solution.py:20
  43.6 0.1 multiply_multiply_fusion
  43.7 2.0 %fusion.58 = (f32[2,512]{1,0:T(2,128)S(1)}, f32[2,512,512]{1,2,0:T(8,128)S(1)}) fusion(f32[512,512]{0,1:T(8,128)} %fusion.31, bf16[2,512,144]{1,2,0:T(8,128)(2,1)S(1)} %bitcast.60), kind=kOutput, calls=%fused_computation.108 | convolution fusion | flops 20446208 | bytes 3215360 | tf_op jit(solution)/shard_map/while/body/eval_jaxpr/hcf,hdf->hcd/dot_general | solution.py:49
  45.7 0.8 fusion.37
  46.6 0.7 copy-done.2
  47.3 0.8 multiply_reduce_fusion
  48.1 0.8 compare_select_fusion.low_ref
  48.9 0.3 slice_reduce_fusion
  49.2 0.1 fusion.35
  49.3 0.9 fusion.13
  50.2 0.4 convolution_multiply_fusion.2
  50.6 0.1 slice_reduce_fusion.2
  50.8 0.5 slice.103
  51.9 0.3 slice_reduce_fusion.1
  52.2 0.7 fusion.23
  52.9 0.9 fusion.12
  53.8 0.8 copy.53.att_ref
  54.6 70.3 %shard_map.130 = (bf16[512,224]{1,0:T(8,128)(2,1)}, f32[1,64]{1,0:T(1,128)}) custom-call(bf16[512,224]{1,0:T(8,128)(2,1)} %copy.53.att_ref, bf16[512,128]{1,0:T(8,128)(2,1)} %compare_select_fusion.low_ref, bf16[224,1792]{1,0:T(8,128)(2,1)} %w_ref.1, bf16[128,1792]{1,0:T(8,128)(2,1)} %u_ref.1, bf16[512,224]{1,0:T(8,128)(2,1)} %slice.108.resid_ref, ...), custom_call_target="tpu_custom_call" | custom-call | tf_op jit(solution)/shard_map/pallas_call | solution.py:249
  125.0 1.8 %copy.54 = bf16[512,224]{0,1:T(8,128)(2,1)} copy(bf16[512,224]{1,0:T(8,128)(2,1)} %get-tuple-element.69) | data formatting | bytes 458752
  126.8 1.0 fusion.20
  127.8 1.1 copy.63
  (44 shorter events, 0.3 us)
Async XLA Ops:
  0.6 3.5 %copy-start = (bf16[512,1792]{1,0:T(8,128)(2,1)S(1)}, bf16[512,1792]{1,0:T(8,128)(2,1)}, u32[]{:S(2)}) copy-start(bf16[512,1792]{1,0:T(8,128)(2,1)} %param.13) | copy-start | bytes 5505028
  6.1 2.2 %copy-start.11 = (bf16[1792,288]{0,1:T(8,128)(2,1)S(1)}, bf16[1792,288]{0,1:T(8,128)(2,1)}, u32[]{:S(2)}) copy-start(bf16[1792,288]{0,1:T(8,128)(2,1)} %param.15) | copy-start | bytes 3096580
  6.1 2.2 %copy-start.13 = (f32[1792]{0:T(1024)S(1)}, f32[1792]{0:T(1024)}, u32[]{:S(2)}) copy-start(f32[1792]{0:T(1024)} %param.14) | copy-start | bytes 21508
  8.3 2.8 %copy-start.1 = (bf16[64,8,1792]{2,1,0:T(8,128)(2,1)S(1)}, bf16[64,8,1792]{2,1,0:T(8,128)(2,1)}, u32[]{:S(2)}) copy-start(bf16[64,8,1792]{2,1,0:T(8,128)(2,1)} %gather_fusion) | copy-start | bytes 5505028
  8.3 2.8 %copy-start.12 = (bf16[1792,128]{1,0:T(8,128)(2,1)S(1)}, bf16[1792,128]{1,0:T(8,128)(2,1)}, u32[]{:S(2)}) copy-start(bf16[1792,128]{1,0:T(8,128)(2,1)} %param.17) | copy-start | bytes 1376260
  11.9 10.2 %copy-start.6 = (s32[512]{0:T(512)S(1)}, s32[512]{0:T(512)}, u32[]{:S(2)}) copy-start(s32[512]{0:T(512)} %param.20) | copy-start | bytes 6148
  11.9 11.5 %copy-start.9 = (s32[128]{0:T(128)S(1)}, s32[128]{0:T(128)}, u32[]{:S(2)}) copy-start(s32[128]{0:T(128)} %param.21) | copy-start | bytes 1540
  11.9 11.7 %copy-start.10 = (s32[64]{0:T(128)S(1)}, s32[64]{0:T(128)}, u32[]{:S(2)}) copy-start(s32[64]{0:T(128)} %param.22) | copy-start | bytes 772
  14.2 19.0 %all-to-all-start = ((bf16[32,2,8,640]{3,2,1,0:T(8,128)(2,1)}), bf16[32,2,8,640]{3,2,1,0:T(8,128)(2,1)S(1)}, u32[]{:S(2)}, u32[]{:S(2)}) async-start(bf16[32,2,8,640]{3,2,1,0:T(8,128)(2,1)} %pad_maximum_fusion.6), calls=%async_computation | async-start | bytes 1310720 | tf_op jit(solution)/shard_map/all_to_all | solution.py:312
  37.0 1.0 copy-start.3
  37.1 2.9 %copy-start.7 = (f32[2,512,16]{1,2,0:T(8,128)}, f32[2,512,16]{1,2,0:T(8,128)S(1)}, u32[]{:S(2)}) copy-start(f32[2,512,16]{1,2,0:T(8,128)S(1)} %get-tuple-element.72) | copy-start | bytes 196612
  41.3 7.6 %collective-permute-start = (bf16[2,274,113]{2,1,0:T(8,128)(2,1)}, bf16[2,274,113]{2,1,0:T(8,128)(2,1)S(1)}, u32[]{:S(2)}, u32[]{:S(2)}) collective-permute-start(bf16[2,274,113]{2,1,0:T(8,128)(2,1)} %scatter.4), channel_id=1, source_target_pairs={{0,8},{8,16},{16,24},{24,32},{32,40},{40,48},{48,56},{56,64},{64,7... | collective-permute-start | bytes 371552 | tf_op jit(solution)/shard_map/ppermute | solution.py:20
  43.7 2.9 %copy-start.5 = (f32[512,512]{0,1:T(8,128)S(1)}, f32[512,512]{0,1:T(8,128)}, u32[]{:S(2)}) copy-start(f32[512,512]{0,1:T(8,128)} %get-tuple-element.79) | copy-start | bytes 3145732
  45.7 1.6 %copy-start.2 = (f32[2,512,512]{1,2,0:T(8,128)S(1)}, f32[2,512,512]{1,2,0:T(8,128)}, u32[]{:S(2)}) copy-start(f32[2,512,512]{1,2,0:T(8,128)} %fusion.43) | copy-start | bytes 6291460
  47.3 2.0 %copy-start.4 = (f32[2,512,16,16]{1,3,2,0:T(8,128)S(1)}, f32[2,512,16,16]{1,3,2,0:T(8,128)}, u32[]{:S(2)}) copy-start(f32[2,512,16,16]{1,3,2,0:T(8,128)} %copy-done.3) | copy-start | bytes 3145732
  47.3 2.0 %copy-start.8 = (f32[2,512,16]{1,2,0:T(8,128)S(1)}, f32[2,512,16]{1,2,0:T(8,128)}, u32[]{:S(2)}) copy-start(f32[2,512,16]{1,2,0:T(8,128)} %copy-done.7) | copy-start | bytes 196612

commit v18 on v14

--- a/solution.py
+++ b/solution.py
@@ -149,21 +149,23 @@
         return parts[chunk, span].astype(jnp.float32)
 
     pending = [None] * len(chains)
+    issued = []
     for step in range(n - 1):
         for chain in range(len(chains)):
             chunk = rs_chunk(chain, step)
             if step == 0:
                 acc[chain, step] = part(chunk, spans[chain]).astype(acc.dtype)
             else:
-                pending[chain].wait()
+                pending[chain].wait_recv()
                 acc[chain, step] = (
                     land[chain, step - 1].astype(jnp.float32) + part(chunk, spans[chain])
                 ).astype(acc.dtype)
             src = acc.at[chain, step]
             pending[chain] = ring_copy(0, chain, step, src, land.at[chain, step])
             pending[chain].start()
+            issued.append(pending[chain])
     for chain in range(len(chains)):
-        pending[chain].wait()
+        pending[chain].wait_recv()
         total = land[chain, n - 2].astype(jnp.float32) + part(me, spans[chain])
         update = total.astype(upd_ref.dtype)
         upd_ref[spans[chain]] = update
@@ -173,17 +175,21 @@
         view = rows.at[me, spans[chain]]
         pending[chain] = ring_copy(1, chain, 0, view, view)
         pending[chain].start()
+        issued.append(pending[chain])
 
     for step in range(1, n - 1):
         for chain in range(len(chains)):
-            pending[chain].wait()
+            pending[chain].wait_recv()
             way = chains[chain][0]
             chunk = lax.rem(me + (n - step if way == 0 else step), n)
             view = rows.at[chunk, spans[chain]]
             pending[chain] = ring_copy(1, chain, step, view, view)
             pending[chain].start()
+            issued.append(pending[chain])
     for chain in range(len(chains)):
-        pending[chain].wait()
+        pending[chain].wait_recv()
+    for copy in issued:
+        copy.wait_send()
 
     own_vocab.wait()
     for copy in vocab_sent:

time: 128 us -> 128 us (level)
  no operation moved by 1% of the time
where the time goes in v18:
time: 128 us; the launch traced here: 127 us
  Pallas kernels  70.5 us (55%)
  local copies, waits for them, and re-layouts  15.6 us (12%)
  matrix products  14.4 us (11%)
  other arithmetic  10.3 us (8%)
  starting transfers between devices  9.8 us (8%)
  waiting for transfers between devices  4.46 us (3%)
  between operations  2.41 us (2%)
    pallas_call x1, Pallas kernels, mp_exchange(): pl.pallas_call(exchange_kernel, out_shape=(jax.ShapeDtypeStruct((rows_her...  70.5 us
    all_to_all x1, starting transfers between devices, on_device(): lax.all_to_all(jnp.concatenate([kept_pages, projected_pages, lowered_page...  7.54 us
    unnamed x34, local copies, waits for them, and re-layouts  4.7 us
    all_to_all x1, waiting for transfers between devices, on_device(): lax.all_to_all(jnp.concatenate([kept_pages, projected_pages, lowered_page...  4.46 us
    dot_general x1, matrix products, on_device(): jnp.einsum('abrd,dc->abrc', normed_pages, qkv_weight, preferred_element_t...  3.07 us
  transfers between devices with their start and end apart: 2, of which 1 were waited for; matrix products, arithmetic and copies ran while one was open for 8% of the time, Pallas kernels for 0%

profile of v18, /device:TPU:8, one launch (start us, length us, event | category | flops | bytes accessed | tf_op | source)
XLA Modules:
  0.0 127.5 jit_solution(1018629487176655444)
XLA Ops:
  0.6 0.0 copy-start
  0.7 0.9 reshape.270
  1.6 0.1 copy.48
  1.7 1.0 sort.17
  2.7 0.1 copy.49
  2.8 0.1 reshape.293
  2.9 0.8 gather_fusion.2
  3.7 0.1 reshape.296
  3.8 0.1 copy.50
  3.9 0.1 copy.51
  4.0 0.1 reshape.279
  4.1 1.9 %gather_fusion = bf16[64,8,1792]{2,1,0:T(8,128)(2,1)} fusion(bf16[64,8,1792]{2,1,0:T(8,128)(2,1)S(1)} %bitcast.54, s32[1024]{0:T(1024)S(1)} %pad_clamp_fusion.1), kind=kCustom, calls=%fused_computation | custom fusion | bytes 3670272 | tf_op jit(solution)/shard_map/gather | solution.py:307
  6.1 2.0 %fusion = f32[32,2,8]{2,1,0:T(2,128)S(1)} fusion(bf16[32,2,8,1792]{3,2,1,0:T(8,128)(2,1)} %bitcast.55), kind=kLoop, calls=%fused_computation.5 | loop fusion | flops 2752000 | bytes 1837056 | tf_op jit(solution)/shard_map/reduce_sum | solution.py:25
  8.0 0.1 copy.52
  8.1 0.1 copy.53
  8.2 0.0 copy-start.14
  8.2 3.1 %fusion.7 = bf16[32,2,8,288]{3,2,1,0:T(8,128)(2,1)S(1)} fusion(bf16[32,2,8,1792]{3,2,1,0:T(8,128)(2,1)} %bitcast.56, f32[1792]{0:T(1024)S(1)} %copy-done.15, f32[32,2,8]{2,1,0:T(2,128)S(1)} %copy.53, bf16[1792,288]{0,1:T(8,128)(2,1)} %param.15), kind=kOutput, calls=%fused_computation.12 | convolution fusion | flops 532299776 | bytes 3171328 | tf_op jit(solution)/shard_map/abrd,dc->abrc/dot_general | solution.py:309
  11.3 0.7 fusion.14
  12.1 1.2 constant_dynamic-slice_fusion.1
  13.3 1.1 pad_maximum_fusion.6
  14.4 7.5 %all-to-all-start = ((bf16[32,2,8,640]{3,2,1,0:T(8,128)(2,1)}), bf16[32,2,8,640]{3,2,1,0:T(8,128)(2,1)S(1)}, u32[]{:S(2)}, u32[]{:S(2)}) async-start(bf16[32,2,8,640]{3,2,1,0:T(8,128)(2,1)} %pad_maximum_fusion.6), calls=%async_computation | async-start | bytes 1310720 | tf_op jit(solution)/shard_map/all_to_all | solution.py:317
  22.0 0.1 fusion.42
  22.0 0.1 reduce_window_sum.11
  22.1 0.2 select_reduce_fusion.2
  22.3 0.6 slice.80
  22.9 1.2 compare_convert_fusion.1
  24.1 0.2 select_reduce_fusion
  24.4 0.1 select_reduce_fusion.1
  24.5 0.5 and_select_fusion
  25.7 0.1 reshape.276
  25.8 0.6 copy.66
  26.5 1.3 fusion.34
  27.7 1.2 fusion.31
  28.9 4.5 %all-to-all-done = bf16[32,2,8,640]{3,2,1,0:T(8,128)(2,1)S(1)} async-done(((bf16[32,2,8,640]{3,2,1,0:T(8,128)(2,1)}), bf16[32,2,8,640]{3,2,1,0:T(8,128)(2,1)S(1)}, u32[]{:S(2)}, u32[]{:S(2)}) %all-to-all-start) | async-done | bytes 655392 | tf_op jit(solution)/shard_map/all_to_all | solution.py:317
  33.4 0.7 gather_fusion.1
  34.0 0.2 slice.97
  34.2 0.2 copy.54
  34.4 0.1 transpose.46
  34.6 1.8 %fusion.43 = f32[2,512,512]{1,2,0:T(8,128)} fusion(bf16[2,512,144]{1,2,0:T(8,128)(2,1)S(1)} %bitcast.62), kind=kOutput, calls=%fused_computation.67 | convolution fusion | flops 16777216 | bytes 2129920 | tf_op jit(solution)/shard_map/while/body/eval_jaxpr/hcf,hdf->hcd/dot_general | solution.py:59
  36.4 0.7 slice.108.resid_ref
  37.1 0.1 multiply_multiply_fusion.1
  37.3 0.9 copy-done.3
  38.2 1.3 %fusion.17 = bf16[2,273,113]{2,1,0:T(8,128)(2,1)S(1)} fusion(f32[2,512,256]{1,2,0:T(8,128)S(1)} %bitcast.72, f32[2,512,16]{1,2,0:T(8,128)S(1)} %get-tuple-element.72, f32[273]{0:T(512)S(1)} %pad.13.clone, f32[512]{0:T(512)S(1)} %copy-done.10, f32[2,512,112]{1,2,0:T(8,128)S(1)} %slice.102), kind=kOutput, calls=%fused_computation.22 | convolution fusion | flops 379911168 | bytes 1699400 | tf_op jit(solution)/shard_map/hcp,hce->hpe/dot_general | solution.py:353
  39.6 2.3 %collective-permute-start = (bf16[2,274,113]{2,1,0:T(8,128)(2,1)S(1)}, bf16[2,274,113]{2,1,0:T(8,128)(2,1)S(1)}, u32[]{:S(2)}, u32[]{:S(2)}) collective-permute-start(bf16[2,274,113]{2,1,0:T(8,128)(2,1)S(1)} %scatter.4), channel_id=1, source_target_pairs={{0,8},{8,16},{16,24},{24,32},{32,40},{40,48},{48,56},{56,64},{64,7... | collective-permute-start | bytes 371552 | tf_op jit(solution)/shard_map/ppermute | solution.py:20
  41.9 0.1 multiply_multiply_fusion
  42.1 2.0 %fusion.58 = (f32[2,512]{1,0:T(2,128)S(1)}, f32[2,512,512]{1,2,0:T(8,128)S(1)}) fusion(f32[512,512]{0,1:T(8,128)} %fusion.31, bf16[2,512,144]{1,2,0:T(8,128)(2,1)S(1)} %bitcast.63), kind=kOutput, calls=%fused_computation.109 | convolution fusion | flops 20446208 | bytes 3215360 | tf_op jit(solution)/shard_map/while/body/eval_jaxpr/hcf,hdf->hcd/dot_general | solution.py:49
  44.1 0.9 fusion.37
  45.0 0.7 copy-done.2
  45.7 0.7 multiply_reduce_fusion
  46.5 0.8 compare_select_fusion.low_ref
  47.3 0.3 slice_reduce_fusion
  47.6 0.1 fusion.35
  47.7 0.9 fusion.13
  48.6 0.4 convolution_multiply_fusion.2
  49.0 0.1 slice_reduce_fusion.2
  49.1 0.5 slice.103
  50.3 0.3 slice_reduce_fusion.1
  50.6 0.7 fusion.23
  51.3 0.9 fusion.12
  52.2 0.8 copy.57.att_ref
  53.0 70.5 %shard_map.130 = (bf16[512,224]{1,0:T(8,128)(2,1)}, f32[1,64]{1,0:T(1,128)}) custom-call(bf16[512,224]{1,0:T(8,128)(2,1)} %copy.57.att_ref, bf16[512,128]{1,0:T(8,128)(2,1)} %compare_select_fusion.low_ref, bf16[224,1792]{1,0:T(8,128)(2,1)} %w_ref.1, bf16[128,1792]{1,0:T(8,128)(2,1)} %u_ref.1, bf16[512,224]{1,0:T(8,128)(2,1)} %slice.108.resid_ref, ...), custom_call_target="tpu_custom_call" | custom-call | tf_op jit(solution)/shard_map/pallas_call | solution.py:254
  123.5 1.8 %copy.58 = bf16[512,224]{0,1:T(8,128)(2,1)} copy(bf16[512,224]{1,0:T(8,128)(2,1)} %get-tuple-element.69) | data formatting | bytes 458752
  125.3 1.0 fusion.20
  126.3 1.2 copy.69
  (50 shorter events, 0.4 us)
Async XLA Ops:
  0.6 3.5 %copy-start = (bf16[512,1792]{1,0:T(8,128)(2,1)S(1)}, bf16[512,1792]{1,0:T(8,128)(2,1)}, u32[]{:S(2)}) copy-start(bf16[512,1792]{1,0:T(8,128)(2,1)} %param.13) | copy-start | bytes 5505028
  6.1 2.1 %copy-start.15 = (f32[1792]{0:T(1024)S(1)}, f32[1792]{0:T(1024)}, u32[]{:S(2)}) copy-start(f32[1792]{0:T(1024)} %param.14) | copy-start | bytes 21508
  8.2 3.1 %copy-start.1 = (bf16[64,8,1792]{2,1,0:T(8,128)(2,1)S(1)}, bf16[64,8,1792]{2,1,0:T(8,128)(2,1)}, u32[]{:S(2)}) copy-start(bf16[64,8,1792]{2,1,0:T(8,128)(2,1)} %gather_fusion) | copy-start | bytes 5505028
  8.2 3.1 %copy-start.14 = (bf16[1792,128]{1,0:T(8,128)(2,1)S(1)}, bf16[1792,128]{1,0:T(8,128)(2,1)}, u32[]{:S(2)}) copy-start(bf16[1792,128]{1,0:T(8,128)(2,1)} %param.17) | copy-start | bytes 1376260
  12.0 10.3 %copy-start.8 = (s32[512]{0:T(512)S(1)}, s32[512]{0:T(512)}, u32[]{:S(2)}) copy-start(s32[512]{0:T(512)} %param.20) | copy-start | bytes 6148
  12.1 12.1 %copy-start.12 = (s32[128]{0:T(128)S(1)}, s32[128]{0:T(128)}, u32[]{:S(2)}) copy-start(s32[128]{0:T(128)} %param.21) | copy-start | bytes 1540
  12.1 12.3 %copy-start.13 = (s32[64]{0:T(128)S(1)}, s32[64]{0:T(128)}, u32[]{:S(2)}) copy-start(s32[64]{0:T(128)} %param.22) | copy-start | bytes 772
  12.1 13.6 %copy-start.9 = (bf16[16,1792]{1,0:T(8,128)(2,1)S(1)}, bf16[16,1792]{1,0:T(8,128)(2,1)}, u32[]{:S(2)}) copy-start(bf16[16,1792]{1,0:T(8,128)(2,1)} %param.19) | copy-start | bytes 172036
  14.4 19.0 %all-to-all-start = ((bf16[32,2,8,640]{3,2,1,0:T(8,128)(2,1)}), bf16[32,2,8,640]{3,2,1,0:T(8,128)(2,1)S(1)}, u32[]{:S(2)}, u32[]{:S(2)}) async-start(bf16[32,2,8,640]{3,2,1,0:T(8,128)(2,1)} %pad_maximum_fusion.6), calls=%async_computation | async-start | bytes 1310720 | tf_op jit(solution)/shard_map/all_to_all | solution.py:317
  34.5 2.8 %copy-start.6 = (f32[2,512,144]{1,2,0:T(8,128)}, f32[2,512,144]{1,2,0:T(8,128)S(1)}, u32[]{:S(2)}) copy-start(f32[2,512,144]{1,2,0:T(8,128)S(1)} %transpose.46) | copy-start | bytes 1769476
  34.5 3.7 %copy-start.10 = (f32[512]{0:T(512)S(1)}, f32[512]{0:T(512)}, u32[]{:S(2)}) copy-start(f32[512]{0:T(512)} %compare_convert_fusion.1) | copy-start | bytes 6148
  37.3 1.0 copy-start.3
  39.6 7.6 %collective-permute-start = (bf16[2,274,113]{2,1,0:T(8,128)(2,1)S(1)}, bf16[2,274,113]{2,1,0:T(8,128)(2,1)S(1)}, u32[]{:S(2)}, u32[]{:S(2)}) collective-permute-start(bf16[2,274,113]{2,1,0:T(8,128)(2,1)S(1)} %scatter.4), channel_id=1, source_target_pairs={{0,8},{8,16},{16,24},{24,32},{32,40},{40,48},{48,56},{56,64},{64,7... | collective-permute-start | bytes 371552 | tf_op jit(solution)/shard_map/ppermute | solution.py:20
  42.1 2.9 %copy-start.5 = (f32[512,512]{0,1:T(8,128)S(1)}, f32[512,512]{0,1:T(8,128)}, u32[]{:S(2)}) copy-start(f32[512,512]{0,1:T(8,128)} %get-tuple-element.79) | copy-start | bytes 3145732
  44.1 1.6 %copy-start.2 = (f32[2,512,512]{1,2,0:T(8,128)S(1)}, f32[2,512,512]{1,2,0:T(8,128)}, u32[]{:S(2)}) copy-start(f32[2,512,512]{1,2,0:T(8,128)} %fusion.43) | copy-start | bytes 6291460
  45.7 0.8 copy-start.11
  45.7 2.0 %copy-start.4 = (f32[2,512,16,16]{1,3,2,0:T(8,128)S(1)}, f32[2,512,16,16]{1,3,2,0:T(8,128)}, u32[]{:S(2)}) copy-start(f32[2,512,16,16]{1,3,2,0:T(8,128)} %copy-done.3) | copy-start | bytes 3145732
  45.7 2.0 %copy-start.7 = (f32[2,512,144]{1,2,0:T(8,128)S(1)}, f32[2,512,144]{1,2,0:T(8,128)}, u32[]{:S(2)}) copy-start(f32[2,512,144]{1,2,0:T(8,128)} %copy-done.6) | copy-start | bytes 1769476
